TPU v7x, 512 devices: a whole 4x4x16 slice. The times are simulated.
512 devices in a mesh: frame: 8 (over y, core), row: 8 (over z_lo), col: 8 (over x, z_hi).
Axes of the slice: x: 4, y: 4, z: 16 (z_hi: 2, z_lo: 8; z = z_hi * 8 + z_lo), core: 2. Of those that a mesh axis runs over, the one named last changes fastest.
Arguments:
- frames_in: bfloat16 [32, 64, 64, 1024], P('frame', 'row', None, 'col'), may hold values from -6 to 6
- spatial_weight: bfloat16 [9, 1024, 1024], P(None, ('frame', 'row'), 'col'), may hold values from -0.0625 to 0.0625
- temporal_weight: bfloat16 [3, 1024, 1024], P(None, ('frame', 'row'), 'col'), may hold values from -0.109375 to 0.109375
- spatial_bias: float32 [1024], P('col'), may hold values from -3 to 3
- temporal_bias: float32 [1024], P('col'), may hold values from -3 to 3
- clip_id: int32 [32], replicated, may hold values from 0 to 7, as said below
Outputs:
- block_out: bfloat16 [32, 64, 64, 1024], P('frame', 'row', None, 'col')
Inputs may be any that keep to these rules, and one draw needn't show every extreme that they name: `clip_id`: clip numbers of the frames in order, never falling; each clip has 1 to 7 frames and one has exactly 7.
All inputs are finite; a program needn't handle non-finite values.
Results may differ from a plain program's by a relative error of at most 0.01.
Values may be sent and summed in bfloat16 or wider, within the bound.
A program may use at most 64 MiB of HBM per device.

v0:
```python
import jax
import jax.numpy as jnp
from jax import lax
from jax.sharding import PartitionSpec as P


def with_halo(block, sides, width):
    for axis, dim in sides:
        count = lax.axis_size(axis)
        forward = [(i, i + 1) for i in range(count - 1)]
        backward = [(target, source) for source, target in forward]
        low = lax.ppermute(
            lax.slice_in_dim(block, block.shape[dim] - width, None, axis=dim), axis, forward
        )
        high = lax.ppermute(lax.slice_in_dim(block, 0, width, axis=dim), axis, backward)
        block = jnp.concatenate([low, block, high], axis=dim)
    return block


def spatial_terms(total, gathered, weights):
    row_count = total.shape[1]
    wide = total.shape[2]
    for tap in range(9):
        shift_y, shift_x = (tap // 3, tap % 3)
        window = gathered[:, shift_y : shift_y + row_count, shift_x : shift_x + wide, :]
        total = total + jnp.einsum(
            "fhwc,cd->fhwd", window, weights[tap], preferred_element_type=jnp.float32
        )
    return total


def temporal_terms(sources, weights):
    result = []
    for tap in range(3):
        window = sources[tap]
        result.append(
            jnp.einsum("fhwc,cd->fhwd", window, weights[tap], preferred_element_type=jnp.float32)
        )
    return (result[0], result[1], result[2])


def body(frames_in, spatial_weight, temporal_weight, spatial_bias, temporal_bias, clip_id):
    fr_count, row_count, wide, col_width = frames_in.shape
    rimmed = with_halo(frames_in, (("row", 1),), 1)
    gathered = lax.all_gather(rimmed, "col", axis=3, tiled=True)
    gathered = jnp.pad(gathered, ((0, 0), (0, 0), (1, 1), (0, 0)))
    blank = jnp.zeros((fr_count, row_count, wide, col_width), jnp.float32)
    full_spatial, full_temporal = (
        lax.all_gather(spatial_weight, ("frame", "row"), axis=1, tiled=True),
        lax.all_gather(temporal_weight, ("frame", "row"), axis=1, tiled=True),
    )
    spatial = spatial_terms(blank, gathered, full_spatial)
    hidden = (spatial + spatial_bias).astype(jnp.bfloat16)
    active = jax.nn.silu(hidden.astype(jnp.float32)).astype(jnp.bfloat16)
    index = lax.axis_index("frame")
    edge_ids = jnp.full((1,), -1, jnp.int32)
    padded_ids = jnp.concatenate([edge_ids, clip_id, edge_ids])
    local_ids = lax.dynamic_slice_in_dim(padded_ids, index * fr_count, fr_count + 2)
    prev_ok = (local_ids[1:-1] == local_ids[:-2]).astype(jnp.float32).reshape(fr_count, 1, 1, 1)
    next_ok = (local_ids[1:-1] == local_ids[2:]).astype(jnp.float32).reshape(fr_count, 1, 1, 1)
    source = with_halo(active, (("frame", 0),), 1)
    whole = lax.all_gather(source, "col", axis=3, tiled=True)
    sources = (whole[:-2], whole[1:-1], whole[2:])
    taps = temporal_terms(sources, full_temporal)
    before, after = (taps[0], taps[2])
    total = (
        hidden.astype(jnp.float32) + temporal_bias + prev_ok * before + taps[1] + next_ok * after
    )
    return total.astype(jnp.bfloat16)


def solution(mesh):
    placed = (
        P("frame", "row", None, "col"),
        P(None, ("frame", "row"), "col"),
        P(None, ("frame", "row"), "col"),
        P("col"),
        P("col"),
        P(),
    )
    return jax.shard_map(
        body, mesh=mesh, in_specs=placed, out_specs=P("frame", "row", None, "col"), check_vma=False
    )
```

profile of v0, /device:TPU:266, one launch (start us, length us, event | category | flops | bytes accessed | tf_op | source)
XLA Modules:
  0.0 734.2 jit_solution(9733512047469235792)
XLA Ops:
  7.3 0.9 fusion.65
  8.2 2.9 collective-permute-start
  11.1 1.3 collective-permute-start.1
  13.0 4.3 collective-permute-done.1
  17.3 2.0 pad_maximum_fusion.1
  19.4 142.3 %all-gather.6.cloned.1.call-done = bf16[9,1024,128]{2,1,0:T(8,128)(2,1)} async-done(((bf16[9,16,128]{2,1,0:T(8,128)(2,1)}), bf16[9,1024,128]{2,1,0:T(8,128)(2,1)}) %all-gather.6.cloned.1.call-update) | async-done | bytes 2359312 | tf_op jit(solution)/shard_map/all_gather | solution.py:49
  161.7 175.7 %all-gather.4.cloned.1.call-done = bf16[4,10,64,1024]{3,2,1,0:T(8,128)(2,1)} async-done(((bf16[4,10,64,128]{3,2,1,0:T(8,128)(2,1)}), bf16[4,10,64,1024]{3,2,1,0:T(8,128)(2,1)}) %all-gather.4.cloned.1.call-update) | async-done | bytes 5242896 | tf_op jit(solution)/shard_map/all_gather | solution.py:45
  337.4 3.6 fusion
  341.3 2.2 fusion.2
  343.5 1.3 fusion.4
  344.8 1.3 fusion.55
  346.1 1.3 fusion.56
  347.3 1.3 fusion.57
  348.6 1.3 fusion.6
  349.9 1.3 fusion.8
  351.2 1.9 fusion.54
  353.2 1.9 collective-permute-start.2
  355.1 3.6 collective-permute-start.3
  359.5 1.8 collective-permute-done.3
  361.2 1.0 pad_maximum_fusion
  362.5 355.9 %all_gather.15 = bf16[3,1024,128]{2,1,0:T(8,128)(2,1)S(1)} all-gather(bf16[3,16,128]{2,1,0:T(8,128)(2,1)S(1)} %copy-done.3), channel_id=1, replica_groups=mesh['frame'=8,'row'=8,'col'=8] {'frame','row'}, dimensions={1}, use_global_device_ids=true | all-gather | bytes 798720 | tf_op jit(solution)/shard_map/all_gather | solution.py:50
  718.4 3.6 convolution_multiply_fusion
  722.0 3.4 fusion.19
  725.5 2.1 fusion.50
  (27 shorter events, 2.6 us)
Async XLA Ops:
  6.5 155.2 %all-gather.6.cloned.1.call-start = ((), (), s32[]{:S(2)}) async-start(), calls=%async_computation.1 | async-start | bytes 2396160 | tf_op jit(solution)/shard_map/all_gather | solution.py:49
  7.3 330.2 %all-gather.4.cloned.1.call-start = ((), (), s32[]{:S(2)}) async-start(), calls=%async_computation | async-start | bytes 5898240 | tf_op jit(solution)/shard_map/all_gather | solution.py:45
  8.2 4.8 collective-permute-start
  11.1 6.2 collective-permute-start.1
  19.3 699.1 %all-gather.8.cloned.1.call-start = ((), (), s32[]{:S(2)}) async-start(), calls=%async_computation.2 | async-start | bytes 7077888 | tf_op jit(solution)/shard_map/all_gather | solution.py:62
  337.4 3.8 copy-start
  337.4 6.1 copy-start.2
  348.6 2.6 copy-start.5
  351.1 11.1 %copy-start.6 = (s32[32]{0:T(128)S(1)}, s32[32]{0:T(128)}, u32[]{:S(2)}) copy-start(s32[32]{0:T(128)} %param.11) | copy-start | bytes 388
  351.2 11.3 %copy-start.3 = (bf16[3,16,128]{2,1,0:T(8,128)(2,1)S(1)}, bf16[3,16,128]{2,1,0:T(8,128)(2,1)}, u32[]{:S(2)}) copy-start(bf16[3,16,128]{2,1,0:T(8,128)(2,1)} %param.8) | copy-start | bytes 36868
  353.1 368.9 %copy-start.4 = (f32[128]{0:T(128)S(1)}, f32[128]{0:T(128)}, u32[]{:S(2)}) copy-start(f32[128]{0:T(128)} %param.10) | copy-start | bytes 1540
  353.2 6.3 collective-permute-start.2
  355.1 6.1 collective-permute-start.3
  718.4 7.1 copy-start.1
Sparse Core Ops, SparseCore 0:
  9.4 152.2 all-gather.5
  164.8 172.6 all-gather.3
  362.4 233.3 all-gather.7
where the time goes:
time: 734 us
  blocking collectives  356 us (49%)
  waiting for transfers between devices  326 us (44%)
  matrix products  24.6 us (3%)
  between operations  13.3 us (2%)
  starting transfers between devices  9.86 us (1%)
    all_gather x1, blocking collectives, body(): lax.all_gather(temporal_weight, ('frame', 'row'), axis=1, tiled=True)  356 us
    all_gather x1, waiting for transfers between devices, body(): gathered = lax.all_gather(rimmed, 'col', axis=3, tiled=True)  176 us
    all_gather x1, waiting for transfers between devices, body(): lax.all_gather(spatial_weight, ('frame', 'row'), axis=1, tiled=True)  142 us
    dot_general x9, matrix products, spatial_terms(): jnp.einsum('fhwc,cd->fhwd', window, weights[tap], preferred_element_type=...  15.4 us
  transfers between devices with their start and end apart: 7, of which 6 were waited for; matrix products, arithmetic and copies ran while one was open for 0% of the time, Pallas kernels for 0%

commit v1 on v0

v1 whole, which is shorter than its diff:
```python
import jax
import jax.numpy as jnp
from jax import lax
from jax.sharding import Mesh
from jax.sharding import PartitionSpec as P

FRAME = ("fy", "fc")
COL = ("cx", "cz")


def shift_halo(block, axis, count, dim, width):
    forward = [(i, i + 1) for i in range(count - 1)]
    backward = [(target, source) for source, target in forward]
    low = lax.ppermute(
        lax.slice_in_dim(block, block.shape[dim] - width, None, axis=dim), axis, forward
    )
    high = lax.ppermute(lax.slice_in_dim(block, 0, width, axis=dim), axis, backward)
    return jnp.concatenate([low, block, high], axis=dim)


def col_gather(block):
    partner = lax.ppermute(block, "cz", [(0, 1), (1, 0)])
    first = lax.axis_index("cz") == 0
    pair = jnp.where(
        first,
        jnp.concatenate([block, partner], axis=3),
        jnp.concatenate([partner, block], axis=3),
    )
    return lax.all_gather(pair, "cx", axis=3, tiled=True)


def weight_gather(weight):
    inner = lax.all_gather(weight, "row", axis=1, tiled=True)
    return lax.all_gather(inner, FRAME, axis=1, tiled=True)


def spatial_terms(total, gathered, weights):
    row_count = total.shape[1]
    wide = total.shape[2]
    for tap in range(9):
        shift_y, shift_x = (tap // 3, tap % 3)
        window = gathered[:, shift_y : shift_y + row_count, shift_x : shift_x + wide, :]
        total = total + jnp.einsum(
            "fhwc,cd->fhwd", window, weights[tap], preferred_element_type=jnp.float32
        )
    return total


def body(frames_in, spatial_weight, temporal_weight, spatial_bias, temporal_bias, clip_id):
    fr_count, row_count, wide, col_width = frames_in.shape
    full_spatial = weight_gather(spatial_weight)
    full_temporal = weight_gather(temporal_weight)
    rimmed = shift_halo(frames_in, "row", lax.axis_size("row"), 1, 1)
    gathered = col_gather(rimmed)
    gathered = jnp.pad(gathered, ((0, 0), (0, 0), (1, 1), (0, 0)))
    gathered, full_spatial, full_temporal = lax.optimization_barrier(
        (gathered, full_spatial, full_temporal)
    )
    blank = jnp.zeros((fr_count, row_count, wide, col_width), jnp.float32)
    spatial = spatial_terms(blank, gathered, full_spatial)
    hidden = (spatial + spatial_bias).astype(jnp.bfloat16)
    active = jax.nn.silu(hidden.astype(jnp.float32)).astype(jnp.bfloat16)
    index = lax.axis_index(FRAME)
    edge_ids = jnp.full((1,), -1, jnp.int32)
    padded_ids = jnp.concatenate([edge_ids, clip_id, edge_ids])
    local_ids = lax.dynamic_slice_in_dim(padded_ids, index * fr_count, fr_count + 2)
    prev_ok = (local_ids[1:-1] == local_ids[:-2]).astype(jnp.float32).reshape(fr_count, 1, 1, 1)
    next_ok = (local_ids[1:-1] == local_ids[2:]).astype(jnp.float32).reshape(fr_count, 1, 1, 1)
    source = shift_halo(active, FRAME, lax.axis_size(FRAME), 0, 1)
    whole = col_gather(source)
    taps = [
        jnp.einsum(
            "fhwc,cd->fhwd",
            whole[tap : tap + fr_count],
            full_temporal[tap],
            preferred_element_type=jnp.float32,
        )
        for tap in range(3)
    ]
    total = (
        hidden.astype(jnp.float32) + temporal_bias + prev_ok * taps[0] + taps[1] + next_ok * taps[2]
    )
    return total.astype(jnp.bfloat16)


def solution(mesh):
    frame_n, row_n, col_n = mesh.devices.shape
    fine = Mesh(
        mesh.devices.reshape(frame_n // 2, 2, row_n, col_n // 2, 2),
        ("fy", "fc", "row", "cx", "cz"),
    )
    act = P(FRAME, "row", None, COL)
    weight = P(None, FRAME + ("row",), COL)
    placed = (act, weight, weight, P(COL), P(COL), P())
    return jax.shard_map(body, mesh=fine, in_specs=placed, out_specs=act, check_vma=False)
```

time: 734 us -> 398 us (0.54)
  the two profiles are of different devices: /device:TPU:266 before, /device:TPU:1 now
where the time goes in v1:
time: 398 us; the launch traced here: 397 us
  waiting for transfers between devices  160 us (40%)
  blocking collectives  152 us (38%)
  starting transfers between devices  33.7 us (8%)
  matrix products  23.6 us (6%)
  between operations  13.3 us (3%)
  local copies, waits for them, and re-layouts  11.8 us (3%)
    all_gather x2, blocking collectives, weight_gather(): inner = lax.all_gather(weight, 'row', axis=1, tiled=True)  124 us
    ppermute x2, waiting for transfers between devices, col_gather(): partner = lax.ppermute(block, 'cz', [(0, 1), (1, 0)])  76.8 us
    all_gather x2, waiting for transfers between devices, col_gather(): return lax.all_gather(pair, 'cx', axis=3, tiled=True)  75.9 us
    all_gather x1, blocking collectives, weight_gather(): return lax.all_gather(inner, FRAME, axis=1, tiled=True)  28 us
    ppermute x2, starting transfers between devices, col_gather(): partner = lax.ppermute(block, 'cz', [(0, 1), (1, 0)])  23.2 us
    dot_general x9, matrix products, spatial_terms(): jnp.einsum('fhwc,cd->fhwd', window, weights[tap], preferred_element_type=...  14.4 us
    dot_general x3, matrix products, body(): jnp.einsum('fhwc,cd->fhwd', whole[tap:tap + fr_count], full_temporal[tap]...  9.19 us
    pad x1, local copies, waits for them, and re-layouts, body(): gathered = jnp.pad(gathered, ((0, 0), (0, 0), (1, 1), (0, 0)))  8.54 us
  transfers between devices with their start and end apart: 9, of which 5 were waited for; matrix products, arithmetic and copies ran while one was open for 2% of the time, Pallas kernels for 0%

profile of v1, /device:TPU:1, one launch (start us, length us, event | category | flops | bytes accessed | tf_op | source)
XLA Modules:
  0.0 397.3 jit_solution(8176659953057499680)
XLA Ops:
  7.4 4.4 %collective-permute-start = (bf16[4,1,64,128]{3,2,1,0:T(8,128)(2,1)S(1)}, bf16[4,1,64,128]{3,2,1,0:T(8,128)(2,1)S(1)}, u32[]{:S(2)}, u32[]{:S(2)}) collective-permute-start(bf16[4,1,64,128]{3,2,1,0:T(8,128)(2,1)S(1)} %get-tuple-element.14), channel_id=1, source_target_pairs={{0,8},{8,16},{16,24},{24,32},{32,40},{40,48},{48,56},{1,9},{9,17},... | collective-permute-start | bytes 196616 | tf_op jit(solution)/shard_map/ppermute | solution.py:14
  11.8 1.3 collective-permute-start.1
  14.3 2.8 collective-permute-done.1
  17.0 14.4 %collective-permute-start.2 = (bf16[4,10,64,128]{3,2,1,0:T(8,128)(2,1)S(1)}, bf16[4,10,64,128]{3,2,1,0:T(8,128)(2,1)S(1)}, u32[]{:S(2)}, u32[]{:S(2)}) collective-permute-start(bf16[4,10,64,128]{3,2,1,0:T(8,128)(2,1)S(1)} %constant_dynamic-update-slice_fusion), channel_id=1, source_target_pairs={{0,1},{1,0},{2,3},{3,2},{4,5},{5,4},{6,7},{7,6},{8,9},{9,8},{10,11... | collective-permute-start | bytes 1966088 | tf_op jit(solution)/shard_map/ppermute | solution.py:22
  31.4 16.3 %collective-permute-done.2 = bf16[4,10,64,128]{3,2,1,0:T(8,128)(2,1)S(1)} collective-permute-done((bf16[4,10,64,128]{3,2,1,0:T(8,128)(2,1)S(1)}, bf16[4,10,64,128]{3,2,1,0:T(8,128)(2,1)S(1)}, u32[]{:S(2)}, u32[]{:S(2)}) %collective-permute-start.2) | collective-permute-done | bytes 655392 | tf_op jit(solution)/shard_map/ppermute | solution.py:22
  47.7 1.7 maximum_select_fusion.1
  49.5 83.2 %all_gather.19 = bf16[9,128,128]{2,1,0:T(8,128)(2,1)} all-gather(bf16[9,16,128]{2,1,0:T(8,128)(2,1)S(1)} %copy-done.3), channel_id=1, replica_groups=mesh['fy'=4,'fc'=2,'row'=8,'cx'=4,'cz'=2] {'row'}, dimensions={1}, use_global_device_ids=true | all-gather | bytes 331776 | tf_op jit(solution)/shard_map/all_gather | solution.py:33
  132.8 40.3 %all_gather.21 = bf16[3,128,128]{2,1,0:T(8,128)(2,1)S(1)} all-gather(bf16[3,16,128]{2,1,0:T(8,128)(2,1)S(1)} %copy-done.4), channel_id=1, replica_groups=mesh['fy'=4,'fc'=2,'row'=8,'cx'=4,'cz'=2] {'row'}, dimensions={1}, use_global_device_ids=true | all-gather | bytes 110592 | tf_op jit(solution)/shard_map/all_gather | solution.py:33
  173.1 28.0 %all_gather.22 = bf16[3,1024,128]{2,1,0:T(8,128)(2,1)S(1)} all-gather(bf16[3,128,128]{2,1,0:T(8,128)(2,1)S(1)} %all_gather.21), channel_id=1, replica_groups=mesh['fy'=4,'fc'=2,'row'=8,'cx'=4,'cz'=2] {'fy','fc'}, dimensions={1}, use_global_device_ids=true | all-gather | bytes 884736 | tf_op jit(solution)/shard_map/all_gather | solution.py:34
  201.1 8.5 %pad.4 = bf16[4,10,66,1024]{3,2,1,0:T(8,128)(2,1)} pad(bf16[4,10,64,1024]{3,2,1,0:T(8,128)(2,1)} %all-gather.4.cloned.1.call-done, bf16[]{:T(256)} %constant.9.clone.1), padding=0_0x0_0x1_1x0_0 | pad | bytes 10649602 | tf_op jit(solution)/shard_map/jit(_pad)/pad | solution.py:55
  209.6 3.8 fusion.14
  219.7 1.3 fusion
  221.0 1.5 fusion.36
  223.8 1.4 fusion.55
  225.2 2.8 collective-permute-start.3
  228.1 1.9 collective-permute-start.4
  230.0 4.3 %collective-permute-done.4 = bf16[1,8,64,128]{3,2,1,0:T(8,128)(2,1)S(1)} collective-permute-done((bf16[1,8,64,128]{3,2,1,0:T(8,128)(2,1)S(1)}, bf16[1,8,64,128]{3,2,1,0:T(8,128)(2,1)S(1)}, u32[]{:S(2)}, u32[]{:S(2)}) %collective-permute-start.4) | collective-permute-done | bytes 131104 | tf_op jit(solution)/shard_map/ppermute | solution.py:17
  234.4 8.8 %collective-permute-start.5 = (bf16[6,8,64,128]{3,2,1,0:T(8,128)(2,1)S(1)}, bf16[6,8,64,128]{3,2,1,0:T(8,128)(2,1)S(1)}, u32[]{:S(2)}, u32[]{:S(2)}) collective-permute-start(bf16[6,8,64,128]{3,2,1,0:T(8,128)(2,1)S(1)} %pad_maximum_fusion), channel_id=1, source_target_pairs={{0,1},{1,0},{2,3},{3,2},{4,5},{5,4},{6,7},{7,6},{8,9},{9,8},{10,11... | collective-permute-start | bytes 2359304 | tf_op jit(solution)/shard_map/ppermute | solution.py:22
  243.3 60.5 %collective-permute-done.5 = bf16[6,8,64,128]{3,2,1,0:T(8,128)(2,1)S(1)} collective-permute-done((bf16[6,8,64,128]{3,2,1,0:T(8,128)(2,1)S(1)}, bf16[6,8,64,128]{3,2,1,0:T(8,128)(2,1)S(1)}, u32[]{:S(2)}, u32[]{:S(2)}) %collective-permute-start.5) | collective-permute-done | bytes 786464 | tf_op jit(solution)/shard_map/ppermute | solution.py:22
  303.8 1.6 maximum_select_fusion
  305.7 75.9 %all-gather.8.cloned.1.call-done = bf16[6,8,64,1024]{3,2,1,0:T(8,128)(2,1)} async-done(((bf16[6,8,64,256]{3,2,1,0:T(8,128)(2,1)}), bf16[6,8,64,1024]{3,2,1,0:T(8,128)(2,1)}) %all-gather.8.cloned.1.call-update) | async-done | bytes 6291472 | tf_op jit(solution)/shard_map/all_gather | solution.py:29
  381.6 3.6 fusion.57
  385.2 3.5 convolution_multiply_fusion
  388.7 2.1 fusion.51
  (40 shorter events, 10.0 us)
Async XLA Ops:
  6.5 42.9 %copy-start.3 = (bf16[9,16,128]{2,1,0:T(8,128)(2,1)S(1)}, bf16[9,16,128]{2,1,0:T(8,128)(2,1)}, u32[]{:S(2)}) copy-start(bf16[9,16,128]{2,1,0:T(8,128)(2,1)} %param.7) | copy-start | bytes 110596
  6.5 126.3 %copy-start.4 = (bf16[3,16,128]{2,1,0:T(8,128)(2,1)S(1)}, bf16[3,16,128]{2,1,0:T(8,128)(2,1)}, u32[]{:S(2)}) copy-start(bf16[3,16,128]{2,1,0:T(8,128)(2,1)} %param.8) | copy-start | bytes 36868
  6.5 194.5 %all-gather.4.cloned.1.call-start = ((), (), s32[]{:S(2)}) async-start(), calls=%async_computation | async-start | bytes 6553600 | tf_op jit(solution)/shard_map/all_gather | solution.py:29
  7.4 5.7 %collective-permute-start = (bf16[4,1,64,128]{3,2,1,0:T(8,128)(2,1)S(1)}, bf16[4,1,64,128]{3,2,1,0:T(8,128)(2,1)S(1)}, u32[]{:S(2)}, u32[]{:S(2)}) collective-permute-start(bf16[4,1,64,128]{3,2,1,0:T(8,128)(2,1)S(1)} %get-tuple-element.14), channel_id=1, source_target_pairs={{0,8},{8,16},{16,24},{24,32},{32,40},{40,48},{48,56},{1,9},{9,17},... | collective-permute-start | bytes 196616 | tf_op jit(solution)/shard_map/ppermute | solution.py:14
  11.8 5.2 %collective-permute-start.1 = (bf16[4,1,64,128]{3,2,1,0:T(8,128)(2,1)S(1)}, bf16[4,1,64,128]{3,2,1,0:T(8,128)(2,1)S(1)}, u32[]{:S(2)}, u32[]{:S(2)}) collective-permute-start(bf16[4,1,64,128]{3,2,1,0:T(8,128)(2,1)S(1)} %get-tuple-element.13), channel_id=1, source_target_pairs={{8,0},{16,8},{24,16},{32,24},{40,32},{48,40},{56,48},{9,1},{17,9},... | collective-permute-start | bytes 196616 | tf_op jit(solution)/shard_map/ppermute | solution.py:17
  17.0 30.7 %collective-permute-start.2 = (bf16[4,10,64,128]{3,2,1,0:T(8,128)(2,1)S(1)}, bf16[4,10,64,128]{3,2,1,0:T(8,128)(2,1)S(1)}, u32[]{:S(2)}, u32[]{:S(2)}) collective-permute-start(bf16[4,10,64,128]{3,2,1,0:T(8,128)(2,1)S(1)} %constant_dynamic-update-slice_fusion), channel_id=1, source_target_pairs={{0,1},{1,0},{2,3},{3,2},{4,5},{5,4},{6,7},{7,6},{8,9},{9,8},{10,11... | collective-permute-start | bytes 1966088 | tf_op jit(solution)/shard_map/ppermute | solution.py:22
  49.4 160.2 %all-gather.6.cloned.1.call-start = ((), (), s32[]{:S(2)}) async-start(), calls=%async_computation.1 | async-start | bytes 2654208 | tf_op jit(solution)/shard_map/all_gather | solution.py:34
  132.7 248.8 %all-gather.8.cloned.1.call-start = ((), (), s32[]{:S(2)}) async-start(), calls=%async_computation.2 | async-start | bytes 7864320 | tf_op jit(solution)/shard_map/all_gather | solution.py:29
  209.6 4.2 %copy-start = (bf16[4,10,66,1024]{3,2,1,0:T(8,128)(2,1)S(1)}, bf16[4,10,66,1024]{3,2,1,0:T(8,128)(2,1)}, u32[]{:S(2)}) copy-start(bf16[4,10,66,1024]{3,2,1,0:T(8,128)(2,1)} %pad.4) | copy-start | bytes 16220164
  209.6 4.9 %copy-start.2 = (bf16[9,1024,128]{2,1,0:T(8,128)(2,1)S(1)}, bf16[9,1024,128]{2,1,0:T(8,128)(2,1)}, u32[]{:S(2)}) copy-start(bf16[9,1024,128]{2,1,0:T(8,128)(2,1)} %all-gather.6.cloned.1.call-done) | copy-start | bytes 7077892
  222.5 1.3 copy-start.6
  225.2 4.8 %collective-permute-start.3 = (bf16[1,8,64,128]{3,2,1,0:T(8,128)(2,1)S(1)}, bf16[1,8,64,128]{3,2,1,0:T(8,128)(2,1)S(1)}, u32[]{:S(2)}, u32[]{:S(2)}) collective-permute-start(bf16[1,8,64,128]{3,2,1,0:T(8,128)(2,1)S(1)} %get-tuple-element.11), channel_id=1, source_target_pairs={{0,64},{64,128},{128,192},{192,256},{256,320},{320,384},{384,448},... | collective-permute-start | bytes 393224 | tf_op jit(solution)/shard_map/ppermute | solution.py:14
  228.0 77.4 %copy-start.7 = (s32[32]{0:T(128)S(1)}, s32[32]{0:T(128)}, u32[]{:S(2)}) copy-start(s32[32]{0:T(128)} %param.11) | copy-start | bytes 388
  228.1 6.3 %collective-permute-start.4 = (bf16[1,8,64,128]{3,2,1,0:T(8,128)(2,1)S(1)}, bf16[1,8,64,128]{3,2,1,0:T(8,128)(2,1)S(1)}, u32[]{:S(2)}, u32[]{:S(2)}) collective-permute-start(bf16[1,8,64,128]{3,2,1,0:T(8,128)(2,1)S(1)} %get-tuple-element.12), channel_id=1, source_target_pairs={{64,0},{128,64},{192,128},{256,192},{320,256},{384,320},{448,384},... | collective-permute-start | bytes 393224 | tf_op jit(solution)/shard_map/ppermute | solution.py:17
  234.4 69.4 %collective-permute-start.5 = (bf16[6,8,64,128]{3,2,1,0:T(8,128)(2,1)S(1)}, bf16[6,8,64,128]{3,2,1,0:T(8,128)(2,1)S(1)}, u32[]{:S(2)}, u32[]{:S(2)}) collective-permute-start(bf16[6,8,64,128]{3,2,1,0:T(8,128)(2,1)S(1)} %pad_maximum_fusion), channel_id=1, source_target_pairs={{0,1},{1,0},{2,3},{3,2},{4,5},{5,4},{6,7},{7,6},{8,9},{9,8},{10,11... | collective-permute-start | bytes 2359304 | tf_op jit(solution)/shard_map/ppermute | solution.py:22
  381.6 7.1 %copy-start.1 = (bf16[6,8,64,1024]{3,2,1,0:T(8,128)(2,1)S(1)}, bf16[6,8,64,1024]{3,2,1,0:T(8,128)(2,1)}, u32[]{:S(2)}) copy-start(bf16[6,8,64,1024]{3,2,1,0:T(8,128)(2,1)} %all-gather.8.cloned.1.call-done) | copy-start | bytes 18874372
  385.2 3.5 copy-start.5
Sparse Core Ops, SparseCore 0:
  49.5 109.2 all-gather.3
  160.9 35.9 all-gather.5
  305.6 75.9 all-gather.7

commit v2 on v1

--- a/solution.py
+++ b/solution.py
@@ -18,20 +18,46 @@
     return jnp.concatenate([low, block, high], axis=dim)
 
 
+def ring_shift(block, axis, count, step):
+    return lax.ppermute(block, axis, [(i, (i + step) % count) for i in range(count)])
+
+
 def col_gather(block):
+    width = block.shape[3]
+    ring = lax.axis_size("cx")
+    me = lax.axis_index("cx")
+    side = lax.axis_index("cz")
     partner = lax.ppermute(block, "cz", [(0, 1), (1, 0)])
-    first = lax.axis_index("cz") == 0
-    pair = jnp.where(
-        first,
-        jnp.concatenate([block, partner], axis=3),
-        jnp.concatenate([partner, block], axis=3),
+    pair = jnp.concatenate([block, partner], axis=3)
+    from_left = ring_shift(pair, "cx", ring, 1)
+    from_right = ring_shift(pair, "cx", ring, -1)
+    far_own = ring_shift(from_right[..., :width], "cx", ring, -1)
+    far_partner = ring_shift(from_left[..., width:], "cx", ring, 1)
+    out = jnp.zeros(block.shape[:3] + (width * 2 * ring,), block.dtype)
+    pieces = (
+        (0, block, partner),
+        (1, from_right[..., :width], from_right[..., width:]),
+        (2, far_own, far_partner),
+        (ring - 1, from_left[..., :width], from_left[..., width:]),
     )
-    return lax.all_gather(pair, "cx", axis=3, tiled=True)
+    for offset, own_side, other_side in pieces:
+        place = (me + offset) % ring
+        out = lax.dynamic_update_slice_in_dim(out, own_side, (2 * place + side) * width, 3)
+        out = lax.dynamic_update_slice_in_dim(out, other_side, (2 * place + 1 - side) * width, 3)
+    return out
 
 
 def weight_gather(weight):
-    inner = lax.all_gather(weight, "row", axis=1, tiled=True)
-    return lax.all_gather(inner, FRAME, axis=1, tiled=True)
+    steps = (("row", 1), ("row", 2), ("row", 4), ("fy", 2), ("fy", 1), ("fc", 1))
+    block = weight
+    for axis, bit in steps:
+        count = lax.axis_size(axis)
+        other = lax.ppermute(block, axis, [(i, i ^ bit) for i in range(count)])
+        high = (lax.axis_index(axis) // bit) % 2 == 1
+        block = jnp.where(high, jnp.stack([other, block]), jnp.stack([block, other]))
+    block = jnp.transpose(block, (6, 2, 1, 0, 3, 4, 5, 7, 8))
+    taps, depth, width = weight.shape
+    return block.reshape(taps, 64 * depth, width)
 
 
 def spatial_terms(total, gathered, weights):
@@ -48,14 +74,11 @@
 
 def body(frames_in, spatial_weight, temporal_weight, spatial_bias, temporal_bias, clip_id):
     fr_count, row_count, wide, col_width = frames_in.shape
-    full_spatial = weight_gather(spatial_weight)
-    full_temporal = weight_gather(temporal_weight)
+    both = weight_gather(jnp.concatenate([spatial_weight, temporal_weight], axis=0))
+    full_spatial, full_temporal = both[:9], both[9:]
     rimmed = shift_halo(frames_in, "row", lax.axis_size("row"), 1, 1)
+    rimmed = jnp.pad(rimmed, ((0, 0), (0, 0), (1, 1), (0, 0)))
     gathered = col_gather(rimmed)
-    gathered = jnp.pad(gathered, ((0, 0), (0, 0), (1, 1), (0, 0)))
-    gathered, full_spatial, full_temporal = lax.optimization_barrier(
-        (gathered, full_spatial, full_temporal)
-    )
     blank = jnp.zeros((fr_count, row_count, wide, col_width), jnp.float32)
     spatial = spatial_terms(blank, gathered, full_spatial)
     hidden = (spatial + spatial_bias).astype(jnp.bfloat16)

time: 398 us -> 392 us (0.985); the launches traced: 397 us -> 387 us
  blocking collectives: 152 us -> 0 us
  waiting for transfers between devices: 160 us -> 219 us
  starting transfers between devices: 33.7 us -> 83.1 us
  local copies, waits for them, and re-layouts: 11.8 us -> 34.8 us
  matrix products: 23.6 us -> 43.8 us
  between operations: 13.3 us -> 0.81 us
    all_gather x3 -> x0, blocking collectives: 152 us -> none  [the longest x2 124 us: weight_gather(): inner = lax.all_gather(weight, 'row', axis=1, tiled=True)]
    ppermute x0 -> x14, waiting for transfers between devices: none -> 151 us  [the longest x6 89.2 us: weight_gather(): other = lax.ppermute(block, axis, [(i, i ^ bit) for i in range(count)])]
    all_gather x3 -> x0, waiting for transfers between devices: 75.9 us -> none  [the longest x2 75.9 us: col_gather(): return lax.all_gather(pair, 'cx', axis=3, tiled=True)]
    ppermute x0 -> x14, starting transfers between devices: none -> 53 us  [the longest x6 27.5 us: weight_gather(): other = lax.ppermute(block, axis, [(i, i ^ bit) for i in range(count)])]
    dot_general x9, matrix products: 14.4 us -> 32.6 us  [spatial_terms(): jnp.einsum('fhwc,cd->fhwd', window, weights[tap], preferred_element_type=...]
    dynamic_update_slice x0 -> x12, local copies, waits for them, and re-layouts: none -> 16.1 us  [the longest x7 9.58 us: col_gather(): lax.dynamic_update_slice_in_dim(out, other_side, (2 * place + 1 - side) *...]
    ppermute x2, waiting for transfers between devices: 76.8 us -> 63.6 us  [col_gather(): partner = lax.ppermute(block, 'cz', [(0, 1), (1, 0)])]
    pad x1, local copies, waits for them, and re-layouts: 8.54 us -> 0.26 us  [body(): rimmed = jnp.pad(rimmed, ((0, 0), (0, 0), (1, 1), (0, 0)))]
  transfers between devices with their start and end apart: 9 -> 20, of which waited for: 5 -> 12; matrix products, arithmetic and copies ran while one was open for 2% -> 7% of each run, Pallas kernels for 0% -> 0%
where the time goes in v2:
time: 392 us; the launch traced here: 387 us
  waiting for transfers between devices  219 us (56%)
  starting transfers between devices  83.1 us (21%)
  matrix products  43.8 us (11%)
  local copies, waits for them, and re-layouts  34.8 us (9%)
  other arithmetic  5.83 us (1%)
    ppermute x6, waiting for transfers between devices, weight_gather(): other = lax.ppermute(block, axis, [(i, i ^ bit) for i in range(count)])  89.2 us
    ppermute x2, waiting for transfers between devices, col_gather(): partner = lax.ppermute(block, 'cz', [(0, 1), (1, 0)])  63.6 us
    ppermute x8, waiting for transfers between devices, ring_shift(): lax.ppermute(block, axis, [(i, (i + step) % count) for i in range(count)])  61.7 us
    dot_general x9, matrix products, spatial_terms(): jnp.einsum('fhwc,cd->fhwd', window, weights[tap], preferred_element_type=...  32.6 us
    ppermute x6, starting transfers between devices, weight_gather(): other = lax.ppermute(block, axis, [(i, i ^ bit) for i in range(count)])  27.5 us
    ppermute x8, starting transfers between devices, ring_shift(): lax.ppermute(block, axis, [(i, (i + step) % count) for i in range(count)])  25.6 us
    ppermute x2, starting transfers between devices, col_gather(): partner = lax.ppermute(block, 'cz', [(0, 1), (1, 0)])  19.2 us
    dot_general x3, matrix products, body(): jnp.einsum('fhwc,cd->fhwd', whole[tap:tap + fr_count], full_temporal[tap]...  11.2 us
  transfers between devices with their start and end apart: 20, of which 12 were waited for; matrix products, arithmetic and copies ran while one was open for 7% of the time, Pallas kernels for 0%

profile of v2, /device:TPU:1, one launch (start us, length us, event | category | flops | bytes accessed | tf_op | source)
XLA Modules:
  0.0 387.1 jit_solution(11725772860080642388)
XLA Ops:
  1.5 4.4 %collective-permute-start.7 = (bf16[12,16,128]{2,1,0:T(8,128)(2,1)S(1)}, bf16[12,16,128]{2,1,0:T(8,128)(2,1)S(1)}, u32[]{:S(2)}, u32[]{:S(2)}) collective-permute-start(bf16[12,16,128]{2,1,0:T(8,128)(2,1)S(1)} %constant_dynamic-update-slice_fusion), channel_id=1, source_target_pairs={{0,8},{8,0},{16,24},{24,16},{32,40},{40,32},{48,56},{56,48},{1,9},... | collective-permute-start | bytes 147464 | tf_op jit(solution)/shard_map/ppermute | solution.py:55
  10.2 7.0 %collective-permute-start.8 = (bf16[2,12,16,128]{3,2,1,0:T(8,128)(2,1)S(1)}, bf16[2,12,16,128]{3,2,1,0:T(8,128)(2,1)S(1)}, u32[]{:S(2)}, u32[]{:S(2)}) collective-permute-start(bf16[2,12,16,128]{3,2,1,0:T(8,128)(2,1)S(1)} %maximum_select_fusion.9), channel_id=1, source_target_pairs={{0,16},{8,24},{16,0},{24,8},{32,48},{40,56},{48,32},{56,40},{1,17}... | collective-permute-start | bytes 294920 | tf_op jit(solution)/shard_map/ppermute | solution.py:55
  21.9 12.8 %collective-permute-start.2 = (bf16[4,10,66,128]{3,0,2,1:T(4,128)(2,1)S(1)}, bf16[4,10,66,128]{3,0,2,1:T(4,128)(2,1)S(1)}, u32[]{:S(2)}, u32[]{:S(2)}) collective-permute-start(bf16[4,10,66,128]{3,0,2,1:T(4,128)(2,1)S(1)} %copy.19), channel_id=1, source_target_pairs={{0,1},{1,0},{2,3},{3,2},{4,5},{5,4},{6,7},{7,6},{8,9},{9,8},{10,11... | collective-permute-start | bytes 2027528 | tf_op jit(solution)/shard_map/ppermute | solution.py:30
  34.8 4.0 %collective-permute-start.9 = (bf16[2,2,12,16,128]{4,3,2,1,0:T(8,128)(2,1)S(1)}, bf16[2,2,12,16,128]{4,3,2,1,0:T(8,128)(2,1)S(1)}, u32[]{:S(2)}, u32[]{:S(2)}) collective-permute-start(bf16[2,2,12,16,128]{4,3,2,1,0:T(8,128)(2,1)S(1)} %maximum_select_fusion.7), channel_id=1, source_target_pairs={{0,32},{8,40},{16,48},{24,56},{32,0},{40,8},{48,16},{56,24},{1,33}... | collective-permute-start | bytes 589832 | tf_op jit(solution)/shard_map/ppermute | solution.py:55
  38.9 73.8 %collective-permute-done.9 = bf16[2,2,12,16,128]{4,3,2,1,0:T(8,128)(2,1)S(1)} collective-permute-done((bf16[2,2,12,16,128]{4,3,2,1,0:T(8,128)(2,1)S(1)}, bf16[2,2,12,16,128]{4,3,2,1,0:T(8,128)(2,1)S(1)}, u32[]{:S(2)}, u32[]{:S(2)}) %collective-permute-start.9) | collective-permute-done | bytes 196640 | tf_op jit(solution)/shard_map/ppermute | solution.py:55
  112.8 4.8 %collective-permute-start.10 = (bf16[2,2,2,12,16,128]{5,4,3,2,1,0:T(8,128)(2,1)S(1)}, bf16[2,2,2,12,16,128]{5,4,3,2,1,0:T(8,128)(2,1)S(1)}, u32[]{:S(2)}, u32[]{:S(2)}) collective-permute-start(bf16[2,2,2,12,16,128]{5,4,3,2,1,0:T(8,128)(2,1)S(1)} %maximum_select_fusion.5), channel_id=1, source_target_pairs={{0,256},{128,384},{256,0},{384,128},{1,257},{129,385},{257,1},{385... | collective-permute-start | bytes 1179656 | tf_op jit(solution)/shard_map/ppermute | solution.py:55
  119.7 4.4 %collective-permute-start.3 = (bf16[4,10,66,256]{3,0,2,1:T(4,128)(2,1)S(1)}, bf16[4,10,66,256]{3,0,2,1:T(4,128)(2,1)}, u32[]{:S(2)}, u32[]{:S(2)}) collective-permute-start(bf16[4,10,66,256]{3,0,2,1:T(4,128)(2,1)S(1)} %copy.22), channel_id=1, source_target_pairs={{0,6},{2,0},{4,2},{6,4},{1,7},{3,1},{5,3},{7,5},{8,14},{10,8},{12,... | collective-permute-start | bytes 4055048 | tf_op jit(solution)/shard_map/ppermute | solution.py:22
  134.3 13.0 %collective-permute-done.11 = bf16[2,2,2,2,12,16,128]{6,5,4,3,2,1,0:T(8,128)(2,1)S(1)} collective-permute-done((bf16[2,2,2,2,12,16,128]{6,5,4,3,2,1,0:T(8,128)(2,1)}, bf16[2,2,2,2,12,16,128]{6,5,4,3,2,1,0:T(8,128)(2,1)S(1)}, u32[]{:S(2)}, u32[]{:S(2)}) %collective-permute-start.11) | collective-permute-done | bytes 786464 | tf_op jit(solution)/shard_map/ppermute | solution.py:55
  147.6 4.1 %collective-permute-start.12 = (bf16[2,2,2,2,2,12,16,128]{7,6,5,4,3,2,1,0:T(8,128)(2,1)S(1)}, bf16[2,2,2,2,2,12,16,128]{7,6,5,4,3,2,1,0:T(8,128)(2,1)S(1)}, u32[]{:S(2)}, u32[]{:S(2)}) collective-permute-start(bf16[2,2,2,2,2,12,16,128]{7,6,5,4,3,2,1,0:T(8,128)(2,1)S(1)} %maximum_select_fusion.1), channel_id=1, source_target_pairs={{0,64},{64,0},{1,65},{65,1},{2,66},{66,2},{3,67},{67,3},{4,68},{68... | collective-permute-start | bytes 4718600 | tf_op jit(solution)/shard_map/ppermute | solution.py:55
  154.0 5.4 %collective-permute-start.4 = (bf16[4,10,66,128]{3,0,2,1:T(4,128)(2,1)S(1)}, bf16[4,10,66,128]{3,0,2,1:T(4,128)(2,1)S(1)}, u32[]{:S(2)}, u32[]{:S(2)}) collective-permute-start(bf16[4,10,66,128]{3,0,2,1:T(4,128)(2,1)S(1)} %get-tuple-element.22), channel_id=1, source_target_pairs={{0,6},{2,0},{4,2},{6,4},{1,7},{3,1},{5,3},{7,5},{8,14},{10,8},{12,... | collective-permute-start | bytes 2027528 | tf_op jit(solution)/shard_map/ppermute | solution.py:22
  159.4 3.9 %collective-permute-done.5 = bf16[4,10,66,256]{3,0,2,1:T(4,128)(2,1)} collective-permute-done((bf16[4,10,66,256]{3,0,2,1:T(4,128)(2,1)S(1)}, bf16[4,10,66,256]{3,0,2,1:T(4,128)(2,1)}, u32[]{:S(2)}, u32[]{:S(2)}) %collective-permute-start.5) | collective-permute-done | bytes 1351712 | tf_op jit(solution)/shard_map/ppermute | solution.py:22
  173.3 9.0 %collective-permute-done.6 = bf16[4,10,66,128]{3,0,2,1:T(4,128)(2,1)S(1)} collective-permute-done((bf16[4,10,66,128]{3,0,2,1:T(4,128)(2,1)S(1)}, bf16[4,10,66,128]{3,0,2,1:T(4,128)(2,1)S(1)}, u32[]{:S(2)}, u32[]{:S(2)}) %collective-permute-start.6) | collective-permute-done | bytes 675872 | tf_op jit(solution)/shard_map/ppermute | solution.py:22
  197.7 3.6 fusion.8
  201.4 3.6 fusion.6
  208.5 3.6 fusion.2
  212.2 3.6 fusion
  215.9 3.9 %fusion.57 = (bf16[4,8,64,128]{3,2,1,0:T(8,128)(2,1)S(1)}, bf16[4,8,64,128]{3,2,1,0:T(8,128)(2,1)S(1)}) fusion(f32[128]{0:T(128)S(1)} %copy-done.3, f32[4,8,64,128]{3,2,1,0:T(8,128)S(1)} %fusion, f32[4,8,64,128]{3,2,1,0:T(8,128)S(1)} %fusion.2, f32[4,8,64,128]{3,2,1,0:T(8,128)S(1)} %fusion.4, f32[4,8,64,128]{3,2,1,0:T(8,128)S(1)} %fusion.6, ...), kind=kOutput, calls=%fused_computation.49 | convolution fusion | flops 541065216 | bytes 13894144 | tf_op jit(solution)/shard_map/fhwc,cd->fhwd/dot_general | solution.py:69
  219.8 5.4 %collective-permute-start.13 = (bf16[1,8,64,128]{3,2,1,0:T(8,128)(2,1)S(1)}, bf16[1,8,64,128]{3,2,1,0:T(8,128)(2,1)S(1)}, u32[]{:S(2)}, u32[]{:S(2)}) collective-permute-start(bf16[1,8,64,128]{3,2,1,0:T(8,128)(2,1)S(1)} %get-tuple-element.29), channel_id=1, source_target_pairs={{0,64},{64,128},{128,192},{192,256},{256,320},{320,384},{384,448},... | collective-permute-start | bytes 393224 | tf_op jit(solution)/shard_map/ppermute | solution.py:14
  227.4 4.3 %collective-permute-done.14 = bf16[1,8,64,128]{3,2,1,0:T(8,128)(2,1)S(1)} collective-permute-done((bf16[1,8,64,128]{3,2,1,0:T(8,128)(2,1)S(1)}, bf16[1,8,64,128]{3,2,1,0:T(8,128)(2,1)S(1)}, u32[]{:S(2)}, u32[]{:S(2)}) %collective-permute-start.14) | collective-permute-done | bytes 131104 | tf_op jit(solution)/shard_map/ppermute | solution.py:17
  236.5 6.5 %collective-permute-start.15 = (bf16[6,8,64,128]{3,2,1,0:T(8,128)(2,1)S(1)}, bf16[6,8,64,128]{3,2,1,0:T(8,128)(2,1)S(1)}, u32[]{:S(2)}, u32[]{:S(2)}) collective-permute-start(bf16[6,8,64,128]{3,2,1,0:T(8,128)(2,1)S(1)} %get-tuple-element.23), channel_id=1, source_target_pairs={{0,1},{1,0},{2,3},{3,2},{4,5},{5,4},{6,7},{7,6},{8,9},{9,8},{10,11... | collective-permute-start | bytes 2359304 | tf_op jit(solution)/shard_map/ppermute | solution.py:30
  243.0 63.6 %collective-permute-done.15 = bf16[6,8,64,128]{3,2,1,0:T(8,128)(2,1)S(1)} collective-permute-done((bf16[6,8,64,128]{3,2,1,0:T(8,128)(2,1)S(1)}, bf16[6,8,64,128]{3,2,1,0:T(8,128)(2,1)S(1)}, u32[]{:S(2)}, u32[]{:S(2)}) %collective-permute-start.15) | collective-permute-done | bytes 786464 | tf_op jit(solution)/shard_map/ppermute | solution.py:30
  313.2 31.2 %collective-permute-done.16 = bf16[6,8,64,256]{3,2,1,0:T(8,128)(2,1)S(1)} collective-permute-done((bf16[6,8,64,256]{3,2,1,0:T(8,128)(2,1)S(1)}, bf16[6,8,64,256]{3,2,1,0:T(8,128)(2,1)S(1)}, u32[]{:S(2)}, u32[]{:S(2)}) %collective-permute-start.16) | collective-permute-done | bytes 1572896 | tf_op jit(solution)/shard_map/ppermute | solution.py:22
  355.0 11.2 %collective-permute-done.17 = bf16[6,8,64,128]{3,2,1,0:T(8,128)(2,1)} collective-permute-done((bf16[6,8,64,128]{3,2,1,0:T(8,128)(2,1)}, bf16[6,8,64,128]{3,2,1,0:T(8,128)(2,1)}, u32[]{:S(2)}, u32[]{:S(2)}) %collective-permute-start.17) | collective-permute-done | bytes 786464 | tf_op jit(solution)/shard_map/ppermute | solution.py:22
  382.8 4.3 %fusion.53 = bf16[4,8,64,128]{3,2,1,0:T(8,128)(2,1)} fusion(f32[4,8,64,128]{3,2,1,0:T(8,128)S(1)} %convolution_multiply_fusion, f32[4,8,64,128]{3,2,1,0:T(8,128)S(1)} %fusion.70, bf16[6,8,64,1024]{3,2,1,0:T(8,128)(2,1)} %constant_dynamic-update-slice_fusion.2, bf16[1024,128,1,1]{1,0,3,2:T(8,128)(2,1)S(1)} %bitcast.107, ...), kind=kOutput, calls=%fused_computation.45 | convolution fusion | flops 538705920 | bytes 9699856 | tf_op jit(solution)/shard_map/fhwc,cd->fhwd/dot_general | solution.py:95
  (98 shorter events, 94.7 us)
Async XLA Ops:
  0.0 20.5 %copy-start.1 = (bf16[4,8,64,128]{3,2,1,0:T(8,128)(2,1)S(1)}, bf16[4,8,64,128]{3,2,1,0:T(8,128)(2,1)}, u32[]{:S(2)}) copy-start(bf16[4,8,64,128]{3,2,1,0:T(8,128)(2,1)} %param.6) | copy-start | bytes 1572868
  1.5 8.6 %collective-permute-start.7 = (bf16[12,16,128]{2,1,0:T(8,128)(2,1)S(1)}, bf16[12,16,128]{2,1,0:T(8,128)(2,1)S(1)}, u32[]{:S(2)}, u32[]{:S(2)}) collective-permute-start(bf16[12,16,128]{2,1,0:T(8,128)(2,1)S(1)} %constant_dynamic-update-slice_fusion), channel_id=1, source_target_pairs={{0,8},{8,0},{16,24},{24,16},{32,40},{40,32},{48,56},{56,48},{1,9},... | collective-permute-start | bytes 147464 | tf_op jit(solution)/shard_map/ppermute | solution.py:55
  6.8 10.4 %collective-permute-start = (bf16[4,1,64,128]{3,2,1,0:T(8,128)(2,1)S(1)}, bf16[4,1,64,128]{3,2,1,0:T(8,128)(2,1)S(1)}, u32[]{:S(2)}, u32[]{:S(2)}) collective-permute-start(bf16[4,1,64,128]{3,2,1,0:T(8,128)(2,1)S(1)} %get-tuple-element.31), channel_id=1, source_target_pairs={{0,8},{8,16},{16,24},{24,32},{32,40},{40,48},{48,56},{1,9},{9,17},... | collective-permute-start | bytes 196616 | tf_op jit(solution)/shard_map/ppermute | solution.py:14
  8.7 8.4 %collective-permute-start.1 = (bf16[4,1,64,128]{3,2,1,0:T(8,128)(2,1)S(1)}, bf16[4,1,64,128]{3,2,1,0:T(8,128)(2,1)S(1)}, u32[]{:S(2)}, u32[]{:S(2)}) collective-permute-start(bf16[4,1,64,128]{3,2,1,0:T(8,128)(2,1)S(1)} %get-tuple-element.32), channel_id=1, source_target_pairs={{8,0},{16,8},{24,16},{32,24},{40,32},{48,40},{56,48},{9,1},{17,9},... | collective-permute-start | bytes 196616 | tf_op jit(solution)/shard_map/ppermute | solution.py:17
  10.2 24.6 %collective-permute-start.8 = (bf16[2,12,16,128]{3,2,1,0:T(8,128)(2,1)S(1)}, bf16[2,12,16,128]{3,2,1,0:T(8,128)(2,1)S(1)}, u32[]{:S(2)}, u32[]{:S(2)}) collective-permute-start(bf16[2,12,16,128]{3,2,1,0:T(8,128)(2,1)S(1)} %maximum_select_fusion.9), channel_id=1, source_target_pairs={{0,16},{8,24},{16,0},{24,8},{32,48},{40,56},{48,32},{56,40},{1,17}... | collective-permute-start | bytes 294920 | tf_op jit(solution)/shard_map/ppermute | solution.py:55
  21.9 95.7 %collective-permute-start.2 = (bf16[4,10,66,128]{3,0,2,1:T(4,128)(2,1)S(1)}, bf16[4,10,66,128]{3,0,2,1:T(4,128)(2,1)S(1)}, u32[]{:S(2)}, u32[]{:S(2)}) collective-permute-start(bf16[4,10,66,128]{3,0,2,1:T(4,128)(2,1)S(1)} %copy.19), channel_id=1, source_target_pairs={{0,1},{1,0},{2,3},{3,2},{4,5},{5,4},{6,7},{7,6},{8,9},{9,8},{10,11... | collective-permute-start | bytes 2027528 | tf_op jit(solution)/shard_map/ppermute | solution.py:30
  34.8 77.9 %collective-permute-start.9 = (bf16[2,2,12,16,128]{4,3,2,1,0:T(8,128)(2,1)S(1)}, bf16[2,2,12,16,128]{4,3,2,1,0:T(8,128)(2,1)S(1)}, u32[]{:S(2)}, u32[]{:S(2)}) collective-permute-start(bf16[2,2,12,16,128]{4,3,2,1,0:T(8,128)(2,1)S(1)} %maximum_select_fusion.7), channel_id=1, source_target_pairs={{0,32},{8,40},{16,48},{24,56},{32,0},{40,8},{48,16},{56,24},{1,33}... | collective-permute-start | bytes 589832 | tf_op jit(solution)/shard_map/ppermute | solution.py:55
  112.8 13.6 %collective-permute-start.10 = (bf16[2,2,2,12,16,128]{5,4,3,2,1,0:T(8,128)(2,1)S(1)}, bf16[2,2,2,12,16,128]{5,4,3,2,1,0:T(8,128)(2,1)S(1)}, u32[]{:S(2)}, u32[]{:S(2)}) collective-permute-start(bf16[2,2,2,12,16,128]{5,4,3,2,1,0:T(8,128)(2,1)S(1)} %maximum_select_fusion.5), channel_id=1, source_target_pairs={{0,256},{128,384},{256,0},{384,128},{1,257},{129,385},{257,1},{385... | collective-permute-start | bytes 1179656 | tf_op jit(solution)/shard_map/ppermute | solution.py:55
  119.7 32.6 %collective-permute-start.3 = (bf16[4,10,66,256]{3,0,2,1:T(4,128)(2,1)S(1)}, bf16[4,10,66,256]{3,0,2,1:T(4,128)(2,1)}, u32[]{:S(2)}, u32[]{:S(2)}) collective-permute-start(bf16[4,10,66,256]{3,0,2,1:T(4,128)(2,1)S(1)} %copy.22), channel_id=1, source_target_pairs={{0,6},{2,0},{4,2},{6,4},{1,7},{3,1},{5,3},{7,5},{8,14},{10,8},{12,... | collective-permute-start | bytes 4055048 | tf_op jit(solution)/shard_map/ppermute | solution.py:22
  127.4 19.9 %collective-permute-start.11 = (bf16[2,2,2,2,12,16,128]{6,5,4,3,2,1,0:T(8,128)(2,1)}, bf16[2,2,2,2,12,16,128]{6,5,4,3,2,1,0:T(8,128)(2,1)S(1)}, u32[]{:S(2)}, u32[]{:S(2)}) collective-permute-start(bf16[2,2,2,2,12,16,128]{6,5,4,3,2,1,0:T(8,128)(2,1)} %maximum_select_fusion.3), channel_id=1, source_target_pairs={{0,128},{128,0},{256,384},{384,256},{1,129},{129,1},{257,385},{385... | collective-permute-start | bytes 2359304 | tf_op jit(solution)/shard_map/ppermute | solution.py:55
  130.6 32.7 %collective-permute-start.5 = (bf16[4,10,66,256]{3,0,2,1:T(4,128)(2,1)S(1)}, bf16[4,10,66,256]{3,0,2,1:T(4,128)(2,1)}, u32[]{:S(2)}, u32[]{:S(2)}) collective-permute-start(bf16[4,10,66,256]{3,0,2,1:T(4,128)(2,1)S(1)} %copy.22), channel_id=1, source_target_pairs={{0,2},{2,4},{4,6},{6,0},{1,3},{3,5},{5,7},{7,1},{8,10},{10,12},{12... | collective-permute-start | bytes 4055048 | tf_op jit(solution)/shard_map/ppermute | solution.py:22
  147.6 37.9 %collective-permute-start.12 = (bf16[2,2,2,2,2,12,16,128]{7,6,5,4,3,2,1,0:T(8,128)(2,1)S(1)}, bf16[2,2,2,2,2,12,16,128]{7,6,5,4,3,2,1,0:T(8,128)(2,1)S(1)}, u32[]{:S(2)}, u32[]{:S(2)}) collective-permute-start(bf16[2,2,2,2,2,12,16,128]{7,6,5,4,3,2,1,0:T(8,128)(2,1)S(1)} %maximum_select_fusion.1), channel_id=1, source_target_pairs={{0,64},{64,0},{1,65},{65,1},{2,66},{66,2},{3,67},{67,3},{4,68},{68... | collective-permute-start | bytes 4718600 | tf_op jit(solution)/shard_map/ppermute | solution.py:55
  154.0 18.2 %collective-permute-start.4 = (bf16[4,10,66,128]{3,0,2,1:T(4,128)(2,1)S(1)}, bf16[4,10,66,128]{3,0,2,1:T(4,128)(2,1)S(1)}, u32[]{:S(2)}, u32[]{:S(2)}) collective-permute-start(bf16[4,10,66,128]{3,0,2,1:T(4,128)(2,1)S(1)} %get-tuple-element.22), channel_id=1, source_target_pairs={{0,6},{2,0},{4,2},{6,4},{1,7},{3,1},{5,3},{7,5},{8,14},{10,8},{12,... | collective-permute-start | bytes 2027528 | tf_op jit(solution)/shard_map/ppermute | solution.py:22
  165.1 17.2 %collective-permute-start.6 = (bf16[4,10,66,128]{3,0,2,1:T(4,128)(2,1)S(1)}, bf16[4,10,66,128]{3,0,2,1:T(4,128)(2,1)S(1)}, u32[]{:S(2)}, u32[]{:S(2)}) collective-permute-start(bf16[4,10,66,128]{3,0,2,1:T(4,128)(2,1)S(1)} %get-tuple-element.20), channel_id=1, source_target_pairs={{0,2},{2,4},{4,6},{6,0},{1,3},{3,5},{5,7},{7,1},{8,10},{10,12},{12... | collective-permute-start | bytes 2027528 | tf_op jit(solution)/shard_map/ppermute | solution.py:22
  219.8 7.6 %collective-permute-start.13 = (bf16[1,8,64,128]{3,2,1,0:T(8,128)(2,1)S(1)}, bf16[1,8,64,128]{3,2,1,0:T(8,128)(2,1)S(1)}, u32[]{:S(2)}, u32[]{:S(2)}) collective-permute-start(bf16[1,8,64,128]{3,2,1,0:T(8,128)(2,1)S(1)} %get-tuple-element.29), channel_id=1, source_target_pairs={{0,64},{64,128},{128,192},{192,256},{256,320},{320,384},{384,448},... | collective-permute-start | bytes 393224 | tf_op jit(solution)/shard_map/ppermute | solution.py:14
  225.3 6.5 %collective-permute-start.14 = (bf16[1,8,64,128]{3,2,1,0:T(8,128)(2,1)S(1)}, bf16[1,8,64,128]{3,2,1,0:T(8,128)(2,1)S(1)}, u32[]{:S(2)}, u32[]{:S(2)}) collective-permute-start(bf16[1,8,64,128]{3,2,1,0:T(8,128)(2,1)S(1)} %get-tuple-element.30), channel_id=1, source_target_pairs={{64,0},{128,64},{192,128},{256,192},{320,256},{384,320},{448,384},... | collective-permute-start | bytes 393224 | tf_op jit(solution)/shard_map/ppermute | solution.py:17
  236.5 115.9 %copy-start.4 = (s32[32]{0:T(128)S(1)}, s32[32]{0:T(128)}, u32[]{:S(2)}) copy-start(s32[32]{0:T(128)} %param.11) | copy-start | bytes 388
  236.5 70.1 %collective-permute-start.15 = (bf16[6,8,64,128]{3,2,1,0:T(8,128)(2,1)S(1)}, bf16[6,8,64,128]{3,2,1,0:T(8,128)(2,1)S(1)}, u32[]{:S(2)}, u32[]{:S(2)}) collective-permute-start(bf16[6,8,64,128]{3,2,1,0:T(8,128)(2,1)S(1)} %get-tuple-element.23), channel_id=1, source_target_pairs={{0,1},{1,0},{2,3},{3,2},{4,5},{5,4},{6,7},{7,6},{8,9},{9,8},{10,11... | collective-permute-start | bytes 2359304 | tf_op jit(solution)/shard_map/ppermute | solution.py:30
  306.9 37.5 %collective-permute-start.16 = (bf16[6,8,64,256]{3,2,1,0:T(8,128)(2,1)S(1)}, bf16[6,8,64,256]{3,2,1,0:T(8,128)(2,1)S(1)}, u32[]{:S(2)}, u32[]{:S(2)}) collective-permute-start(bf16[6,8,64,256]{3,2,1,0:T(8,128)(2,1)S(1)} %pad_maximum_fusion), channel_id=1, source_target_pairs={{0,6},{2,0},{4,2},{6,4},{1,7},{3,1},{5,3},{7,5},{8,14},{10,8},{12,... | collective-permute-start | bytes 4718600 | tf_op jit(solution)/shard_map/ppermute | solution.py:22
  309.1 40.4 %collective-permute-start.18 = (bf16[6,8,64,256]{3,2,1,0:T(8,128)(2,1)S(1)}, bf16[6,8,64,256]{3,2,1,0:T(8,128)(2,1)S(1)}, u32[]{:S(2)}, u32[]{:S(2)}) collective-permute-start(bf16[6,8,64,256]{3,2,1,0:T(8,128)(2,1)S(1)} %pad_maximum_fusion), channel_id=1, source_target_pairs={{0,2},{2,4},{4,6},{6,0},{1,3},{3,5},{5,7},{7,1},{8,10},{10,12},{12... | collective-permute-start | bytes 4718600 | tf_op jit(solution)/shard_map/ppermute | solution.py:22
  344.3 5.1 %copy-start = (bf16[6,8,64,256]{3,2,1,0:T(8,128)(2,1)}, bf16[6,8,64,256]{3,2,1,0:T(8,128)(2,1)S(1)}, u32[]{:S(2)}) copy-start(bf16[6,8,64,256]{3,2,1,0:T(8,128)(2,1)S(1)} %collective-permute-done.16) | copy-start | bytes 4718596
  346.1 20.0 %collective-permute-start.17 = (bf16[6,8,64,128]{3,2,1,0:T(8,128)(2,1)}, bf16[6,8,64,128]{3,2,1,0:T(8,128)(2,1)}, u32[]{:S(2)}, u32[]{:S(2)}) collective-permute-start(bf16[6,8,64,128]{3,2,1,0:T(8,128)(2,1)} %get-tuple-element.17), channel_id=1, source_target_pairs={{0,6},{2,0},{4,2},{6,4},{1,7},{3,1},{5,3},{7,5},{8,14},{10,8},{12,... | collective-permute-start | bytes 2359304 | tf_op jit(solution)/shard_map/ppermute | solution.py:22
  350.5 20.9 %collective-permute-start.19 = (bf16[6,8,64,128]{3,2,1,0:T(8,128)(2,1)}, bf16[6,8,64,128]{3,2,1,0:T(8,128)(2,1)}, u32[]{:S(2)}, u32[]{:S(2)}) collective-permute-start(bf16[6,8,64,128]{3,2,1,0:T(8,128)(2,1)} %slice.215), channel_id=1, source_target_pairs={{0,2},{2,4},{4,6},{6,0},{1,3},{3,5},{5,7},{7,1},{8,10},{10,12},{12... | collective-permute-start | bytes 2359304 | tf_op jit(solution)/shard_map/ppermute | solution.py:22
  375.9 6.9 %copy-start.2 = (f32[128]{0:T(128)S(1)}, f32[128]{0:T(128)}, u32[]{:S(2)}) copy-start(f32[128]{0:T(128)} %param.10) | copy-start | bytes 1540
  (1 other events, 3.7 us)

commit v3 on v2

v3 whole, which is shorter than its diff:
```python
import jax
import jax.numpy as jnp
from jax import lax
from jax.sharding import Mesh
from jax.sharding import PartitionSpec as P

FRAME = ("fy", "fc")
COL = ("cx", "cz")
SWAP = [(0, 1), (1, 0)]


def shift_halo(block, axis, count, dim, width):
    forward = [(i, i + 1) for i in range(count - 1)]
    backward = [(target, source) for source, target in forward]
    low = lax.ppermute(
        lax.slice_in_dim(block, block.shape[dim] - width, None, axis=dim), axis, forward
    )
    high = lax.ppermute(lax.slice_in_dim(block, 0, width, axis=dim), axis, backward)
    return jnp.concatenate([low, block, high], axis=dim)


def ring_shift(block, axis, count, step):
    return lax.ppermute(block, axis, [(i, (i + step) % count) for i in range(count)])


def ordered_pair(own, other, high, dim):
    return jnp.where(
        high, jnp.concatenate([other, own], axis=dim), jnp.concatenate([own, other], axis=dim)
    )


def x_gather(pair, pad):
    ring = lax.axis_size("cx")
    me = lax.axis_index("cx")
    width = pair.shape[3]
    half = width // 2
    from_left = ring_shift(pair, "cx", ring, 1)
    from_right = ring_shift(pair, "cx", ring, -1)
    far_low = ring_shift(from_right[..., :half], "cx", ring, -1)
    far_high = ring_shift(from_left[..., half:], "cx", ring, 1)
    frames, rows, wide, _ = pair.shape
    out = jnp.zeros((frames, rows, wide + 2 * pad, width * ring), pair.dtype)
    pieces = ((0, pair, 0), (1, from_right, 0), (ring - 1, from_left, 0), (2, far_low, 0), (2, far_high, half))
    for offset, piece, shift in pieces:
        base = ((me + offset) % ring) * width + shift
        out = lax.dynamic_update_slice(out, piece, (0, 0, pad, base))
    return out


def weight_gather(weight):
    steps = (("cz", 1), ("row", 4), ("row", 2), ("row", 1), ("fy", 2), ("fy", 1), ("fc", 1))
    block = weight
    for axis, bit in steps:
        count = lax.axis_size(axis)
        other = lax.ppermute(block, axis, [(i, i ^ bit) for i in range(count)])
        high = (lax.axis_index(axis) // bit) % 2 == 1
        block = jnp.where(high, jnp.stack([other, block]), jnp.stack([block, other]))
    block = jnp.transpose(block, (7, 2, 1, 0, 5, 4, 3, 8, 6, 9))
    taps, depth, width = weight.shape
    return block.reshape(taps, 64 * depth, 2 * width)


def spatial_terms(gathered, weights, row_count, wide):
    total = None
    for tap in range(9):
        shift_y, shift_x = (tap // 3, tap % 3)
        window = gathered[:, shift_y : shift_y + row_count, shift_x : shift_x + wide, :]
        term = jnp.einsum("fhwc,cd->fhwd", window, weights[tap], preferred_element_type=jnp.float32)
        total = term if total is None else total + term
    return total


def body(frames_in, spatial_weight, temporal_weight, spatial_bias, temporal_bias, clip_id):
    fr_count, row_count, wide, col_width = frames_in.shape
    half = row_count // 2
    side = lax.axis_index("cz")
    high = side == 1
    both = weight_gather(jnp.concatenate([spatial_weight, temporal_weight], axis=0))
    full_spatial, full_temporal = both[:9], both[9:]
    biases = jnp.stack([spatial_bias, temporal_bias])
    biases = ordered_pair(biases, lax.ppermute(biases, "cz", SWAP), high, 1)
    rimmed = shift_halo(frames_in, "row", lax.axis_size("row"), 1, 1)
    mine = lax.dynamic_slice_in_dim(rimmed, side * half, half + 2, axis=1)
    wanted = lax.dynamic_slice_in_dim(rimmed, (1 - side) * half, half + 2, axis=1)
    partner = lax.ppermute(wanted, "cz", SWAP)
    gathered = x_gather(ordered_pair(mine, partner, high, 3), 1)
    spatial = spatial_terms(gathered, full_spatial, half, wide)
    hidden = (spatial + biases[0]).astype(jnp.bfloat16)
    active = jax.nn.silu(hidden.astype(jnp.float32)).astype(jnp.bfloat16)
    index = lax.axis_index(FRAME)
    edge_ids = jnp.full((1,), -1, jnp.int32)
    padded_ids = jnp.concatenate([edge_ids, clip_id, edge_ids])
    local_ids = lax.dynamic_slice_in_dim(padded_ids, index * fr_count, fr_count + 2)
    prev_ok = (local_ids[1:-1] == local_ids[:-2]).astype(jnp.float32).reshape(fr_count, 1, 1, 1)
    next_ok = (local_ids[1:-1] == local_ids[2:]).astype(jnp.float32).reshape(fr_count, 1, 1, 1)
    source = shift_halo(active, FRAME, lax.axis_size(FRAME), 0, 1)
    whole = x_gather(source, 0)
    taps = [
        jnp.einsum(
            "fhwc,cd->fhwd",
            whole[tap : tap + fr_count],
            full_temporal[tap],
            preferred_element_type=jnp.float32,
        )
        for tap in range(3)
    ]
    total = (
        hidden.astype(jnp.float32) + biases[1] + prev_ok * taps[0] + taps[1] + next_ok * taps[2]
    ).astype(jnp.bfloat16)
    kept = lax.dynamic_slice_in_dim(total, side * col_width, col_width, axis=3)
    given = lax.dynamic_slice_in_dim(total, (1 - side) * col_width, col_width, axis=3)
    returned = lax.ppermute(given, "cz", SWAP)
    return ordered_pair(kept, returned, high, 1)


def solution(mesh):
    frame_n, row_n, col_n = mesh.devices.shape
    fine = Mesh(
        mesh.devices.reshape(frame_n // 2, 2, row_n, col_n // 2, 2),
        ("fy", "fc", "row", "cx", "cz"),
    )
    act = P(FRAME, "row", None, COL)
    weight = P(None, FRAME + ("row",), COL)
    placed = (act, weight, weight, P(COL), P(COL), P())
    return jax.shard_map(body, mesh=fine, in_specs=placed, out_specs=act, check_vma=False)
```

time: 392 us -> 439 us (1.12)
  the two profiles are of different devices: /device:TPU:1 before, /device:TPU:175 now
where the time goes in v3:
time: 439 us; the launch traced here: 434 us
  waiting for transfers between devices  163 us (37%)
  local copies, waits for them, and re-layouts  122 us (28%)
  starting transfers between devices  95.9 us (22%)
  matrix products  32.8 us (7%)
  other arithmetic  18.5 us (4%)
    dynamic_update_slice x9, local copies, waits for them, and re-layouts, x_gather(): out = lax.dynamic_update_slice(out, piece, (0, 0, pad, base))  80.5 us
    ppermute x7, waiting for transfers between devices, weight_gather(): other = lax.ppermute(block, axis, [(i, i ^ bit) for i in range(count)])  78.8 us
    ppermute x1, waiting for transfers between devices, body(): partner = lax.ppermute(wanted, 'cz', SWAP)  38.7 us
    ppermute x7, starting transfers between devices, weight_gather(): other = lax.ppermute(block, axis, [(i, i ^ bit) for i in range(count)])  35.8 us
    dot_general x9, matrix products, spatial_terms(): jnp.einsum('fhwc,cd->fhwd', window, weights[tap], preferred_element_type=...  30.6 us
    ppermute x8, starting transfers between devices, ring_shift(): lax.ppermute(block, axis, [(i, (i + step) % count) for i in range(count)])  25.9 us
    ppermute x8, waiting for transfers between devices, ring_shift(): lax.ppermute(block, axis, [(i, (i + step) % count) for i in range(count)])  23.9 us
    ppermute x1, waiting for transfers between devices, body(): returned = lax.ppermute(given, 'cz', SWAP)  14.7 us
  transfers between devices with their start and end apart: 22, of which 12 were waited for; matrix products, arithmetic and copies ran while one was open for 25% of the time, Pallas kernels for 0%

profile of v3, /device:TPU:175, one launch (start us, length us, event | category | flops | bytes accessed | tf_op | source)
XLA Modules:
  0.0 434.0 jit_solution(13250088296703936941)
XLA Ops:
  1.5 9.7 %collective-permute-start.7 = (bf16[12,16,128]{2,1,0:T(8,128)(2,1)S(1)}, bf16[12,16,128]{2,1,0:T(8,128)(2,1)S(1)}, u32[]{:S(2)}, u32[]{:S(2)}) collective-permute-start(bf16[12,16,128]{2,1,0:T(8,128)(2,1)S(1)} %constant_dynamic-update-slice_fusion.3), channel_id=1, source_target_pairs={{0,1},{1,0},{2,3},{3,2},{4,5},{5,4},{6,7},{7,6},{8,9},{9,8},{10,11... | collective-permute-start | bytes 147464 | tf_op jit(solution)/shard_map/ppermute | solution.py:55
  17.9 7.1 %collective-permute-done.8 = bf16[2,12,16,128]{3,2,1,0:T(8,128)(2,1)S(1)} collective-permute-done((bf16[2,12,16,128]{3,2,1,0:T(8,128)(2,1)S(1)}, bf16[2,12,16,128]{3,2,1,0:T(8,128)(2,1)S(1)}, u32[]{:S(2)}, u32[]{:S(2)}) %collective-permute-start.8) | collective-permute-done | bytes 98336 | tf_op jit(solution)/shard_map/ppermute | solution.py:55
  25.0 9.8 %collective-permute-start.9 = (bf16[2,2,12,16,128]{4,3,2,1,0:T(8,128)(2,1)S(1)}, bf16[2,2,12,16,128]{4,3,2,1,0:T(8,128)(2,1)S(1)}, u32[]{:S(2)}, u32[]{:S(2)}) collective-permute-start(bf16[2,2,12,16,128]{4,3,2,1,0:T(8,128)(2,1)S(1)} %maximum_select_fusion.11), channel_id=1, source_target_pairs={{0,16},{8,24},{16,0},{24,8},{32,48},{40,56},{48,32},{56,40},{1,17}... | collective-permute-start | bytes 589832 | tf_op jit(solution)/shard_map/ppermute | solution.py:55
  34.9 8.0 %collective-permute-done.9 = bf16[2,2,12,16,128]{4,3,2,1,0:T(8,128)(2,1)S(1)} collective-permute-done((bf16[2,2,12,16,128]{4,3,2,1,0:T(8,128)(2,1)S(1)}, bf16[2,2,12,16,128]{4,3,2,1,0:T(8,128)(2,1)S(1)}, u32[]{:S(2)}, u32[]{:S(2)}) %collective-permute-start.9) | collective-permute-done | bytes 196640 | tf_op jit(solution)/shard_map/ppermute | solution.py:55
  45.4 9.7 %collective-permute-done.10 = bf16[2,2,2,12,16,128]{5,4,3,2,1,0:T(8,128)(2,1)S(1)} collective-permute-done((bf16[2,2,2,12,16,128]{5,4,3,2,1,0:T(8,128)(2,1)S(1)}, bf16[2,2,2,12,16,128]{5,4,3,2,1,0:T(8,128)(2,1)S(1)}, u32[]{:S(2)}, u32[]{:S(2)}) %collective-permute-start.10) | collective-permute-done | bytes 393248 | tf_op jit(solution)/shard_map/ppermute | solution.py:55
  59.3 16.9 %collective-permute-done.11 = bf16[2,2,2,2,12,16,128]{6,5,4,3,2,1,0:T(8,128)(2,1)S(1)} collective-permute-done((bf16[2,2,2,2,12,16,128]{6,5,4,3,2,1,0:T(8,128)(2,1)S(1)}, bf16[2,2,2,2,12,16,128]{6,5,4,3,2,1,0:T(8,128)(2,1)S(1)}, u32[]{:S(2)}, u32[]{:S(2)}) %collective-permute-start.11) | collective-permute-done | bytes 786464 | tf_op jit(solution)/shard_map/ppermute | solution.py:55
  80.2 33.2 %collective-permute-done.12 = bf16[2,2,2,2,2,12,16,128]{7,6,5,4,3,2,1,0:T(8,128)(2,1)S(1)} collective-permute-done((bf16[2,2,2,2,2,12,16,128]{7,6,5,4,3,2,1,0:T(8,128)(2,1)}, bf16[2,2,2,2,2,12,16,128]{7,6,5,4,3,2,1,0:T(8,128)(2,1)S(1)}, u32[]{:S(2)}, u32[]{:S(2)}) %collective-permute-start.12) | collective-permute-done | bytes 1572896 | tf_op jit(solution)/shard_map/ppermute | solution.py:55
  115.6 5.2 %collective-permute-start.13 = (bf16[2,2,2,2,2,2,12,16,128]{8,7,6,5,4,3,2,1,0:T(8,128)(2,1)}, bf16[2,2,2,2,2,2,12,16,128]{8,7,6,5,4,3,2,1,0:T(8,128)(2,1)}, u32[]{:S(2)}, u32[]{:S(2)}) collective-permute-start(bf16[2,2,2,2,2,2,12,16,128]{8,7,6,5,4,3,2,1,0:T(8,128)(2,1)} %maximum_select_fusion.1), channel_id=1, source_target_pairs={{0,64},{64,0},{1,65},{65,1},{2,66},{66,2},{3,67},{67,3},{4,68},{68... | collective-permute-start | bytes 9437192 | tf_op jit(solution)/shard_map/ppermute | solution.py:55
  130.4 8.2 %collective-permute-start.2 = (bf16[4,6,64,128]{3,2,1,0:T(8,128)(2,1)S(1)}, bf16[4,6,64,128]{3,2,1,0:T(8,128)(2,1)S(1)}, u32[]{:S(2)}, u32[]{:S(2)}) collective-permute-start(bf16[4,6,64,128]{3,2,1,0:T(8,128)(2,1)S(1)} %get-tuple-element.19), channel_id=1, source_target_pairs={{0,1},{1,0},{2,3},{3,2},{4,5},{5,4},{6,7},{7,6},{8,9},{9,8},{10,11... | collective-permute-start | bytes 1179656 | tf_op jit(solution)/shard_map/ppermute | solution.py:85
  138.6 38.7 %collective-permute-done.2 = bf16[4,6,64,128]{3,2,1,0:T(8,128)(2,1)S(1)} collective-permute-done((bf16[4,6,64,128]{3,2,1,0:T(8,128)(2,1)S(1)}, bf16[4,6,64,128]{3,2,1,0:T(8,128)(2,1)S(1)}, u32[]{:S(2)}, u32[]{:S(2)}) %collective-permute-start.2) | collective-permute-done | bytes 393248 | tf_op jit(solution)/shard_map/ppermute | solution.py:85
  184.2 6.3 %collective-permute-start.14 = (f32[2,128]{1,0:T(2,128)S(1)}, f32[2,128]{1,0:T(2,128)S(1)}, u32[]{:S(2)}, u32[]{:S(2)}) collective-permute-start(f32[2,128]{1,0:T(2,128)S(1)} %pad_maximum_fusion.1), channel_id=1, source_target_pairs={{0,1},{1,0},{2,3},{3,2},{4,5},{5,4},{6,7},{7,6},{8,9},{9,8},{10,11... | collective-permute-start | bytes 3080 | tf_op jit(solution)/shard_map/ppermute | solution.py:81
  190.6 8.7 %collective-permute-done.3 = bf16[4,6,64,256]{3,2,1,0:T(8,128)(2,1)S(1)} collective-permute-done((bf16[4,6,64,256]{3,2,1,0:T(8,128)(2,1)S(1)}, bf16[4,6,64,256]{3,2,1,0:T(8,128)(2,1)S(1)}, u32[]{:S(2)}, u32[]{:S(2)}) %collective-permute-start.3) | collective-permute-done | bytes 786464 | tf_op jit(solution)/shard_map/ppermute | solution.py:23
  203.1 4.6 %collective-permute-start.6 = (bf16[4,6,64,128]{3,2,1,0:T(8,128)(2,1)}, bf16[4,6,64,128]{3,2,1,0:T(8,128)(2,1)}, u32[]{:S(2)}, u32[]{:S(2)}) collective-permute-start(bf16[4,6,64,128]{3,2,1,0:T(8,128)(2,1)} %slice.178), channel_id=1, source_target_pairs={{0,2},{2,4},{4,6},{6,0},{1,3},{3,5},{5,7},{7,1},{8,10},{10,12},{12... | collective-permute-start | bytes 1179656 | tf_op jit(solution)/shard_map/ppermute | solution.py:23
  208.2 21.1 %dynamic_update_slice.30 = bf16[4,6,66,1024]{3,2,1,0:T(8,128)(2,1)S(1)} dynamic-update-slice(bf16[4,6,66,1024]{3,2,1,0:T(8,128)(2,1)S(1)} %broadcast_in_dim.6, bf16[4,6,64,256]{3,2,1,0:T(8,128)(2,1)} %copy-done.5, s32[]{:T(128)} %constant.152.clone.1, s32[]{:T(128)} %constant.152.clone.1, s32[]{:T(128)} %constant.150.clone.1, s32[]{:T(128)S(6)} %select_n.305) | dynamic-update-slice | bytes 1572868 | tf_op jit(solution)/shard_map/dynamic_update_slice | solution.py:46
  229.3 21.5 %dynamic_update_slice.31 = bf16[4,6,66,1024]{3,2,1,0:T(8,128)(2,1)S(1)} dynamic-update-slice(bf16[4,6,66,1024]{3,2,1,0:T(8,128)(2,1)S(1)} %dynamic_update_slice.30, bf16[4,6,64,256]{3,2,1,0:T(8,128)(2,1)} %copy-done.16, s32[]{:T(128)} %constant.152.clone.1, s32[]{:T(128)} %constant.152.clone.1, s32[]{:T(128)} %constant.150.clone.1, s32[]{:T(128)S(6)} %select_n.307) | dynamic-update-slice | bytes 1572868 | tf_op jit(solution)/shard_map/dynamic_update_slice | solution.py:46
  250.8 21.5 %dynamic_update_slice.32 = bf16[4,6,66,1024]{3,2,1,0:T(8,128)(2,1)S(1)} dynamic-update-slice(bf16[4,6,66,1024]{3,2,1,0:T(8,128)(2,1)S(1)} %dynamic_update_slice.31, bf16[4,6,64,256]{3,2,1,0:T(8,128)(2,1)} %copy-done.17, s32[]{:T(128)} %constant.152.clone.1, s32[]{:T(128)} %constant.152.clone.1, s32[]{:T(128)} %constant.150.clone.1, s32[]{:T(128)S(6)} %select_n.309) | dynamic-update-slice | bytes 1572868 | tf_op jit(solution)/shard_map/dynamic_update_slice | solution.py:46
  275.6 5.8 %dynamic_update_slice.33 = bf16[4,6,66,1024]{3,2,1,0:T(8,128)(2,1)S(1)} dynamic-update-slice(bf16[4,6,66,1024]{3,2,1,0:T(8,128)(2,1)S(1)} %dynamic_update_slice.32, bf16[4,6,64,128]{3,2,1,0:T(8,128)(2,1)} %collective-permute-done.5, s32[]{:T(128)} %constant.152.clone.1, s32[]{:T(128)} %constant.152.clone.1, s32[]{:T(128)} %constant.150.clone.1, s32[]{:T(128)S(6)} %select_n.311) | dynamic-update-slice | bytes 786436 | tf_op jit(solution)/shard_map/dynamic_update_slice | solution.py:46
  281.4 5.8 %dynamic_update_slice.34 = bf16[4,6,66,1024]{3,2,1,0:T(8,128)(2,1)S(1)} dynamic-update-slice(bf16[4,6,66,1024]{3,2,1,0:T(8,128)(2,1)S(1)} %dynamic_update_slice.33, bf16[4,6,64,128]{3,2,1,0:T(8,128)(2,1)} %collective-permute-done.6, s32[]{:T(128)} %constant.152.clone.1, s32[]{:T(128)} %constant.152.clone.1, s32[]{:T(128)} %constant.150.clone.1, s32[]{:T(128)S(6)} %select_n.312) | dynamic-update-slice | bytes 786436 | tf_op jit(solution)/shard_map/dynamic_update_slice | solution.py:46
  341.8 5.4 %fusion.56 = (bf16[4,4,64,256]{3,2,1,0:T(8,128)(2,1)S(1)}, bf16[4,4,64,256]{3,2,1,0:T(8,128)(2,1)}) fusion(f32[256]{0:T(256)S(1)} %bitcast.93, f32[4,4,64,256]{3,2,1,0:T(8,128)} %fusion.1, f32[4,4,64,256]{3,2,1,0:T(8,128)} %fusion.3, f32[4,4,64,256]{3,2,1,0:T(8,128)} %fusion.5, f32[4,4,64,256]{3,2,1,0:T(8,128)} %fusion.7, f32[4,4,64,256]{3,2,1,0:T(8,128)} %fusion.9, ...), kind=kOutput, calls=%fused_computation.46 | convolution fusion | flops 541065216 | bytes 12059648 | tf_op jit(solution)/shard_map/fhwc,cd->fhwd/dot_general | solution.py:68
  347.2 5.1 %collective-permute-start.15 = (bf16[1,4,64,256]{3,2,1,0:T(8,128)(2,1)S(1)}, bf16[1,4,64,256]{3,2,1,0:T(8,128)(2,1)S(1)}, u32[]{:S(2)}, u32[]{:S(2)}) collective-permute-start(bf16[1,4,64,256]{3,2,1,0:T(8,128)(2,1)S(1)} %get-tuple-element.23), channel_id=1, source_target_pairs={{0,64},{64,128},{128,192},{192,256},{256,320},{320,384},{384,448},... | collective-permute-start | bytes 393224 | tf_op jit(solution)/shard_map/ppermute | solution.py:15
  361.9 4.6 %collective-permute-start.18 = (bf16[6,4,64,256]{3,2,1,0:T(8,128)(2,1)}, bf16[6,4,64,256]{3,2,1,0:T(8,128)(2,1)}, u32[]{:S(2)}, u32[]{:S(2)}) collective-permute-start(bf16[6,4,64,256]{3,2,1,0:T(8,128)(2,1)} %get-tuple-element.17), channel_id=1, source_target_pairs={{0,2},{2,4},{4,6},{6,0},{1,3},{3,5},{5,7},{7,1},{8,10},{10,12},{12... | collective-permute-start | bytes 2359304 | tf_op jit(solution)/shard_map/ppermute | solution.py:23
  366.7 15.2 %collective-permute-done.17 = bf16[6,4,64,256]{3,2,1,0:T(8,128)(2,1)} collective-permute-done((bf16[6,4,64,256]{3,2,1,0:T(8,128)(2,1)}, bf16[6,4,64,256]{3,2,1,0:T(8,128)(2,1)}, u32[]{:S(2)}, u32[]{:S(2)}) %collective-permute-start.17) | collective-permute-done | bytes 786464 | tf_op jit(solution)/shard_map/ppermute | solution.py:23
  412.2 6.3 %collective-permute-start.21 = (bf16[4,4,64,128]{3,2,1,0:T(8,128)(2,1)S(1)}, bf16[4,4,64,128]{3,2,1,0:T(8,128)(2,1)S(1)}, u32[]{:S(2)}, u32[]{:S(2)}) collective-permute-start(bf16[4,4,64,128]{3,2,1,0:T(8,128)(2,1)S(1)} %get-tuple-element.21), channel_id=1, source_target_pairs={{0,1},{1,0},{2,3},{3,2},{4,5},{5,4},{6,7},{7,6},{8,9},{9,8},{10,11... | collective-permute-start | bytes 786440 | tf_op jit(solution)/shard_map/ppermute | solution.py:112
  418.5 14.7 %collective-permute-done.21 = bf16[4,4,64,128]{3,2,1,0:T(8,128)(2,1)S(1)} collective-permute-done((bf16[4,4,64,128]{3,2,1,0:T(8,128)(2,1)S(1)}, bf16[4,4,64,128]{3,2,1,0:T(8,128)(2,1)S(1)}, u32[]{:S(2)}, u32[]{:S(2)}) %collective-permute-start.21) | collective-permute-done | bytes 262176 | tf_op jit(solution)/shard_map/ppermute | solution.py:112
  (156 shorter events, 140.0 us)
Async XLA Ops:
  1.5 13.6 %collective-permute-start.7 = (bf16[12,16,128]{2,1,0:T(8,128)(2,1)S(1)}, bf16[12,16,128]{2,1,0:T(8,128)(2,1)S(1)}, u32[]{:S(2)}, u32[]{:S(2)}) collective-permute-start(bf16[12,16,128]{2,1,0:T(8,128)(2,1)S(1)} %constant_dynamic-update-slice_fusion.3), channel_id=1, source_target_pairs={{0,1},{1,0},{2,3},{3,2},{4,5},{5,4},{6,7},{7,6},{8,9},{9,8},{10,11... | collective-permute-start | bytes 147464 | tf_op jit(solution)/shard_map/ppermute | solution.py:55
  15.1 9.8 %collective-permute-start.8 = (bf16[2,12,16,128]{3,2,1,0:T(8,128)(2,1)S(1)}, bf16[2,12,16,128]{3,2,1,0:T(8,128)(2,1)S(1)}, u32[]{:S(2)}, u32[]{:S(2)}) collective-permute-start(bf16[2,12,16,128]{3,2,1,0:T(8,128)(2,1)S(1)} %maximum_select_fusion.13), channel_id=1, source_target_pairs={{0,32},{8,40},{16,48},{24,56},{32,0},{40,8},{48,16},{56,24},{1,33}... | collective-permute-start | bytes 294920 | tf_op jit(solution)/shard_map/ppermute | solution.py:55
  25.0 17.9 %collective-permute-start.9 = (bf16[2,2,12,16,128]{4,3,2,1,0:T(8,128)(2,1)S(1)}, bf16[2,2,12,16,128]{4,3,2,1,0:T(8,128)(2,1)S(1)}, u32[]{:S(2)}, u32[]{:S(2)}) collective-permute-start(bf16[2,2,12,16,128]{4,3,2,1,0:T(8,128)(2,1)S(1)} %maximum_select_fusion.11), channel_id=1, source_target_pairs={{0,16},{8,24},{16,0},{24,8},{32,48},{40,56},{48,32},{56,40},{1,17}... | collective-permute-start | bytes 589832 | tf_op jit(solution)/shard_map/ppermute | solution.py:55
  43.0 12.1 %collective-permute-start.10 = (bf16[2,2,2,12,16,128]{5,4,3,2,1,0:T(8,128)(2,1)S(1)}, bf16[2,2,2,12,16,128]{5,4,3,2,1,0:T(8,128)(2,1)S(1)}, u32[]{:S(2)}, u32[]{:S(2)}) collective-permute-start(bf16[2,2,2,12,16,128]{5,4,3,2,1,0:T(8,128)(2,1)S(1)} %maximum_select_fusion.9), channel_id=1, source_target_pairs={{0,8},{8,0},{16,24},{24,16},{32,40},{40,32},{48,56},{56,48},{1,9},... | collective-permute-start | bytes 1179656 | tf_op jit(solution)/shard_map/ppermute | solution.py:55
  55.2 21.1 %collective-permute-start.11 = (bf16[2,2,2,2,12,16,128]{6,5,4,3,2,1,0:T(8,128)(2,1)S(1)}, bf16[2,2,2,2,12,16,128]{6,5,4,3,2,1,0:T(8,128)(2,1)S(1)}, u32[]{:S(2)}, u32[]{:S(2)}) collective-permute-start(bf16[2,2,2,2,12,16,128]{6,5,4,3,2,1,0:T(8,128)(2,1)S(1)} %maximum_select_fusion.6), channel_id=1, source_target_pairs={{0,256},{128,384},{256,0},{384,128},{1,257},{129,385},{257,1},{385... | collective-permute-start | bytes 2359304 | tf_op jit(solution)/shard_map/ppermute | solution.py:55
  77.7 35.7 %collective-permute-start.12 = (bf16[2,2,2,2,2,12,16,128]{7,6,5,4,3,2,1,0:T(8,128)(2,1)}, bf16[2,2,2,2,2,12,16,128]{7,6,5,4,3,2,1,0:T(8,128)(2,1)S(1)}, u32[]{:S(2)}, u32[]{:S(2)}) collective-permute-start(bf16[2,2,2,2,2,12,16,128]{7,6,5,4,3,2,1,0:T(8,128)(2,1)} %maximum_select_fusion.3), channel_id=1, source_target_pairs={{0,128},{128,0},{256,384},{384,256},{1,129},{129,1},{257,385},{385... | collective-permute-start | bytes 4718600 | tf_op jit(solution)/shard_map/ppermute | solution.py:55
  115.6 68.6 %copy-start.21 = (f32[128]{0:T(128)S(1)}, f32[128]{0:T(128)}, u32[]{:S(2)}) copy-start(f32[128]{0:T(128)} %param.10) | copy-start | bytes 1540
  115.6 68.6 %copy-start.22 = (f32[128]{0:T(128)S(1)}, f32[128]{0:T(128)}, u32[]{:S(2)}) copy-start(f32[128]{0:T(128)} %param.9) | copy-start | bytes 1540
  115.6 176.0 %collective-permute-start.13 = (bf16[2,2,2,2,2,2,12,16,128]{8,7,6,5,4,3,2,1,0:T(8,128)(2,1)}, bf16[2,2,2,2,2,2,12,16,128]{8,7,6,5,4,3,2,1,0:T(8,128)(2,1)}, u32[]{:S(2)}, u32[]{:S(2)}) collective-permute-start(bf16[2,2,2,2,2,2,12,16,128]{8,7,6,5,4,3,2,1,0:T(8,128)(2,1)} %maximum_select_fusion.1), channel_id=1, source_target_pairs={{0,64},{64,0},{1,65},{65,1},{2,66},{66,2},{3,67},{67,3},{4,68},{68... | collective-permute-start | bytes 9437192 | tf_op jit(solution)/shard_map/ppermute | solution.py:55
  120.8 6.4 %collective-permute-start = (bf16[4,1,64,128]{3,2,1,0:T(8,128)(2,1)S(1)}, bf16[4,1,64,128]{3,2,1,0:T(8,128)(2,1)S(1)}, u32[]{:S(2)}, u32[]{:S(2)}) collective-permute-start(bf16[4,1,64,128]{3,2,1,0:T(8,128)(2,1)S(1)} %get-tuple-element.26), channel_id=1, source_target_pairs={{0,8},{8,16},{16,24},{24,32},{32,40},{40,48},{48,56},{1,9},{9,17},... | collective-permute-start | bytes 196616 | tf_op jit(solution)/shard_map/ppermute | solution.py:15
  125.3 5.0 %collective-permute-start.1 = (bf16[4,1,64,128]{3,2,1,0:T(8,128)(2,1)S(1)}, bf16[4,1,64,128]{3,2,1,0:T(8,128)(2,1)S(1)}, u32[]{:S(2)}, u32[]{:S(2)}) collective-permute-start(bf16[4,1,64,128]{3,2,1,0:T(8,128)(2,1)S(1)} %get-tuple-element.25), channel_id=1, source_target_pairs={{8,0},{16,8},{24,16},{32,24},{40,32},{48,40},{56,48},{9,1},{17,9},... | collective-permute-start | bytes 196616 | tf_op jit(solution)/shard_map/ppermute | solution.py:18
  130.4 46.9 %collective-permute-start.2 = (bf16[4,6,64,128]{3,2,1,0:T(8,128)(2,1)S(1)}, bf16[4,6,64,128]{3,2,1,0:T(8,128)(2,1)S(1)}, u32[]{:S(2)}, u32[]{:S(2)}) collective-permute-start(bf16[4,6,64,128]{3,2,1,0:T(8,128)(2,1)S(1)} %get-tuple-element.19), channel_id=1, source_target_pairs={{0,1},{1,0},{2,3},{3,2},{4,5},{5,4},{6,7},{7,6},{8,9},{9,8},{10,11... | collective-permute-start | bytes 1179656 | tf_op jit(solution)/shard_map/ppermute | solution.py:85
  177.7 21.6 %collective-permute-start.3 = (bf16[4,6,64,256]{3,2,1,0:T(8,128)(2,1)S(1)}, bf16[4,6,64,256]{3,2,1,0:T(8,128)(2,1)S(1)}, u32[]{:S(2)}, u32[]{:S(2)}) collective-permute-start(bf16[4,6,64,256]{3,2,1,0:T(8,128)(2,1)S(1)} %maximum_select_fusion.5), channel_id=1, source_target_pairs={{0,6},{2,0},{4,2},{6,4},{1,7},{3,1},{5,3},{7,5},{8,14},{10,8},{12,... | collective-permute-start | bytes 2359304 | tf_op jit(solution)/shard_map/ppermute | solution.py:23
  180.1 22.0 %collective-permute-start.4 = (bf16[4,6,64,256]{3,2,1,0:T(8,128)(2,1)S(1)}, bf16[4,6,64,256]{3,2,1,0:T(8,128)(2,1)S(1)}, u32[]{:S(2)}, u32[]{:S(2)}) collective-permute-start(bf16[4,6,64,256]{3,2,1,0:T(8,128)(2,1)S(1)} %maximum_select_fusion.5), channel_id=1, source_target_pairs={{0,2},{2,4},{4,6},{6,0},{1,3},{3,5},{5,7},{7,1},{8,10},{10,12},{12... | collective-permute-start | bytes 2359304 | tf_op jit(solution)/shard_map/ppermute | solution.py:23
  184.2 23.5 %collective-permute-start.14 = (f32[2,128]{1,0:T(2,128)S(1)}, f32[2,128]{1,0:T(2,128)S(1)}, u32[]{:S(2)}, u32[]{:S(2)}) collective-permute-start(f32[2,128]{1,0:T(2,128)S(1)} %pad_maximum_fusion.1), channel_id=1, source_target_pairs={{0,1},{1,0},{2,3},{3,2},{4,5},{5,4},{6,7},{7,6},{8,9},{9,8},{10,11... | collective-permute-start | bytes 3080 | tf_op jit(solution)/shard_map/ppermute | solution.py:81
  200.2 75.4 %collective-permute-start.5 = (bf16[4,6,64,128]{3,2,1,0:T(8,128)(2,1)}, bf16[4,6,64,128]{3,2,1,0:T(8,128)(2,1)}, u32[]{:S(2)}, u32[]{:S(2)}) collective-permute-start(bf16[4,6,64,128]{3,2,1,0:T(8,128)(2,1)} %slice.177), channel_id=1, source_target_pairs={{0,6},{2,0},{4,2},{6,4},{1,7},{3,1},{5,3},{7,5},{8,14},{10,8},{12,... | collective-permute-start | bytes 1179656 | tf_op jit(solution)/shard_map/ppermute | solution.py:23
  203.1 78.3 %collective-permute-start.6 = (bf16[4,6,64,128]{3,2,1,0:T(8,128)(2,1)}, bf16[4,6,64,128]{3,2,1,0:T(8,128)(2,1)}, u32[]{:S(2)}, u32[]{:S(2)}) collective-permute-start(bf16[4,6,64,128]{3,2,1,0:T(8,128)(2,1)} %slice.178), channel_id=1, source_target_pairs={{0,2},{2,4},{4,6},{6,0},{1,3},{3,5},{5,7},{7,1},{8,10},{10,12},{12... | collective-permute-start | bytes 1179656 | tf_op jit(solution)/shard_map/ppermute | solution.py:23
  347.2 7.0 %collective-permute-start.15 = (bf16[1,4,64,256]{3,2,1,0:T(8,128)(2,1)S(1)}, bf16[1,4,64,256]{3,2,1,0:T(8,128)(2,1)S(1)}, u32[]{:S(2)}, u32[]{:S(2)}) collective-permute-start(bf16[1,4,64,256]{3,2,1,0:T(8,128)(2,1)S(1)} %get-tuple-element.23), channel_id=1, source_target_pairs={{0,64},{64,128},{128,192},{192,256},{256,320},{320,384},{384,448},... | collective-permute-start | bytes 393224 | tf_op jit(solution)/shard_map/ppermute | solution.py:15
  352.3 6.3 %collective-permute-start.16 = (bf16[1,4,64,256]{3,2,1,0:T(8,128)(2,1)S(1)}, bf16[1,4,64,256]{3,2,1,0:T(8,128)(2,1)S(1)}, u32[]{:S(2)}, u32[]{:S(2)}) collective-permute-start(bf16[1,4,64,256]{3,2,1,0:T(8,128)(2,1)S(1)} %get-tuple-element.24), channel_id=1, source_target_pairs={{64,0},{128,64},{192,128},{256,192},{320,256},{384,320},{448,384},... | collective-permute-start | bytes 393224 | tf_op jit(solution)/shard_map/ppermute | solution.py:18
  360.0 21.8 %collective-permute-start.17 = (bf16[6,4,64,256]{3,2,1,0:T(8,128)(2,1)}, bf16[6,4,64,256]{3,2,1,0:T(8,128)(2,1)}, u32[]{:S(2)}, u32[]{:S(2)}) collective-permute-start(bf16[6,4,64,256]{3,2,1,0:T(8,128)(2,1)} %get-tuple-element.17), channel_id=1, source_target_pairs={{0,6},{2,0},{4,2},{6,4},{1,7},{3,1},{5,3},{7,5},{8,14},{10,8},{12,... | collective-permute-start | bytes 2359304 | tf_op jit(solution)/shard_map/ppermute | solution.py:23
  361.9 22.9 %collective-permute-start.18 = (bf16[6,4,64,256]{3,2,1,0:T(8,128)(2,1)}, bf16[6,4,64,256]{3,2,1,0:T(8,128)(2,1)}, u32[]{:S(2)}, u32[]{:S(2)}) collective-permute-start(bf16[6,4,64,256]{3,2,1,0:T(8,128)(2,1)} %get-tuple-element.17), channel_id=1, source_target_pairs={{0,2},{2,4},{4,6},{6,0},{1,3},{3,5},{5,7},{7,1},{8,10},{10,12},{12... | collective-permute-start | bytes 2359304 | tf_op jit(solution)/shard_map/ppermute | solution.py:23
  382.9 24.6 %collective-permute-start.19 = (bf16[6,4,64,128]{3,2,1,0:T(8,128)(2,1)S(1)}, bf16[6,4,64,128]{3,2,1,0:T(8,128)(2,1)}, u32[]{:S(2)}, u32[]{:S(2)}) collective-permute-start(bf16[6,4,64,128]{3,2,1,0:T(8,128)(2,1)S(1)} %slice.201), channel_id=1, source_target_pairs={{0,6},{2,0},{4,2},{6,4},{1,7},{3,1},{5,3},{7,5},{8,14},{10,8},{12,... | collective-permute-start | bytes 1179656 | tf_op jit(solution)/shard_map/ppermute | solution.py:23
  386.6 22.0 %collective-permute-start.20 = (bf16[6,4,64,128]{3,2,1,0:T(8,128)(2,1)}, bf16[6,4,64,128]{3,2,1,0:T(8,128)(2,1)}, u32[]{:S(2)}, u32[]{:S(2)}) collective-permute-start(bf16[6,4,64,128]{3,2,1,0:T(8,128)(2,1)} %slice.202), channel_id=1, source_target_pairs={{0,2},{2,4},{4,6},{6,0},{1,3},{3,5},{5,7},{7,1},{8,10},{10,12},{12... | collective-permute-start | bytes 1179656 | tf_op jit(solution)/shard_map/ppermute | solution.py:23
  412.2 21.0 %collective-permute-start.21 = (bf16[4,4,64,128]{3,2,1,0:T(8,128)(2,1)S(1)}, bf16[4,4,64,128]{3,2,1,0:T(8,128)(2,1)S(1)}, u32[]{:S(2)}, u32[]{:S(2)}) collective-permute-start(bf16[4,4,64,128]{3,2,1,0:T(8,128)(2,1)S(1)} %get-tuple-element.21), channel_id=1, source_target_pairs={{0,1},{1,0},{2,3},{3,2},{4,5},{5,4},{6,7},{7,6},{8,9},{9,8},{10,11... | collective-permute-start | bytes 786440 | tf_op jit(solution)/shard_map/ppermute | solution.py:112
  (22 other events, 179.2 us)

commit v4 on v3

--- a/solution.py
+++ b/solution.py
@@ -29,45 +29,51 @@
     )
 
 
-def x_gather(pair, pad):
+def x_gather(pair):
     ring = lax.axis_size("cx")
-    me = lax.axis_index("cx")
-    width = pair.shape[3]
-    half = width // 2
+    half = pair.shape[3] // 2
     from_left = ring_shift(pair, "cx", ring, 1)
     from_right = ring_shift(pair, "cx", ring, -1)
     far_low = ring_shift(from_right[..., :half], "cx", ring, -1)
     far_high = ring_shift(from_left[..., half:], "cx", ring, 1)
-    frames, rows, wide, _ = pair.shape
-    out = jnp.zeros((frames, rows, wide + 2 * pad, width * ring), pair.dtype)
-    pieces = ((0, pair, 0), (1, from_right, 0), (ring - 1, from_left, 0), (2, far_low, 0), (2, far_high, half))
-    for offset, piece, shift in pieces:
-        base = ((me + offset) % ring) * width + shift
-        out = lax.dynamic_update_slice(out, piece, (0, 0, pad, base))
+    return jnp.concatenate([pair, from_right, far_low, far_high, from_left], axis=3)
+
+
+def ring_gather(block, axis):
+    ring = lax.axis_size(axis)
+    me = lax.axis_index(axis)
+    half = block.shape[0] // 2
+    from_left = ring_shift(block, axis, ring, 1)
+    from_right = ring_shift(block, axis, ring, -1)
+    far_low = ring_shift(from_right[:half], axis, ring, -1)
+    far_high = ring_shift(from_left[half:], axis, ring, 1)
+    far = jnp.concatenate([far_low, far_high], axis=0)
+    out = jnp.zeros((ring,) + block.shape, block.dtype)
+    for offset, piece in ((0, block), (1, from_right), (2, far), (ring - 1, from_left)):
+        start = ((me + offset) % ring,) + (0,) * block.ndim
+        out = lax.dynamic_update_slice(out, piece[None], start)
     return out
 
 
-def weight_gather(weight):
-    steps = (("cz", 1), ("row", 4), ("row", 2), ("row", 1), ("fy", 2), ("fy", 1), ("fc", 1))
-    block = weight
-    for axis, bit in steps:
-        count = lax.axis_size(axis)
-        other = lax.ppermute(block, axis, [(i, i ^ bit) for i in range(count)])
-        high = (lax.axis_index(axis) // bit) % 2 == 1
-        block = jnp.where(high, jnp.stack([other, block]), jnp.stack([block, other]))
-    block = jnp.transpose(block, (7, 2, 1, 0, 5, 4, 3, 8, 6, 9))
-    taps, depth, width = weight.shape
-    return block.reshape(taps, 64 * depth, 2 * width)
+def swap_stack(block, axis, bit):
+    count = lax.axis_size(axis)
+    other = lax.ppermute(block, axis, [(i, i ^ bit) for i in range(count)])
+    high = (lax.axis_index(axis) // bit) % 2 == 1
+    return jnp.where(high, jnp.stack([other, block]), jnp.stack([block, other]))
 
 
-def spatial_terms(gathered, weights, row_count, wide):
-    total = None
-    for tap in range(9):
-        shift_y, shift_x = (tap // 3, tap % 3)
-        window = gathered[:, shift_y : shift_y + row_count, shift_x : shift_x + wide, :]
-        term = jnp.einsum("fhwc,cd->fhwd", window, weights[tap], preferred_element_type=jnp.float32)
-        total = term if total is None else total + term
-    return total
+def weight_gather(weight):
+    block = swap_stack(weight, "cz", 1)
+    for bit in (4, 2, 1):
+        block = swap_stack(block, "row", bit)
+    block = ring_gather(block, "fy")
+    block = swap_stack(block, "fc", 1)
+    block = jnp.transpose(block, (6, 1, 0, 4, 3, 2, 7, 5, 8))
+    taps, depth, width = weight.shape
+    full = block.reshape(taps, 64 * depth, 2 * width)
+    doubled = jnp.concatenate([full, full], axis=1)
+    shift = lax.axis_index("cx") * 2 * width
+    return lax.dynamic_slice_in_dim(doubled, shift, 64 * depth, axis=1)
 
 
 def body(frames_in, spatial_weight, temporal_weight, spatial_bias, temporal_bias, clip_id):
@@ -83,8 +89,16 @@
     mine = lax.dynamic_slice_in_dim(rimmed, side * half, half + 2, axis=1)
     wanted = lax.dynamic_slice_in_dim(rimmed, (1 - side) * half, half + 2, axis=1)
     partner = lax.ppermute(wanted, "cz", SWAP)
-    gathered = x_gather(ordered_pair(mine, partner, high, 3), 1)
-    spatial = spatial_terms(gathered, full_spatial, half, wide)
+    gathered = x_gather(ordered_pair(mine, partner, high, 3))
+    kernel = full_spatial.reshape((3, 3) + full_spatial.shape[1:])
+    spatial = lax.conv_general_dilated(
+        gathered,
+        kernel,
+        (1, 1),
+        ((0, 0), (1, 1)),
+        dimension_numbers=("NHWC", "HWIO", "NHWC"),
+        preferred_element_type=jnp.float32,
+    )
     hidden = (spatial + biases[0]).astype(jnp.bfloat16)
     active = jax.nn.silu(hidden.astype(jnp.float32)).astype(jnp.bfloat16)
     index = lax.axis_index(FRAME)
@@ -94,7 +108,7 @@
     prev_ok = (local_ids[1:-1] == local_ids[:-2]).astype(jnp.float32).reshape(fr_count, 1, 1, 1)
     next_ok = (local_ids[1:-1] == local_ids[2:]).astype(jnp.float32).reshape(fr_count, 1, 1, 1)
     source = shift_halo(active, FRAME, lax.axis_size(FRAME), 0, 1)
-    whole = x_gather(source, 0)
+    whole = x_gather(source)
     taps = [
         jnp.einsum(
             "fhwc,cd->fhwd",

time: 439 us -> 327 us (0.74)
  the two profiles are of different devices: /device:TPU:175 before, /device:TPU:233 now
where the time goes in v4:
time: 327 us; the launch traced here: 325 us
  waiting for transfers between devices  151 us (46%)
  starting transfers between devices  85.3 us (26%)
  local copies, waits for them, and re-layouts  46.5 us (14%)
  other arithmetic  29.1 us (9%)
  matrix products  12.5 us (4%)
    ppermute x12, waiting for transfers between devices, ring_shift(): lax.ppermute(block, axis, [(i, (i + step) % count) for i in range(count)])  50.4 us
    ppermute x5, waiting for transfers between devices, swap_stack(): other = lax.ppermute(block, axis, [(i, i ^ bit) for i in range(count)])  39.6 us
    ppermute x1, waiting for transfers between devices, body(): partner = lax.ppermute(wanted, 'cz', SWAP)  38.9 us
    ppermute x12, starting transfers between devices, ring_shift(): lax.ppermute(block, axis, [(i, (i + step) % count) for i in range(count)])  35.2 us
    ppermute x5, starting transfers between devices, swap_stack(): other = lax.ppermute(block, axis, [(i, i ^ bit) for i in range(count)])  19.1 us
    ppermute x1, waiting for transfers between devices, body(): returned = lax.ppermute(given, 'cz', SWAP)  16.7 us
    transpose x1, other arithmetic, weight_gather(): block = jnp.transpose(block, (6, 1, 0, 4, 3, 2, 7, 5, 8))  14.2 us
    unnamed x39, local copies, waits for them, and re-layouts  13.6 us
  transfers between devices with their start and end apart: 24, of which 16 were waited for; matrix products, arithmetic and copies ran while one was open for 10% of the time, Pallas kernels for 0%

profile of v4, /device:TPU:233, one launch (start us, length us, event | category | flops | bytes accessed | tf_op | source)
XLA Modules:
  0.0 325.2 jit_solution(2422451653326813272)
XLA Ops:
  1.5 7.9 %collective-permute-start.7 = (bf16[12,16,128]{2,1,0:T(8,128)(2,1)S(1)}, bf16[12,16,128]{2,1,0:T(8,128)(2,1)S(1)}, u32[]{:S(2)}, u32[]{:S(2)}) collective-permute-start(bf16[12,16,128]{2,1,0:T(8,128)(2,1)S(1)} %constant_dynamic-update-slice_fusion.8), channel_id=1, source_target_pairs={{0,1},{1,0},{2,3},{3,2},{4,5},{5,4},{6,7},{7,6},{8,9},{9,8},{10,11... | collective-permute-start | bytes 147464 | tf_op jit(solution)/shard_map/ppermute | solution.py:60
  9.5 5.5 %collective-permute-done.7 = bf16[12,16,128]{2,1,0:T(8,128)(2,1)S(1)} collective-permute-done((bf16[12,16,128]{2,1,0:T(8,128)(2,1)S(1)}, bf16[12,16,128]{2,1,0:T(8,128)(2,1)S(1)}, u32[]{:S(2)}, u32[]{:S(2)}) %collective-permute-start.7) | collective-permute-done | bytes 49184 | tf_op jit(solution)/shard_map/ppermute | solution.py:60
  17.0 12.9 %collective-permute-done.8 = bf16[2,12,16,128]{3,2,1,0:T(8,128)(2,1)S(1)} collective-permute-done((bf16[2,12,16,128]{3,2,1,0:T(8,128)(2,1)S(1)}, bf16[2,12,16,128]{3,2,1,0:T(8,128)(2,1)S(1)}, u32[]{:S(2)}, u32[]{:S(2)}) %collective-permute-start.8) | collective-permute-done | bytes 98336 | tf_op jit(solution)/shard_map/ppermute | solution.py:60
  32.0 11.1 %collective-permute-done.9 = bf16[2,2,12,16,128]{4,3,2,1,0:T(8,128)(2,1)S(1)} collective-permute-done((bf16[2,2,12,16,128]{4,3,2,1,0:T(8,128)(2,1)S(1)}, bf16[2,2,12,16,128]{4,3,2,1,0:T(8,128)(2,1)S(1)}, u32[]{:S(2)}, u32[]{:S(2)}) %collective-permute-start.9) | collective-permute-done | bytes 196640 | tf_op jit(solution)/shard_map/ppermute | solution.py:60
  45.1 10.1 %collective-permute-done.10 = bf16[2,2,2,12,16,128]{5,4,3,2,1,0:T(8,128)(2,1)S(1)} collective-permute-done((bf16[2,2,2,12,16,128]{5,4,3,2,1,0:T(8,128)(2,1)S(1)}, bf16[2,2,2,12,16,128]{5,4,3,2,1,0:T(8,128)(2,1)S(1)}, u32[]{:S(2)}, u32[]{:S(2)}) %collective-permute-start.10) | collective-permute-done | bytes 393248 | tf_op jit(solution)/shard_map/ppermute | solution.py:60
  68.4 7.7 %collective-permute-done.13 = bf16[2,2,2,2,12,16,128]{6,5,4,3,2,1,0:T(8,128)(2,1)S(1)} collective-permute-done((bf16[2,2,2,2,12,16,128]{6,5,4,3,2,1,0:T(8,128)(2,1)}, bf16[2,2,2,2,12,16,128]{6,5,4,3,2,1,0:T(8,128)(2,1)S(1)}, u32[]{:S(2)}, u32[]{:S(2)}) %collective-permute-start.13) | collective-permute-done | bytes 786464 | tf_op jit(solution)/shard_map/ppermute | solution.py:23
  92.5 5.4 %collective-permute-start.15 = (bf16[4,2,2,2,2,12,16,128]{7,4,6,1,2,3,0,5:T(2,128)(2,1)S(1)}, bf16[4,2,2,2,2,12,16,128]{7,4,6,1,2,3,0,5:T(2,128)(2,1)}, u32[]{:S(2)}, u32[]{:S(2)}) collective-permute-start(bf16[4,2,2,2,2,12,16,128]{7,4,6,1,2,3,0,5:T(2,128)(2,1)S(1)} %copy_dynamic-update-slice_fusion), channel_id=1, source_target_pairs={{0,64},{64,0},{1,65},{65,1},{2,66},{66,2},{3,67},{67,3},{4,68},{68... | collective-permute-start | bytes 9437192 | tf_op jit(solution)/shard_map/ppermute | solution.py:60
  98.7 8.2 %collective-permute-start.2 = (bf16[4,6,64,128]{3,2,1,0:T(8,128)(2,1)}, bf16[4,6,64,128]{3,2,1,0:T(8,128)(2,1)}, u32[]{:S(2)}, u32[]{:S(2)}) collective-permute-start(bf16[4,6,64,128]{3,2,1,0:T(8,128)(2,1)} %get-tuple-element.10), channel_id=1, source_target_pairs={{0,1},{1,0},{2,3},{3,2},{4,5},{5,4},{6,7},{7,6},{8,9},{9,8},{10,11... | collective-permute-start | bytes 1179656 | tf_op jit(solution)/shard_map/ppermute | solution.py:91
  106.9 38.9 %collective-permute-done.2 = bf16[4,6,64,128]{3,2,1,0:T(8,128)(2,1)} collective-permute-done((bf16[4,6,64,128]{3,2,1,0:T(8,128)(2,1)}, bf16[4,6,64,128]{3,2,1,0:T(8,128)(2,1)}, u32[]{:S(2)}, u32[]{:S(2)}) %collective-permute-start.2) | collective-permute-done | bytes 393248 | tf_op jit(solution)/shard_map/ppermute | solution.py:91
  148.5 4.4 %collective-permute-start.3 = (bf16[4,6,64,256]{3,2,1,0:T(8,128)(2,1)}, bf16[4,6,64,256]{3,2,1,0:T(8,128)(2,1)}, u32[]{:S(2)}, u32[]{:S(2)}) collective-permute-start(bf16[4,6,64,256]{3,2,1,0:T(8,128)(2,1)} %get-tuple-element.6), channel_id=1, source_target_pairs={{0,6},{2,0},{4,2},{6,4},{1,7},{3,1},{5,3},{7,5},{8,14},{10,8},{12,... | collective-permute-start | bytes 2359304 | tf_op jit(solution)/shard_map/ppermute | solution.py:23
  154.8 5.1 %collective-permute-start.16 = (f32[2,128]{1,0:T(2,128)S(1)}, f32[2,128]{1,0:T(2,128)S(1)}, u32[]{:S(2)}, u32[]{:S(2)}) collective-permute-start(f32[2,128]{1,0:T(2,128)S(1)} %pad_maximum_fusion.1), channel_id=1, source_target_pairs={{0,1},{1,0},{2,3},{3,2},{4,5},{5,4},{6,7},{7,6},{8,9},{9,8},{10,11... | collective-permute-start | bytes 3080 | tf_op jit(solution)/shard_map/ppermute | solution.py:87
  160.0 9.6 %collective-permute-done.3 = bf16[4,6,64,256]{3,2,1,0:T(8,128)(2,1)} collective-permute-done((bf16[4,6,64,256]{3,2,1,0:T(8,128)(2,1)}, bf16[4,6,64,256]{3,2,1,0:T(8,128)(2,1)}, u32[]{:S(2)}, u32[]{:S(2)}) %collective-permute-start.3) | collective-permute-done | bytes 786464 | tf_op jit(solution)/shard_map/ppermute | solution.py:23
  170.6 5.3 %collective-permute-start.4 = (bf16[4,6,64,128]{3,2,1,0:T(8,128)(2,1)S(1)}, bf16[4,6,64,128]{3,2,1,0:T(8,128)(2,1)S(1)}, u32[]{:S(2)}, u32[]{:S(2)}) collective-permute-start(bf16[4,6,64,128]{3,2,1,0:T(8,128)(2,1)S(1)} %slice.96), channel_id=1, source_target_pairs={{0,6},{2,0},{4,2},{6,4},{1,7},{3,1},{5,3},{7,5},{8,14},{10,8},{12,... | collective-permute-start | bytes 1179656 | tf_op jit(solution)/shard_map/ppermute | solution.py:23
  183.8 5.3 %collective-permute-done.6 = bf16[4,6,64,128]{3,2,1,0:T(8,128)(2,1)S(1)} collective-permute-done((bf16[4,6,64,128]{3,2,1,0:T(8,128)(2,1)S(1)}, bf16[4,6,64,128]{3,2,1,0:T(8,128)(2,1)S(1)}, u32[]{:S(2)}, u32[]{:S(2)}) %collective-permute-start.6) | collective-permute-done | bytes 393248 | tf_op jit(solution)/shard_map/ppermute | solution.py:23
  192.1 4.3 %copy.28 = bf16[6,4,64,1024]{3,1,2,0:T(4,128)(2,1)S(1)} copy(bf16[6,4,64,1024]{3,2,0,1:T(8,128)(2,1)} %bitcast.79) | data formatting | bytes 6291456
  201.8 14.2 %fusion.1 = bf16[12,4,2,2,2,2,16,2,128]{8,7,6,5,4,3,2,1,0:T(2,128)(2,1)} fusion(pred[]{:T(512)S(6)} %eq.35, bf16[1,4,2,2,2,2,12,16,128]{8,5,7,2,3,4,0,1,6:T(2,128)(2,1)S(1)} %bitcast.78, bf16[1,4,2,2,2,2,12,16,128]{8,5,7,2,3,4,0,1,6:T(2,128)(2,1)} %bitcast.19), kind=kLoop, calls=%fused_computation.5 | loop fusion | flops 9437184 | bytes 12582913 | tf_op jit(solution)/shard_map/transpose | solution.py:71
  216.0 10.9 %reshape.422 = bf16[12,1024,256]{2,1,0:T(8,128)(2,1)} reshape(bf16[12,4,2,2,2,2,16,2,128]{8,7,6,5,4,3,2,1,0:T(2,128)(2,1)} %fusion.1) | data formatting | bytes 12582912 | tf_op jit(solution)/shard_map/reshape | solution.py:73
  226.9 5.2 %fusion.2 = bf16[12,1024,256]{2,1,0:T(8,128)(2,1)S(1)} fusion(s32[]{:T(128)S(6)} %select_n.252, bf16[12,1024,256]{2,1,0:T(8,128)(2,1)} %reshape.422), kind=kLoop, calls=%fused_computation.6 | loop fusion | flops 12582912 | bytes 12582916 | tf_op jit(solution)/shard_map/concatenate | solution.py:74
  234.8 7.2 %convert_add_fusion = (f32[4,32,9,256]{3,1,2,0:T(8,128)}, bf16[4,32,9,256]{3,1,2,0:T(8,128)(2,1)S(1)}) fusion(f32[256]{0:T(256)S(1)} %bitcast.107, f32[256]{0:T(256)S(1)} %bitcast.108, bf16[3,3,1024,256]{3,2,1,0:T(8,128)(2,1)S(1)} %bitcast.80, bf16[6,4,8,11,1024]{4,1,3,2,0:T(4,128)(2,1)S(1)} %bitcast.82, pred[32,9]{0,1:T(8,128)(4,1)S(1)} %copy-done.11), kind=kOutput, calls=%fused_computation.13 | convolution fusion | flops 5438767104 | bytes 10815776 | tf_op jit(solution)/shard_map/conv_general_dilated | solution.py:94
  242.7 5.3 %collective-permute-start.17 = (bf16[1,4,64,256]{3,2,1,0:T(8,128)(2,1)S(1)}, bf16[1,4,64,256]{3,2,1,0:T(8,128)(2,1)S(1)}, u32[]{:S(2)}, u32[]{:S(2)}) collective-permute-start(bf16[1,4,64,256]{3,2,1,0:T(8,128)(2,1)S(1)} %get-tuple-element.15), channel_id=1, source_target_pairs={{0,64},{64,128},{128,192},{192,256},{256,320},{320,384},{384,448},... | collective-permute-start | bytes 393224 | tf_op jit(solution)/shard_map/ppermute | solution.py:15
  250.0 4.3 %collective-permute-done.18 = bf16[1,4,64,256]{3,2,1,0:T(8,128)(2,1)S(1)} collective-permute-done((bf16[1,4,64,256]{3,2,1,0:T(8,128)(2,1)S(1)}, bf16[1,4,64,256]{3,2,1,0:T(8,128)(2,1)S(1)}, u32[]{:S(2)}, u32[]{:S(2)}) %collective-permute-start.18) | collective-permute-done | bytes 131104 | tf_op jit(solution)/shard_map/ppermute | solution.py:18
  260.7 15.9 %collective-permute-done.19 = bf16[6,4,64,256]{3,2,1,0:T(8,128)(2,1)S(1)} collective-permute-done((bf16[6,4,64,256]{3,2,1,0:T(8,128)(2,1)}, bf16[6,4,64,256]{3,2,1,0:T(8,128)(2,1)S(1)}, u32[]{:S(2)}, u32[]{:S(2)}) %collective-permute-start.19) | collective-permute-done | bytes 786464 | tf_op jit(solution)/shard_map/ppermute | solution.py:23
  302.5 5.1 %collective-permute-start.23 = (bf16[4,4,64,128]{3,2,1,0:T(8,128)(2,1)S(1)}, bf16[4,4,64,128]{3,2,1,0:T(8,128)(2,1)S(1)}, u32[]{:S(2)}, u32[]{:S(2)}) collective-permute-start(bf16[4,4,64,128]{3,2,1,0:T(8,128)(2,1)S(1)} %get-tuple-element.13), channel_id=1, source_target_pairs={{0,1},{1,0},{2,3},{3,2},{4,5},{5,4},{6,7},{7,6},{8,9},{9,8},{10,11... | collective-permute-start | bytes 786440 | tf_op jit(solution)/shard_map/ppermute | solution.py:126
  307.7 16.7 %collective-permute-done.23 = bf16[4,4,64,128]{3,2,1,0:T(8,128)(2,1)S(1)} collective-permute-done((bf16[4,4,64,128]{3,2,1,0:T(8,128)(2,1)S(1)}, bf16[4,4,64,128]{3,2,1,0:T(8,128)(2,1)S(1)}, u32[]{:S(2)}, u32[]{:S(2)}) %collective-permute-start.23) | collective-permute-done | bytes 262176 | tf_op jit(solution)/shard_map/ppermute | solution.py:126
  (119 shorter events, 97.9 us)
Async XLA Ops:
  1.5 13.5 %collective-permute-start.7 = (bf16[12,16,128]{2,1,0:T(8,128)(2,1)S(1)}, bf16[12,16,128]{2,1,0:T(8,128)(2,1)S(1)}, u32[]{:S(2)}, u32[]{:S(2)}) collective-permute-start(bf16[12,16,128]{2,1,0:T(8,128)(2,1)S(1)} %constant_dynamic-update-slice_fusion.8), channel_id=1, source_target_pairs={{0,1},{1,0},{2,3},{3,2},{4,5},{5,4},{6,7},{7,6},{8,9},{9,8},{10,11... | collective-permute-start | bytes 147464 | tf_op jit(solution)/shard_map/ppermute | solution.py:60
  15.1 14.9 %collective-permute-start.8 = (bf16[2,12,16,128]{3,2,1,0:T(8,128)(2,1)S(1)}, bf16[2,12,16,128]{3,2,1,0:T(8,128)(2,1)S(1)}, u32[]{:S(2)}, u32[]{:S(2)}) collective-permute-start(bf16[2,12,16,128]{3,2,1,0:T(8,128)(2,1)S(1)} %maximum_select_fusion.8), channel_id=1, source_target_pairs={{0,32},{8,40},{16,48},{24,56},{32,0},{40,8},{48,16},{56,24},{1,33}... | collective-permute-start | bytes 294920 | tf_op jit(solution)/shard_map/ppermute | solution.py:60
  30.0 13.1 %collective-permute-start.9 = (bf16[2,2,12,16,128]{4,3,2,1,0:T(8,128)(2,1)S(1)}, bf16[2,2,12,16,128]{4,3,2,1,0:T(8,128)(2,1)S(1)}, u32[]{:S(2)}, u32[]{:S(2)}) collective-permute-start(bf16[2,2,12,16,128]{4,3,2,1,0:T(8,128)(2,1)S(1)} %maximum_select_fusion.6), channel_id=1, source_target_pairs={{0,16},{8,24},{16,0},{24,8},{32,48},{40,56},{48,32},{56,40},{1,17}... | collective-permute-start | bytes 589832 | tf_op jit(solution)/shard_map/ppermute | solution.py:60
  43.1 12.1 %collective-permute-start.10 = (bf16[2,2,2,12,16,128]{5,4,3,2,1,0:T(8,128)(2,1)S(1)}, bf16[2,2,2,12,16,128]{5,4,3,2,1,0:T(8,128)(2,1)S(1)}, u32[]{:S(2)}, u32[]{:S(2)}) collective-permute-start(bf16[2,2,2,12,16,128]{5,4,3,2,1,0:T(8,128)(2,1)S(1)} %maximum_select_fusion.4), channel_id=1, source_target_pairs={{0,8},{8,0},{16,24},{24,16},{32,40},{40,32},{48,56},{56,48},{1,9},... | collective-permute-start | bytes 1179656 | tf_op jit(solution)/shard_map/ppermute | solution.py:60
  56.2 19.8 %collective-permute-start.13 = (bf16[2,2,2,2,12,16,128]{6,5,4,3,2,1,0:T(8,128)(2,1)}, bf16[2,2,2,2,12,16,128]{6,5,4,3,2,1,0:T(8,128)(2,1)S(1)}, u32[]{:S(2)}, u32[]{:S(2)}) collective-permute-start(bf16[2,2,2,2,12,16,128]{6,5,4,3,2,1,0:T(8,128)(2,1)} %maximum_select_fusion.2), channel_id=1, source_target_pairs={{0,128},{128,256},{256,384},{384,0},{1,129},{129,257},{257,385},{3... | collective-permute-start | bytes 2359304 | tf_op jit(solution)/shard_map/ppermute | solution.py:23
  59.4 19.8 %collective-permute-start.11 = (bf16[2,2,2,2,12,16,128]{6,5,4,3,2,1,0:T(8,128)(2,1)}, bf16[2,2,2,2,12,16,128]{6,5,4,3,2,1,0:T(8,128)(2,1)S(1)}, u32[]{:S(2)}, u32[]{:S(2)}) collective-permute-start(bf16[2,2,2,2,12,16,128]{6,5,4,3,2,1,0:T(8,128)(2,1)} %maximum_select_fusion.2), channel_id=1, source_target_pairs={{0,384},{128,0},{256,128},{384,256},{1,385},{129,1},{257,129},{385... | collective-permute-start | bytes 2359304 | tf_op jit(solution)/shard_map/ppermute | solution.py:23
  61.5 5.4 %collective-permute-start = (bf16[4,1,64,128]{3,2,1,0:T(8,128)(2,1)S(1)}, bf16[4,1,64,128]{3,2,1,0:T(8,128)(2,1)S(1)}, u32[]{:S(2)}, u32[]{:S(2)}) collective-permute-start(bf16[4,1,64,128]{3,2,1,0:T(8,128)(2,1)S(1)} %get-tuple-element.18), channel_id=1, source_target_pairs={{0,8},{8,16},{16,24},{24,32},{32,40},{40,48},{48,56},{1,9},{9,17},... | collective-permute-start | bytes 196616 | tf_op jit(solution)/shard_map/ppermute | solution.py:15
  62.8 5.3 %collective-permute-start.1 = (bf16[4,1,64,128]{3,2,1,0:T(8,128)(2,1)S(1)}, bf16[4,1,64,128]{3,2,1,0:T(8,128)(2,1)S(1)}, u32[]{:S(2)}, u32[]{:S(2)}) collective-permute-start(bf16[4,1,64,128]{3,2,1,0:T(8,128)(2,1)S(1)} %get-tuple-element.17), channel_id=1, source_target_pairs={{8,0},{16,8},{24,16},{32,24},{40,32},{48,40},{56,48},{9,1},{17,9},... | collective-permute-start | bytes 196616 | tf_op jit(solution)/shard_map/ppermute | solution.py:18
  76.1 11.9 %collective-permute-start.14 = (bf16[1,2,2,2,12,16,128]{6,5,4,3,2,1,0:T(8,128)(2,1)S(1)}, bf16[1,2,2,2,12,16,128]{6,5,4,3,2,1,0:T(8,128)(2,1)S(1)}, u32[]{:S(2)}, u32[]{:S(2)}) collective-permute-start(bf16[1,2,2,2,12,16,128]{6,5,4,3,2,1,0:T(8,128)(2,1)S(1)} %slice.100), channel_id=1, source_target_pairs={{0,128},{128,256},{256,384},{384,0},{1,129},{129,257},{257,385},{3... | collective-permute-start | bytes 1179656 | tf_op jit(solution)/shard_map/ppermute | solution.py:23
  80.2 9.9 %collective-permute-start.12 = (bf16[1,2,2,2,12,16,128]{6,5,4,3,2,1,0:T(8,128)(2,1)S(1)}, bf16[1,2,2,2,12,16,128]{6,5,4,3,2,1,0:T(8,128)(2,1)S(1)}, u32[]{:S(2)}, u32[]{:S(2)}) collective-permute-start(bf16[1,2,2,2,12,16,128]{6,5,4,3,2,1,0:T(8,128)(2,1)S(1)} %slice.99), channel_id=1, source_target_pairs={{0,384},{128,0},{256,128},{384,256},{1,385},{129,1},{257,129},{385... | collective-permute-start | bytes 1179656 | tf_op jit(solution)/shard_map/ppermute | solution.py:23
  92.5 109.3 %collective-permute-start.15 = (bf16[4,2,2,2,2,12,16,128]{7,4,6,1,2,3,0,5:T(2,128)(2,1)S(1)}, bf16[4,2,2,2,2,12,16,128]{7,4,6,1,2,3,0,5:T(2,128)(2,1)}, u32[]{:S(2)}, u32[]{:S(2)}) collective-permute-start(bf16[4,2,2,2,2,12,16,128]{7,4,6,1,2,3,0,5:T(2,128)(2,1)S(1)} %copy_dynamic-update-slice_fusion), channel_id=1, source_target_pairs={{0,64},{64,0},{1,65},{65,1},{2,66},{66,2},{3,67},{67,3},{4,68},{68... | collective-permute-start | bytes 9437192 | tf_op jit(solution)/shard_map/ppermute | solution.py:60
  98.7 47.1 %collective-permute-start.2 = (bf16[4,6,64,128]{3,2,1,0:T(8,128)(2,1)}, bf16[4,6,64,128]{3,2,1,0:T(8,128)(2,1)}, u32[]{:S(2)}, u32[]{:S(2)}) collective-permute-start(bf16[4,6,64,128]{3,2,1,0:T(8,128)(2,1)} %get-tuple-element.10), channel_id=1, source_target_pairs={{0,1},{1,0},{2,3},{3,2},{4,5},{5,4},{6,7},{7,6},{8,9},{9,8},{10,11... | collective-permute-start | bytes 1179656 | tf_op jit(solution)/shard_map/ppermute | solution.py:91
  148.5 21.1 %collective-permute-start.3 = (bf16[4,6,64,256]{3,2,1,0:T(8,128)(2,1)}, bf16[4,6,64,256]{3,2,1,0:T(8,128)(2,1)}, u32[]{:S(2)}, u32[]{:S(2)}) collective-permute-start(bf16[4,6,64,256]{3,2,1,0:T(8,128)(2,1)} %get-tuple-element.6), channel_id=1, source_target_pairs={{0,6},{2,0},{4,2},{6,4},{1,7},{3,1},{5,3},{7,5},{8,14},{10,8},{12,... | collective-permute-start | bytes 2359304 | tf_op jit(solution)/shard_map/ppermute | solution.py:23
  152.9 23.1 %collective-permute-start.5 = (bf16[4,6,64,256]{3,2,1,0:T(8,128)(2,1)}, bf16[4,6,64,256]{3,2,1,0:T(8,128)(2,1)}, u32[]{:S(2)}, u32[]{:S(2)}) collective-permute-start(bf16[4,6,64,256]{3,2,1,0:T(8,128)(2,1)} %get-tuple-element.6), channel_id=1, source_target_pairs={{0,2},{2,4},{4,6},{6,0},{1,3},{3,5},{5,7},{7,1},{8,10},{10,12},{12... | collective-permute-start | bytes 2359304 | tf_op jit(solution)/shard_map/ppermute | solution.py:23
  154.8 21.1 %collective-permute-start.16 = (f32[2,128]{1,0:T(2,128)S(1)}, f32[2,128]{1,0:T(2,128)S(1)}, u32[]{:S(2)}, u32[]{:S(2)}) collective-permute-start(f32[2,128]{1,0:T(2,128)S(1)} %pad_maximum_fusion.1), channel_id=1, source_target_pairs={{0,1},{1,0},{2,3},{3,2},{4,5},{5,4},{6,7},{7,6},{8,9},{9,8},{10,11... | collective-permute-start | bytes 3080 | tf_op jit(solution)/shard_map/ppermute | solution.py:87
  170.6 12.4 %collective-permute-start.4 = (bf16[4,6,64,128]{3,2,1,0:T(8,128)(2,1)S(1)}, bf16[4,6,64,128]{3,2,1,0:T(8,128)(2,1)S(1)}, u32[]{:S(2)}, u32[]{:S(2)}) collective-permute-start(bf16[4,6,64,128]{3,2,1,0:T(8,128)(2,1)S(1)} %slice.96), channel_id=1, source_target_pairs={{0,6},{2,0},{4,2},{6,4},{1,7},{3,1},{5,3},{7,5},{8,14},{10,8},{12,... | collective-permute-start | bytes 1179656 | tf_op jit(solution)/shard_map/ppermute | solution.py:23
  177.0 12.1 %collective-permute-start.6 = (bf16[4,6,64,128]{3,2,1,0:T(8,128)(2,1)S(1)}, bf16[4,6,64,128]{3,2,1,0:T(8,128)(2,1)S(1)}, u32[]{:S(2)}, u32[]{:S(2)}) collective-permute-start(bf16[4,6,64,128]{3,2,1,0:T(8,128)(2,1)S(1)} %slice.97), channel_id=1, source_target_pairs={{0,2},{2,4},{4,6},{6,0},{1,3},{3,5},{5,7},{7,1},{8,10},{10,12},{12... | collective-permute-start | bytes 1179656 | tf_op jit(solution)/shard_map/ppermute | solution.py:23
  242.7 7.3 %collective-permute-start.17 = (bf16[1,4,64,256]{3,2,1,0:T(8,128)(2,1)S(1)}, bf16[1,4,64,256]{3,2,1,0:T(8,128)(2,1)S(1)}, u32[]{:S(2)}, u32[]{:S(2)}) collective-permute-start(bf16[1,4,64,256]{3,2,1,0:T(8,128)(2,1)S(1)} %get-tuple-element.15), channel_id=1, source_target_pairs={{0,64},{64,128},{128,192},{192,256},{256,320},{320,384},{384,448},... | collective-permute-start | bytes 393224 | tf_op jit(solution)/shard_map/ppermute | solution.py:15
  248.1 6.3 %collective-permute-start.18 = (bf16[1,4,64,256]{3,2,1,0:T(8,128)(2,1)S(1)}, bf16[1,4,64,256]{3,2,1,0:T(8,128)(2,1)S(1)}, u32[]{:S(2)}, u32[]{:S(2)}) collective-permute-start(bf16[1,4,64,256]{3,2,1,0:T(8,128)(2,1)S(1)} %get-tuple-element.16), channel_id=1, source_target_pairs={{64,0},{128,64},{192,128},{256,192},{320,256},{384,320},{448,384},... | collective-permute-start | bytes 393224 | tf_op jit(solution)/shard_map/ppermute | solution.py:18
  255.4 21.2 %collective-permute-start.19 = (bf16[6,4,64,256]{3,2,1,0:T(8,128)(2,1)}, bf16[6,4,64,256]{3,2,1,0:T(8,128)(2,1)S(1)}, u32[]{:S(2)}, u32[]{:S(2)}) collective-permute-start(bf16[6,4,64,256]{3,2,1,0:T(8,128)(2,1)} %get-tuple-element.7), channel_id=1, source_target_pairs={{0,6},{2,0},{4,2},{6,4},{1,7},{3,1},{5,3},{7,5},{8,14},{10,8},{12,... | collective-permute-start | bytes 2359304 | tf_op jit(solution)/shard_map/ppermute | solution.py:23
  257.3 23.6 %collective-permute-start.21 = (bf16[6,4,64,256]{3,2,1,0:T(8,128)(2,1)}, bf16[6,4,64,256]{3,2,1,0:T(8,128)(2,1)}, u32[]{:S(2)}, u32[]{:S(2)}) collective-permute-start(bf16[6,4,64,256]{3,2,1,0:T(8,128)(2,1)} %get-tuple-element.7), channel_id=1, source_target_pairs={{0,2},{2,4},{4,6},{6,0},{1,3},{3,5},{5,7},{7,1},{8,10},{10,12},{12... | collective-permute-start | bytes 2359304 | tf_op jit(solution)/shard_map/ppermute | solution.py:23
  278.3 13.0 %collective-permute-start.20 = (bf16[6,4,64,128]{3,2,1,0:T(8,128)(2,1)}, bf16[6,4,64,128]{3,2,1,0:T(8,128)(2,1)S(1)}, u32[]{:S(2)}, u32[]{:S(2)}) collective-permute-start(bf16[6,4,64,128]{3,2,1,0:T(8,128)(2,1)} %slice.108), channel_id=1, source_target_pairs={{0,6},{2,0},{4,2},{6,4},{1,7},{3,1},{5,3},{7,5},{8,14},{10,8},{12,... | collective-permute-start | bytes 1179656 | tf_op jit(solution)/shard_map/ppermute | solution.py:23
  282.0 13.7 %collective-permute-start.22 = (bf16[6,4,64,128]{3,2,1,0:T(8,128)(2,1)S(1)}, bf16[6,4,64,128]{3,2,1,0:T(8,128)(2,1)S(1)}, u32[]{:S(2)}, u32[]{:S(2)}) collective-permute-start(bf16[6,4,64,128]{3,2,1,0:T(8,128)(2,1)S(1)} %slice.109), channel_id=1, source_target_pairs={{0,2},{2,4},{4,6},{6,0},{1,3},{3,5},{5,7},{7,1},{8,10},{10,12},{12... | collective-permute-start | bytes 1179656 | tf_op jit(solution)/shard_map/ppermute | solution.py:23
  302.5 21.8 %collective-permute-start.23 = (bf16[4,4,64,128]{3,2,1,0:T(8,128)(2,1)S(1)}, bf16[4,4,64,128]{3,2,1,0:T(8,128)(2,1)S(1)}, u32[]{:S(2)}, u32[]{:S(2)}) collective-permute-start(bf16[4,4,64,128]{3,2,1,0:T(8,128)(2,1)S(1)} %get-tuple-element.13), channel_id=1, source_target_pairs={{0,1},{1,0},{2,3},{3,2},{4,5},{5,4},{6,7},{7,6},{8,9},{9,8},{10,11... | collective-permute-start | bytes 786440 | tf_op jit(solution)/shard_map/ppermute | solution.py:126
  (14 other events, 280.5 us)

commit v5 on v4

--- a/solution.py
+++ b/solution.py
@@ -39,41 +39,41 @@
     return jnp.concatenate([pair, from_right, far_low, far_high, from_left], axis=3)
 
 
-def ring_gather(block, axis):
+def ring_gather(block, axis, dim, rotate):
     ring = lax.axis_size(axis)
     me = lax.axis_index(axis)
-    half = block.shape[0] // 2
+    half = block.shape[dim] // 2
     from_left = ring_shift(block, axis, ring, 1)
     from_right = ring_shift(block, axis, ring, -1)
-    far_low = ring_shift(from_right[:half], axis, ring, -1)
-    far_high = ring_shift(from_left[half:], axis, ring, 1)
-    far = jnp.concatenate([far_low, far_high], axis=0)
-    out = jnp.zeros((ring,) + block.shape, block.dtype)
+    far_low = ring_shift(lax.slice_in_dim(from_right, 0, half, axis=dim), axis, ring, -1)
+    far_high = ring_shift(lax.slice_in_dim(from_left, half, None, axis=dim), axis, ring, 1)
+    far = jnp.concatenate([far_low, far_high], axis=dim)
+    shape = block.shape[:dim] + (ring,) + block.shape[dim:]
+    out = jnp.zeros(shape, block.dtype)
     for offset, piece in ((0, block), (1, from_right), (2, far), (ring - 1, from_left)):
-        start = ((me + offset) % ring,) + (0,) * block.ndim
-        out = lax.dynamic_update_slice(out, piece[None], start)
+        start = [0] * len(shape)
+        start[dim] = (me + offset - rotate + 2 * ring) % ring
+        out = lax.dynamic_update_slice(out, jnp.expand_dims(piece, dim), start)
     return out
 
 
-def swap_stack(block, axis, bit):
-    count = lax.axis_size(axis)
-    other = lax.ppermute(block, axis, [(i, i ^ bit) for i in range(count)])
-    high = (lax.axis_index(axis) // bit) % 2 == 1
-    return jnp.where(high, jnp.stack([other, block]), jnp.stack([block, other]))
-
-
 def weight_gather(weight):
-    block = swap_stack(weight, "cz", 1)
-    for bit in (4, 2, 1):
-        block = swap_stack(block, "row", bit)
-    block = ring_gather(block, "fy")
-    block = swap_stack(block, "fc", 1)
-    block = jnp.transpose(block, (6, 1, 0, 4, 3, 2, 7, 5, 8))
     taps, depth, width = weight.shape
-    full = block.reshape(taps, 64 * depth, 2 * width)
-    doubled = jnp.concatenate([full, full], axis=1)
-    shift = lax.axis_index("cx") * 2 * width
-    return lax.dynamic_slice_in_dim(doubled, shift, 64 * depth, axis=1)
+    high_z = lax.axis_index("cz") == 1
+    block = ordered_pair(weight, lax.ppermute(weight, "cz", SWAP), high_z, 2)
+    row_n = lax.axis_size("row")
+    for pos, bit in enumerate((4, 2, 1)):
+        other = lax.ppermute(block, "row", [(i, i ^ bit) for i in range(row_n)])
+        high = (lax.axis_index("row") // bit) % 2 == 1
+        block = jnp.where(
+            high, jnp.stack([other, block], axis=1 + pos), jnp.stack([block, other], axis=1 + pos)
+        )
+    block = block.reshape(taps, row_n * depth, 2 * width)
+    block = ring_gather(block, "fy", 1, lax.axis_index("cx"))
+    high_c = lax.axis_index("fc") == 1
+    other = lax.ppermute(block, "fc", SWAP)
+    block = jnp.where(high_c, jnp.stack([other, block], axis=2), jnp.stack([block, other], axis=2))
+    return block.reshape(taps, -1, 2 * width)
 
 
 def body(frames_in, spatial_weight, temporal_weight, spatial_bias, temporal_bias, clip_id):

time: 327 us -> 289 us (0.88)
  other arithmetic: 29.1 us -> 10.2 us
  local copies, waits for them, and re-layouts: 46.5 us -> 29.7 us
    transpose x1 -> x0, other arithmetic: 14.2 us -> none  [weight_gather(): block = jnp.transpose(block, (6, 1, 0, 4, 3, 2, 7, 5, 8))]
    reshape x1 -> x0, local copies, waits for them, and re-layouts: 10.9 us -> none  [weight_gather(): full = block.reshape(taps, 64 * depth, 2 * width)]
    concatenate x1 -> x0, other arithmetic: 5.18 us -> none  [weight_gather(): doubled = jnp.concatenate([full, full], axis=1)]
    dynamic_update_slice x4 -> x3, local copies, waits for them, and re-layouts: 4.52 us -> 0.23 us  [ring_gather(): out = lax.dynamic_update_slice(out, jnp.expand_dims(piece, dim), start)]
    unnamed x39 -> x35, local copies, waits for them, and re-layouts: 13.6 us -> 13.7 us
  transfers between devices with their start and end apart: 24 -> 24, of which waited for: 16 -> 17; matrix products, arithmetic and copies ran while one was open for 10% -> 9% of each run, Pallas kernels for 0% -> 0%
where the time goes in v5:
time: 289 us; the launch traced here: 288 us
  waiting for transfers between devices  152 us (53%)
  starting transfers between devices  85.3 us (30%)
  local copies, waits for them, and re-layouts  29.7 us (10%)
  other arithmetic  10.2 us (4%)
  matrix products  9.43 us (3%)
    ppermute x12, waiting for transfers between devices, ring_shift(): lax.ppermute(block, axis, [(i, (i + step) % count) for i in range(count)])  51.7 us
    ppermute x1, waiting for transfers between devices, body(): partner = lax.ppermute(wanted, 'cz', SWAP)  38.6 us
    ppermute x12, starting transfers between devices, ring_shift(): lax.ppermute(block, axis, [(i, (i + step) % count) for i in range(count)])  35.2 us
    ppermute x3, waiting for transfers between devices, weight_gather(): other = lax.ppermute(block, 'row', [(i, i ^ bit) for i in range(row_n)])  34.1 us
    ppermute x1, waiting for transfers between devices, body(): returned = lax.ppermute(given, 'cz', SWAP)  16.7 us
    unnamed x35, local copies, waits for them, and re-layouts  13.7 us
    ppermute x1, starting transfers between devices, body(): partner = lax.ppermute(wanted, 'cz', SWAP)  8.18 us
    ppermute x1, starting transfers between devices, weight_gather(): block = ordered_pair(weight, lax.ppermute(weight, 'cz', SWAP), high_z, 2)  7.93 us
  transfers between devices with their start and end apart: 24, of which 17 were waited for; matrix products, arithmetic and copies ran while one was open for 9% of the time, Pallas kernels for 0%

profile of v5, /device:TPU:233, one launch (start us, length us, event | category | flops | bytes accessed | tf_op | source)
XLA Modules:
  0.0 287.5 jit_solution(16365692240525063361)
XLA Ops:
  1.5 7.9 %collective-permute-start.7 = (bf16[12,16,128]{2,1,0:T(8,128)(2,1)S(1)}, bf16[12,16,128]{2,1,0:T(8,128)(2,1)S(1)}, u32[]{:S(2)}, u32[]{:S(2)}) collective-permute-start(bf16[12,16,128]{2,1,0:T(8,128)(2,1)S(1)} %constant_dynamic-update-slice_fusion.8), channel_id=1, source_target_pairs={{0,1},{1,0},{2,3},{3,2},{4,5},{5,4},{6,7},{7,6},{8,9},{9,8},{10,11... | collective-permute-start | bytes 147464 | tf_op jit(solution)/shard_map/ppermute | solution.py:63
  9.5 5.5 %collective-permute-done.7 = bf16[12,16,128]{2,1,0:T(8,128)(2,1)S(1)} collective-permute-done((bf16[12,16,128]{2,1,0:T(8,128)(2,1)S(1)}, bf16[12,16,128]{2,1,0:T(8,128)(2,1)S(1)}, u32[]{:S(2)}, u32[]{:S(2)}) %collective-permute-start.7) | collective-permute-done | bytes 49184 | tf_op jit(solution)/shard_map/ppermute | solution.py:63
  17.1 12.9 %collective-permute-done.8 = bf16[12,16,256]{2,1,0:T(8,128)(2,1)S(1)} collective-permute-done((bf16[12,16,256]{2,1,0:T(8,128)(2,1)S(1)}, bf16[12,16,256]{2,1,0:T(8,128)(2,1)S(1)}, u32[]{:S(2)}, u32[]{:S(2)}) %collective-permute-start.8) | collective-permute-done | bytes 98336 | tf_op jit(solution)/shard_map/ppermute | solution.py:66
  32.0 11.1 %collective-permute-done.9 = bf16[12,2,16,256]{3,2,1,0:T(8,128)(2,1)S(1)} collective-permute-done((bf16[12,2,16,256]{3,2,1,0:T(8,128)(2,1)S(1)}, bf16[12,2,16,256]{3,2,1,0:T(8,128)(2,1)S(1)}, u32[]{:S(2)}, u32[]{:S(2)}) %collective-permute-start.9) | collective-permute-done | bytes 196640 | tf_op jit(solution)/shard_map/ppermute | solution.py:66
  45.1 10.1 %collective-permute-done.10 = bf16[12,2,2,16,256]{4,3,1,0,2:T(8,128)(2,1)S(1)} collective-permute-done((bf16[12,2,2,16,256]{4,3,1,0,2:T(8,128)(2,1)S(1)}, bf16[12,2,2,16,256]{4,3,1,0,2:T(8,128)(2,1)S(1)}, u32[]{:S(2)}, u32[]{:S(2)}) %collective-permute-start.10) | collective-permute-done | bytes 393248 | tf_op jit(solution)/shard_map/ppermute | solution.py:66
  62.0 4.0 %collective-permute-start.1 = (bf16[4,1,64,128]{3,2,1,0:T(8,128)(2,1)S(1)}, bf16[4,1,64,128]{3,2,1,0:T(8,128)(2,1)S(1)}, u32[]{:S(2)}, u32[]{:S(2)}) collective-permute-start(bf16[4,1,64,128]{3,2,1,0:T(8,128)(2,1)S(1)} %get-tuple-element.20), channel_id=1, source_target_pairs={{8,0},{16,8},{24,16},{32,24},{40,32},{48,40},{56,48},{9,1},{17,9},... | collective-permute-start | bytes 196616 | tf_op jit(solution)/shard_map/ppermute | solution.py:18
  67.3 7.6 %collective-permute-done.13 = bf16[12,128,256]{2,1,0:T(8,128)(2,1)S(1)} collective-permute-done((bf16[12,128,256]{2,1,0:T(8,128)(2,1)S(1)}, bf16[12,128,256]{2,1,0:T(8,128)(2,1)S(1)}, u32[]{:S(2)}, u32[]{:S(2)}) %collective-permute-start.13) | collective-permute-done | bytes 786464 | tf_op jit(solution)/shard_map/ppermute | solution.py:23
  88.4 5.4 %collective-permute-start.15 = (bf16[12,4,128,256]{3,2,1,0:T(8,128)(2,1)S(1)}, bf16[12,4,128,256]{3,2,1,0:T(8,128)(2,1)}, u32[]{:S(2)}, u32[]{:S(2)}) collective-permute-start(bf16[12,4,128,256]{3,2,1,0:T(8,128)(2,1)S(1)} %bitcast_dynamic-update-slice_fusion), channel_id=1, source_target_pairs={{0,64},{64,0},{1,65},{65,1},{2,66},{66,2},{3,67},{67,3},{4,68},{68... | collective-permute-start | bytes 9437192 | tf_op jit(solution)/shard_map/ppermute | solution.py:74
  93.9 8.2 %collective-permute-start.2 = (bf16[4,6,64,128]{3,2,1,0:T(8,128)(2,1)S(1)}, bf16[4,6,64,128]{3,2,1,0:T(8,128)(2,1)S(1)}, u32[]{:S(2)}, u32[]{:S(2)}) collective-permute-start(bf16[4,6,64,128]{3,2,1,0:T(8,128)(2,1)S(1)} %get-tuple-element.13), channel_id=1, source_target_pairs={{0,1},{1,0},{2,3},{3,2},{4,5},{5,4},{6,7},{7,6},{8,9},{9,8},{10,11... | collective-permute-start | bytes 1179656 | tf_op jit(solution)/shard_map/ppermute | solution.py:91
  102.1 38.6 %collective-permute-done.2 = bf16[4,6,64,128]{3,2,1,0:T(8,128)(2,1)S(1)} collective-permute-done((bf16[4,6,64,128]{3,2,1,0:T(8,128)(2,1)S(1)}, bf16[4,6,64,128]{3,2,1,0:T(8,128)(2,1)S(1)}, u32[]{:S(2)}, u32[]{:S(2)}) %collective-permute-start.2) | collective-permute-done | bytes 393248 | tf_op jit(solution)/shard_map/ppermute | solution.py:91
  142.2 4.4 %collective-permute-start.3 = (bf16[4,6,64,256]{3,2,1,0:T(8,128)(2,1)}, bf16[4,6,64,256]{3,2,1,0:T(8,128)(2,1)}, u32[]{:S(2)}, u32[]{:S(2)}) collective-permute-start(bf16[4,6,64,256]{3,2,1,0:T(8,128)(2,1)} %get-tuple-element.6), channel_id=1, source_target_pairs={{0,6},{2,0},{4,2},{6,4},{1,7},{3,1},{5,3},{7,5},{8,14},{10,8},{12,... | collective-permute-start | bytes 2359304 | tf_op jit(solution)/shard_map/ppermute | solution.py:23
  148.5 5.1 %collective-permute-start.16 = (f32[2,128]{1,0:T(2,128)S(1)}, f32[2,128]{1,0:T(2,128)S(1)}, u32[]{:S(2)}, u32[]{:S(2)}) collective-permute-start(f32[2,128]{1,0:T(2,128)S(1)} %pad_maximum_fusion.3), channel_id=1, source_target_pairs={{0,1},{1,0},{2,3},{3,2},{4,5},{5,4},{6,7},{7,6},{8,9},{9,8},{10,11... | collective-permute-start | bytes 3080 | tf_op jit(solution)/shard_map/ppermute | solution.py:87
  153.7 9.6 %collective-permute-done.3 = bf16[4,6,64,256]{3,2,1,0:T(8,128)(2,1)} collective-permute-done((bf16[4,6,64,256]{3,2,1,0:T(8,128)(2,1)}, bf16[4,6,64,256]{3,2,1,0:T(8,128)(2,1)}, u32[]{:S(2)}, u32[]{:S(2)}) %collective-permute-start.3) | collective-permute-done | bytes 786464 | tf_op jit(solution)/shard_map/ppermute | solution.py:23
  164.3 5.3 %collective-permute-start.4 = (bf16[4,6,64,128]{3,2,1,0:T(8,128)(2,1)S(1)}, bf16[4,6,64,128]{3,2,1,0:T(8,128)(2,1)S(1)}, u32[]{:S(2)}, u32[]{:S(2)}) collective-permute-start(bf16[4,6,64,128]{3,2,1,0:T(8,128)(2,1)S(1)} %slice.101), channel_id=1, source_target_pairs={{0,6},{2,0},{4,2},{6,4},{1,7},{3,1},{5,3},{7,5},{8,14},{10,8},{12,... | collective-permute-start | bytes 1179656 | tf_op jit(solution)/shard_map/ppermute | solution.py:23
  177.5 5.3 %collective-permute-done.6 = bf16[4,6,64,128]{3,2,1,0:T(8,128)(2,1)S(1)} collective-permute-done((bf16[4,6,64,128]{3,2,1,0:T(8,128)(2,1)S(1)}, bf16[4,6,64,128]{3,2,1,0:T(8,128)(2,1)S(1)}, u32[]{:S(2)}, u32[]{:S(2)}) %collective-permute-start.6) | collective-permute-done | bytes 393248 | tf_op jit(solution)/shard_map/ppermute | solution.py:23
  185.8 4.3 %copy.33 = bf16[6,4,64,1024]{3,1,2,0:T(4,128)(2,1)S(1)} copy(bf16[6,4,64,1024]{3,2,0,1:T(8,128)(2,1)} %bitcast.91) | data formatting | bytes 6291456
  194.0 4.3 %maximum_select_fusion = bf16[12,4,2,128,256]{4,3,2,1,0:T(8,128)(2,1)S(1)} fusion(bf16[12,4,1,128,256]{4,3,2,1,0:T(8,128)(2,1)S(1)} %bitcast.90, bf16[12,4,1,128,256]{4,3,2,1,0:T(8,128)(2,1)} %bitcast.23, pred[]{:T(512)S(6)} %eq.31), kind=kLoop, calls=%fused_computation.2 | loop fusion | flops 9437184 | bytes 12582913 | tf_op jit(solution)/shard_map/jit(_where)/select_n | solution.py:75
  201.0 7.2 %convert_add_fusion = (f32[4,32,9,256]{3,1,2,0:T(8,128)}, bf16[4,32,9,256]{3,1,2,0:T(8,128)(2,1)S(1)}) fusion(f32[256]{0:T(256)S(1)} %bitcast.116, f32[256]{0:T(256)S(1)} %bitcast.117, bf16[3,3,1024,256]{3,2,1,0:T(8,128)(2,1)S(1)} %bitcast.92, bf16[6,4,8,11,1024]{4,1,3,2,0:T(4,128)(2,1)S(1)} %fusion.1, pred[32,9]{0,1:T(8,128)(4,1)S(1)} %copy-done.11), kind=kOutput, calls=%fused_computation.9 | convolution fusion | flops 5438767104 | bytes 10815776 | tf_op jit(solution)/shard_map/conv_general_dilated | solution.py:94
  209.0 5.3 %collective-permute-start.17 = (bf16[1,4,64,256]{3,2,1,0:T(8,128)(2,1)S(1)}, bf16[1,4,64,256]{3,2,1,0:T(8,128)(2,1)S(1)}, u32[]{:S(2)}, u32[]{:S(2)}) collective-permute-start(bf16[1,4,64,256]{3,2,1,0:T(8,128)(2,1)S(1)} %get-tuple-element.18), channel_id=1, source_target_pairs={{0,64},{64,128},{128,192},{192,256},{256,320},{320,384},{384,448},... | collective-permute-start | bytes 393224 | tf_op jit(solution)/shard_map/ppermute | solution.py:15
  216.3 4.3 %collective-permute-done.18 = bf16[1,4,64,256]{3,2,1,0:T(8,128)(2,1)S(1)} collective-permute-done((bf16[1,4,64,256]{3,2,1,0:T(8,128)(2,1)S(1)}, bf16[1,4,64,256]{3,2,1,0:T(8,128)(2,1)S(1)}, u32[]{:S(2)}, u32[]{:S(2)}) %collective-permute-start.18) | collective-permute-done | bytes 131104 | tf_op jit(solution)/shard_map/ppermute | solution.py:18
  229.7 13.2 %collective-permute-done.19 = bf16[6,4,64,256]{3,2,1,0:T(8,128)(2,1)} collective-permute-done((bf16[6,4,64,256]{3,2,1,0:T(8,128)(2,1)}, bf16[6,4,64,256]{3,2,1,0:T(8,128)(2,1)}, u32[]{:S(2)}, u32[]{:S(2)}) %collective-permute-start.19) | collective-permute-done | bytes 786464 | tf_op jit(solution)/shard_map/ppermute | solution.py:23
  256.8 4.4 %collective-permute-done.22 = bf16[6,4,64,128]{3,2,1,0:T(8,128)(2,1)S(1)} collective-permute-done((bf16[6,4,64,128]{3,2,1,0:T(8,128)(2,1)S(1)}, bf16[6,4,64,128]{3,2,1,0:T(8,128)(2,1)S(1)}, u32[]{:S(2)}, u32[]{:S(2)}) %collective-permute-start.22) | collective-permute-done | bytes 393248 | tf_op jit(solution)/shard_map/ppermute | solution.py:23
  264.9 5.1 %collective-permute-start.23 = (bf16[4,4,64,128]{3,2,1,0:T(8,128)(2,1)S(1)}, bf16[4,4,64,128]{3,2,1,0:T(8,128)(2,1)S(1)}, u32[]{:S(2)}, u32[]{:S(2)}) collective-permute-start(bf16[4,4,64,128]{3,2,1,0:T(8,128)(2,1)S(1)} %get-tuple-element.16), channel_id=1, source_target_pairs={{0,1},{1,0},{2,3},{3,2},{4,5},{5,4},{6,7},{7,6},{8,9},{9,8},{10,11... | collective-permute-start | bytes 786440 | tf_op jit(solution)/shard_map/ppermute | solution.py:126
  270.0 16.7 %collective-permute-done.23 = bf16[4,4,64,128]{3,2,1,0:T(8,128)(2,1)S(1)} collective-permute-done((bf16[4,4,64,128]{3,2,1,0:T(8,128)(2,1)S(1)}, bf16[4,4,64,128]{3,2,1,0:T(8,128)(2,1)S(1)}, u32[]{:S(2)}, u32[]{:S(2)}) %collective-permute-start.23) | collective-permute-done | bytes 262176 | tf_op jit(solution)/shard_map/ppermute | solution.py:126
  (110 shorter events, 80.7 us)
Async XLA Ops:
  1.5 13.5 %collective-permute-start.7 = (bf16[12,16,128]{2,1,0:T(8,128)(2,1)S(1)}, bf16[12,16,128]{2,1,0:T(8,128)(2,1)S(1)}, u32[]{:S(2)}, u32[]{:S(2)}) collective-permute-start(bf16[12,16,128]{2,1,0:T(8,128)(2,1)S(1)} %constant_dynamic-update-slice_fusion.8), channel_id=1, source_target_pairs={{0,1},{1,0},{2,3},{3,2},{4,5},{5,4},{6,7},{7,6},{8,9},{9,8},{10,11... | collective-permute-start | bytes 147464 | tf_op jit(solution)/shard_map/ppermute | solution.py:63
  15.1 14.9 %collective-permute-start.8 = (bf16[12,16,256]{2,1,0:T(8,128)(2,1)S(1)}, bf16[12,16,256]{2,1,0:T(8,128)(2,1)S(1)}, u32[]{:S(2)}, u32[]{:S(2)}) collective-permute-start(bf16[12,16,256]{2,1,0:T(8,128)(2,1)S(1)} %maximum_select_fusion.7), channel_id=1, source_target_pairs={{0,32},{8,40},{16,48},{24,56},{32,0},{40,8},{48,16},{56,24},{1,33}... | collective-permute-start | bytes 294920 | tf_op jit(solution)/shard_map/ppermute | solution.py:66
  30.0 13.1 %collective-permute-start.9 = (bf16[12,2,16,256]{3,2,1,0:T(8,128)(2,1)S(1)}, bf16[12,2,16,256]{3,2,1,0:T(8,128)(2,1)S(1)}, u32[]{:S(2)}, u32[]{:S(2)}) collective-permute-start(bf16[12,2,16,256]{3,2,1,0:T(8,128)(2,1)S(1)} %maximum_select_fusion.6), channel_id=1, source_target_pairs={{0,16},{8,24},{16,0},{24,8},{32,48},{40,56},{48,32},{56,40},{1,17}... | collective-permute-start | bytes 589832 | tf_op jit(solution)/shard_map/ppermute | solution.py:66
  43.1 12.1 %collective-permute-start.10 = (bf16[12,2,2,16,256]{4,3,1,0,2:T(8,128)(2,1)S(1)}, bf16[12,2,2,16,256]{4,3,1,0,2:T(8,128)(2,1)S(1)}, u32[]{:S(2)}, u32[]{:S(2)}) collective-permute-start(bf16[12,2,2,16,256]{4,3,1,0,2:T(8,128)(2,1)S(1)} %maximum_select_fusion.4), channel_id=1, source_target_pairs={{0,8},{8,0},{16,24},{24,16},{32,40},{40,32},{48,56},{56,48},{1,9},... | collective-permute-start | bytes 1179656 | tf_op jit(solution)/shard_map/ppermute | solution.py:66
  55.4 19.6 %collective-permute-start.13 = (bf16[12,128,256]{2,1,0:T(8,128)(2,1)S(1)}, bf16[12,128,256]{2,1,0:T(8,128)(2,1)S(1)}, u32[]{:S(2)}, u32[]{:S(2)}) collective-permute-start(bf16[12,128,256]{2,1,0:T(8,128)(2,1)S(1)} %bitcast.96), channel_id=1, source_target_pairs={{0,128},{128,256},{256,384},{384,0},{1,129},{129,257},{257,385},{3... | collective-permute-start | bytes 2359304 | tf_op jit(solution)/shard_map/ppermute | solution.py:23
  58.6 19.6 %collective-permute-start.11 = (bf16[12,128,256]{2,1,0:T(8,128)(2,1)S(1)}, bf16[12,128,256]{2,1,0:T(8,128)(2,1)S(1)}, u32[]{:S(2)}, u32[]{:S(2)}) collective-permute-start(bf16[12,128,256]{2,1,0:T(8,128)(2,1)S(1)} %bitcast.97), channel_id=1, source_target_pairs={{0,384},{128,0},{256,128},{384,256},{1,385},{129,1},{257,129},{385... | collective-permute-start | bytes 2359304 | tf_op jit(solution)/shard_map/ppermute | solution.py:23
  60.7 5.4 %collective-permute-start = (bf16[4,1,64,128]{3,2,1,0:T(8,128)(2,1)S(1)}, bf16[4,1,64,128]{3,2,1,0:T(8,128)(2,1)S(1)}, u32[]{:S(2)}, u32[]{:S(2)}) collective-permute-start(bf16[4,1,64,128]{3,2,1,0:T(8,128)(2,1)S(1)} %get-tuple-element.21), channel_id=1, source_target_pairs={{0,8},{8,16},{16,24},{24,32},{32,40},{40,48},{48,56},{1,9},{9,17},... | collective-permute-start | bytes 196616 | tf_op jit(solution)/shard_map/ppermute | solution.py:15
  62.0 5.3 %collective-permute-start.1 = (bf16[4,1,64,128]{3,2,1,0:T(8,128)(2,1)S(1)}, bf16[4,1,64,128]{3,2,1,0:T(8,128)(2,1)S(1)}, u32[]{:S(2)}, u32[]{:S(2)}) collective-permute-start(bf16[4,1,64,128]{3,2,1,0:T(8,128)(2,1)S(1)} %get-tuple-element.20), channel_id=1, source_target_pairs={{8,0},{16,8},{24,16},{32,24},{40,32},{48,40},{56,48},{9,1},{17,9},... | collective-permute-start | bytes 196616 | tf_op jit(solution)/shard_map/ppermute | solution.py:18
  75.0 10.6 %collective-permute-start.14 = (bf16[12,64,256]{2,1,0:T(8,128)(2,1)S(1)}, bf16[12,64,256]{2,1,0:T(8,128)(2,1)S(1)}, u32[]{:S(2)}, u32[]{:S(2)}) collective-permute-start(bf16[12,64,256]{2,1,0:T(8,128)(2,1)S(1)} %slice.105), channel_id=1, source_target_pairs={{0,128},{128,256},{256,384},{384,0},{1,129},{129,257},{257,385},{3... | collective-permute-start | bytes 1179656 | tf_op jit(solution)/shard_map/ppermute | solution.py:23
  78.2 10.0 %collective-permute-start.12 = (bf16[12,64,256]{2,1,0:T(8,128)(2,1)S(1)}, bf16[12,64,256]{2,1,0:T(8,128)(2,1)S(1)}, u32[]{:S(2)}, u32[]{:S(2)}) collective-permute-start(bf16[12,64,256]{2,1,0:T(8,128)(2,1)S(1)} %slice.104), channel_id=1, source_target_pairs={{0,384},{128,0},{256,128},{384,256},{1,385},{129,1},{257,129},{385... | collective-permute-start | bytes 1179656 | tf_op jit(solution)/shard_map/ppermute | solution.py:23
  88.4 105.6 %collective-permute-start.15 = (bf16[12,4,128,256]{3,2,1,0:T(8,128)(2,1)S(1)}, bf16[12,4,128,256]{3,2,1,0:T(8,128)(2,1)}, u32[]{:S(2)}, u32[]{:S(2)}) collective-permute-start(bf16[12,4,128,256]{3,2,1,0:T(8,128)(2,1)S(1)} %bitcast_dynamic-update-slice_fusion), channel_id=1, source_target_pairs={{0,64},{64,0},{1,65},{65,1},{2,66},{66,2},{3,67},{67,3},{4,68},{68... | collective-permute-start | bytes 9437192 | tf_op jit(solution)/shard_map/ppermute | solution.py:74
  93.9 46.8 %collective-permute-start.2 = (bf16[4,6,64,128]{3,2,1,0:T(8,128)(2,1)S(1)}, bf16[4,6,64,128]{3,2,1,0:T(8,128)(2,1)S(1)}, u32[]{:S(2)}, u32[]{:S(2)}) collective-permute-start(bf16[4,6,64,128]{3,2,1,0:T(8,128)(2,1)S(1)} %get-tuple-element.13), channel_id=1, source_target_pairs={{0,1},{1,0},{2,3},{3,2},{4,5},{5,4},{6,7},{7,6},{8,9},{9,8},{10,11... | collective-permute-start | bytes 1179656 | tf_op jit(solution)/shard_map/ppermute | solution.py:91
  142.2 21.1 %collective-permute-start.3 = (bf16[4,6,64,256]{3,2,1,0:T(8,128)(2,1)}, bf16[4,6,64,256]{3,2,1,0:T(8,128)(2,1)}, u32[]{:S(2)}, u32[]{:S(2)}) collective-permute-start(bf16[4,6,64,256]{3,2,1,0:T(8,128)(2,1)} %get-tuple-element.6), channel_id=1, source_target_pairs={{0,6},{2,0},{4,2},{6,4},{1,7},{3,1},{5,3},{7,5},{8,14},{10,8},{12,... | collective-permute-start | bytes 2359304 | tf_op jit(solution)/shard_map/ppermute | solution.py:23
  146.6 23.1 %collective-permute-start.5 = (bf16[4,6,64,256]{3,2,1,0:T(8,128)(2,1)}, bf16[4,6,64,256]{3,2,1,0:T(8,128)(2,1)}, u32[]{:S(2)}, u32[]{:S(2)}) collective-permute-start(bf16[4,6,64,256]{3,2,1,0:T(8,128)(2,1)} %get-tuple-element.6), channel_id=1, source_target_pairs={{0,2},{2,4},{4,6},{6,0},{1,3},{3,5},{5,7},{7,1},{8,10},{10,12},{12... | collective-permute-start | bytes 2359304 | tf_op jit(solution)/shard_map/ppermute | solution.py:23
  148.5 21.1 %collective-permute-start.16 = (f32[2,128]{1,0:T(2,128)S(1)}, f32[2,128]{1,0:T(2,128)S(1)}, u32[]{:S(2)}, u32[]{:S(2)}) collective-permute-start(f32[2,128]{1,0:T(2,128)S(1)} %pad_maximum_fusion.3), channel_id=1, source_target_pairs={{0,1},{1,0},{2,3},{3,2},{4,5},{5,4},{6,7},{7,6},{8,9},{9,8},{10,11... | collective-permute-start | bytes 3080 | tf_op jit(solution)/shard_map/ppermute | solution.py:87
  164.3 12.4 %collective-permute-start.4 = (bf16[4,6,64,128]{3,2,1,0:T(8,128)(2,1)S(1)}, bf16[4,6,64,128]{3,2,1,0:T(8,128)(2,1)S(1)}, u32[]{:S(2)}, u32[]{:S(2)}) collective-permute-start(bf16[4,6,64,128]{3,2,1,0:T(8,128)(2,1)S(1)} %slice.101), channel_id=1, source_target_pairs={{0,6},{2,0},{4,2},{6,4},{1,7},{3,1},{5,3},{7,5},{8,14},{10,8},{12,... | collective-permute-start | bytes 1179656 | tf_op jit(solution)/shard_map/ppermute | solution.py:23
  170.7 12.1 %collective-permute-start.6 = (bf16[4,6,64,128]{3,2,1,0:T(8,128)(2,1)S(1)}, bf16[4,6,64,128]{3,2,1,0:T(8,128)(2,1)S(1)}, u32[]{:S(2)}, u32[]{:S(2)}) collective-permute-start(bf16[4,6,64,128]{3,2,1,0:T(8,128)(2,1)S(1)} %slice.102), channel_id=1, source_target_pairs={{0,2},{2,4},{4,6},{6,0},{1,3},{3,5},{5,7},{7,1},{8,10},{10,12},{12... | collective-permute-start | bytes 1179656 | tf_op jit(solution)/shard_map/ppermute | solution.py:23
  209.0 7.3 %collective-permute-start.17 = (bf16[1,4,64,256]{3,2,1,0:T(8,128)(2,1)S(1)}, bf16[1,4,64,256]{3,2,1,0:T(8,128)(2,1)S(1)}, u32[]{:S(2)}, u32[]{:S(2)}) collective-permute-start(bf16[1,4,64,256]{3,2,1,0:T(8,128)(2,1)S(1)} %get-tuple-element.18), channel_id=1, source_target_pairs={{0,64},{64,128},{128,192},{192,256},{256,320},{320,384},{384,448},... | collective-permute-start | bytes 393224 | tf_op jit(solution)/shard_map/ppermute | solution.py:15
  214.4 6.3 %collective-permute-start.18 = (bf16[1,4,64,256]{3,2,1,0:T(8,128)(2,1)S(1)}, bf16[1,4,64,256]{3,2,1,0:T(8,128)(2,1)S(1)}, u32[]{:S(2)}, u32[]{:S(2)}) collective-permute-start(bf16[1,4,64,256]{3,2,1,0:T(8,128)(2,1)S(1)} %get-tuple-element.19), channel_id=1, source_target_pairs={{64,0},{128,64},{192,128},{256,192},{320,256},{384,320},{448,384},... | collective-permute-start | bytes 393224 | tf_op jit(solution)/shard_map/ppermute | solution.py:18
  221.7 21.2 %collective-permute-start.19 = (bf16[6,4,64,256]{3,2,1,0:T(8,128)(2,1)}, bf16[6,4,64,256]{3,2,1,0:T(8,128)(2,1)}, u32[]{:S(2)}, u32[]{:S(2)}) collective-permute-start(bf16[6,4,64,256]{3,2,1,0:T(8,128)(2,1)} %get-tuple-element.10), channel_id=1, source_target_pairs={{0,6},{2,0},{4,2},{6,4},{1,7},{3,1},{5,3},{7,5},{8,14},{10,8},{12,... | collective-permute-start | bytes 2359304 | tf_op jit(solution)/shard_map/ppermute | solution.py:23
  223.6 22.9 %collective-permute-start.21 = (bf16[6,4,64,256]{3,2,1,0:T(8,128)(2,1)}, bf16[6,4,64,256]{3,2,1,0:T(8,128)(2,1)}, u32[]{:S(2)}, u32[]{:S(2)}) collective-permute-start(bf16[6,4,64,256]{3,2,1,0:T(8,128)(2,1)} %get-tuple-element.10), channel_id=1, source_target_pairs={{0,2},{2,4},{4,6},{6,0},{1,3},{3,5},{5,7},{7,1},{8,10},{10,12},{12... | collective-permute-start | bytes 2359304 | tf_op jit(solution)/shard_map/ppermute | solution.py:23
  243.9 12.8 %collective-permute-start.20 = (bf16[6,4,64,128]{3,2,1,0:T(8,128)(2,1)S(1)}, bf16[6,4,64,128]{3,2,1,0:T(8,128)(2,1)S(1)}, u32[]{:S(2)}, u32[]{:S(2)}) collective-permute-start(bf16[6,4,64,128]{3,2,1,0:T(8,128)(2,1)S(1)} %slice.113), channel_id=1, source_target_pairs={{0,6},{2,0},{4,2},{6,4},{1,7},{3,1},{5,3},{7,5},{8,14},{10,8},{12,... | collective-permute-start | bytes 1179656 | tf_op jit(solution)/shard_map/ppermute | solution.py:23
  247.5 13.7 %collective-permute-start.22 = (bf16[6,4,64,128]{3,2,1,0:T(8,128)(2,1)S(1)}, bf16[6,4,64,128]{3,2,1,0:T(8,128)(2,1)S(1)}, u32[]{:S(2)}, u32[]{:S(2)}) collective-permute-start(bf16[6,4,64,128]{3,2,1,0:T(8,128)(2,1)S(1)} %slice.114), channel_id=1, source_target_pairs={{0,2},{2,4},{4,6},{6,0},{1,3},{3,5},{5,7},{7,1},{8,10},{10,12},{12... | collective-permute-start | bytes 1179656 | tf_op jit(solution)/shard_map/ppermute | solution.py:23
  264.9 21.8 %collective-permute-start.23 = (bf16[4,4,64,128]{3,2,1,0:T(8,128)(2,1)S(1)}, bf16[4,4,64,128]{3,2,1,0:T(8,128)(2,1)S(1)}, u32[]{:S(2)}, u32[]{:S(2)}) collective-permute-start(bf16[4,4,64,128]{3,2,1,0:T(8,128)(2,1)S(1)} %get-tuple-element.16), channel_id=1, source_target_pairs={{0,1},{1,0},{2,3},{3,2},{4,5},{5,4},{6,7},{7,6},{8,9},{9,8},{10,11... | collective-permute-start | bytes 786440 | tf_op jit(solution)/shard_map/ppermute | solution.py:126
  (12 other events, 247.5 us)

commit v6 on v4

--- a/solution.py
+++ b/solution.py
@@ -39,41 +39,11 @@
     return jnp.concatenate([pair, from_right, far_low, far_high, from_left], axis=3)
 
 
-def ring_gather(block, axis):
-    ring = lax.axis_size(axis)
-    me = lax.axis_index(axis)
-    half = block.shape[0] // 2
-    from_left = ring_shift(block, axis, ring, 1)
-    from_right = ring_shift(block, axis, ring, -1)
-    far_low = ring_shift(from_right[:half], axis, ring, -1)
-    far_high = ring_shift(from_left[half:], axis, ring, 1)
-    far = jnp.concatenate([far_low, far_high], axis=0)
-    out = jnp.zeros((ring,) + block.shape, block.dtype)
-    for offset, piece in ((0, block), (1, from_right), (2, far), (ring - 1, from_left)):
-        start = ((me + offset) % ring,) + (0,) * block.ndim
-        out = lax.dynamic_update_slice(out, piece[None], start)
-    return out
-
-
-def swap_stack(block, axis, bit):
+def xor_stack(block, axis, bit, pos):
     count = lax.axis_size(axis)
     other = lax.ppermute(block, axis, [(i, i ^ bit) for i in range(count)])
     high = (lax.axis_index(axis) // bit) % 2 == 1
-    return jnp.where(high, jnp.stack([other, block]), jnp.stack([block, other]))
-
-
-def weight_gather(weight):
-    block = swap_stack(weight, "cz", 1)
-    for bit in (4, 2, 1):
-        block = swap_stack(block, "row", bit)
-    block = ring_gather(block, "fy")
-    block = swap_stack(block, "fc", 1)
-    block = jnp.transpose(block, (6, 1, 0, 4, 3, 2, 7, 5, 8))
-    taps, depth, width = weight.shape
-    full = block.reshape(taps, 64 * depth, 2 * width)
-    doubled = jnp.concatenate([full, full], axis=1)
-    shift = lax.axis_index("cx") * 2 * width
-    return lax.dynamic_slice_in_dim(doubled, shift, 64 * depth, axis=1)
+    return jnp.where(high, jnp.stack([other, block], axis=pos), jnp.stack([block, other], axis=pos))
 
 
 def body(frames_in, spatial_weight, temporal_weight, spatial_bias, temporal_bias, clip_id):
@@ -81,15 +51,50 @@
     half = row_count // 2
     side = lax.axis_index("cz")
     high = side == 1
-    both = weight_gather(jnp.concatenate([spatial_weight, temporal_weight], axis=0))
-    full_spatial, full_temporal = both[:9], both[9:]
+    row_n = lax.axis_size("row")
+    ring = lax.axis_size("cx")
+    weight = jnp.concatenate([spatial_weight, temporal_weight], axis=0)
+    taps, depth, _ = weight.shape
     biases = jnp.stack([spatial_bias, temporal_bias])
     biases = ordered_pair(biases, lax.ppermute(biases, "cz", SWAP), high, 1)
-    rimmed = shift_halo(frames_in, "row", lax.axis_size("row"), 1, 1)
+    rimmed = shift_halo(frames_in, "row", row_n, 1, 1)
+    w_block = ordered_pair(weight, lax.ppermute(weight, "cz", SWAP), high, 2)
+    rimmed, w_block = lax.optimization_barrier((rimmed, w_block))
     mine = lax.dynamic_slice_in_dim(rimmed, side * half, half + 2, axis=1)
     wanted = lax.dynamic_slice_in_dim(rimmed, (1 - side) * half, half + 2, axis=1)
     partner = lax.ppermute(wanted, "cz", SWAP)
-    gathered = x_gather(ordered_pair(mine, partner, high, 3))
+    for pos, bit in enumerate((4, 2, 1)):
+        w_block = xor_stack(w_block, "row", bit, 1 + pos)
+    w_block = w_block.reshape(taps, row_n * depth, -1)
+    partner, w_block = lax.optimization_barrier((partner, w_block))
+    pair = ordered_pair(mine, partner, high, 3)
+    from_left = ring_shift(pair, "cx", ring, 1)
+    from_right = ring_shift(pair, "cx", ring, -1)
+    fy_n = lax.axis_size("fy")
+    w_left = ring_shift(w_block, "fy", fy_n, 1)
+    w_right = ring_shift(w_block, "fy", fy_n, -1)
+    from_left, from_right, w_left, w_right = lax.optimization_barrier(
+        (from_left, from_right, w_left, w_right)
+    )
+    cut = pair.shape[3] // 2
+    far_low = ring_shift(from_right[..., :cut], "cx", ring, -1)
+    far_high = ring_shift(from_left[..., cut:], "cx", ring, 1)
+    w_cut = w_block.shape[1] // 2
+    w_far_low = ring_shift(w_right[:, :w_cut], "fy", fy_n, -1)
+    w_far_high = ring_shift(w_left[:, w_cut:], "fy", fy_n, 1)
+    far_low, far_high, w_far_low, w_far_high = lax.optimization_barrier(
+        (far_low, far_high, w_far_low, w_far_high)
+    )
+    gathered = jnp.concatenate([pair, from_right, far_low, far_high, from_left], axis=3)
+    me_fy = lax.axis_index("fy")
+    rotate = lax.axis_index("cx")
+    w_far = jnp.concatenate([w_far_low, w_far_high], axis=1)
+    w_out = jnp.zeros((taps, fy_n) + w_block.shape[1:], w_block.dtype)
+    for offset, piece in ((0, w_block), (1, w_right), (2, w_far), (fy_n - 1, w_left)):
+        place = (me_fy + offset - rotate + 2 * fy_n) % fy_n
+        w_out = lax.dynamic_update_slice(w_out, piece[:, None], (0, place, 0, 0))
+    both = xor_stack(w_out, "fc", 1, 2).reshape(taps, -1, w_block.shape[2])
+    full_spatial, full_temporal = both[:9], both[9:]
     kernel = full_spatial.reshape((3, 3) + full_spatial.shape[1:])
     spatial = lax.conv_general_dilated(
         gathered,
@@ -109,7 +114,7 @@
     next_ok = (local_ids[1:-1] == local_ids[2:]).astype(jnp.float32).reshape(fr_count, 1, 1, 1)
     source = shift_halo(active, FRAME, lax.axis_size(FRAME), 0, 1)
     whole = x_gather(source)
-    taps = [
+    taps_out = [
         jnp.einsum(
             "fhwc,cd->fhwd",
             whole[tap : tap + fr_count],
@@ -119,7 +124,11 @@
         for tap in range(3)
     ]
     total = (
-        hidden.astype(jnp.float32) + biases[1] + prev_ok * taps[0] + taps[1] + next_ok * taps[2]
+        hidden.astype(jnp.float32)
+        + biases[1]
+        + prev_ok * taps_out[0]
+        + taps_out[1]
+        + next_ok * taps_out[2]
     ).astype(jnp.bfloat16)
     kept = lax.dynamic_slice_in_dim(total, side * col_width, col_width, axis=3)
     given = lax.dynamic_slice_in_dim(total, (1 - side) * col_width, col_width, axis=3)

time: 327 us -> 283 us (0.87)
  the two profiles are of different devices: /device:TPU:233 before, /device:TPU:1 now
where the time goes in v6:
time: 283 us; the launch traced here: 280 us
  waiting for transfers between devices  129 us (46%)
  starting transfers between devices  99 us (35%)
  local copies, waits for them, and re-layouts  31.1 us (11%)
  other arithmetic  11.2 us (4%)
  matrix products  9.44 us (3%)
    ppermute x4, waiting for transfers between devices, xor_stack(): other = lax.ppermute(block, axis, [(i, i ^ bit) for i in range(count)])  48.2 us
    ppermute x12, waiting for transfers between devices, ring_shift(): lax.ppermute(block, axis, [(i, (i + step) % count) for i in range(count)])  41.6 us
    ppermute x12, starting transfers between devices, ring_shift(): lax.ppermute(block, axis, [(i, (i + step) % count) for i in range(count)])  40.2 us
    ppermute x1, waiting for transfers between devices, body(): partner = lax.ppermute(wanted, 'cz', SWAP)  16.5 us
    ppermute x1, starting transfers between devices, body(): w_block = ordered_pair(weight, lax.ppermute(weight, 'cz', SWAP), high, 2)  16.3 us
    unnamed x35, local copies, waits for them, and re-layouts  15 us
    ppermute x4, starting transfers between devices, xor_stack(): other = lax.ppermute(block, axis, [(i, i ^ bit) for i in range(count)])  13.8 us
    ppermute x1, waiting for transfers between devices, body(): returned = lax.ppermute(given, 'cz', SWAP)  11 us
  transfers between devices with their start and end apart: 24, of which 17 were waited for; matrix products, arithmetic and copies ran while one was open for 9% of the time, Pallas kernels for 0%

profile of v6, /device:TPU:1, one launch (start us, length us, event | category | flops | bytes accessed | tf_op | source)
XLA Modules:
  0.0 280.1 jit_solution(15455247297599095438)
XLA Ops:
  1.5 16.3 %collective-permute-start.2 = (bf16[12,16,128]{2,1,0:T(8,128)(2,1)S(1)}, bf16[12,16,128]{2,1,0:T(8,128)(2,1)S(1)}, u32[]{:S(2)}, u32[]{:S(2)}) collective-permute-start(bf16[12,16,128]{2,1,0:T(8,128)(2,1)S(1)} %constant_dynamic-update-slice_fusion), channel_id=1, source_target_pairs={{0,1},{1,0},{2,3},{3,2},{4,5},{5,4},{6,7},{7,6},{8,9},{9,8},{10,11... | collective-permute-start | bytes 147464 | tf_op jit(solution)/shard_map/ppermute | solution.py:61
  27.4 4.3 %collective-permute-start.4 = (bf16[12,16,256]{2,1,0:T(8,128)(2,1)S(1)}, bf16[12,16,256]{2,1,0:T(8,128)(2,1)S(1)}, u32[]{:S(2)}, u32[]{:S(2)}) collective-permute-start(bf16[12,16,256]{2,1,0:T(8,128)(2,1)S(1)} %maximum_select_fusion.7), channel_id=1, source_target_pairs={{0,32},{8,40},{16,48},{24,56},{32,0},{40,8},{48,16},{56,24},{1,33}... | collective-permute-start | bytes 294920 | tf_op jit(solution)/shard_map/ppermute | solution.py:44
  31.8 12.0 %collective-permute-done.4 = bf16[12,16,256]{2,1,0:T(8,128)(2,1)S(1)} collective-permute-done((bf16[12,16,256]{2,1,0:T(8,128)(2,1)S(1)}, bf16[12,16,256]{2,1,0:T(8,128)(2,1)S(1)}, u32[]{:S(2)}, u32[]{:S(2)}) %collective-permute-start.4) | collective-permute-done | bytes 98336 | tf_op jit(solution)/shard_map/ppermute | solution.py:44
  45.8 9.7 %collective-permute-done.5 = bf16[12,2,16,256]{3,2,1,0:T(8,128)(2,1)S(1)} collective-permute-done((bf16[12,2,16,256]{3,2,1,0:T(8,128)(2,1)S(1)}, bf16[12,2,16,256]{3,2,1,0:T(8,128)(2,1)S(1)}, u32[]{:S(2)}, u32[]{:S(2)}) %collective-permute-start.5) | collective-permute-done | bytes 196640 | tf_op jit(solution)/shard_map/ppermute | solution.py:44
  59.5 26.6 %collective-permute-done.6 = bf16[12,2,2,16,256]{4,3,1,0,2:T(8,128)(2,1)S(1)} collective-permute-done((bf16[12,2,2,16,256]{4,3,1,0,2:T(8,128)(2,1)S(1)}, bf16[12,2,2,16,256]{4,3,1,0,2:T(8,128)(2,1)S(1)}, u32[]{:S(2)}, u32[]{:S(2)}) %collective-permute-start.6) | collective-permute-done | bytes 393248 | tf_op jit(solution)/shard_map/ppermute | solution.py:44
  86.2 16.5 %collective-permute-done.3 = bf16[4,6,64,128]{3,2,1,0:T(8,128)(2,1)S(1)} collective-permute-done((bf16[4,6,64,128]{3,2,1,0:T(8,128)(2,1)S(1)}, bf16[4,6,64,128]{3,2,1,0:T(8,128)(2,1)S(1)}, u32[]{:S(2)}, u32[]{:S(2)}) %collective-permute-start.3) | collective-permute-done | bytes 393248 | tf_op jit(solution)/shard_map/ppermute | solution.py:65
  102.7 4.6 %collective-permute-start.10 = (bf16[12,128,256]{2,1,0:T(8,128)(2,1)S(1)}, bf16[12,128,256]{2,1,0:T(8,128)(2,1)}, u32[]{:S(2)}, u32[]{:S(2)}) collective-permute-start(bf16[12,128,256]{2,1,0:T(8,128)(2,1)S(1)} %bitcast.88), channel_id=1, source_target_pairs={{0,384},{128,0},{256,128},{384,256},{1,385},{129,1},{257,129},{385... | collective-permute-start | bytes 2359304 | tf_op jit(solution)/shard_map/ppermute | solution.py:23
  110.8 4.4 %collective-permute-start.8 = (bf16[4,6,64,256]{3,2,1,0:T(8,128)(2,1)}, bf16[4,6,64,256]{3,2,1,0:T(8,128)(2,1)S(1)}, u32[]{:S(2)}, u32[]{:S(2)}) collective-permute-start(bf16[4,6,64,256]{3,2,1,0:T(8,128)(2,1)} %get-tuple-element.30), channel_id=1, source_target_pairs={{0,6},{2,0},{4,2},{6,4},{1,7},{3,1},{5,3},{7,5},{8,14},{10,8},{12,... | collective-permute-start | bytes 2359304 | tf_op jit(solution)/shard_map/ppermute | solution.py:23
  117.1 6.5 %collective-permute-done.10 = bf16[12,128,256]{2,1,0:T(8,128)(2,1)} collective-permute-done((bf16[12,128,256]{2,1,0:T(8,128)(2,1)S(1)}, bf16[12,128,256]{2,1,0:T(8,128)(2,1)}, u32[]{:S(2)}, u32[]{:S(2)}) %collective-permute-start.10) | collective-permute-done | bytes 786464 | tf_op jit(solution)/shard_map/ppermute | solution.py:23
  123.6 5.0 %collective-permute-done.9 = bf16[12,128,256]{2,1,0:T(8,128)(2,1)S(1)} collective-permute-done((bf16[12,128,256]{2,1,0:T(8,128)(2,1)S(1)}, bf16[12,128,256]{2,1,0:T(8,128)(2,1)S(1)}, u32[]{:S(2)}, u32[]{:S(2)}) %collective-permute-start.9) | collective-permute-done | bytes 786464 | tf_op jit(solution)/shard_map/ppermute | solution.py:23
  131.4 4.9 %collective-permute-done.7 = bf16[4,6,64,256]{3,2,1,0:T(8,128)(2,1)S(1)} collective-permute-done((bf16[4,6,64,256]{3,2,1,0:T(8,128)(2,1)}, bf16[4,6,64,256]{3,2,1,0:T(8,128)(2,1)S(1)}, u32[]{:S(2)}, u32[]{:S(2)}) %collective-permute-start.7) | collective-permute-done | bytes 786464 | tf_op jit(solution)/shard_map/ppermute | solution.py:23
  139.6 4.6 %collective-permute-start.13 = (bf16[12,64,256]{2,1,0:T(8,128)(2,1)S(1)}, bf16[12,64,256]{2,1,0:T(8,128)(2,1)S(1)}, u32[]{:S(2)}, u32[]{:S(2)}) collective-permute-start(bf16[12,64,256]{2,1,0:T(8,128)(2,1)S(1)} %slice.80), channel_id=1, source_target_pairs={{0,384},{128,0},{256,128},{384,256},{1,385},{129,1},{257,129},{385... | collective-permute-start | bytes 1179656 | tf_op jit(solution)/shard_map/ppermute | solution.py:23
  146.2 4.6 %collective-permute-start.11 = (bf16[4,6,64,128]{3,2,1,0:T(8,128)(2,1)S(1)}, bf16[4,6,64,128]{3,2,1,0:T(8,128)(2,1)S(1)}, u32[]{:S(2)}, u32[]{:S(2)}) collective-permute-start(bf16[4,6,64,128]{3,2,1,0:T(8,128)(2,1)S(1)} %slice.78), channel_id=1, source_target_pairs={{0,6},{2,0},{4,2},{6,4},{1,7},{3,1},{5,3},{7,5},{8,14},{10,8},{12,... | collective-permute-start | bytes 1179656 | tf_op jit(solution)/shard_map/ppermute | solution.py:23
  157.0 5.7 %collective-permute-start.15 = (bf16[12,4,128,256]{3,2,1,0:T(8,128)(2,1)S(1)}, bf16[12,4,128,256]{3,2,1,0:T(8,128)(2,1)}, u32[]{:S(2)}, u32[]{:S(2)}) collective-permute-start(bf16[12,4,128,256]{3,2,1,0:T(8,128)(2,1)S(1)} %bitcast_dynamic-update-slice_fusion), channel_id=1, source_target_pairs={{0,64},{64,0},{1,65},{65,1},{2,66},{66,2},{3,67},{67,3},{4,68},{68... | collective-permute-start | bytes 9437192 | tf_op jit(solution)/shard_map/ppermute | solution.py:44
  162.8 9.3 %collective-permute-start.16 = (f32[2,128]{1,0:T(2,128)S(1)}, f32[2,128]{1,0:T(2,128)S(1)}, u32[]{:S(2)}, u32[]{:S(2)}) collective-permute-start(f32[2,128]{1,0:T(2,128)S(1)} %pad_maximum_fusion.4), channel_id=1, source_target_pairs={{0,1},{1,0},{2,3},{3,2},{4,5},{5,4},{6,7},{7,6},{8,9},{9,8},{10,11... | collective-permute-start | bytes 3080 | tf_op jit(solution)/shard_map/ppermute | solution.py:59
  181.7 4.3 %copy.32 = bf16[6,4,64,1024]{3,1,2,0:T(4,128)(2,1)S(1)} copy(bf16[6,4,64,1024]{3,2,0,1:T(8,128)(2,1)} %bitcast.83) | data formatting | bytes 6291456
  190.0 4.2 %maximum_select_fusion = bf16[12,4,2,128,256]{4,3,2,1,0:T(8,128)(2,1)S(1)} fusion(bf16[12,4,1,128,256]{4,3,2,1,0:T(8,128)(2,1)S(1)} %bitcast.82, bf16[12,4,1,128,256]{4,3,2,1,0:T(8,128)(2,1)} %bitcast.20, pred[]{:T(512)S(6)} %eq.34), kind=kLoop, calls=%fused_computation.2 | loop fusion | flops 9437184 | bytes 12582913 | tf_op jit(solution)/shard_map/jit(_where)/select_n | solution.py:46
  196.9 7.2 %convert_add_fusion = (f32[4,32,9,256]{3,1,2,0:T(8,128)}, bf16[4,32,9,256]{3,1,2,0:T(8,128)(2,1)S(1)}) fusion(f32[256]{0:T(256)S(1)} %bitcast.107, f32[256]{0:T(256)S(1)} %bitcast.108, bf16[3,3,1024,256]{3,2,1,0:T(8,128)(2,1)S(1)} %bitcast.84, bf16[6,4,8,11,1024]{4,1,3,2,0:T(4,128)(2,1)S(1)} %fusion.1, pred[32,9]{0,1:T(8,128)(4,1)S(1)} %copy-done.12), kind=kOutput, calls=%fused_computation.9 | convolution fusion | flops 5438767104 | bytes 10815776 | tf_op jit(solution)/shard_map/conv_general_dilated | solution.py:99
  214.2 5.3 %collective-permute-start.19 = (bf16[6,4,64,256]{3,2,1,0:T(8,128)(2,1)}, bf16[6,4,64,256]{3,2,1,0:T(8,128)(2,1)}, u32[]{:S(2)}, u32[]{:S(2)}) collective-permute-start(bf16[6,4,64,256]{3,2,1,0:T(8,128)(2,1)} %get-tuple-element.34), channel_id=1, source_target_pairs={{0,6},{2,0},{4,2},{6,4},{1,7},{3,1},{5,3},{7,5},{8,14},{10,8},{12,... | collective-permute-start | bytes 2359304 | tf_op jit(solution)/shard_map/ppermute | solution.py:23
  224.1 11.0 %collective-permute-done.19 = bf16[6,4,64,256]{3,2,1,0:T(8,128)(2,1)} collective-permute-done((bf16[6,4,64,256]{3,2,1,0:T(8,128)(2,1)}, bf16[6,4,64,256]{3,2,1,0:T(8,128)(2,1)}, u32[]{:S(2)}, u32[]{:S(2)}) %collective-permute-start.19) | collective-permute-done | bytes 786464 | tf_op jit(solution)/shard_map/ppermute | solution.py:23
  236.1 5.0 %collective-permute-start.20 = (bf16[6,4,64,128]{3,2,1,0:T(8,128)(2,1)S(1)}, bf16[6,4,64,128]{3,2,1,0:T(8,128)(2,1)S(1)}, u32[]{:S(2)}, u32[]{:S(2)}) collective-permute-start(bf16[6,4,64,128]{3,2,1,0:T(8,128)(2,1)S(1)} %slice.109), channel_id=1, source_target_pairs={{0,6},{2,0},{4,2},{6,4},{1,7},{3,1},{5,3},{7,5},{8,14},{10,8},{12,... | collective-permute-start | bytes 1179656 | tf_op jit(solution)/shard_map/ppermute | solution.py:23
  249.2 6.2 %collective-permute-done.22 = bf16[6,4,64,128]{3,2,1,0:T(8,128)(2,1)S(1)} collective-permute-done((bf16[6,4,64,128]{3,2,1,0:T(8,128)(2,1)S(1)}, bf16[6,4,64,128]{3,2,1,0:T(8,128)(2,1)S(1)}, u32[]{:S(2)}, u32[]{:S(2)}) %collective-permute-start.22) | collective-permute-done | bytes 393248 | tf_op jit(solution)/shard_map/ppermute | solution.py:23
  259.1 9.1 %collective-permute-start.23 = (bf16[4,4,64,128]{3,2,1,0:T(8,128)(2,1)S(1)}, bf16[4,4,64,128]{3,2,1,0:T(8,128)(2,1)S(1)}, u32[]{:S(2)}, u32[]{:S(2)}) collective-permute-start(bf16[4,4,64,128]{3,2,1,0:T(8,128)(2,1)S(1)} %get-tuple-element.40), channel_id=1, source_target_pairs={{0,1},{1,0},{2,3},{3,2},{4,5},{5,4},{6,7},{7,6},{8,9},{9,8},{10,11... | collective-permute-start | bytes 786440 | tf_op jit(solution)/shard_map/ppermute | solution.py:135
  268.3 11.0 %collective-permute-done.23 = bf16[4,4,64,128]{3,2,1,0:T(8,128)(2,1)S(1)} collective-permute-done((bf16[4,4,64,128]{3,2,1,0:T(8,128)(2,1)S(1)}, bf16[4,4,64,128]{3,2,1,0:T(8,128)(2,1)S(1)}, u32[]{:S(2)}, u32[]{:S(2)}) %collective-permute-start.23) | collective-permute-done | bytes 262176 | tf_op jit(solution)/shard_map/ppermute | solution.py:135
  (109 shorter events, 81.0 us)
Async XLA Ops:
  1.5 21.1 %collective-permute-start.2 = (bf16[12,16,128]{2,1,0:T(8,128)(2,1)S(1)}, bf16[12,16,128]{2,1,0:T(8,128)(2,1)S(1)}, u32[]{:S(2)}, u32[]{:S(2)}) collective-permute-start(bf16[12,16,128]{2,1,0:T(8,128)(2,1)S(1)} %constant_dynamic-update-slice_fusion), channel_id=1, source_target_pairs={{0,1},{1,0},{2,3},{3,2},{4,5},{5,4},{6,7},{7,6},{8,9},{9,8},{10,11... | collective-permute-start | bytes 147464 | tf_op jit(solution)/shard_map/ppermute | solution.py:61
  18.6 4.0 %collective-permute-start = (bf16[4,1,64,128]{3,2,1,0:T(8,128)(2,1)S(1)}, bf16[4,1,64,128]{3,2,1,0:T(8,128)(2,1)S(1)}, u32[]{:S(2)}, u32[]{:S(2)}) collective-permute-start(bf16[4,1,64,128]{3,2,1,0:T(8,128)(2,1)S(1)} %get-tuple-element.44), channel_id=1, source_target_pairs={{0,8},{8,16},{16,24},{24,32},{32,40},{40,48},{48,56},{1,9},{9,17},... | collective-permute-start | bytes 196616 | tf_op jit(solution)/shard_map/ppermute | solution.py:15
  21.3 5.0 %collective-permute-start.1 = (bf16[4,1,64,128]{3,2,1,0:T(8,128)(2,1)S(1)}, bf16[4,1,64,128]{3,2,1,0:T(8,128)(2,1)S(1)}, u32[]{:S(2)}, u32[]{:S(2)}) collective-permute-start(bf16[4,1,64,128]{3,2,1,0:T(8,128)(2,1)S(1)} %get-tuple-element.45), channel_id=1, source_target_pairs={{8,0},{16,8},{24,16},{32,24},{40,32},{48,40},{56,48},{9,1},{17,9},... | collective-permute-start | bytes 196616 | tf_op jit(solution)/shard_map/ppermute | solution.py:18
  27.4 16.3 %collective-permute-start.4 = (bf16[12,16,256]{2,1,0:T(8,128)(2,1)S(1)}, bf16[12,16,256]{2,1,0:T(8,128)(2,1)S(1)}, u32[]{:S(2)}, u32[]{:S(2)}) collective-permute-start(bf16[12,16,256]{2,1,0:T(8,128)(2,1)S(1)} %maximum_select_fusion.7), channel_id=1, source_target_pairs={{0,32},{8,40},{16,48},{24,56},{32,0},{40,8},{48,16},{56,24},{1,33}... | collective-permute-start | bytes 294920 | tf_op jit(solution)/shard_map/ppermute | solution.py:44
  43.8 11.7 %collective-permute-start.5 = (bf16[12,2,16,256]{3,2,1,0:T(8,128)(2,1)S(1)}, bf16[12,2,16,256]{3,2,1,0:T(8,128)(2,1)S(1)}, u32[]{:S(2)}, u32[]{:S(2)}) collective-permute-start(bf16[12,2,16,256]{3,2,1,0:T(8,128)(2,1)S(1)} %maximum_select_fusion.6), channel_id=1, source_target_pairs={{0,16},{8,24},{16,0},{24,8},{32,48},{40,56},{48,32},{56,40},{1,17}... | collective-permute-start | bytes 589832 | tf_op jit(solution)/shard_map/ppermute | solution.py:44
  55.5 30.6 %collective-permute-start.6 = (bf16[12,2,2,16,256]{4,3,1,0,2:T(8,128)(2,1)S(1)}, bf16[12,2,2,16,256]{4,3,1,0,2:T(8,128)(2,1)S(1)}, u32[]{:S(2)}, u32[]{:S(2)}) collective-permute-start(bf16[12,2,2,16,256]{4,3,1,0,2:T(8,128)(2,1)S(1)} %maximum_select_fusion.4), channel_id=1, source_target_pairs={{0,8},{8,0},{16,24},{24,16},{32,40},{40,32},{48,56},{56,48},{1,9},... | collective-permute-start | bytes 1179656 | tf_op jit(solution)/shard_map/ppermute | solution.py:44
  57.5 45.2 %collective-permute-start.3 = (bf16[4,6,64,128]{3,2,1,0:T(8,128)(2,1)S(1)}, bf16[4,6,64,128]{3,2,1,0:T(8,128)(2,1)S(1)}, u32[]{:S(2)}, u32[]{:S(2)}) collective-permute-start(bf16[4,6,64,128]{3,2,1,0:T(8,128)(2,1)S(1)} %get-tuple-element.37), channel_id=1, source_target_pairs={{0,1},{1,0},{2,3},{3,2},{4,5},{5,4},{6,7},{7,6},{8,9},{9,8},{10,11... | collective-permute-start | bytes 1179656 | tf_op jit(solution)/shard_map/ppermute | solution.py:65
  102.7 20.9 %collective-permute-start.10 = (bf16[12,128,256]{2,1,0:T(8,128)(2,1)S(1)}, bf16[12,128,256]{2,1,0:T(8,128)(2,1)}, u32[]{:S(2)}, u32[]{:S(2)}) collective-permute-start(bf16[12,128,256]{2,1,0:T(8,128)(2,1)S(1)} %bitcast.88), channel_id=1, source_target_pairs={{0,384},{128,0},{256,128},{384,256},{1,385},{129,1},{257,129},{385... | collective-permute-start | bytes 2359304 | tf_op jit(solution)/shard_map/ppermute | solution.py:23
  107.3 21.3 %collective-permute-start.9 = (bf16[12,128,256]{2,1,0:T(8,128)(2,1)S(1)}, bf16[12,128,256]{2,1,0:T(8,128)(2,1)S(1)}, u32[]{:S(2)}, u32[]{:S(2)}) collective-permute-start(bf16[12,128,256]{2,1,0:T(8,128)(2,1)S(1)} %bitcast.89), channel_id=1, source_target_pairs={{0,128},{128,256},{256,384},{384,0},{1,129},{129,257},{257,385},{3... | collective-permute-start | bytes 2359304 | tf_op jit(solution)/shard_map/ppermute | solution.py:23
  110.8 20.7 %collective-permute-start.8 = (bf16[4,6,64,256]{3,2,1,0:T(8,128)(2,1)}, bf16[4,6,64,256]{3,2,1,0:T(8,128)(2,1)S(1)}, u32[]{:S(2)}, u32[]{:S(2)}) collective-permute-start(bf16[4,6,64,256]{3,2,1,0:T(8,128)(2,1)} %get-tuple-element.30), channel_id=1, source_target_pairs={{0,6},{2,0},{4,2},{6,4},{1,7},{3,1},{5,3},{7,5},{8,14},{10,8},{12,... | collective-permute-start | bytes 2359304 | tf_op jit(solution)/shard_map/ppermute | solution.py:23
  115.2 21.2 %collective-permute-start.7 = (bf16[4,6,64,256]{3,2,1,0:T(8,128)(2,1)}, bf16[4,6,64,256]{3,2,1,0:T(8,128)(2,1)S(1)}, u32[]{:S(2)}, u32[]{:S(2)}) collective-permute-start(bf16[4,6,64,256]{3,2,1,0:T(8,128)(2,1)} %get-tuple-element.30), channel_id=1, source_target_pairs={{0,2},{2,4},{4,6},{6,0},{1,3},{3,5},{5,7},{7,1},{8,10},{10,12},{12... | collective-permute-start | bytes 2359304 | tf_op jit(solution)/shard_map/ppermute | solution.py:23
  137.7 15.5 %collective-permute-start.14 = (bf16[12,64,256]{2,1,0:T(8,128)(2,1)S(1)}, bf16[12,64,256]{2,1,0:T(8,128)(2,1)S(1)}, u32[]{:S(2)}, u32[]{:S(2)}) collective-permute-start(bf16[12,64,256]{2,1,0:T(8,128)(2,1)S(1)} %slice.81), channel_id=1, source_target_pairs={{0,128},{128,256},{256,384},{384,0},{1,129},{129,257},{257,385},{3... | collective-permute-start | bytes 1179656 | tf_op jit(solution)/shard_map/ppermute | solution.py:23
  139.6 13.6 %collective-permute-start.13 = (bf16[12,64,256]{2,1,0:T(8,128)(2,1)S(1)}, bf16[12,64,256]{2,1,0:T(8,128)(2,1)S(1)}, u32[]{:S(2)}, u32[]{:S(2)}) collective-permute-start(bf16[12,64,256]{2,1,0:T(8,128)(2,1)S(1)} %slice.80), channel_id=1, source_target_pairs={{0,384},{128,0},{256,128},{384,256},{1,385},{129,1},{257,129},{385... | collective-permute-start | bytes 1179656 | tf_op jit(solution)/shard_map/ppermute | solution.py:23
  144.2 11.1 %collective-permute-start.12 = (bf16[4,6,64,128]{3,2,1,0:T(8,128)(2,1)S(1)}, bf16[4,6,64,128]{3,2,1,0:T(8,128)(2,1)S(1)}, u32[]{:S(2)}, u32[]{:S(2)}) collective-permute-start(bf16[4,6,64,128]{3,2,1,0:T(8,128)(2,1)S(1)} %slice.79), channel_id=1, source_target_pairs={{0,2},{2,4},{4,6},{6,0},{1,3},{3,5},{5,7},{7,1},{8,10},{10,12},{12... | collective-permute-start | bytes 1179656 | tf_op jit(solution)/shard_map/ppermute | solution.py:23
  146.2 10.1 %collective-permute-start.11 = (bf16[4,6,64,128]{3,2,1,0:T(8,128)(2,1)S(1)}, bf16[4,6,64,128]{3,2,1,0:T(8,128)(2,1)S(1)}, u32[]{:S(2)}, u32[]{:S(2)}) collective-permute-start(bf16[4,6,64,128]{3,2,1,0:T(8,128)(2,1)S(1)} %slice.78), channel_id=1, source_target_pairs={{0,6},{2,0},{4,2},{6,4},{1,7},{3,1},{5,3},{7,5},{8,14},{10,8},{12,... | collective-permute-start | bytes 1179656 | tf_op jit(solution)/shard_map/ppermute | solution.py:23
  157.0 33.0 %collective-permute-start.15 = (bf16[12,4,128,256]{3,2,1,0:T(8,128)(2,1)S(1)}, bf16[12,4,128,256]{3,2,1,0:T(8,128)(2,1)}, u32[]{:S(2)}, u32[]{:S(2)}) collective-permute-start(bf16[12,4,128,256]{3,2,1,0:T(8,128)(2,1)S(1)} %bitcast_dynamic-update-slice_fusion), channel_id=1, source_target_pairs={{0,64},{64,0},{1,65},{65,1},{2,66},{66,2},{3,67},{67,3},{4,68},{68... | collective-permute-start | bytes 9437192 | tf_op jit(solution)/shard_map/ppermute | solution.py:44
  162.8 13.0 %collective-permute-start.16 = (f32[2,128]{1,0:T(2,128)S(1)}, f32[2,128]{1,0:T(2,128)S(1)}, u32[]{:S(2)}, u32[]{:S(2)}) collective-permute-start(f32[2,128]{1,0:T(2,128)S(1)} %pad_maximum_fusion.4), channel_id=1, source_target_pairs={{0,1},{1,0},{2,3},{3,2},{4,5},{5,4},{6,7},{7,6},{8,9},{9,8},{10,11... | collective-permute-start | bytes 3080 | tf_op jit(solution)/shard_map/ppermute | solution.py:59
  204.9 4.4 %collective-permute-start.17 = (bf16[1,4,64,256]{3,2,1,0:T(8,128)(2,1)S(1)}, bf16[1,4,64,256]{3,2,1,0:T(8,128)(2,1)S(1)}, u32[]{:S(2)}, u32[]{:S(2)}) collective-permute-start(bf16[1,4,64,256]{3,2,1,0:T(8,128)(2,1)S(1)} %get-tuple-element.42), channel_id=1, source_target_pairs={{0,64},{64,128},{128,192},{192,256},{256,320},{320,384},{384,448},... | collective-permute-start | bytes 393224 | tf_op jit(solution)/shard_map/ppermute | solution.py:15
  206.9 6.3 %collective-permute-start.18 = (bf16[1,4,64,256]{3,2,1,0:T(8,128)(2,1)S(1)}, bf16[1,4,64,256]{3,2,1,0:T(8,128)(2,1)S(1)}, u32[]{:S(2)}, u32[]{:S(2)}) collective-permute-start(bf16[1,4,64,256]{3,2,1,0:T(8,128)(2,1)S(1)} %get-tuple-element.43), channel_id=1, source_target_pairs={{64,0},{128,64},{192,128},{256,192},{320,256},{384,320},{448,384},... | collective-permute-start | bytes 393224 | tf_op jit(solution)/shard_map/ppermute | solution.py:18
  214.2 20.9 %collective-permute-start.19 = (bf16[6,4,64,256]{3,2,1,0:T(8,128)(2,1)}, bf16[6,4,64,256]{3,2,1,0:T(8,128)(2,1)}, u32[]{:S(2)}, u32[]{:S(2)}) collective-permute-start(bf16[6,4,64,256]{3,2,1,0:T(8,128)(2,1)} %get-tuple-element.34), channel_id=1, source_target_pairs={{0,6},{2,0},{4,2},{6,4},{1,7},{3,1},{5,3},{7,5},{8,14},{10,8},{12,... | collective-permute-start | bytes 2359304 | tf_op jit(solution)/shard_map/ppermute | solution.py:23
  219.5 21.7 %collective-permute-start.21 = (bf16[6,4,64,256]{3,2,1,0:T(8,128)(2,1)}, bf16[6,4,64,256]{3,2,1,0:T(8,128)(2,1)}, u32[]{:S(2)}, u32[]{:S(2)}) collective-permute-start(bf16[6,4,64,256]{3,2,1,0:T(8,128)(2,1)} %get-tuple-element.34), channel_id=1, source_target_pairs={{0,2},{2,4},{4,6},{6,0},{1,3},{3,5},{5,7},{7,1},{8,10},{10,12},{12... | collective-permute-start | bytes 2359304 | tf_op jit(solution)/shard_map/ppermute | solution.py:23
  236.1 13.0 %collective-permute-start.20 = (bf16[6,4,64,128]{3,2,1,0:T(8,128)(2,1)S(1)}, bf16[6,4,64,128]{3,2,1,0:T(8,128)(2,1)S(1)}, u32[]{:S(2)}, u32[]{:S(2)}) collective-permute-start(bf16[6,4,64,128]{3,2,1,0:T(8,128)(2,1)S(1)} %slice.109), channel_id=1, source_target_pairs={{0,6},{2,0},{4,2},{6,4},{1,7},{3,1},{5,3},{7,5},{8,14},{10,8},{12,... | collective-permute-start | bytes 1179656 | tf_op jit(solution)/shard_map/ppermute | solution.py:23
  242.2 13.3 %collective-permute-start.22 = (bf16[6,4,64,128]{3,2,1,0:T(8,128)(2,1)S(1)}, bf16[6,4,64,128]{3,2,1,0:T(8,128)(2,1)S(1)}, u32[]{:S(2)}, u32[]{:S(2)}) collective-permute-start(bf16[6,4,64,128]{3,2,1,0:T(8,128)(2,1)S(1)} %slice.110), channel_id=1, source_target_pairs={{0,2},{2,4},{4,6},{6,0},{1,3},{3,5},{5,7},{7,1},{8,10},{10,12},{12... | collective-permute-start | bytes 1179656 | tf_op jit(solution)/shard_map/ppermute | solution.py:23
  259.1 20.2 %collective-permute-start.23 = (bf16[4,4,64,128]{3,2,1,0:T(8,128)(2,1)S(1)}, bf16[4,4,64,128]{3,2,1,0:T(8,128)(2,1)S(1)}, u32[]{:S(2)}, u32[]{:S(2)}) collective-permute-start(bf16[4,4,64,128]{3,2,1,0:T(8,128)(2,1)S(1)} %get-tuple-element.40), channel_id=1, source_target_pairs={{0,1},{1,0},{2,3},{3,2},{4,5},{5,4},{6,7},{7,6},{8,9},{9,8},{10,11... | collective-permute-start | bytes 786440 | tf_op jit(solution)/shard_map/ppermute | solution.py:135
  (13 other events, 161.5 us)

commit v7 on v6

--- a/solution.py
+++ b/solution.py
@@ -58,34 +58,41 @@
     biases = jnp.stack([spatial_bias, temporal_bias])
     biases = ordered_pair(biases, lax.ppermute(biases, "cz", SWAP), high, 1)
     rimmed = shift_halo(frames_in, "row", row_n, 1, 1)
+    sent = lax.dynamic_slice_in_dim(frames_in, (1 - side) * (half - 1), half + 1, axis=1)
+    partner = lax.ppermute(sent, "cz", SWAP)
+    edge = lax.dynamic_slice_in_dim(frames_in, side * (row_count - 1), 1, axis=1)
+    diagonal = [(q * 2 + 1, q * 2 + 2) for q in range(row_n - 1)]
+    diagonal += [(q * 2, q * 2 - 1) for q in range(1, row_n)]
+    rim = lax.ppermute(edge, ("row", "cz"), diagonal)
     w_block = ordered_pair(weight, lax.ppermute(weight, "cz", SWAP), high, 2)
     rimmed, w_block = lax.optimization_barrier((rimmed, w_block))
     mine = lax.dynamic_slice_in_dim(rimmed, side * half, half + 2, axis=1)
-    wanted = lax.dynamic_slice_in_dim(rimmed, (1 - side) * half, half + 2, axis=1)
-    partner = lax.ppermute(wanted, "cz", SWAP)
+    own_left = ring_shift(mine, "cx", ring, 1)
+    own_right = ring_shift(mine, "cx", ring, -1)
     for pos, bit in enumerate((4, 2, 1)):
         w_block = xor_stack(w_block, "row", bit, 1 + pos)
     w_block = w_block.reshape(taps, row_n * depth, -1)
-    partner, w_block = lax.optimization_barrier((partner, w_block))
-    pair = ordered_pair(mine, partner, high, 3)
-    from_left = ring_shift(pair, "cx", ring, 1)
-    from_right = ring_shift(pair, "cx", ring, -1)
+    own_left, own_right, w_block, partner, rim = lax.optimization_barrier(
+        (own_left, own_right, w_block, partner, rim)
+    )
+    other = ordered_pair(rim, partner, high, 1)
+    other_left = ring_shift(other, "cx", ring, 1)
+    other_right = ring_shift(other, "cx", ring, -1)
+    far_own = ring_shift(own_right, "cx", ring, -1)
     fy_n = lax.axis_size("fy")
     w_left = ring_shift(w_block, "fy", fy_n, 1)
     w_right = ring_shift(w_block, "fy", fy_n, -1)
-    from_left, from_right, w_left, w_right = lax.optimization_barrier(
-        (from_left, from_right, w_left, w_right)
+    other_left, other_right, far_own, w_left, w_right = lax.optimization_barrier(
+        (other_left, other_right, far_own, w_left, w_right)
     )
-    cut = pair.shape[3] // 2
-    far_low = ring_shift(from_right[..., :cut], "cx", ring, -1)
-    far_high = ring_shift(from_left[..., cut:], "cx", ring, 1)
+    far_other = ring_shift(other_left, "cx", ring, 1)
     w_cut = w_block.shape[1] // 2
     w_far_low = ring_shift(w_right[:, :w_cut], "fy", fy_n, -1)
     w_far_high = ring_shift(w_left[:, w_cut:], "fy", fy_n, 1)
-    far_low, far_high, w_far_low, w_far_high = lax.optimization_barrier(
-        (far_low, far_high, w_far_low, w_far_high)
+    far_other, w_far_low, w_far_high = lax.optimization_barrier((far_other, w_far_low, w_far_high))
+    gathered = jnp.concatenate(
+        [mine, other, own_right, other_right, far_own, far_other, own_left, other_left], axis=3
     )
-    gathered = jnp.concatenate([pair, from_right, far_low, far_high, from_left], axis=3)
     me_fy = lax.axis_index("fy")
     rotate = lax.axis_index("cx")
     w_far = jnp.concatenate([w_far_low, w_far_high], axis=1)
@@ -93,7 +100,10 @@
     for offset, piece in ((0, w_block), (1, w_right), (2, w_far), (fy_n - 1, w_left)):
         place = (me_fy + offset - rotate + 2 * fy_n) % fy_n
         w_out = lax.dynamic_update_slice(w_out, piece[:, None], (0, place, 0, 0))
-    both = xor_stack(w_out, "fc", 1, 2).reshape(taps, -1, w_block.shape[2])
+    w_other = lax.ppermute(w_out, "fc", SWAP)
+    flip = (lax.axis_index("fc") + side) % 2 == 1
+    both = jnp.where(flip, jnp.stack([w_other, w_out], axis=2), jnp.stack([w_out, w_other], axis=2))
+    both = both.reshape(taps, -1, w_block.shape[2])
     full_spatial, full_temporal = both[:9], both[9:]
     kernel = full_spatial.reshape((3, 3) + full_spatial.shape[1:])
     spatial = lax.conv_general_dilated(
@@ -113,6 +123,9 @@
     prev_ok = (local_ids[1:-1] == local_ids[:-2]).astype(jnp.float32).reshape(fr_count, 1, 1, 1)
     next_ok = (local_ids[1:-1] == local_ids[2:]).astype(jnp.float32).reshape(fr_count, 1, 1, 1)
     source = shift_halo(active, FRAME, lax.axis_size(FRAME), 0, 1)
+    source = jnp.where(
+        high, jnp.concatenate([source[..., col_width:], source[..., :col_width]], axis=3), source
+    )
     whole = x_gather(source)
     taps_out = [
         jnp.einsum(

time: 283 us -> 296 us (1.046)
  the two profiles are of different devices: /device:TPU:1 before, /device:TPU:54 now
where the time goes in v7:
time: 296 us; the launch traced here: 294 us
  waiting for transfers between devices  137 us (46%)
  starting transfers between devices  99.8 us (34%)
  local copies, waits for them, and re-layouts  35.6 us (12%)
  other arithmetic  12.3 us (4%)
  matrix products  9.46 us (3%)
    ppermute x14, waiting for transfers between devices, ring_shift(): lax.ppermute(block, axis, [(i, (i + step) % count) for i in range(count)])  44.6 us
    ppermute x14, starting transfers between devices, ring_shift(): lax.ppermute(block, axis, [(i, (i + step) % count) for i in range(count)])  42.5 us
    ppermute x1, waiting for transfers between devices, body(): rim = lax.ppermute(edge, ('row', 'cz'), diagonal)  32.3 us
    ppermute x1, waiting for transfers between devices, body(): returned = lax.ppermute(given, 'cz', SWAP)  26.8 us
    unnamed x42, local copies, waits for them, and re-layouts  19.5 us
    ppermute x3, waiting for transfers between devices, xor_stack(): other = lax.ppermute(block, axis, [(i, i ^ bit) for i in range(count)])  15.3 us
    ppermute x1, starting transfers between devices, body(): w_block = ordered_pair(weight, lax.ppermute(weight, 'cz', SWAP), high, 2)  14.8 us
    ppermute x1, waiting for transfers between devices, body(): biases = ordered_pair(biases, lax.ppermute(biases, 'cz', SWAP), high, 1)  12.1 us
  transfers between devices with their start and end apart: 27, of which 16 were waited for; matrix products, arithmetic and copies ran while one was open for 11% of the time, Pallas kernels for 0%

profile of v7, /device:TPU:54, one launch (start us, length us, event | category | flops | bytes accessed | tf_op | source)
XLA Modules:
  0.0 294.5 jit_solution(2556828345651897956)
XLA Ops:
  1.5 14.8 %collective-permute-start.2 = (bf16[12,16,128]{2,1,0:T(8,128)(2,1)S(1)}, bf16[12,16,128]{2,1,0:T(8,128)(2,1)S(1)}, u32[]{:S(2)}, u32[]{:S(2)}) collective-permute-start(bf16[12,16,128]{2,1,0:T(8,128)(2,1)S(1)} %constant_dynamic-update-slice_fusion), channel_id=1, source_target_pairs={{0,1},{1,0},{2,3},{3,2},{4,5},{5,4},{6,7},{7,6},{8,9},{9,8},{10,11... | collective-permute-start | bytes 147464 | tf_op jit(solution)/shard_map/ppermute | solution.py:67
  28.1 4.5 %collective-permute-start.5 = (bf16[12,16,256]{2,1,0:T(8,128)(2,1)S(1)}, bf16[12,16,256]{2,1,0:T(8,128)(2,1)S(1)}, u32[]{:S(2)}, u32[]{:S(2)}) collective-permute-start(bf16[12,16,256]{2,1,0:T(8,128)(2,1)S(1)} %maximum_select_fusion.8), channel_id=1, source_target_pairs={{0,32},{8,40},{16,48},{24,56},{32,0},{40,8},{48,16},{56,24},{1,33}... | collective-permute-start | bytes 294920 | tf_op jit(solution)/shard_map/ppermute | solution.py:44
  32.7 8.4 %collective-permute-done.5 = bf16[12,16,256]{2,1,0:T(8,128)(2,1)S(1)} collective-permute-done((bf16[12,16,256]{2,1,0:T(8,128)(2,1)S(1)}, bf16[12,16,256]{2,1,0:T(8,128)(2,1)S(1)}, u32[]{:S(2)}, u32[]{:S(2)}) %collective-permute-start.5) | collective-permute-done | bytes 98336 | tf_op jit(solution)/shard_map/ppermute | solution.py:44
  43.1 6.9 %collective-permute-done.6 = bf16[12,2,16,256]{3,2,1,0:T(8,128)(2,1)S(1)} collective-permute-done((bf16[12,2,16,256]{3,2,1,0:T(8,128)(2,1)S(1)}, bf16[12,2,16,256]{3,2,1,0:T(8,128)(2,1)S(1)}, u32[]{:S(2)}, u32[]{:S(2)}) %collective-permute-start.6) | collective-permute-done | bytes 196640 | tf_op jit(solution)/shard_map/ppermute | solution.py:44
  50.1 5.4 %collective-permute-start.7 = (bf16[12,2,2,16,256]{4,3,1,0,2:T(8,128)(2,1)S(1)}, bf16[12,2,2,16,256]{4,3,1,0,2:T(8,128)(2,1)S(1)}, u32[]{:S(2)}, u32[]{:S(2)}) collective-permute-start(bf16[12,2,2,16,256]{4,3,1,0,2:T(8,128)(2,1)S(1)} %maximum_select_fusion.4), channel_id=1, source_target_pairs={{0,8},{8,0},{16,24},{24,16},{32,40},{40,32},{48,56},{56,48},{1,9},... | collective-permute-start | bytes 1179656 | tf_op jit(solution)/shard_map/ppermute | solution.py:44
  59.3 4.3 %collective-permute-start.3 = (bf16[4,6,64,128]{3,2,1,0:T(8,128)(2,1)S(1)}, bf16[4,6,64,128]{3,2,1,0:T(8,128)(2,1)S(1)}, u32[]{:S(2)}, u32[]{:S(2)}) collective-permute-start(bf16[4,6,64,128]{3,2,1,0:T(8,128)(2,1)S(1)} %get-tuple-element.40), channel_id=1, source_target_pairs={{0,2},{2,4},{4,6},{6,0},{1,3},{3,5},{5,7},{7,1},{8,10},{10,12},{12... | collective-permute-start | bytes 1179656 | tf_op jit(solution)/shard_map/ppermute | solution.py:23
  64.4 6.0 %collective-permute-start.8 = (bf16[4,5,64,128]{3,2,1,0:T(8,128)(2,1)}, bf16[4,5,64,128]{3,2,1,0:T(8,128)(2,1)}, u32[]{:S(2)}, u32[]{:S(2)}) collective-permute-start(bf16[4,5,64,128]{3,2,1,0:T(8,128)(2,1)} %constant_dynamic-slice_fusion.3), channel_id=1, source_target_pairs={{0,1},{1,0},{2,3},{3,2},{4,5},{5,4},{6,7},{7,6},{8,9},{9,8},{10,11... | collective-permute-start | bytes 983048 | tf_op jit(solution)/shard_map/ppermute | solution.py:62
  70.4 7.1 %collective-permute-start.9 = (bf16[4,1,64,128]{3,2,1,0:T(8,128)(2,1)}, bf16[4,1,64,128]{3,2,1,0:T(8,128)(2,1)}, u32[]{:S(2)}, u32[]{:S(2)}) collective-permute-start(bf16[4,1,64,128]{3,2,1,0:T(8,128)(2,1)} %get-tuple-element.52), channel_id=1, source_target_pairs={{1,8},{9,16},{17,24},{25,32},{33,40},{41,48},{49,56},{8,1},{16,9},... | collective-permute-start | bytes 196616 | tf_op jit(solution)/shard_map/ppermute | solution.py:66
  77.7 32.3 %collective-permute-done.9 = bf16[4,1,64,128]{3,2,1,0:T(8,128)(2,1)} collective-permute-done((bf16[4,1,64,128]{3,2,1,0:T(8,128)(2,1)}, bf16[4,1,64,128]{3,2,1,0:T(8,128)(2,1)}, u32[]{:S(2)}, u32[]{:S(2)}) %collective-permute-start.9) | collective-permute-done | bytes 65568 | tf_op jit(solution)/shard_map/ppermute | solution.py:66
  112.4 3.5 %collective-permute-start.13 = (bf16[12,128,256]{2,1,0:T(8,128)(2,1)S(1)}, bf16[12,128,256]{2,1,0:T(8,128)(2,1)S(1)}, u32[]{:S(2)}, u32[]{:S(2)}) collective-permute-start(bf16[12,128,256]{2,1,0:T(8,128)(2,1)S(1)} %bitcast.90), channel_id=1, source_target_pairs={{0,128},{128,256},{256,384},{384,0},{1,129},{129,257},{257,385},{3... | collective-permute-start | bytes 2359304 | tf_op jit(solution)/shard_map/ppermute | solution.py:23
  120.0 5.1 %collective-permute-start.10 = (bf16[4,6,64,128]{3,2,1,0:T(8,128)(2,1)}, bf16[4,6,64,128]{3,2,1,0:T(8,128)(2,1)}, u32[]{:S(2)}, u32[]{:S(2)}) collective-permute-start(bf16[4,6,64,128]{3,2,1,0:T(8,128)(2,1)} %get-tuple-element.38), channel_id=1, source_target_pairs={{0,2},{2,4},{4,6},{6,0},{1,3},{3,5},{5,7},{7,1},{8,10},{10,12},{12... | collective-permute-start | bytes 1179656 | tf_op jit(solution)/shard_map/ppermute | solution.py:23
  127.2 6.3 %collective-permute-done.11 = bf16[4,6,64,128]{3,2,1,0:T(8,128)(2,1)S(1)} collective-permute-done((bf16[4,6,64,128]{3,2,1,0:T(8,128)(2,1)}, bf16[4,6,64,128]{3,2,1,0:T(8,128)(2,1)S(1)}, u32[]{:S(2)}, u32[]{:S(2)}) %collective-permute-start.11) | collective-permute-done | bytes 393248 | tf_op jit(solution)/shard_map/ppermute | solution.py:23
  133.5 7.0 %collective-permute-done.12 = bf16[4,6,64,128]{3,2,1,0:T(8,128)(2,1)} collective-permute-done((bf16[4,6,64,128]{3,2,1,0:T(8,128)(2,1)S(1)}, bf16[4,6,64,128]{3,2,1,0:T(8,128)(2,1)}, u32[]{:S(2)}, u32[]{:S(2)}) %collective-permute-start.12) | collective-permute-done | bytes 393248 | tf_op jit(solution)/shard_map/ppermute | solution.py:23
  140.5 4.4 %collective-permute-start.17 = (bf16[12,64,256]{2,1,0:T(8,128)(2,1)S(1)}, bf16[12,64,256]{2,1,0:T(8,128)(2,1)S(1)}, u32[]{:S(2)}, u32[]{:S(2)}) collective-permute-start(bf16[12,64,256]{2,1,0:T(8,128)(2,1)S(1)} %slice.79), channel_id=1, source_target_pairs={{0,128},{128,256},{256,384},{384,0},{1,129},{129,257},{257,385},{3... | collective-permute-start | bytes 1179656 | tf_op jit(solution)/shard_map/ppermute | solution.py:23
  152.0 4.1 %collective-permute-done.16 = bf16[12,64,256]{2,1,0:T(8,128)(2,1)S(1)} collective-permute-done((bf16[12,64,256]{2,1,0:T(8,128)(2,1)S(1)}, bf16[12,64,256]{2,1,0:T(8,128)(2,1)S(1)}, u32[]{:S(2)}, u32[]{:S(2)}) %collective-permute-start.16) | collective-permute-done | bytes 393248 | tf_op jit(solution)/shard_map/ppermute | solution.py:23
  163.1 12.1 %collective-permute-done.19 = f32[2,128]{1,0:T(2,128)S(1)} collective-permute-done((f32[2,128]{1,0:T(2,128)S(1)}, f32[2,128]{1,0:T(2,128)S(1)}, u32[]{:S(2)}, u32[]{:S(2)}) %collective-permute-start.19) | collective-permute-done | bytes 1056 | tf_op jit(solution)/shard_map/ppermute | solution.py:59
  185.1 4.3 %copy.32 = bf16[6,4,64,1024]{3,1,2,0:T(4,128)(2,1)S(1)} copy(bf16[6,4,64,1024]{3,2,0,1:T(8,128)(2,1)} %bitcast.88) | data formatting | bytes 6291456
  193.4 4.2 %maximum_select_fusion = bf16[12,4,2,128,256]{4,3,2,1,0:T(8,128)(2,1)S(1)} fusion(bf16[12,4,1,128,256]{4,3,2,1,0:T(8,128)(2,1)S(1)} %bitcast.82, bf16[12,4,1,128,256]{4,3,2,1,0:T(8,128)(2,1)} %bitcast.20, pred[]{:T(512)S(6)} %eq.34), kind=kLoop, calls=%fused_computation.2 | loop fusion | flops 9437184 | bytes 12582913 | tf_op jit(solution)/shard_map/jit(_where)/select_n | solution.py:105
  200.3 7.3 %convert_add_fusion = (f32[4,32,9,256]{3,1,2,0:T(8,128)}, bf16[4,32,9,256]{3,1,2,0:T(8,128)(2,1)S(1)}) fusion(f32[256]{0:T(256)S(1)} %bitcast.108, f32[256]{0:T(256)S(1)} %bitcast.109, bf16[3,3,1024,256]{3,2,1,0:T(8,128)(2,1)S(1)} %bitcast.86, bf16[6,4,8,11,1024]{4,1,3,2,0:T(4,128)(2,1)S(1)} %fusion.1, pred[32,9]{0,1:T(8,128)(4,1)S(1)} %copy-done.14), kind=kOutput, calls=%fused_computation.9 | convolution fusion | flops 5438767104 | bytes 10815776 | tf_op jit(solution)/shard_map/conv_general_dilated | solution.py:109
  210.3 3.9 %collective-permute-start.21 = (bf16[1,4,64,256]{3,2,1,0:T(8,128)(2,1)S(1)}, bf16[1,4,64,256]{3,2,1,0:T(8,128)(2,1)S(1)}, u32[]{:S(2)}, u32[]{:S(2)}) collective-permute-start(bf16[1,4,64,256]{3,2,1,0:T(8,128)(2,1)S(1)} %get-tuple-element.51), channel_id=1, source_target_pairs={{64,0},{128,64},{192,128},{256,192},{320,256},{384,320},{448,384},... | collective-permute-start | bytes 393224 | tf_op jit(solution)/shard_map/ppermute | solution.py:18
  226.3 13.3 %collective-permute-done.24 = bf16[6,4,64,256]{3,2,1,0:T(8,128)(2,1)} collective-permute-done((bf16[6,4,64,256]{3,2,1,0:T(8,128)(2,1)}, bf16[6,4,64,256]{3,2,1,0:T(8,128)(2,1)}, u32[]{:S(2)}, u32[]{:S(2)}) %collective-permute-start.24) | collective-permute-done | bytes 786464 | tf_op jit(solution)/shard_map/ppermute | solution.py:23
  240.7 4.6 %collective-permute-start.25 = (bf16[6,4,64,128]{3,2,1,0:T(8,128)(2,1)S(1)}, bf16[6,4,64,128]{3,2,1,0:T(8,128)(2,1)S(1)}, u32[]{:S(2)}, u32[]{:S(2)}) collective-permute-start(bf16[6,4,64,128]{3,2,1,0:T(8,128)(2,1)S(1)} %slice.112), channel_id=1, source_target_pairs={{0,2},{2,4},{4,6},{6,0},{1,3},{3,5},{5,7},{7,1},{8,10},{10,12},{12... | collective-permute-start | bytes 1179656 | tf_op jit(solution)/shard_map/ppermute | solution.py:23
  251.0 10.0 %collective-permute-done.23 = bf16[6,4,64,128]{3,2,1,0:T(8,128)(2,1)S(1)} collective-permute-done((bf16[6,4,64,128]{3,2,1,0:T(8,128)(2,1)S(1)}, bf16[6,4,64,128]{3,2,1,0:T(8,128)(2,1)S(1)}, u32[]{:S(2)}, u32[]{:S(2)}) %collective-permute-start.23) | collective-permute-done | bytes 393248 | tf_op jit(solution)/shard_map/ppermute | solution.py:23
  266.8 26.8 %collective-permute-done.26 = bf16[4,4,64,128]{3,2,1,0:T(8,128)(2,1)S(1)} collective-permute-done((bf16[4,4,64,128]{3,2,1,0:T(8,128)(2,1)S(1)}, bf16[4,4,64,128]{3,2,1,0:T(8,128)(2,1)S(1)}, u32[]{:S(2)}, u32[]{:S(2)}) %collective-permute-start.26) | collective-permute-done | bytes 262176 | tf_op jit(solution)/shard_map/ppermute | solution.py:148
  (122 shorter events, 86.9 us)
Async XLA Ops:
  1.5 22.2 %collective-permute-start.2 = (bf16[12,16,128]{2,1,0:T(8,128)(2,1)S(1)}, bf16[12,16,128]{2,1,0:T(8,128)(2,1)S(1)}, u32[]{:S(2)}, u32[]{:S(2)}) collective-permute-start(bf16[12,16,128]{2,1,0:T(8,128)(2,1)S(1)} %constant_dynamic-update-slice_fusion), channel_id=1, source_target_pairs={{0,1},{1,0},{2,3},{3,2},{4,5},{5,4},{6,7},{7,6},{8,9},{9,8},{10,11... | collective-permute-start | bytes 147464 | tf_op jit(solution)/shard_map/ppermute | solution.py:67
  28.1 13.0 %collective-permute-start.5 = (bf16[12,16,256]{2,1,0:T(8,128)(2,1)S(1)}, bf16[12,16,256]{2,1,0:T(8,128)(2,1)S(1)}, u32[]{:S(2)}, u32[]{:S(2)}) collective-permute-start(bf16[12,16,256]{2,1,0:T(8,128)(2,1)S(1)} %maximum_select_fusion.8), channel_id=1, source_target_pairs={{0,32},{8,40},{16,48},{24,56},{32,0},{40,8},{48,16},{56,24},{1,33}... | collective-permute-start | bytes 294920 | tf_op jit(solution)/shard_map/ppermute | solution.py:44
  41.1 8.9 %collective-permute-start.6 = (bf16[12,2,16,256]{3,2,1,0:T(8,128)(2,1)S(1)}, bf16[12,2,16,256]{3,2,1,0:T(8,128)(2,1)S(1)}, u32[]{:S(2)}, u32[]{:S(2)}) collective-permute-start(bf16[12,2,16,256]{3,2,1,0:T(8,128)(2,1)S(1)} %maximum_select_fusion.7), channel_id=1, source_target_pairs={{0,16},{8,24},{16,0},{24,8},{32,48},{40,56},{48,32},{56,40},{1,17}... | collective-permute-start | bytes 589832 | tf_op jit(solution)/shard_map/ppermute | solution.py:44
  50.1 27.5 %collective-permute-start.7 = (bf16[12,2,2,16,256]{4,3,1,0,2:T(8,128)(2,1)S(1)}, bf16[12,2,2,16,256]{4,3,1,0,2:T(8,128)(2,1)S(1)}, u32[]{:S(2)}, u32[]{:S(2)}) collective-permute-start(bf16[12,2,2,16,256]{4,3,1,0,2:T(8,128)(2,1)S(1)} %maximum_select_fusion.4), channel_id=1, source_target_pairs={{0,8},{8,0},{16,24},{24,16},{32,40},{40,32},{48,56},{56,48},{1,9},... | collective-permute-start | bytes 1179656 | tf_op jit(solution)/shard_map/ppermute | solution.py:44
  56.6 53.4 %collective-permute-start.4 = (bf16[4,6,64,128]{3,2,1,0:T(8,128)(2,1)S(1)}, bf16[4,6,64,128]{3,2,1,0:T(8,128)(2,1)S(1)}, u32[]{:S(2)}, u32[]{:S(2)}) collective-permute-start(bf16[4,6,64,128]{3,2,1,0:T(8,128)(2,1)S(1)} %get-tuple-element.40), channel_id=1, source_target_pairs={{0,6},{2,0},{4,2},{6,4},{1,7},{3,1},{5,3},{7,5},{8,14},{10,8},{12,... | collective-permute-start | bytes 1179656 | tf_op jit(solution)/shard_map/ppermute | solution.py:23
  59.3 50.7 %collective-permute-start.3 = (bf16[4,6,64,128]{3,2,1,0:T(8,128)(2,1)S(1)}, bf16[4,6,64,128]{3,2,1,0:T(8,128)(2,1)S(1)}, u32[]{:S(2)}, u32[]{:S(2)}) collective-permute-start(bf16[4,6,64,128]{3,2,1,0:T(8,128)(2,1)S(1)} %get-tuple-element.40), channel_id=1, source_target_pairs={{0,2},{2,4},{4,6},{6,0},{1,3},{3,5},{5,7},{7,1},{8,10},{10,12},{12... | collective-permute-start | bytes 1179656 | tf_op jit(solution)/shard_map/ppermute | solution.py:23
  64.4 45.6 %collective-permute-start.8 = (bf16[4,5,64,128]{3,2,1,0:T(8,128)(2,1)}, bf16[4,5,64,128]{3,2,1,0:T(8,128)(2,1)}, u32[]{:S(2)}, u32[]{:S(2)}) collective-permute-start(bf16[4,5,64,128]{3,2,1,0:T(8,128)(2,1)} %constant_dynamic-slice_fusion.3), channel_id=1, source_target_pairs={{0,1},{1,0},{2,3},{3,2},{4,5},{5,4},{6,7},{7,6},{8,9},{9,8},{10,11... | collective-permute-start | bytes 983048 | tf_op jit(solution)/shard_map/ppermute | solution.py:62
  70.4 39.6 %collective-permute-start.9 = (bf16[4,1,64,128]{3,2,1,0:T(8,128)(2,1)}, bf16[4,1,64,128]{3,2,1,0:T(8,128)(2,1)}, u32[]{:S(2)}, u32[]{:S(2)}) collective-permute-start(bf16[4,1,64,128]{3,2,1,0:T(8,128)(2,1)} %get-tuple-element.52), channel_id=1, source_target_pairs={{1,8},{9,16},{17,24},{25,32},{33,40},{41,48},{49,56},{8,1},{16,9},... | collective-permute-start | bytes 196616 | tf_op jit(solution)/shard_map/ppermute | solution.py:66
  110.0 30.4 %collective-permute-start.14 = (bf16[12,128,256]{2,1,0:T(8,128)(2,1)S(1)}, bf16[12,128,256]{2,1,0:T(8,128)(2,1)S(1)}, u32[]{:S(2)}, u32[]{:S(2)}) collective-permute-start(bf16[12,128,256]{2,1,0:T(8,128)(2,1)S(1)} %bitcast.89), channel_id=1, source_target_pairs={{0,384},{128,0},{256,128},{384,256},{1,385},{129,1},{257,129},{385... | collective-permute-start | bytes 2359304 | tf_op jit(solution)/shard_map/ppermute | solution.py:23
  112.4 28.1 %collective-permute-start.13 = (bf16[12,128,256]{2,1,0:T(8,128)(2,1)S(1)}, bf16[12,128,256]{2,1,0:T(8,128)(2,1)S(1)}, u32[]{:S(2)}, u32[]{:S(2)}) collective-permute-start(bf16[12,128,256]{2,1,0:T(8,128)(2,1)S(1)} %bitcast.90), channel_id=1, source_target_pairs={{0,128},{128,256},{256,384},{384,0},{1,129},{129,257},{257,385},{3... | collective-permute-start | bytes 2359304 | tf_op jit(solution)/shard_map/ppermute | solution.py:23
  118.1 15.4 %collective-permute-start.11 = (bf16[4,6,64,128]{3,2,1,0:T(8,128)(2,1)}, bf16[4,6,64,128]{3,2,1,0:T(8,128)(2,1)S(1)}, u32[]{:S(2)}, u32[]{:S(2)}) collective-permute-start(bf16[4,6,64,128]{3,2,1,0:T(8,128)(2,1)} %get-tuple-element.38), channel_id=1, source_target_pairs={{0,6},{2,0},{4,2},{6,4},{1,7},{3,1},{5,3},{7,5},{8,14},{10,8},{12,... | collective-permute-start | bytes 1179656 | tf_op jit(solution)/shard_map/ppermute | solution.py:23
  120.0 13.4 %collective-permute-start.10 = (bf16[4,6,64,128]{3,2,1,0:T(8,128)(2,1)}, bf16[4,6,64,128]{3,2,1,0:T(8,128)(2,1)}, u32[]{:S(2)}, u32[]{:S(2)}) collective-permute-start(bf16[4,6,64,128]{3,2,1,0:T(8,128)(2,1)} %get-tuple-element.38), channel_id=1, source_target_pairs={{0,2},{2,4},{4,6},{6,0},{1,3},{3,5},{5,7},{7,1},{8,10},{10,12},{12... | collective-permute-start | bytes 1179656 | tf_op jit(solution)/shard_map/ppermute | solution.py:23
  125.2 15.3 %collective-permute-start.12 = (bf16[4,6,64,128]{3,2,1,0:T(8,128)(2,1)S(1)}, bf16[4,6,64,128]{3,2,1,0:T(8,128)(2,1)}, u32[]{:S(2)}, u32[]{:S(2)}) collective-permute-start(bf16[4,6,64,128]{3,2,1,0:T(8,128)(2,1)S(1)} %collective-permute-done.4), channel_id=1, source_target_pairs={{0,6},{2,0},{4,2},{6,4},{1,7},{3,1},{5,3},{7,5},{8,14},{10,8},{12,... | collective-permute-start | bytes 1179656 | tf_op jit(solution)/shard_map/ppermute | solution.py:23
  140.5 11.5 %collective-permute-start.17 = (bf16[12,64,256]{2,1,0:T(8,128)(2,1)S(1)}, bf16[12,64,256]{2,1,0:T(8,128)(2,1)S(1)}, u32[]{:S(2)}, u32[]{:S(2)}) collective-permute-start(bf16[12,64,256]{2,1,0:T(8,128)(2,1)S(1)} %slice.79), channel_id=1, source_target_pairs={{0,128},{128,256},{256,384},{384,0},{1,129},{129,257},{257,385},{3... | collective-permute-start | bytes 1179656 | tf_op jit(solution)/shard_map/ppermute | solution.py:23
  144.9 11.2 %collective-permute-start.16 = (bf16[12,64,256]{2,1,0:T(8,128)(2,1)S(1)}, bf16[12,64,256]{2,1,0:T(8,128)(2,1)S(1)}, u32[]{:S(2)}, u32[]{:S(2)}) collective-permute-start(bf16[12,64,256]{2,1,0:T(8,128)(2,1)S(1)} %slice.78), channel_id=1, source_target_pairs={{0,384},{128,0},{256,128},{384,256},{1,385},{129,1},{257,129},{385... | collective-permute-start | bytes 1179656 | tf_op jit(solution)/shard_map/ppermute | solution.py:23
  146.9 11.4 %collective-permute-start.15 = (bf16[4,6,64,128]{3,2,1,0:T(8,128)(2,1)}, bf16[4,6,64,128]{3,2,1,0:T(8,128)(2,1)S(1)}, u32[]{:S(2)}, u32[]{:S(2)}) collective-permute-start(bf16[4,6,64,128]{3,2,1,0:T(8,128)(2,1)} %collective-permute-done.10), channel_id=1, source_target_pairs={{0,2},{2,4},{4,6},{6,0},{1,3},{3,5},{5,7},{7,1},{8,10},{10,12},{12... | collective-permute-start | bytes 1179656 | tf_op jit(solution)/shard_map/ppermute | solution.py:23
  159.0 34.4 %collective-permute-start.18 = (bf16[12,4,128,256]{3,2,1,0:T(8,128)(2,1)S(1)}, bf16[12,4,128,256]{3,2,1,0:T(8,128)(2,1)}, u32[]{:S(2)}, u32[]{:S(2)}) collective-permute-start(bf16[12,4,128,256]{3,2,1,0:T(8,128)(2,1)S(1)} %bitcast_dynamic-update-slice_fusion), channel_id=1, source_target_pairs={{0,64},{64,0},{1,65},{65,1},{2,66},{66,2},{3,67},{67,3},{4,68},{68... | collective-permute-start | bytes 9437192 | tf_op jit(solution)/shard_map/ppermute | solution.py:103
  161.0 14.2 %collective-permute-start.19 = (f32[2,128]{1,0:T(2,128)S(1)}, f32[2,128]{1,0:T(2,128)S(1)}, u32[]{:S(2)}, u32[]{:S(2)}) collective-permute-start(f32[2,128]{1,0:T(2,128)S(1)} %pad_maximum_fusion.4), channel_id=1, source_target_pairs={{0,1},{1,0},{2,3},{3,2},{4,5},{5,4},{6,7},{7,6},{8,9},{9,8},{10,11... | collective-permute-start | bytes 3080 | tf_op jit(solution)/shard_map/ppermute | solution.py:59
  208.4 6.3 %collective-permute-start.20 = (bf16[1,4,64,256]{3,2,1,0:T(8,128)(2,1)S(1)}, bf16[1,4,64,256]{3,2,1,0:T(8,128)(2,1)S(1)}, u32[]{:S(2)}, u32[]{:S(2)}) collective-permute-start(bf16[1,4,64,256]{3,2,1,0:T(8,128)(2,1)S(1)} %get-tuple-element.50), channel_id=1, source_target_pairs={{0,64},{64,128},{128,192},{192,256},{256,320},{320,384},{384,448},... | collective-permute-start | bytes 393224 | tf_op jit(solution)/shard_map/ppermute | solution.py:15
  218.0 21.6 %collective-permute-start.24 = (bf16[6,4,64,256]{3,2,1,0:T(8,128)(2,1)}, bf16[6,4,64,256]{3,2,1,0:T(8,128)(2,1)}, u32[]{:S(2)}, u32[]{:S(2)}) collective-permute-start(bf16[6,4,64,256]{3,2,1,0:T(8,128)(2,1)} %get-tuple-element.36), channel_id=1, source_target_pairs={{0,2},{2,4},{4,6},{6,0},{1,3},{3,5},{5,7},{7,1},{8,10},{10,12},{12... | collective-permute-start | bytes 2359304 | tf_op jit(solution)/shard_map/ppermute | solution.py:23
  221.4 23.9 %collective-permute-start.22 = (bf16[6,4,64,256]{3,2,1,0:T(8,128)(2,1)}, bf16[6,4,64,256]{3,2,1,0:T(8,128)(2,1)}, u32[]{:S(2)}, u32[]{:S(2)}) collective-permute-start(bf16[6,4,64,256]{3,2,1,0:T(8,128)(2,1)} %get-tuple-element.36), channel_id=1, source_target_pairs={{0,6},{2,0},{4,2},{6,4},{1,7},{3,1},{5,3},{7,5},{8,14},{10,8},{12,... | collective-permute-start | bytes 2359304 | tf_op jit(solution)/shard_map/ppermute | solution.py:23
  240.7 20.5 %collective-permute-start.25 = (bf16[6,4,64,128]{3,2,1,0:T(8,128)(2,1)S(1)}, bf16[6,4,64,128]{3,2,1,0:T(8,128)(2,1)S(1)}, u32[]{:S(2)}, u32[]{:S(2)}) collective-permute-start(bf16[6,4,64,128]{3,2,1,0:T(8,128)(2,1)S(1)} %slice.112), channel_id=1, source_target_pairs={{0,2},{2,4},{4,6},{6,0},{1,3},{3,5},{5,7},{7,1},{8,10},{10,12},{12... | collective-permute-start | bytes 1179656 | tf_op jit(solution)/shard_map/ppermute | solution.py:23
  246.3 14.7 %collective-permute-start.23 = (bf16[6,4,64,128]{3,2,1,0:T(8,128)(2,1)S(1)}, bf16[6,4,64,128]{3,2,1,0:T(8,128)(2,1)S(1)}, u32[]{:S(2)}, u32[]{:S(2)}) collective-permute-start(bf16[6,4,64,128]{3,2,1,0:T(8,128)(2,1)S(1)} %slice.111), channel_id=1, source_target_pairs={{0,6},{2,0},{4,2},{6,4},{1,7},{3,1},{5,3},{7,5},{8,14},{10,8},{12,... | collective-permute-start | bytes 1179656 | tf_op jit(solution)/shard_map/ppermute | solution.py:23
  264.9 28.8 %collective-permute-start.26 = (bf16[4,4,64,128]{3,2,1,0:T(8,128)(2,1)S(1)}, bf16[4,4,64,128]{3,2,1,0:T(8,128)(2,1)S(1)}, u32[]{:S(2)}, u32[]{:S(2)}) collective-permute-start(bf16[4,4,64,128]{3,2,1,0:T(8,128)(2,1)S(1)} %get-tuple-element.48), channel_id=1, source_target_pairs={{0,1},{1,0},{2,3},{3,2},{4,5},{5,4},{6,7},{7,6},{8,9},{9,8},{10,11... | collective-permute-start | bytes 786440 | tf_op jit(solution)/shard_map/ppermute | solution.py:148
  (18 other events, 267.0 us)

commit v8 on v6

--- a/solution.py
+++ b/solution.py
@@ -58,33 +58,32 @@
     biases = jnp.stack([spatial_bias, temporal_bias])
     biases = ordered_pair(biases, lax.ppermute(biases, "cz", SWAP), high, 1)
     rimmed = shift_halo(frames_in, "row", row_n, 1, 1)
+    sent = lax.dynamic_slice_in_dim(frames_in, (1 - side) * (half - 1), half + 1, axis=1)
+    partner = lax.ppermute(sent, "cz", SWAP)
+    edge = lax.dynamic_slice_in_dim(frames_in, side * (row_count - 1), 1, axis=1)
+    diagonal = [(q * 2 + 1, q * 2 + 2) for q in range(row_n - 1)]
+    diagonal += [(q * 2, q * 2 - 1) for q in range(1, row_n)]
+    rim = lax.ppermute(edge, ("row", "cz"), diagonal)
     w_block = ordered_pair(weight, lax.ppermute(weight, "cz", SWAP), high, 2)
-    rimmed, w_block = lax.optimization_barrier((rimmed, w_block))
+    rimmed, partner, rim, w_block = lax.optimization_barrier((rimmed, partner, rim, w_block))
     mine = lax.dynamic_slice_in_dim(rimmed, side * half, half + 2, axis=1)
-    wanted = lax.dynamic_slice_in_dim(rimmed, (1 - side) * half, half + 2, axis=1)
-    partner = lax.ppermute(wanted, "cz", SWAP)
+    pair = ordered_pair(mine, ordered_pair(rim, partner, high, 1), high, 3)
+    from_left = ring_shift(pair, "cx", ring, 1)
+    from_right = ring_shift(pair, "cx", ring, -1)
     for pos, bit in enumerate((4, 2, 1)):
         w_block = xor_stack(w_block, "row", bit, 1 + pos)
     w_block = w_block.reshape(taps, row_n * depth, -1)
-    partner, w_block = lax.optimization_barrier((partner, w_block))
-    pair = ordered_pair(mine, partner, high, 3)
-    from_left = ring_shift(pair, "cx", ring, 1)
-    from_right = ring_shift(pair, "cx", ring, -1)
+    from_left, from_right, w_block = lax.optimization_barrier((from_left, from_right, w_block))
     fy_n = lax.axis_size("fy")
     w_left = ring_shift(w_block, "fy", fy_n, 1)
     w_right = ring_shift(w_block, "fy", fy_n, -1)
-    from_left, from_right, w_left, w_right = lax.optimization_barrier(
-        (from_left, from_right, w_left, w_right)
-    )
     cut = pair.shape[3] // 2
     far_low = ring_shift(from_right[..., :cut], "cx", ring, -1)
     far_high = ring_shift(from_left[..., cut:], "cx", ring, 1)
+    far_low, far_high, w_left, w_right = lax.optimization_barrier((far_low, far_high, w_left, w_right))
     w_cut = w_block.shape[1] // 2
     w_far_low = ring_shift(w_right[:, :w_cut], "fy", fy_n, -1)
     w_far_high = ring_shift(w_left[:, w_cut:], "fy", fy_n, 1)
-    far_low, far_high, w_far_low, w_far_high = lax.optimization_barrier(
-        (far_low, far_high, w_far_low, w_far_high)
-    )
     gathered = jnp.concatenate([pair, from_right, far_low, far_high, from_left], axis=3)
     me_fy = lax.axis_index("fy")
     rotate = lax.axis_index("cx")

time: 283 us -> 281 us (level)
  the two profiles are of different devices: /device:TPU:1 before, /device:TPU:81 now
where the time goes in v8:
time: 281 us; the launch traced here: 280 us
  starting transfers between devices  115 us (41%)
  waiting for transfers between devices  110 us (39%)
  local copies, waits for them, and re-layouts  33.2 us (12%)
  other arithmetic  11 us (4%)
  matrix products  9.43 us (3%)
    ppermute x12, starting transfers between devices, ring_shift(): lax.ppermute(block, axis, [(i, (i + step) % count) for i in range(count)])  37.1 us
    ppermute x12, waiting for transfers between devices, ring_shift(): lax.ppermute(block, axis, [(i, (i + step) % count) for i in range(count)])  34.8 us
    ppermute x4, starting transfers between devices, xor_stack(): other = lax.ppermute(block, axis, [(i, i ^ bit) for i in range(count)])  29.2 us
    ppermute x1, waiting for transfers between devices, body(): returned = lax.ppermute(given, 'cz', SWAP)  28.7 us
    unnamed x33, local copies, waits for them, and re-layouts  14.4 us
    ppermute x4, waiting for transfers between devices, xor_stack(): other = lax.ppermute(block, axis, [(i, i ^ bit) for i in range(count)])  14.3 us
    ppermute x1, starting transfers between devices, body(): w_block = ordered_pair(weight, lax.ppermute(weight, 'cz', SWAP), high, 2)  13.6 us
    ppermute x2, waiting for transfers between devices, shift_halo(): lax.ppermute(lax.slice_in_dim(block, 0, width, axis=dim), axis, backward)  11.7 us
  transfers between devices with their start and end apart: 25, of which 16 were waited for; matrix products, arithmetic and copies ran while one was open for 11% of the time, Pallas kernels for 0%

profile of v8, /device:TPU:81, one launch (start us, length us, event | category | flops | bytes accessed | tf_op | source)
XLA Modules:
  0.0 279.8 jit_solution(1170546989947476907)
XLA Ops:
  1.5 13.6 %collective-permute-start.4 = (bf16[12,16,128]{2,1,0:T(8,128)(2,1)S(1)}, bf16[12,16,128]{2,1,0:T(8,128)(2,1)S(1)}, u32[]{:S(2)}, u32[]{:S(2)}) collective-permute-start(bf16[12,16,128]{2,1,0:T(8,128)(2,1)S(1)} %constant_dynamic-update-slice_fusion), channel_id=1, source_target_pairs={{0,1},{1,0},{2,3},{3,2},{4,5},{5,4},{6,7},{7,6},{8,9},{9,8},{10,11... | collective-permute-start | bytes 147464 | tf_op jit(solution)/shard_map/ppermute | solution.py:67
  19.0 11.6 %collective-permute-start.3 = (bf16[4,1,64,128]{3,2,1,0:T(8,128)(2,1)S(1)}, bf16[4,1,64,128]{3,2,1,0:T(8,128)(2,1)S(1)}, u32[]{:S(2)}, u32[]{:S(2)}) collective-permute-start(bf16[4,1,64,128]{3,2,1,0:T(8,128)(2,1)S(1)} %get-tuple-element.40), channel_id=1, source_target_pairs={{1,8},{9,16},{17,24},{25,32},{33,40},{41,48},{49,56},{8,1},{16,9},... | collective-permute-start | bytes 196616 | tf_op jit(solution)/shard_map/ppermute | solution.py:66
  36.0 7.4 %collective-permute-done.1 = bf16[4,1,64,128]{3,2,1,0:T(8,128)(2,1)S(1)} collective-permute-done((bf16[4,1,64,128]{3,2,1,0:T(8,128)(2,1)S(1)}, bf16[4,1,64,128]{3,2,1,0:T(8,128)(2,1)S(1)}, u32[]{:S(2)}, u32[]{:S(2)}) %collective-permute-start.1) | collective-permute-done | bytes 65568 | tf_op jit(solution)/shard_map/ppermute | solution.py:18
  43.4 11.2 %collective-permute-done = bf16[4,1,64,128]{3,2,1,0:T(8,128)(2,1)S(1)} collective-permute-done((bf16[4,1,64,128]{3,2,1,0:T(8,128)(2,1)S(1)}, bf16[4,1,64,128]{3,2,1,0:T(8,128)(2,1)S(1)}, u32[]{:S(2)}, u32[]{:S(2)}) %collective-permute-start) | collective-permute-done | bytes 65568 | tf_op jit(solution)/shard_map/ppermute | solution.py:15
  56.7 8.2 %collective-permute-start.7 = (bf16[12,16,256]{2,1,0:T(8,128)(2,1)S(1)}, bf16[12,16,256]{2,1,0:T(8,128)(2,1)S(1)}, u32[]{:S(2)}, u32[]{:S(2)}) collective-permute-start(bf16[12,16,256]{2,1,0:T(8,128)(2,1)S(1)} %maximum_select_fusion.8), channel_id=1, source_target_pairs={{0,32},{8,40},{16,48},{24,56},{32,0},{40,8},{48,16},{56,24},{1,33}... | collective-permute-start | bytes 294920 | tf_op jit(solution)/shard_map/ppermute | solution.py:44
  66.3 4.4 %collective-permute-start.6 = (bf16[4,6,64,256]{3,2,1,0:T(8,128)(2,1)S(1)}, bf16[4,6,64,256]{3,2,1,0:T(8,128)(2,1)S(1)}, u32[]{:S(2)}, u32[]{:S(2)}) collective-permute-start(bf16[4,6,64,256]{3,2,1,0:T(8,128)(2,1)S(1)} %get-tuple-element.28), channel_id=1, source_target_pairs={{0,6},{2,0},{4,2},{6,4},{1,7},{3,1},{5,3},{7,5},{8,14},{10,8},{12,... | collective-permute-start | bytes 2359304 | tf_op jit(solution)/shard_map/ppermute | solution.py:23
  74.7 5.3 %collective-permute-done.8 = bf16[12,2,16,256]{3,2,1,0:T(8,128)(2,1)S(1)} collective-permute-done((bf16[12,2,16,256]{3,2,1,0:T(8,128)(2,1)S(1)}, bf16[12,2,16,256]{3,2,1,0:T(8,128)(2,1)S(1)}, u32[]{:S(2)}, u32[]{:S(2)}) %collective-permute-start.8) | collective-permute-done | bytes 196640 | tf_op jit(solution)/shard_map/ppermute | solution.py:44
  80.0 14.1 %collective-permute-start.9 = (bf16[12,2,2,16,256]{4,3,1,0,2:T(8,128)(2,1)S(1)}, bf16[12,2,2,16,256]{4,3,1,0,2:T(8,128)(2,1)S(1)}, u32[]{:S(2)}, u32[]{:S(2)}) collective-permute-start(bf16[12,2,2,16,256]{4,3,1,0,2:T(8,128)(2,1)S(1)} %maximum_select_fusion.5), channel_id=1, source_target_pairs={{0,8},{8,0},{16,24},{24,16},{32,40},{40,32},{48,56},{56,48},{1,9},... | collective-permute-start | bytes 1179656 | tf_op jit(solution)/shard_map/ppermute | solution.py:44
  94.2 9.0 %collective-permute-done.9 = bf16[12,2,2,16,256]{4,3,1,0,2:T(8,128)(2,1)S(1)} collective-permute-done((bf16[12,2,2,16,256]{4,3,1,0,2:T(8,128)(2,1)S(1)}, bf16[12,2,2,16,256]{4,3,1,0,2:T(8,128)(2,1)S(1)}, u32[]{:S(2)}, u32[]{:S(2)}) %collective-permute-start.9) | collective-permute-done | bytes 393248 | tf_op jit(solution)/shard_map/ppermute | solution.py:44
  116.9 5.8 %collective-permute-done.11 = bf16[4,6,64,128]{3,2,1,0:T(8,128)(2,1)S(1)} collective-permute-done((bf16[4,6,64,128]{3,2,1,0:T(8,128)(2,1)}, bf16[4,6,64,128]{3,2,1,0:T(8,128)(2,1)S(1)}, u32[]{:S(2)}, u32[]{:S(2)}) %collective-permute-start.11) | collective-permute-done | bytes 393248 | tf_op jit(solution)/shard_map/ppermute | solution.py:23
  137.5 4.5 %collective-permute-done.14 = bf16[12,64,256]{2,1,0:T(8,128)(2,1)S(1)} collective-permute-done((bf16[12,64,256]{2,1,0:T(8,128)(2,1)S(1)}, bf16[12,64,256]{2,1,0:T(8,128)(2,1)S(1)}, u32[]{:S(2)}, u32[]{:S(2)}) %collective-permute-start.14) | collective-permute-done | bytes 393248 | tf_op jit(solution)/shard_map/ppermute | solution.py:23
  142.2 5.0 %collective-permute-start.16 = (bf16[12,4,128,256]{3,2,1,0:T(8,128)(2,1)S(1)}, bf16[12,4,128,256]{3,2,1,0:T(8,128)(2,1)}, u32[]{:S(2)}, u32[]{:S(2)}) collective-permute-start(bf16[12,4,128,256]{3,2,1,0:T(8,128)(2,1)S(1)} %bitcast_dynamic-update-slice_fusion), channel_id=1, source_target_pairs={{0,64},{64,0},{1,65},{65,1},{2,66},{66,2},{3,67},{67,3},{4,68},{68... | collective-permute-start | bytes 9437192 | tf_op jit(solution)/shard_map/ppermute | solution.py:44
  147.2 4.5 %collective-permute-start.17 = (f32[2,128]{1,0:T(2,128)S(1)}, f32[2,128]{1,0:T(2,128)S(1)}, u32[]{:S(2)}, u32[]{:S(2)}) collective-permute-start(f32[2,128]{1,0:T(2,128)S(1)} %pad_maximum_fusion.4), channel_id=1, source_target_pairs={{0,1},{1,0},{2,3},{3,2},{4,5},{5,4},{6,7},{7,6},{8,9},{9,8},{10,11... | collective-permute-start | bytes 3080 | tf_op jit(solution)/shard_map/ppermute | solution.py:59
  151.7 8.5 %collective-permute-done.17 = f32[2,128]{1,0:T(2,128)S(1)} collective-permute-done((f32[2,128]{1,0:T(2,128)S(1)}, f32[2,128]{1,0:T(2,128)S(1)}, u32[]{:S(2)}, u32[]{:S(2)}) %collective-permute-start.17) | collective-permute-done | bytes 1056 | tf_op jit(solution)/shard_map/ppermute | solution.py:59
  166.1 4.3 %copy.32 = bf16[6,4,64,1024]{3,1,2,0:T(4,128)(2,1)S(1)} copy(bf16[6,4,64,1024]{3,2,0,1:T(8,128)(2,1)} %bitcast.83) | data formatting | bytes 6291456
  181.3 7.2 %convert_add_fusion = (f32[4,32,9,256]{3,1,2,0:T(8,128)}, bf16[4,32,9,256]{3,1,2,0:T(8,128)(2,1)S(1)}) fusion(f32[256]{0:T(256)S(1)} %bitcast.107, f32[256]{0:T(256)S(1)} %bitcast.108, bf16[3,3,1024,256]{3,2,1,0:T(8,128)(2,1)S(1)} %bitcast.84, bf16[6,4,8,11,1024]{4,1,3,2,0:T(4,128)(2,1)S(1)} %fusion.1, pred[32,9]{0,1:T(8,128)(4,1)S(1)} %copy-done.11), kind=kOutput, calls=%fused_computation.9 | convolution fusion | flops 5438767104 | bytes 10815776 | tf_op jit(solution)/shard_map/conv_general_dilated | solution.py:98
  189.4 5.6 %collective-permute-start.18 = (bf16[1,4,64,256]{3,2,1,0:T(8,128)(2,1)S(1)}, bf16[1,4,64,256]{3,2,1,0:T(8,128)(2,1)S(1)}, u32[]{:S(2)}, u32[]{:S(2)}) collective-permute-start(bf16[1,4,64,256]{3,2,1,0:T(8,128)(2,1)S(1)} %get-tuple-element.38), channel_id=1, source_target_pairs={{0,64},{64,128},{128,192},{192,256},{256,320},{320,384},{384,448},... | collective-permute-start | bytes 393224 | tf_op jit(solution)/shard_map/ppermute | solution.py:15
  196.9 4.3 %collective-permute-done.19 = bf16[1,4,64,256]{3,2,1,0:T(8,128)(2,1)S(1)} collective-permute-done((bf16[1,4,64,256]{3,2,1,0:T(8,128)(2,1)S(1)}, bf16[1,4,64,256]{3,2,1,0:T(8,128)(2,1)S(1)}, u32[]{:S(2)}, u32[]{:S(2)}) %collective-permute-start.19) | collective-permute-done | bytes 131104 | tf_op jit(solution)/shard_map/ppermute | solution.py:18
  202.3 4.4 %collective-permute-start.20 = (bf16[6,4,64,256]{3,2,1,0:T(8,128)(2,1)}, bf16[6,4,64,256]{3,2,1,0:T(8,128)(2,1)}, u32[]{:S(2)}, u32[]{:S(2)}) collective-permute-start(bf16[6,4,64,256]{3,2,1,0:T(8,128)(2,1)} %get-tuple-element.32), channel_id=1, source_target_pairs={{0,6},{2,0},{4,2},{6,4},{1,7},{3,1},{5,3},{7,5},{8,14},{10,8},{12,... | collective-permute-start | bytes 2359304 | tf_op jit(solution)/shard_map/ppermute | solution.py:23
  211.3 10.8 %collective-permute-done.20 = bf16[6,4,64,256]{3,2,1,0:T(8,128)(2,1)} collective-permute-done((bf16[6,4,64,256]{3,2,1,0:T(8,128)(2,1)}, bf16[6,4,64,256]{3,2,1,0:T(8,128)(2,1)}, u32[]{:S(2)}, u32[]{:S(2)}) %collective-permute-start.20) | collective-permute-done | bytes 786464 | tf_op jit(solution)/shard_map/ppermute | solution.py:23
  223.1 5.0 %collective-permute-start.21 = (bf16[6,4,64,128]{3,2,1,0:T(8,128)(2,1)S(1)}, bf16[6,4,64,128]{3,2,1,0:T(8,128)(2,1)S(1)}, u32[]{:S(2)}, u32[]{:S(2)}) collective-permute-start(bf16[6,4,64,128]{3,2,1,0:T(8,128)(2,1)S(1)} %slice.109), channel_id=1, source_target_pairs={{0,6},{2,0},{4,2},{6,4},{1,7},{3,1},{5,3},{7,5},{8,14},{10,8},{12,... | collective-permute-start | bytes 1179656 | tf_op jit(solution)/shard_map/ppermute | solution.py:23
  236.1 6.2 %collective-permute-done.23 = bf16[6,4,64,128]{3,2,1,0:T(8,128)(2,1)S(1)} collective-permute-done((bf16[6,4,64,128]{3,2,1,0:T(8,128)(2,1)S(1)}, bf16[6,4,64,128]{3,2,1,0:T(8,128)(2,1)S(1)}, u32[]{:S(2)}, u32[]{:S(2)}) %collective-permute-start.23) | collective-permute-done | bytes 393248 | tf_op jit(solution)/shard_map/ppermute | solution.py:23
  246.0 4.3 %collective-permute-start.24 = (bf16[4,4,64,128]{3,2,1,0:T(8,128)(2,1)S(1)}, bf16[4,4,64,128]{3,2,1,0:T(8,128)(2,1)S(1)}, u32[]{:S(2)}, u32[]{:S(2)}) collective-permute-start(bf16[4,4,64,128]{3,2,1,0:T(8,128)(2,1)S(1)} %get-tuple-element.36), channel_id=1, source_target_pairs={{0,1},{1,0},{2,3},{3,2},{4,5},{5,4},{6,7},{7,6},{8,9},{9,8},{10,11... | collective-permute-start | bytes 786440 | tf_op jit(solution)/shard_map/ppermute | solution.py:134
  250.3 28.7 %collective-permute-done.24 = bf16[4,4,64,128]{3,2,1,0:T(8,128)(2,1)S(1)} collective-permute-done((bf16[4,4,64,128]{3,2,1,0:T(8,128)(2,1)S(1)}, bf16[4,4,64,128]{3,2,1,0:T(8,128)(2,1)S(1)}, u32[]{:S(2)}, u32[]{:S(2)}) %collective-permute-start.24) | collective-permute-done | bytes 262176 | tf_op jit(solution)/shard_map/ppermute | solution.py:134
  (111 shorter events, 85.0 us)
Async XLA Ops:
  1.5 34.5 %collective-permute-start.4 = (bf16[12,16,128]{2,1,0:T(8,128)(2,1)S(1)}, bf16[12,16,128]{2,1,0:T(8,128)(2,1)S(1)}, u32[]{:S(2)}, u32[]{:S(2)}) collective-permute-start(bf16[12,16,128]{2,1,0:T(8,128)(2,1)S(1)} %constant_dynamic-update-slice_fusion), channel_id=1, source_target_pairs={{0,1},{1,0},{2,3},{3,2},{4,5},{5,4},{6,7},{7,6},{8,9},{9,8},{10,11... | collective-permute-start | bytes 147464 | tf_op jit(solution)/shard_map/ppermute | solution.py:67
  16.1 40.6 %collective-permute-start.2 = (bf16[4,5,64,128]{3,2,1,0:T(8,128)(2,1)S(1)}, bf16[4,5,64,128]{3,2,1,0:T(8,128)(2,1)S(1)}, u32[]{:S(2)}, u32[]{:S(2)}) collective-permute-start(bf16[4,5,64,128]{3,2,1,0:T(8,128)(2,1)S(1)} %constant_dynamic-slice_fusion.4), channel_id=1, source_target_pairs={{0,1},{1,0},{2,3},{3,2},{4,5},{5,4},{6,7},{7,6},{8,9},{9,8},{10,11... | collective-permute-start | bytes 983048 | tf_op jit(solution)/shard_map/ppermute | solution.py:62
  19.0 37.7 %collective-permute-start.3 = (bf16[4,1,64,128]{3,2,1,0:T(8,128)(2,1)S(1)}, bf16[4,1,64,128]{3,2,1,0:T(8,128)(2,1)S(1)}, u32[]{:S(2)}, u32[]{:S(2)}) collective-permute-start(bf16[4,1,64,128]{3,2,1,0:T(8,128)(2,1)S(1)} %get-tuple-element.40), channel_id=1, source_target_pairs={{1,8},{9,16},{17,24},{25,32},{33,40},{41,48},{49,56},{8,1},{16,9},... | collective-permute-start | bytes 196616 | tf_op jit(solution)/shard_map/ppermute | solution.py:66
  30.6 12.8 %collective-permute-start.1 = (bf16[4,1,64,128]{3,2,1,0:T(8,128)(2,1)S(1)}, bf16[4,1,64,128]{3,2,1,0:T(8,128)(2,1)S(1)}, u32[]{:S(2)}, u32[]{:S(2)}) collective-permute-start(bf16[4,1,64,128]{3,2,1,0:T(8,128)(2,1)S(1)} %get-tuple-element.41), channel_id=1, source_target_pairs={{8,0},{16,8},{24,16},{32,24},{40,32},{48,40},{56,48},{9,1},{17,9},... | collective-permute-start | bytes 196616 | tf_op jit(solution)/shard_map/ppermute | solution.py:18
  33.3 21.3 %collective-permute-start = (bf16[4,1,64,128]{3,2,1,0:T(8,128)(2,1)S(1)}, bf16[4,1,64,128]{3,2,1,0:T(8,128)(2,1)S(1)}, u32[]{:S(2)}, u32[]{:S(2)}) collective-permute-start(bf16[4,1,64,128]{3,2,1,0:T(8,128)(2,1)S(1)} %get-tuple-element.42), channel_id=1, source_target_pairs={{0,8},{8,16},{16,24},{24,32},{32,40},{40,48},{48,56},{1,9},{9,17},... | collective-permute-start | bytes 196616 | tf_op jit(solution)/shard_map/ppermute | solution.py:15
  56.7 15.9 %collective-permute-start.7 = (bf16[12,16,256]{2,1,0:T(8,128)(2,1)S(1)}, bf16[12,16,256]{2,1,0:T(8,128)(2,1)S(1)}, u32[]{:S(2)}, u32[]{:S(2)}) collective-permute-start(bf16[12,16,256]{2,1,0:T(8,128)(2,1)S(1)} %maximum_select_fusion.8), channel_id=1, source_target_pairs={{0,32},{8,40},{16,48},{24,56},{32,0},{40,8},{48,16},{56,24},{1,33}... | collective-permute-start | bytes 294920 | tf_op jit(solution)/shard_map/ppermute | solution.py:44
  66.3 37.0 %collective-permute-start.6 = (bf16[4,6,64,256]{3,2,1,0:T(8,128)(2,1)S(1)}, bf16[4,6,64,256]{3,2,1,0:T(8,128)(2,1)S(1)}, u32[]{:S(2)}, u32[]{:S(2)}) collective-permute-start(bf16[4,6,64,256]{3,2,1,0:T(8,128)(2,1)S(1)} %get-tuple-element.28), channel_id=1, source_target_pairs={{0,6},{2,0},{4,2},{6,4},{1,7},{3,1},{5,3},{7,5},{8,14},{10,8},{12,... | collective-permute-start | bytes 2359304 | tf_op jit(solution)/shard_map/ppermute | solution.py:23
  70.7 32.7 %collective-permute-start.5 = (bf16[4,6,64,256]{3,2,1,0:T(8,128)(2,1)S(1)}, bf16[4,6,64,256]{3,2,1,0:T(8,128)(2,1)S(1)}, u32[]{:S(2)}, u32[]{:S(2)}) collective-permute-start(bf16[4,6,64,256]{3,2,1,0:T(8,128)(2,1)S(1)} %get-tuple-element.28), channel_id=1, source_target_pairs={{0,2},{2,4},{4,6},{6,0},{1,3},{3,5},{5,7},{7,1},{8,10},{10,12},{12... | collective-permute-start | bytes 2359304 | tf_op jit(solution)/shard_map/ppermute | solution.py:23
  72.7 7.3 %collective-permute-start.8 = (bf16[12,2,16,256]{3,2,1,0:T(8,128)(2,1)S(1)}, bf16[12,2,16,256]{3,2,1,0:T(8,128)(2,1)S(1)}, u32[]{:S(2)}, u32[]{:S(2)}) collective-permute-start(bf16[12,2,16,256]{3,2,1,0:T(8,128)(2,1)S(1)} %maximum_select_fusion.7), channel_id=1, source_target_pairs={{0,16},{8,24},{16,0},{24,8},{32,48},{40,56},{48,32},{56,40},{1,17}... | collective-permute-start | bytes 589832 | tf_op jit(solution)/shard_map/ppermute | solution.py:44
  80.0 23.2 %collective-permute-start.9 = (bf16[12,2,2,16,256]{4,3,1,0,2:T(8,128)(2,1)S(1)}, bf16[12,2,2,16,256]{4,3,1,0,2:T(8,128)(2,1)S(1)}, u32[]{:S(2)}, u32[]{:S(2)}) collective-permute-start(bf16[12,2,2,16,256]{4,3,1,0,2:T(8,128)(2,1)S(1)} %maximum_select_fusion.5), channel_id=1, source_target_pairs={{0,8},{8,0},{16,24},{24,16},{32,40},{40,32},{48,56},{56,48},{1,9},... | collective-permute-start | bytes 1179656 | tf_op jit(solution)/shard_map/ppermute | solution.py:44
  103.4 21.1 %collective-permute-start.13 = (bf16[12,128,256]{2,1,0:T(8,128)(2,1)S(1)}, bf16[12,128,256]{2,1,0:T(8,128)(2,1)}, u32[]{:S(2)}, u32[]{:S(2)}) collective-permute-start(bf16[12,128,256]{2,1,0:T(8,128)(2,1)S(1)} %bitcast.88), channel_id=1, source_target_pairs={{0,384},{128,0},{256,128},{384,256},{1,385},{129,1},{257,129},{385... | collective-permute-start | bytes 2359304 | tf_op jit(solution)/shard_map/ppermute | solution.py:23
  105.5 19.8 %collective-permute-start.12 = (bf16[12,128,256]{2,1,0:T(8,128)(2,1)S(1)}, bf16[12,128,256]{2,1,0:T(8,128)(2,1)S(1)}, u32[]{:S(2)}, u32[]{:S(2)}) collective-permute-start(bf16[12,128,256]{2,1,0:T(8,128)(2,1)S(1)} %bitcast.89), channel_id=1, source_target_pairs={{0,128},{128,256},{256,384},{384,0},{1,129},{129,257},{257,385},{3... | collective-permute-start | bytes 2359304 | tf_op jit(solution)/shard_map/ppermute | solution.py:23
  110.3 12.4 %collective-permute-start.11 = (bf16[4,6,64,128]{3,2,1,0:T(8,128)(2,1)}, bf16[4,6,64,128]{3,2,1,0:T(8,128)(2,1)S(1)}, u32[]{:S(2)}, u32[]{:S(2)}) collective-permute-start(bf16[4,6,64,128]{3,2,1,0:T(8,128)(2,1)} %slice.79), channel_id=1, source_target_pairs={{0,2},{2,4},{4,6},{6,0},{1,3},{3,5},{5,7},{7,1},{8,10},{10,12},{12... | collective-permute-start | bytes 1179656 | tf_op jit(solution)/shard_map/ppermute | solution.py:23
  113.5 11.0 %collective-permute-start.10 = (bf16[4,6,64,128]{3,2,1,0:T(8,128)(2,1)}, bf16[4,6,64,128]{3,2,1,0:T(8,128)(2,1)}, u32[]{:S(2)}, u32[]{:S(2)}) collective-permute-start(bf16[4,6,64,128]{3,2,1,0:T(8,128)(2,1)} %slice.78), channel_id=1, source_target_pairs={{0,6},{2,0},{4,2},{6,4},{1,7},{3,1},{5,3},{7,5},{8,14},{10,8},{12,... | collective-permute-start | bytes 1179656 | tf_op jit(solution)/shard_map/ppermute | solution.py:23
  126.6 11.0 %collective-permute-start.15 = (bf16[12,64,256]{2,1,0:T(8,128)(2,1)S(1)}, bf16[12,64,256]{2,1,0:T(8,128)(2,1)S(1)}, u32[]{:S(2)}, u32[]{:S(2)}) collective-permute-start(bf16[12,64,256]{2,1,0:T(8,128)(2,1)S(1)} %slice.81), channel_id=1, source_target_pairs={{0,128},{128,256},{256,384},{384,0},{1,129},{129,257},{257,385},{3... | collective-permute-start | bytes 1179656 | tf_op jit(solution)/shard_map/ppermute | solution.py:23
  130.0 12.0 %collective-permute-start.14 = (bf16[12,64,256]{2,1,0:T(8,128)(2,1)S(1)}, bf16[12,64,256]{2,1,0:T(8,128)(2,1)S(1)}, u32[]{:S(2)}, u32[]{:S(2)}) collective-permute-start(bf16[12,64,256]{2,1,0:T(8,128)(2,1)S(1)} %slice.80), channel_id=1, source_target_pairs={{0,384},{128,0},{256,128},{384,256},{1,385},{129,1},{257,129},{385... | collective-permute-start | bytes 1179656 | tf_op jit(solution)/shard_map/ppermute | solution.py:23
  142.2 32.2 %collective-permute-start.16 = (bf16[12,4,128,256]{3,2,1,0:T(8,128)(2,1)S(1)}, bf16[12,4,128,256]{3,2,1,0:T(8,128)(2,1)}, u32[]{:S(2)}, u32[]{:S(2)}) collective-permute-start(bf16[12,4,128,256]{3,2,1,0:T(8,128)(2,1)S(1)} %bitcast_dynamic-update-slice_fusion), channel_id=1, source_target_pairs={{0,64},{64,0},{1,65},{65,1},{2,66},{66,2},{3,67},{67,3},{4,68},{68... | collective-permute-start | bytes 9437192 | tf_op jit(solution)/shard_map/ppermute | solution.py:44
  147.2 13.0 %collective-permute-start.17 = (f32[2,128]{1,0:T(2,128)S(1)}, f32[2,128]{1,0:T(2,128)S(1)}, u32[]{:S(2)}, u32[]{:S(2)}) collective-permute-start(f32[2,128]{1,0:T(2,128)S(1)} %pad_maximum_fusion.4), channel_id=1, source_target_pairs={{0,1},{1,0},{2,3},{3,2},{4,5},{5,4},{6,7},{7,6},{8,9},{9,8},{10,11... | collective-permute-start | bytes 3080 | tf_op jit(solution)/shard_map/ppermute | solution.py:59
  189.4 7.6 %collective-permute-start.18 = (bf16[1,4,64,256]{3,2,1,0:T(8,128)(2,1)S(1)}, bf16[1,4,64,256]{3,2,1,0:T(8,128)(2,1)S(1)}, u32[]{:S(2)}, u32[]{:S(2)}) collective-permute-start(bf16[1,4,64,256]{3,2,1,0:T(8,128)(2,1)S(1)} %get-tuple-element.38), channel_id=1, source_target_pairs={{0,64},{64,128},{128,192},{192,256},{256,320},{320,384},{384,448},... | collective-permute-start | bytes 393224 | tf_op jit(solution)/shard_map/ppermute | solution.py:15
  202.3 19.8 %collective-permute-start.20 = (bf16[6,4,64,256]{3,2,1,0:T(8,128)(2,1)}, bf16[6,4,64,256]{3,2,1,0:T(8,128)(2,1)}, u32[]{:S(2)}, u32[]{:S(2)}) collective-permute-start(bf16[6,4,64,256]{3,2,1,0:T(8,128)(2,1)} %get-tuple-element.32), channel_id=1, source_target_pairs={{0,6},{2,0},{4,2},{6,4},{1,7},{3,1},{5,3},{7,5},{8,14},{10,8},{12,... | collective-permute-start | bytes 2359304 | tf_op jit(solution)/shard_map/ppermute | solution.py:23
  206.7 21.5 %collective-permute-start.22 = (bf16[6,4,64,256]{3,2,1,0:T(8,128)(2,1)}, bf16[6,4,64,256]{3,2,1,0:T(8,128)(2,1)}, u32[]{:S(2)}, u32[]{:S(2)}) collective-permute-start(bf16[6,4,64,256]{3,2,1,0:T(8,128)(2,1)} %get-tuple-element.32), channel_id=1, source_target_pairs={{0,2},{2,4},{4,6},{6,0},{1,3},{3,5},{5,7},{7,1},{8,10},{10,12},{12... | collective-permute-start | bytes 2359304 | tf_op jit(solution)/shard_map/ppermute | solution.py:23
  223.1 12.8 %collective-permute-start.21 = (bf16[6,4,64,128]{3,2,1,0:T(8,128)(2,1)S(1)}, bf16[6,4,64,128]{3,2,1,0:T(8,128)(2,1)S(1)}, u32[]{:S(2)}, u32[]{:S(2)}) collective-permute-start(bf16[6,4,64,128]{3,2,1,0:T(8,128)(2,1)S(1)} %slice.109), channel_id=1, source_target_pairs={{0,6},{2,0},{4,2},{6,4},{1,7},{3,1},{5,3},{7,5},{8,14},{10,8},{12,... | collective-permute-start | bytes 1179656 | tf_op jit(solution)/shard_map/ppermute | solution.py:23
  229.2 13.1 %collective-permute-start.23 = (bf16[6,4,64,128]{3,2,1,0:T(8,128)(2,1)S(1)}, bf16[6,4,64,128]{3,2,1,0:T(8,128)(2,1)S(1)}, u32[]{:S(2)}, u32[]{:S(2)}) collective-permute-start(bf16[6,4,64,128]{3,2,1,0:T(8,128)(2,1)S(1)} %slice.110), channel_id=1, source_target_pairs={{0,2},{2,4},{4,6},{6,0},{1,3},{3,5},{5,7},{7,1},{8,10},{10,12},{12... | collective-permute-start | bytes 1179656 | tf_op jit(solution)/shard_map/ppermute | solution.py:23
  246.0 33.0 %collective-permute-start.24 = (bf16[4,4,64,128]{3,2,1,0:T(8,128)(2,1)S(1)}, bf16[4,4,64,128]{3,2,1,0:T(8,128)(2,1)S(1)}, u32[]{:S(2)}, u32[]{:S(2)}) collective-permute-start(bf16[4,4,64,128]{3,2,1,0:T(8,128)(2,1)S(1)} %get-tuple-element.36), channel_id=1, source_target_pairs={{0,1},{1,0},{2,3},{3,2},{4,5},{5,4},{6,7},{7,6},{8,9},{9,8},{10,11... | collective-permute-start | bytes 786440 | tf_op jit(solution)/shard_map/ppermute | solution.py:134
  (13 other events, 167.6 us)

commit v9 on v8

--- a/solution.py
+++ b/solution.py
@@ -70,9 +70,17 @@
     pair = ordered_pair(mine, ordered_pair(rim, partner, high, 1), high, 3)
     from_left = ring_shift(pair, "cx", ring, 1)
     from_right = ring_shift(pair, "cx", ring, -1)
-    for pos, bit in enumerate((4, 2, 1)):
-        w_block = xor_stack(w_block, "row", bit, 1 + pos)
-    w_block = w_block.reshape(taps, row_n * depth, -1)
+    w_block = xor_stack(w_block, "row", row_n // 2, 1)
+    low_n = row_n // 2
+    low = lax.axis_index("row") % low_n
+    w_group = jnp.zeros((taps, 2, low_n) + w_block.shape[2:], w_block.dtype)
+    for flip in range(low_n):
+        if flip == 0:
+            piece = w_block
+        else:
+            piece = lax.ppermute(w_block, "row", [(i, i ^ flip) for i in range(row_n)])
+        w_group = lax.dynamic_update_slice(w_group, piece[:, :, None], (0, 0, low ^ flip, 0, 0))
+    w_block = w_group.reshape(taps, row_n * depth, -1)
     from_left, from_right, w_block = lax.optimization_barrier((from_left, from_right, w_block))
     fy_n = lax.axis_size("fy")
     w_left = ring_shift(w_block, "fy", fy_n, 1)

time: 281 us -> 286 us (1.018)
  the two profiles are of different devices: /device:TPU:81 before, /device:TPU:49 now
where the time goes in v9:
time: 286 us; the launch traced here: 285 us
  waiting for transfers between devices  124 us (43%)
  starting transfers between devices  109 us (38%)
  local copies, waits for them, and re-layouts  30.3 us (11%)
  other arithmetic  10.8 us (4%)
  matrix products  9.47 us (3%)
    ppermute x12, waiting for transfers between devices, ring_shift(): lax.ppermute(block, axis, [(i, (i + step) % count) for i in range(count)])  36.6 us
    ppermute x12, starting transfers between devices, ring_shift(): lax.ppermute(block, axis, [(i, (i + step) % count) for i in range(count)])  35.5 us
    ppermute x1, waiting for transfers between devices, body(): returned = lax.ppermute(given, 'cz', SWAP)  25.7 us
    ppermute x2, waiting for transfers between devices, shift_halo(): lax.ppermute(lax.slice_in_dim(block, 0, width, axis=dim), axis, backward)  18.5 us
    ppermute x1, starting transfers between devices, body(): w_block = ordered_pair(weight, lax.ppermute(weight, 'cz', SWAP), high, 2)  14.5 us
    unnamed x39, local copies, waits for them, and re-layouts  14.5 us
    ppermute x1, waiting for transfers between devices, body(): rim = lax.ppermute(edge, ('row', 'cz'), diagonal)  12 us
    ppermute x1, starting transfers between devices, body(): rim = lax.ppermute(edge, ('row', 'cz'), diagonal)  11.6 us
  transfers between devices with their start and end apart: 26, of which 18 were waited for; matrix products, arithmetic and copies ran while one was open for 10% of the time, Pallas kernels for 0%

profile of v9, /device:TPU:49, one launch (start us, length us, event | category | flops | bytes accessed | tf_op | source)
XLA Modules:
  0.0 284.6 jit_solution(11760847106539085116)
XLA Ops:
  1.5 14.5 %collective-permute-start.4 = (bf16[12,16,128]{2,1,0:T(8,128)(2,1)S(1)}, bf16[12,16,128]{2,1,0:T(8,128)(2,1)S(1)}, u32[]{:S(2)}, u32[]{:S(2)}) collective-permute-start(bf16[12,16,128]{2,1,0:T(8,128)(2,1)S(1)} %constant_dynamic-update-slice_fusion), channel_id=1, source_target_pairs={{0,1},{1,0},{2,3},{3,2},{4,5},{5,4},{6,7},{7,6},{8,9},{9,8},{10,11... | collective-permute-start | bytes 147464 | tf_op jit(solution)/shard_map/ppermute | solution.py:67
  19.9 11.6 %collective-permute-start.3 = (bf16[4,1,64,128]{3,2,1,0:T(8,128)(2,1)S(1)}, bf16[4,1,64,128]{3,2,1,0:T(8,128)(2,1)S(1)}, u32[]{:S(2)}, u32[]{:S(2)}) collective-permute-start(bf16[4,1,64,128]{3,2,1,0:T(8,128)(2,1)S(1)} %get-tuple-element.40), channel_id=1, source_target_pairs={{1,8},{9,16},{17,24},{25,32},{33,40},{41,48},{49,56},{8,1},{16,9},... | collective-permute-start | bytes 196616 | tf_op jit(solution)/shard_map/ppermute | solution.py:66
  36.9 14.2 %collective-permute-done.1 = bf16[4,1,64,128]{3,2,1,0:T(8,128)(2,1)S(1)} collective-permute-done((bf16[4,1,64,128]{3,2,1,0:T(8,128)(2,1)S(1)}, bf16[4,1,64,128]{3,2,1,0:T(8,128)(2,1)S(1)}, u32[]{:S(2)}, u32[]{:S(2)}) %collective-permute-start.1) | collective-permute-done | bytes 65568 | tf_op jit(solution)/shard_map/ppermute | solution.py:18
  56.2 12.0 %collective-permute-done.3 = bf16[4,1,64,128]{3,2,1,0:T(8,128)(2,1)S(1)} collective-permute-done((bf16[4,1,64,128]{3,2,1,0:T(8,128)(2,1)S(1)}, bf16[4,1,64,128]{3,2,1,0:T(8,128)(2,1)S(1)}, u32[]{:S(2)}, u32[]{:S(2)}) %collective-permute-start.3) | collective-permute-done | bytes 65568 | tf_op jit(solution)/shard_map/ppermute | solution.py:66
  70.2 10.3 %collective-permute-done.7 = bf16[12,16,256]{2,1,0:T(8,128)(2,1)S(1)} collective-permute-done((bf16[12,16,256]{2,1,0:T(8,128)(2,1)S(1)}, bf16[12,16,256]{2,1,0:T(8,128)(2,1)S(1)}, u32[]{:S(2)}, u32[]{:S(2)}) %collective-permute-start.7) | collective-permute-done | bytes 98336 | tf_op jit(solution)/shard_map/ppermute | solution.py:44
  83.7 4.4 %collective-permute-start.6 = (bf16[4,6,64,256]{3,2,1,0:T(8,128)(2,1)S(1)}, bf16[4,6,64,256]{3,2,1,0:T(8,128)(2,1)S(1)}, u32[]{:S(2)}, u32[]{:S(2)}) collective-permute-start(bf16[4,6,64,256]{3,2,1,0:T(8,128)(2,1)S(1)} %get-tuple-element.28), channel_id=1, source_target_pairs={{0,6},{2,0},{4,2},{6,4},{1,7},{3,1},{5,3},{7,5},{8,14},{10,8},{12,... | collective-permute-start | bytes 2359304 | tf_op jit(solution)/shard_map/ppermute | solution.py:23
  92.0 5.4 %collective-permute-start.9 = (bf16[12,2,16,256]{3,2,0,1:T(8,128)(2,1)S(1)}, bf16[12,2,16,256]{3,2,0,1:T(8,128)(2,1)S(1)}, u32[]{:S(2)}, u32[]{:S(2)}) collective-permute-start(bf16[12,2,16,256]{3,2,0,1:T(8,128)(2,1)S(1)} %maximum_select_fusion.5), channel_id=1, source_target_pairs={{0,16},{8,24},{16,0},{24,8},{32,48},{40,56},{48,32},{56,40},{1,17}... | collective-permute-start | bytes 589832 | tf_op jit(solution)/shard_map/ppermute | solution.py:81
  97.6 10.7 %collective-permute-done.9 = bf16[12,2,16,256]{3,2,0,1:T(8,128)(2,1)S(1)} collective-permute-done((bf16[12,2,16,256]{3,2,0,1:T(8,128)(2,1)S(1)}, bf16[12,2,16,256]{3,2,0,1:T(8,128)(2,1)S(1)}, u32[]{:S(2)}, u32[]{:S(2)}) %collective-permute-start.9) | collective-permute-done | bytes 196640 | tf_op jit(solution)/shard_map/ppermute | solution.py:81
  117.5 4.6 %collective-permute-start.11 = (bf16[4,6,64,128]{3,2,1,0:T(8,128)(2,1)S(1)}, bf16[4,6,64,128]{3,2,1,0:T(8,128)(2,1)S(1)}, u32[]{:S(2)}, u32[]{:S(2)}) collective-permute-start(bf16[4,6,64,128]{3,2,1,0:T(8,128)(2,1)S(1)} %slice.78), channel_id=1, source_target_pairs={{0,6},{2,0},{4,2},{6,4},{1,7},{3,1},{5,3},{7,5},{8,14},{10,8},{12,... | collective-permute-start | bytes 1179656 | tf_op jit(solution)/shard_map/ppermute | solution.py:23
  122.1 5.0 %collective-permute-done.12 = bf16[4,6,64,128]{3,2,1,0:T(8,128)(2,1)S(1)} collective-permute-done((bf16[4,6,64,128]{3,2,1,0:T(8,128)(2,1)}, bf16[4,6,64,128]{3,2,1,0:T(8,128)(2,1)S(1)}, u32[]{:S(2)}, u32[]{:S(2)}) %collective-permute-start.12) | collective-permute-done | bytes 393248 | tf_op jit(solution)/shard_map/ppermute | solution.py:23
  140.5 4.7 %collective-permute-done.15 = bf16[12,64,256]{2,1,0:T(8,128)(2,1)S(1)} collective-permute-done((bf16[12,64,256]{2,1,0:T(8,128)(2,1)S(1)}, bf16[12,64,256]{2,1,0:T(8,128)(2,1)S(1)}, u32[]{:S(2)}, u32[]{:S(2)}) %collective-permute-start.15) | collective-permute-done | bytes 393248 | tf_op jit(solution)/shard_map/ppermute | solution.py:23
  145.3 5.8 %collective-permute-start.17 = (bf16[12,4,128,256]{3,2,1,0:T(8,128)(2,1)S(1)}, bf16[12,4,128,256]{3,2,1,0:T(8,128)(2,1)}, u32[]{:S(2)}, u32[]{:S(2)}) collective-permute-start(bf16[12,4,128,256]{3,2,1,0:T(8,128)(2,1)S(1)} %bitcast_dynamic-update-slice_fusion.2), channel_id=1, source_target_pairs={{0,64},{64,0},{1,65},{65,1},{2,66},{66,2},{3,67},{67,3},{4,68},{68... | collective-permute-start | bytes 9437192 | tf_op jit(solution)/shard_map/ppermute | solution.py:44
  151.2 6.6 %collective-permute-start.18 = (f32[2,128]{1,0:T(2,128)S(1)}, f32[2,128]{1,0:T(2,128)S(1)}, u32[]{:S(2)}, u32[]{:S(2)}) collective-permute-start(f32[2,128]{1,0:T(2,128)S(1)} %pad_maximum_fusion.2), channel_id=1, source_target_pairs={{0,1},{1,0},{2,3},{3,2},{4,5},{5,4},{6,7},{7,6},{8,9},{9,8},{10,11... | collective-permute-start | bytes 3080 | tf_op jit(solution)/shard_map/ppermute | solution.py:59
  157.9 6.3 %collective-permute-done.18 = f32[2,128]{1,0:T(2,128)S(1)} collective-permute-done((f32[2,128]{1,0:T(2,128)S(1)}, f32[2,128]{1,0:T(2,128)S(1)}, u32[]{:S(2)}, u32[]{:S(2)}) %collective-permute-start.18) | collective-permute-done | bytes 1056 | tf_op jit(solution)/shard_map/ppermute | solution.py:59
  170.1 4.3 %copy.32 = bf16[6,4,64,1024]{3,1,2,0:T(4,128)(2,1)S(1)} copy(bf16[6,4,64,1024]{3,2,0,1:T(8,128)(2,1)} %bitcast.86) | data formatting | bytes 6291456
  178.4 4.2 %maximum_select_fusion = bf16[12,4,2,128,256]{4,3,2,1,0:T(8,128)(2,1)S(1)} fusion(bf16[12,4,1,128,256]{4,3,2,1,0:T(8,128)(2,1)S(1)} %bitcast.85, bf16[12,4,1,128,256]{4,3,2,1,0:T(8,128)(2,1)} %bitcast.19, pred[]{:T(512)S(6)} %eq.25), kind=kLoop, calls=%fused_computation.2 | loop fusion | flops 9437184 | bytes 12582913 | tf_op jit(solution)/shard_map/jit(_where)/select_n | solution.py:46
  185.3 7.3 %convert_add_fusion = (f32[4,32,9,256]{3,1,2,0:T(8,128)}, bf16[4,32,9,256]{3,1,2,0:T(8,128)(2,1)S(1)}) fusion(f32[256]{0:T(256)S(1)} %bitcast.106, f32[256]{0:T(256)S(1)} %bitcast.107, bf16[3,3,1024,256]{3,2,1,0:T(8,128)(2,1)S(1)} %bitcast.87, bf16[6,4,8,11,1024]{4,1,3,2,0:T(4,128)(2,1)S(1)} %fusion.1, pred[32,9]{0,1:T(8,128)(4,1)S(1)} %copy-done.14), kind=kOutput, calls=%fused_computation.9 | convolution fusion | flops 5438767104 | bytes 10815776 | tf_op jit(solution)/shard_map/conv_general_dilated | solution.py:106
  193.4 5.6 %collective-permute-start.19 = (bf16[1,4,64,256]{3,2,1,0:T(8,128)(2,1)S(1)}, bf16[1,4,64,256]{3,2,1,0:T(8,128)(2,1)S(1)}, u32[]{:S(2)}, u32[]{:S(2)}) collective-permute-start(bf16[1,4,64,256]{3,2,1,0:T(8,128)(2,1)S(1)} %get-tuple-element.38), channel_id=1, source_target_pairs={{0,64},{64,128},{128,192},{192,256},{256,320},{320,384},{384,448},... | collective-permute-start | bytes 393224 | tf_op jit(solution)/shard_map/ppermute | solution.py:15
  200.9 4.3 %collective-permute-done.20 = bf16[1,4,64,256]{3,2,1,0:T(8,128)(2,1)S(1)} collective-permute-done((bf16[1,4,64,256]{3,2,1,0:T(8,128)(2,1)S(1)}, bf16[1,4,64,256]{3,2,1,0:T(8,128)(2,1)S(1)}, u32[]{:S(2)}, u32[]{:S(2)}) %collective-permute-start.20) | collective-permute-done | bytes 131104 | tf_op jit(solution)/shard_map/ppermute | solution.py:18
  214.4 11.5 %collective-permute-done.21 = bf16[6,4,64,256]{3,2,1,0:T(8,128)(2,1)} collective-permute-done((bf16[6,4,64,256]{3,2,1,0:T(8,128)(2,1)}, bf16[6,4,64,256]{3,2,1,0:T(8,128)(2,1)}, u32[]{:S(2)}, u32[]{:S(2)}) %collective-permute-start.21) | collective-permute-done | bytes 786464 | tf_op jit(solution)/shard_map/ppermute | solution.py:23
  226.9 4.4 %collective-permute-start.22 = (bf16[6,4,64,128]{3,2,1,0:T(8,128)(2,1)S(1)}, bf16[6,4,64,128]{3,2,1,0:T(8,128)(2,1)S(1)}, u32[]{:S(2)}, u32[]{:S(2)}) collective-permute-start(bf16[6,4,64,128]{3,2,1,0:T(8,128)(2,1)S(1)} %slice.109), channel_id=1, source_target_pairs={{0,6},{2,0},{4,2},{6,4},{1,7},{3,1},{5,3},{7,5},{8,14},{10,8},{12,... | collective-permute-start | bytes 1179656 | tf_op jit(solution)/shard_map/ppermute | solution.py:23
  239.2 6.2 %collective-permute-done.24 = bf16[6,4,64,128]{3,2,1,0:T(8,128)(2,1)S(1)} collective-permute-done((bf16[6,4,64,128]{3,2,1,0:T(8,128)(2,1)S(1)}, bf16[6,4,64,128]{3,2,1,0:T(8,128)(2,1)S(1)}, u32[]{:S(2)}, u32[]{:S(2)}) %collective-permute-start.24) | collective-permute-done | bytes 393248 | tf_op jit(solution)/shard_map/ppermute | solution.py:23
  249.1 9.1 %collective-permute-start.25 = (bf16[4,4,64,128]{3,2,1,0:T(8,128)(2,1)S(1)}, bf16[4,4,64,128]{3,2,1,0:T(8,128)(2,1)S(1)}, u32[]{:S(2)}, u32[]{:S(2)}) collective-permute-start(bf16[4,4,64,128]{3,2,1,0:T(8,128)(2,1)S(1)} %get-tuple-element.36), channel_id=1, source_target_pairs={{0,1},{1,0},{2,3},{3,2},{4,5},{5,4},{6,7},{7,6},{8,9},{9,8},{10,11... | collective-permute-start | bytes 786440 | tf_op jit(solution)/shard_map/ppermute | solution.py:142
  258.1 25.7 %collective-permute-done.25 = bf16[4,4,64,128]{3,2,1,0:T(8,128)(2,1)S(1)} collective-permute-done((bf16[4,4,64,128]{3,2,1,0:T(8,128)(2,1)S(1)}, bf16[4,4,64,128]{3,2,1,0:T(8,128)(2,1)S(1)}, u32[]{:S(2)}, u32[]{:S(2)}) %collective-permute-start.25) | collective-permute-done | bytes 262176 | tf_op jit(solution)/shard_map/ppermute | solution.py:142
  (118 shorter events, 85.0 us)
Async XLA Ops:
  1.5 35.4 %collective-permute-start.4 = (bf16[12,16,128]{2,1,0:T(8,128)(2,1)S(1)}, bf16[12,16,128]{2,1,0:T(8,128)(2,1)S(1)}, u32[]{:S(2)}, u32[]{:S(2)}) collective-permute-start(bf16[12,16,128]{2,1,0:T(8,128)(2,1)S(1)} %constant_dynamic-update-slice_fusion), channel_id=1, source_target_pairs={{0,1},{1,0},{2,3},{3,2},{4,5},{5,4},{6,7},{7,6},{8,9},{9,8},{10,11... | collective-permute-start | bytes 147464 | tf_op jit(solution)/shard_map/ppermute | solution.py:67
  17.0 51.2 %collective-permute-start.2 = (bf16[4,5,64,128]{3,2,1,0:T(8,128)(2,1)S(1)}, bf16[4,5,64,128]{3,2,1,0:T(8,128)(2,1)S(1)}, u32[]{:S(2)}, u32[]{:S(2)}) collective-permute-start(bf16[4,5,64,128]{3,2,1,0:T(8,128)(2,1)S(1)} %constant_dynamic-slice_fusion.4), channel_id=1, source_target_pairs={{0,1},{1,0},{2,3},{3,2},{4,5},{5,4},{6,7},{7,6},{8,9},{9,8},{10,11... | collective-permute-start | bytes 983048 | tf_op jit(solution)/shard_map/ppermute | solution.py:62
  19.9 48.3 %collective-permute-start.3 = (bf16[4,1,64,128]{3,2,1,0:T(8,128)(2,1)S(1)}, bf16[4,1,64,128]{3,2,1,0:T(8,128)(2,1)S(1)}, u32[]{:S(2)}, u32[]{:S(2)}) collective-permute-start(bf16[4,1,64,128]{3,2,1,0:T(8,128)(2,1)S(1)} %get-tuple-element.40), channel_id=1, source_target_pairs={{1,8},{9,16},{17,24},{25,32},{33,40},{41,48},{49,56},{8,1},{16,9},... | collective-permute-start | bytes 196616 | tf_op jit(solution)/shard_map/ppermute | solution.py:66
  31.5 19.6 %collective-permute-start.1 = (bf16[4,1,64,128]{3,2,1,0:T(8,128)(2,1)S(1)}, bf16[4,1,64,128]{3,2,1,0:T(8,128)(2,1)S(1)}, u32[]{:S(2)}, u32[]{:S(2)}) collective-permute-start(bf16[4,1,64,128]{3,2,1,0:T(8,128)(2,1)S(1)} %get-tuple-element.41), channel_id=1, source_target_pairs={{8,0},{16,8},{24,16},{32,24},{40,32},{48,40},{56,48},{9,1},{17,9},... | collective-permute-start | bytes 196616 | tf_op jit(solution)/shard_map/ppermute | solution.py:18
  33.5 21.6 %collective-permute-start = (bf16[4,1,64,128]{3,2,1,0:T(8,128)(2,1)S(1)}, bf16[4,1,64,128]{3,2,1,0:T(8,128)(2,1)S(1)}, u32[]{:S(2)}, u32[]{:S(2)}) collective-permute-start(bf16[4,1,64,128]{3,2,1,0:T(8,128)(2,1)S(1)} %get-tuple-element.42), channel_id=1, source_target_pairs={{0,8},{8,16},{16,24},{24,32},{32,40},{40,48},{48,56},{1,9},{9,17},... | collective-permute-start | bytes 196616 | tf_op jit(solution)/shard_map/ppermute | solution.py:15
  68.2 12.3 %collective-permute-start.7 = (bf16[12,16,256]{2,1,0:T(8,128)(2,1)S(1)}, bf16[12,16,256]{2,1,0:T(8,128)(2,1)S(1)}, u32[]{:S(2)}, u32[]{:S(2)}) collective-permute-start(bf16[12,16,256]{2,1,0:T(8,128)(2,1)S(1)} %maximum_select_fusion.6), channel_id=1, source_target_pairs={{0,32},{8,40},{16,48},{24,56},{32,0},{40,8},{48,16},{56,24},{1,33}... | collective-permute-start | bytes 294920 | tf_op jit(solution)/shard_map/ppermute | solution.py:44
  80.6 16.9 %collective-permute-start.8 = (bf16[12,2,16,256]{3,2,0,1:T(8,128)(2,1)S(1)}, bf16[12,2,16,256]{3,2,0,1:T(8,128)(2,1)S(1)}, u32[]{:S(2)}, u32[]{:S(2)}) collective-permute-start(bf16[12,2,16,256]{3,2,0,1:T(8,128)(2,1)S(1)} %maximum_select_fusion.5), channel_id=1, source_target_pairs={{0,8},{8,0},{16,24},{24,16},{32,40},{40,32},{48,56},{56,48},{1,9},... | collective-permute-start | bytes 589832 | tf_op jit(solution)/shard_map/ppermute | solution.py:81
  83.7 24.7 %collective-permute-start.6 = (bf16[4,6,64,256]{3,2,1,0:T(8,128)(2,1)S(1)}, bf16[4,6,64,256]{3,2,1,0:T(8,128)(2,1)S(1)}, u32[]{:S(2)}, u32[]{:S(2)}) collective-permute-start(bf16[4,6,64,256]{3,2,1,0:T(8,128)(2,1)S(1)} %get-tuple-element.28), channel_id=1, source_target_pairs={{0,6},{2,0},{4,2},{6,4},{1,7},{3,1},{5,3},{7,5},{8,14},{10,8},{12,... | collective-permute-start | bytes 2359304 | tf_op jit(solution)/shard_map/ppermute | solution.py:23
  88.1 21.3 %collective-permute-start.5 = (bf16[4,6,64,256]{3,2,1,0:T(8,128)(2,1)S(1)}, bf16[4,6,64,256]{3,2,1,0:T(8,128)(2,1)S(1)}, u32[]{:S(2)}, u32[]{:S(2)}) collective-permute-start(bf16[4,6,64,256]{3,2,1,0:T(8,128)(2,1)S(1)} %get-tuple-element.28), channel_id=1, source_target_pairs={{0,2},{2,4},{4,6},{6,0},{1,3},{3,5},{5,7},{7,1},{8,10},{10,12},{12... | collective-permute-start | bytes 2359304 | tf_op jit(solution)/shard_map/ppermute | solution.py:23
  90.0 18.3 %collective-permute-start.10 = (bf16[12,2,16,256]{3,2,0,1:T(8,128)(2,1)S(1)}, bf16[12,2,16,256]{3,2,0,1:T(8,128)(2,1)S(1)}, u32[]{:S(2)}, u32[]{:S(2)}) collective-permute-start(bf16[12,2,16,256]{3,2,0,1:T(8,128)(2,1)S(1)} %maximum_select_fusion.5), channel_id=1, source_target_pairs={{0,24},{8,16},{16,8},{24,0},{32,56},{40,48},{48,40},{56,32},{1,25}... | collective-permute-start | bytes 589832 | tf_op jit(solution)/shard_map/ppermute | solution.py:81
  92.0 16.3 %collective-permute-start.9 = (bf16[12,2,16,256]{3,2,0,1:T(8,128)(2,1)S(1)}, bf16[12,2,16,256]{3,2,0,1:T(8,128)(2,1)S(1)}, u32[]{:S(2)}, u32[]{:S(2)}) collective-permute-start(bf16[12,2,16,256]{3,2,0,1:T(8,128)(2,1)S(1)} %maximum_select_fusion.5), channel_id=1, source_target_pairs={{0,16},{8,24},{16,0},{24,8},{32,48},{40,56},{48,32},{56,40},{1,17}... | collective-permute-start | bytes 589832 | tf_op jit(solution)/shard_map/ppermute | solution.py:81
  109.4 19.1 %collective-permute-start.14 = (bf16[12,128,256]{2,1,0:T(8,128)(2,1)S(1)}, bf16[12,128,256]{2,1,0:T(8,128)(2,1)S(1)}, u32[]{:S(2)}, u32[]{:S(2)}) collective-permute-start(bf16[12,128,256]{2,1,0:T(8,128)(2,1)S(1)} %bitcast.91), channel_id=1, source_target_pairs={{0,384},{128,0},{256,128},{384,256},{1,385},{129,1},{257,129},{385... | collective-permute-start | bytes 2359304 | tf_op jit(solution)/shard_map/ppermute | solution.py:23
  111.5 18.9 %collective-permute-start.13 = (bf16[12,128,256]{2,1,0:T(8,128)(2,1)S(1)}, bf16[12,128,256]{2,1,0:T(8,128)(2,1)S(1)}, u32[]{:S(2)}, u32[]{:S(2)}) collective-permute-start(bf16[12,128,256]{2,1,0:T(8,128)(2,1)S(1)} %bitcast.92), channel_id=1, source_target_pairs={{0,128},{128,256},{256,384},{384,0},{1,129},{129,257},{257,385},{3... | collective-permute-start | bytes 2359304 | tf_op jit(solution)/shard_map/ppermute | solution.py:23
  115.6 11.6 %collective-permute-start.12 = (bf16[4,6,64,128]{3,2,1,0:T(8,128)(2,1)}, bf16[4,6,64,128]{3,2,1,0:T(8,128)(2,1)S(1)}, u32[]{:S(2)}, u32[]{:S(2)}) collective-permute-start(bf16[4,6,64,128]{3,2,1,0:T(8,128)(2,1)} %slice.79), channel_id=1, source_target_pairs={{0,2},{2,4},{4,6},{6,0},{1,3},{3,5},{5,7},{7,1},{8,10},{10,12},{12... | collective-permute-start | bytes 1179656 | tf_op jit(solution)/shard_map/ppermute | solution.py:23
  117.5 10.3 %collective-permute-start.11 = (bf16[4,6,64,128]{3,2,1,0:T(8,128)(2,1)S(1)}, bf16[4,6,64,128]{3,2,1,0:T(8,128)(2,1)S(1)}, u32[]{:S(2)}, u32[]{:S(2)}) collective-permute-start(bf16[4,6,64,128]{3,2,1,0:T(8,128)(2,1)S(1)} %slice.78), channel_id=1, source_target_pairs={{0,6},{2,0},{4,2},{6,4},{1,7},{3,1},{5,3},{7,5},{8,14},{10,8},{12,... | collective-permute-start | bytes 1179656 | tf_op jit(solution)/shard_map/ppermute | solution.py:23
  130.4 10.1 %collective-permute-start.16 = (bf16[12,64,256]{2,1,0:T(8,128)(2,1)S(1)}, bf16[12,64,256]{2,1,0:T(8,128)(2,1)S(1)}, u32[]{:S(2)}, u32[]{:S(2)}) collective-permute-start(bf16[12,64,256]{2,1,0:T(8,128)(2,1)S(1)} %slice.81), channel_id=1, source_target_pairs={{0,128},{128,256},{256,384},{384,0},{1,129},{129,257},{257,385},{3... | collective-permute-start | bytes 1179656 | tf_op jit(solution)/shard_map/ppermute | solution.py:23
  133.7 11.5 %collective-permute-start.15 = (bf16[12,64,256]{2,1,0:T(8,128)(2,1)S(1)}, bf16[12,64,256]{2,1,0:T(8,128)(2,1)S(1)}, u32[]{:S(2)}, u32[]{:S(2)}) collective-permute-start(bf16[12,64,256]{2,1,0:T(8,128)(2,1)S(1)} %slice.80), channel_id=1, source_target_pairs={{0,384},{128,0},{256,128},{384,256},{1,385},{129,1},{257,129},{385... | collective-permute-start | bytes 1179656 | tf_op jit(solution)/shard_map/ppermute | solution.py:23
  145.3 33.0 %collective-permute-start.17 = (bf16[12,4,128,256]{3,2,1,0:T(8,128)(2,1)S(1)}, bf16[12,4,128,256]{3,2,1,0:T(8,128)(2,1)}, u32[]{:S(2)}, u32[]{:S(2)}) collective-permute-start(bf16[12,4,128,256]{3,2,1,0:T(8,128)(2,1)S(1)} %bitcast_dynamic-update-slice_fusion.2), channel_id=1, source_target_pairs={{0,64},{64,0},{1,65},{65,1},{2,66},{66,2},{3,67},{67,3},{4,68},{68... | collective-permute-start | bytes 9437192 | tf_op jit(solution)/shard_map/ppermute | solution.py:44
  151.2 13.0 %collective-permute-start.18 = (f32[2,128]{1,0:T(2,128)S(1)}, f32[2,128]{1,0:T(2,128)S(1)}, u32[]{:S(2)}, u32[]{:S(2)}) collective-permute-start(f32[2,128]{1,0:T(2,128)S(1)} %pad_maximum_fusion.2), channel_id=1, source_target_pairs={{0,1},{1,0},{2,3},{3,2},{4,5},{5,4},{6,7},{7,6},{8,9},{9,8},{10,11... | collective-permute-start | bytes 3080 | tf_op jit(solution)/shard_map/ppermute | solution.py:59
  206.3 19.5 %collective-permute-start.21 = (bf16[6,4,64,256]{3,2,1,0:T(8,128)(2,1)}, bf16[6,4,64,256]{3,2,1,0:T(8,128)(2,1)}, u32[]{:S(2)}, u32[]{:S(2)}) collective-permute-start(bf16[6,4,64,256]{3,2,1,0:T(8,128)(2,1)} %get-tuple-element.32), channel_id=1, source_target_pairs={{0,6},{2,0},{4,2},{6,4},{1,7},{3,1},{5,3},{7,5},{8,14},{10,8},{12,... | collective-permute-start | bytes 2359304 | tf_op jit(solution)/shard_map/ppermute | solution.py:23
  209.7 21.5 %collective-permute-start.23 = (bf16[6,4,64,256]{3,2,1,0:T(8,128)(2,1)}, bf16[6,4,64,256]{3,2,1,0:T(8,128)(2,1)}, u32[]{:S(2)}, u32[]{:S(2)}) collective-permute-start(bf16[6,4,64,256]{3,2,1,0:T(8,128)(2,1)} %get-tuple-element.32), channel_id=1, source_target_pairs={{0,2},{2,4},{4,6},{6,0},{1,3},{3,5},{5,7},{7,1},{8,10},{10,12},{12... | collective-permute-start | bytes 2359304 | tf_op jit(solution)/shard_map/ppermute | solution.py:23
  226.9 12.1 %collective-permute-start.22 = (bf16[6,4,64,128]{3,2,1,0:T(8,128)(2,1)S(1)}, bf16[6,4,64,128]{3,2,1,0:T(8,128)(2,1)S(1)}, u32[]{:S(2)}, u32[]{:S(2)}) collective-permute-start(bf16[6,4,64,128]{3,2,1,0:T(8,128)(2,1)S(1)} %slice.109), channel_id=1, source_target_pairs={{0,6},{2,0},{4,2},{6,4},{1,7},{3,1},{5,3},{7,5},{8,14},{10,8},{12,... | collective-permute-start | bytes 1179656 | tf_op jit(solution)/shard_map/ppermute | solution.py:23
  232.3 13.1 %collective-permute-start.24 = (bf16[6,4,64,128]{3,2,1,0:T(8,128)(2,1)S(1)}, bf16[6,4,64,128]{3,2,1,0:T(8,128)(2,1)S(1)}, u32[]{:S(2)}, u32[]{:S(2)}) collective-permute-start(bf16[6,4,64,128]{3,2,1,0:T(8,128)(2,1)S(1)} %slice.110), channel_id=1, source_target_pairs={{0,2},{2,4},{4,6},{6,0},{1,3},{3,5},{5,7},{7,1},{8,10},{10,12},{12... | collective-permute-start | bytes 1179656 | tf_op jit(solution)/shard_map/ppermute | solution.py:23
  249.1 34.7 %collective-permute-start.25 = (bf16[4,4,64,128]{3,2,1,0:T(8,128)(2,1)S(1)}, bf16[4,4,64,128]{3,2,1,0:T(8,128)(2,1)S(1)}, u32[]{:S(2)}, u32[]{:S(2)}) collective-permute-start(bf16[4,4,64,128]{3,2,1,0:T(8,128)(2,1)S(1)} %get-tuple-element.36), channel_id=1, source_target_pairs={{0,1},{1,0},{2,3},{3,2},{4,5},{5,4},{6,7},{7,6},{8,9},{9,8},{10,11... | collective-permute-start | bytes 786440 | tf_op jit(solution)/shard_map/ppermute | solution.py:142
  (17 other events, 140.3 us)

commit v10 on v8

--- a/solution.py
+++ b/solution.py
@@ -111,8 +111,7 @@
     local_ids = lax.dynamic_slice_in_dim(padded_ids, index * fr_count, fr_count + 2)
     prev_ok = (local_ids[1:-1] == local_ids[:-2]).astype(jnp.float32).reshape(fr_count, 1, 1, 1)
     next_ok = (local_ids[1:-1] == local_ids[2:]).astype(jnp.float32).reshape(fr_count, 1, 1, 1)
-    source = shift_halo(active, FRAME, lax.axis_size(FRAME), 0, 1)
-    whole = x_gather(source)
+    whole = shift_halo(x_gather(active), FRAME, lax.axis_size(FRAME), 0, 1)
     taps_out = [
         jnp.einsum(
             "fhwc,cd->fhwd",

time: 281 us -> 269 us (0.957)
  the two profiles are of different devices: /device:TPU:81 before, /device:TPU:87 now
where the time goes in v10:
time: 269 us; the launch traced here: 267 us
  starting transfers between devices  113 us (42%)
  waiting for transfers between devices  107 us (40%)
  local copies, waits for them, and re-layouts  27.7 us (10%)
  other arithmetic  10 us (4%)
  matrix products  8.5 us (3%)
    ppermute x12, starting transfers between devices, ring_shift(): lax.ppermute(block, axis, [(i, (i + step) % count) for i in range(count)])  33.4 us
    ppermute x12, waiting for transfers between devices, ring_shift(): lax.ppermute(block, axis, [(i, (i + step) % count) for i in range(count)])  30.5 us
    ppermute x1, waiting for transfers between devices, body(): returned = lax.ppermute(given, 'cz', SWAP)  29.2 us
    ppermute x4, starting transfers between devices, xor_stack(): other = lax.ppermute(block, axis, [(i, i ^ bit) for i in range(count)])  28.7 us
    ppermute x4, waiting for transfers between devices, xor_stack(): other = lax.ppermute(block, axis, [(i, i ^ bit) for i in range(count)])  14.6 us
    ppermute x1, starting transfers between devices, body(): w_block = ordered_pair(weight, lax.ppermute(weight, 'cz', SWAP), high, 2)  13.6 us
    unnamed x34, local copies, waits for them, and re-layouts  13.2 us
    ppermute x2, waiting for transfers between devices, shift_halo(): lax.ppermute(lax.slice_in_dim(block, block.shape[dim] - width, None, axis...  12.9 us
  transfers between devices with their start and end apart: 25, of which 16 were waited for; matrix products, arithmetic and copies ran while one was open for 10% of the time, Pallas kernels for 0%

profile of v10, /device:TPU:87, one launch (start us, length us, event | category | flops | bytes accessed | tf_op | source)
XLA Modules:
  0.0 267.3 jit_solution(9495706099016100866)
XLA Ops:
  1.5 13.6 %collective-permute-start.4 = (bf16[12,16,128]{2,1,0:T(8,128)(2,1)S(1)}, bf16[12,16,128]{2,1,0:T(8,128)(2,1)S(1)}, u32[]{:S(2)}, u32[]{:S(2)}) collective-permute-start(bf16[12,16,128]{2,1,0:T(8,128)(2,1)S(1)} %constant_dynamic-update-slice_fusion), channel_id=1, source_target_pairs={{0,1},{1,0},{2,3},{3,2},{4,5},{5,4},{6,7},{7,6},{8,9},{9,8},{10,11... | collective-permute-start | bytes 147464 | tf_op jit(solution)/shard_map/ppermute | solution.py:67
  19.0 11.6 %collective-permute-start.3 = (bf16[4,1,64,128]{3,2,1,0:T(8,128)(2,1)S(1)}, bf16[4,1,64,128]{3,2,1,0:T(8,128)(2,1)S(1)}, u32[]{:S(2)}, u32[]{:S(2)}) collective-permute-start(bf16[4,1,64,128]{3,2,1,0:T(8,128)(2,1)S(1)} %get-tuple-element.38), channel_id=1, source_target_pairs={{1,8},{9,16},{17,24},{25,32},{33,40},{41,48},{49,56},{8,1},{16,9},... | collective-permute-start | bytes 196616 | tf_op jit(solution)/shard_map/ppermute | solution.py:66
  36.0 7.4 %collective-permute-done.1 = bf16[4,1,64,128]{3,2,1,0:T(8,128)(2,1)S(1)} collective-permute-done((bf16[4,1,64,128]{3,2,1,0:T(8,128)(2,1)S(1)}, bf16[4,1,64,128]{3,2,1,0:T(8,128)(2,1)S(1)}, u32[]{:S(2)}, u32[]{:S(2)}) %collective-permute-start.1) | collective-permute-done | bytes 65568 | tf_op jit(solution)/shard_map/ppermute | solution.py:18
  43.4 11.2 %collective-permute-done = bf16[4,1,64,128]{3,2,1,0:T(8,128)(2,1)S(1)} collective-permute-done((bf16[4,1,64,128]{3,2,1,0:T(8,128)(2,1)S(1)}, bf16[4,1,64,128]{3,2,1,0:T(8,128)(2,1)S(1)}, u32[]{:S(2)}, u32[]{:S(2)}) %collective-permute-start) | collective-permute-done | bytes 65568 | tf_op jit(solution)/shard_map/ppermute | solution.py:15
  56.7 8.2 %collective-permute-start.7 = (bf16[12,16,256]{2,1,0:T(8,128)(2,1)S(1)}, bf16[12,16,256]{2,1,0:T(8,128)(2,1)S(1)}, u32[]{:S(2)}, u32[]{:S(2)}) collective-permute-start(bf16[12,16,256]{2,1,0:T(8,128)(2,1)S(1)} %maximum_select_fusion.8), channel_id=1, source_target_pairs={{0,32},{8,40},{16,48},{24,56},{32,0},{40,8},{48,16},{56,24},{1,33}... | collective-permute-start | bytes 294920 | tf_op jit(solution)/shard_map/ppermute | solution.py:44
  68.8 4.0 %collective-permute-start.5 = (bf16[4,6,64,256]{3,2,1,0:T(8,128)(2,1)S(1)}, bf16[4,6,64,256]{3,2,1,0:T(8,128)(2,1)S(1)}, u32[]{:S(2)}, u32[]{:S(2)}) collective-permute-start(bf16[4,6,64,256]{3,2,1,0:T(8,128)(2,1)S(1)} %get-tuple-element.28), channel_id=1, source_target_pairs={{0,2},{2,4},{4,6},{6,0},{1,3},{3,5},{5,7},{7,1},{8,10},{10,12},{12... | collective-permute-start | bytes 2359304 | tf_op jit(solution)/shard_map/ppermute | solution.py:23
  74.8 5.6 %collective-permute-done.8 = bf16[12,2,16,256]{3,2,1,0:T(8,128)(2,1)S(1)} collective-permute-done((bf16[12,2,16,256]{3,2,1,0:T(8,128)(2,1)S(1)}, bf16[12,2,16,256]{3,2,1,0:T(8,128)(2,1)S(1)}, u32[]{:S(2)}, u32[]{:S(2)}) %collective-permute-start.8) | collective-permute-done | bytes 196640 | tf_op jit(solution)/shard_map/ppermute | solution.py:44
  80.5 13.6 %collective-permute-start.9 = (bf16[12,2,2,16,256]{4,3,1,0,2:T(8,128)(2,1)S(1)}, bf16[12,2,2,16,256]{4,3,1,0,2:T(8,128)(2,1)S(1)}, u32[]{:S(2)}, u32[]{:S(2)}) collective-permute-start(bf16[12,2,2,16,256]{4,3,1,0,2:T(8,128)(2,1)S(1)} %maximum_select_fusion.5), channel_id=1, source_target_pairs={{0,8},{8,0},{16,24},{24,16},{32,40},{40,32},{48,56},{56,48},{1,9},... | collective-permute-start | bytes 1179656 | tf_op jit(solution)/shard_map/ppermute | solution.py:44
  94.2 9.0 %collective-permute-done.9 = bf16[12,2,2,16,256]{4,3,1,0,2:T(8,128)(2,1)S(1)} collective-permute-done((bf16[12,2,2,16,256]{4,3,1,0,2:T(8,128)(2,1)S(1)}, bf16[12,2,2,16,256]{4,3,1,0,2:T(8,128)(2,1)S(1)}, u32[]{:S(2)}, u32[]{:S(2)}) %collective-permute-start.9) | collective-permute-done | bytes 393248 | tf_op jit(solution)/shard_map/ppermute | solution.py:44
  115.7 5.9 %collective-permute-done.11 = bf16[4,6,64,128]{3,2,1,0:T(8,128)(2,1)S(1)} collective-permute-done((bf16[4,6,64,128]{3,2,1,0:T(8,128)(2,1)}, bf16[4,6,64,128]{3,2,1,0:T(8,128)(2,1)S(1)}, u32[]{:S(2)}, u32[]{:S(2)}) %collective-permute-start.11) | collective-permute-done | bytes 393248 | tf_op jit(solution)/shard_map/ppermute | solution.py:23
  126.5 3.6 %collective-permute-start.15 = (bf16[12,64,256]{2,1,0:T(8,128)(2,1)S(1)}, bf16[12,64,256]{2,1,0:T(8,128)(2,1)S(1)}, u32[]{:S(2)}, u32[]{:S(2)}) collective-permute-start(bf16[12,64,256]{2,1,0:T(8,128)(2,1)S(1)} %slice.80), channel_id=1, source_target_pairs={{0,128},{128,256},{256,384},{384,0},{1,129},{129,257},{257,385},{3... | collective-permute-start | bytes 1179656 | tf_op jit(solution)/shard_map/ppermute | solution.py:23
  137.4 4.6 %collective-permute-done.14 = bf16[12,64,256]{2,1,0:T(8,128)(2,1)S(1)} collective-permute-done((bf16[12,64,256]{2,1,0:T(8,128)(2,1)S(1)}, bf16[12,64,256]{2,1,0:T(8,128)(2,1)S(1)}, u32[]{:S(2)}, u32[]{:S(2)}) %collective-permute-start.14) | collective-permute-done | bytes 393248 | tf_op jit(solution)/shard_map/ppermute | solution.py:23
  142.1 5.0 %collective-permute-start.16 = (bf16[12,4,128,256]{3,2,1,0:T(8,128)(2,1)S(1)}, bf16[12,4,128,256]{3,2,1,0:T(8,128)(2,1)}, u32[]{:S(2)}, u32[]{:S(2)}) collective-permute-start(bf16[12,4,128,256]{3,2,1,0:T(8,128)(2,1)S(1)} %bitcast_dynamic-update-slice_fusion), channel_id=1, source_target_pairs={{0,64},{64,0},{1,65},{65,1},{2,66},{66,2},{3,67},{67,3},{4,68},{68... | collective-permute-start | bytes 9437192 | tf_op jit(solution)/shard_map/ppermute | solution.py:44
  147.2 4.5 %collective-permute-start.17 = (f32[2,128]{1,0:T(2,128)S(1)}, f32[2,128]{1,0:T(2,128)S(1)}, u32[]{:S(2)}, u32[]{:S(2)}) collective-permute-start(f32[2,128]{1,0:T(2,128)S(1)} %pad_maximum_fusion.3), channel_id=1, source_target_pairs={{0,1},{1,0},{2,3},{3,2},{4,5},{5,4},{6,7},{7,6},{8,9},{9,8},{10,11... | collective-permute-start | bytes 3080 | tf_op jit(solution)/shard_map/ppermute | solution.py:59
  151.7 8.5 %collective-permute-done.17 = f32[2,128]{1,0:T(2,128)S(1)} collective-permute-done((f32[2,128]{1,0:T(2,128)S(1)}, f32[2,128]{1,0:T(2,128)S(1)}, u32[]{:S(2)}, u32[]{:S(2)}) %collective-permute-start.17) | collective-permute-done | bytes 1056 | tf_op jit(solution)/shard_map/ppermute | solution.py:59
  166.1 4.3 %copy.32 = bf16[6,4,64,1024]{3,1,2,0:T(4,128)(2,1)S(1)} copy(bf16[6,4,64,1024]{3,2,0,1:T(8,128)(2,1)} %bitcast.83) | data formatting | bytes 6291456
  174.4 4.2 %maximum_select_fusion = bf16[12,4,2,128,256]{4,3,2,1,0:T(8,128)(2,1)S(1)} fusion(bf16[12,4,1,128,256]{4,3,2,1,0:T(8,128)(2,1)S(1)} %bitcast.82, bf16[12,4,1,128,256]{4,3,2,1,0:T(8,128)(2,1)} %bitcast.20, pred[]{:T(512)S(6)} %eq.34), kind=kLoop, calls=%fused_computation.2 | loop fusion | flops 9437184 | bytes 12582913 | tf_op jit(solution)/shard_map/jit(_where)/select_n | solution.py:46
  181.3 6.3 %convert_add_fusion = (f32[4,32,9,256]{3,1,2,0:T(8,128)S(1)}, bf16[4,32,9,256]{3,1,2,0:T(8,128)(2,1)S(1)}) fusion(f32[256]{0:T(256)S(1)} %bitcast.107, f32[256]{0:T(256)S(1)} %bitcast.108, bf16[3,3,1024,256]{3,2,1,0:T(8,128)(2,1)S(1)} %bitcast.84, bf16[6,4,8,11,1024]{4,1,3,2,0:T(4,128)(2,1)S(1)} %fusion.1, pred[32,9]{0,1:T(8,128)(4,1)S(1)} %copy-done.11), kind=kOutput, calls=%fused_computation.17 | convolution fusion | flops 5438767104 | bytes 10815776 | tf_op jit(solution)/shard_map/conv_general_dilated | solution.py:98
  193.9 8.6 %collective-permute-done.20 = bf16[4,4,64,256]{3,2,1,0:T(8,128)(2,1)S(1)} collective-permute-done((bf16[4,4,64,256]{3,2,1,0:T(8,128)(2,1)S(1)}, bf16[4,4,64,256]{3,2,1,0:T(8,128)(2,1)S(1)}, u32[]{:S(2)}, u32[]{:S(2)}) %collective-permute-start.20) | collective-permute-done | bytes 524320 | tf_op jit(solution)/shard_map/ppermute | solution.py:23
  209.2 5.0 %collective-permute-done.19 = bf16[4,4,64,128]{3,2,1,0:T(8,128)(2,1)S(1)} collective-permute-done((bf16[4,4,64,128]{3,2,1,0:T(8,128)(2,1)S(1)}, bf16[4,4,64,128]{3,2,1,0:T(8,128)(2,1)S(1)}, u32[]{:S(2)}, u32[]{:S(2)}) %collective-permute-start.19) | collective-permute-done | bytes 262176 | tf_op jit(solution)/shard_map/ppermute | solution.py:23
  214.6 5.4 %collective-permute-start.23 = (bf16[1,4,64,1024]{3,2,1,0:T(8,128)(2,1)S(1)}, bf16[1,4,64,1024]{3,2,1,0:T(8,128)(2,1)S(1)}, u32[]{:S(2)}, u32[]{:S(2)}) collective-permute-start(bf16[1,4,64,1024]{3,2,1,0:T(8,128)(2,1)S(1)} %get-tuple-element.33), channel_id=1, source_target_pairs={{64,0},{128,64},{192,128},{256,192},{320,256},{384,320},{448,384},... | collective-permute-start | bytes 1572872 | tf_op jit(solution)/shard_map/ppermute | solution.py:18
  221.5 4.5 %collective-permute-start.22 = (bf16[1,4,64,1024]{3,2,1,0:T(8,128)(2,1)S(1)}, bf16[1,4,64,1024]{3,2,1,0:T(8,128)(2,1)S(1)}, u32[]{:S(2)}, u32[]{:S(2)}) collective-permute-start(bf16[1,4,64,1024]{3,2,1,0:T(8,128)(2,1)S(1)} %get-tuple-element.32), channel_id=1, source_target_pairs={{0,64},{64,128},{128,192},{192,256},{256,320},{320,384},{384,448},... | collective-permute-start | bytes 1572872 | tf_op jit(solution)/shard_map/ppermute | solution.py:15
  233.0 4.3 %collective-permute-start.24 = (bf16[4,4,64,128]{3,2,1,0:T(8,128)(2,1)S(1)}, bf16[4,4,64,128]{3,2,1,0:T(8,128)(2,1)S(1)}, u32[]{:S(2)}, u32[]{:S(2)}) collective-permute-start(bf16[4,4,64,128]{3,2,1,0:T(8,128)(2,1)S(1)} %get-tuple-element.36), channel_id=1, source_target_pairs={{0,1},{1,0},{2,3},{3,2},{4,5},{5,4},{6,7},{7,6},{8,9},{9,8},{10,11... | collective-permute-start | bytes 786440 | tf_op jit(solution)/shard_map/ppermute | solution.py:133
  237.3 29.2 %collective-permute-done.24 = bf16[4,4,64,128]{3,2,1,0:T(8,128)(2,1)S(1)} collective-permute-done((bf16[4,4,64,128]{3,2,1,0:T(8,128)(2,1)S(1)}, bf16[4,4,64,128]{3,2,1,0:T(8,128)(2,1)S(1)}, u32[]{:S(2)}, u32[]{:S(2)}) %collective-permute-start.24) | collective-permute-done | bytes 262176 | tf_op jit(solution)/shard_map/ppermute | solution.py:133
  (111 shorter events, 78.3 us)
Async XLA Ops:
  1.5 34.5 %collective-permute-start.4 = (bf16[12,16,128]{2,1,0:T(8,128)(2,1)S(1)}, bf16[12,16,128]{2,1,0:T(8,128)(2,1)S(1)}, u32[]{:S(2)}, u32[]{:S(2)}) collective-permute-start(bf16[12,16,128]{2,1,0:T(8,128)(2,1)S(1)} %constant_dynamic-update-slice_fusion), channel_id=1, source_target_pairs={{0,1},{1,0},{2,3},{3,2},{4,5},{5,4},{6,7},{7,6},{8,9},{9,8},{10,11... | collective-permute-start | bytes 147464 | tf_op jit(solution)/shard_map/ppermute | solution.py:67
  16.1 40.6 %collective-permute-start.2 = (bf16[4,5,64,128]{3,2,1,0:T(8,128)(2,1)S(1)}, bf16[4,5,64,128]{3,2,1,0:T(8,128)(2,1)S(1)}, u32[]{:S(2)}, u32[]{:S(2)}) collective-permute-start(bf16[4,5,64,128]{3,2,1,0:T(8,128)(2,1)S(1)} %constant_dynamic-slice_fusion.4), channel_id=1, source_target_pairs={{0,1},{1,0},{2,3},{3,2},{4,5},{5,4},{6,7},{7,6},{8,9},{9,8},{10,11... | collective-permute-start | bytes 983048 | tf_op jit(solution)/shard_map/ppermute | solution.py:62
  19.0 37.7 %collective-permute-start.3 = (bf16[4,1,64,128]{3,2,1,0:T(8,128)(2,1)S(1)}, bf16[4,1,64,128]{3,2,1,0:T(8,128)(2,1)S(1)}, u32[]{:S(2)}, u32[]{:S(2)}) collective-permute-start(bf16[4,1,64,128]{3,2,1,0:T(8,128)(2,1)S(1)} %get-tuple-element.38), channel_id=1, source_target_pairs={{1,8},{9,16},{17,24},{25,32},{33,40},{41,48},{49,56},{8,1},{16,9},... | collective-permute-start | bytes 196616 | tf_op jit(solution)/shard_map/ppermute | solution.py:66
  30.6 12.8 %collective-permute-start.1 = (bf16[4,1,64,128]{3,2,1,0:T(8,128)(2,1)S(1)}, bf16[4,1,64,128]{3,2,1,0:T(8,128)(2,1)S(1)}, u32[]{:S(2)}, u32[]{:S(2)}) collective-permute-start(bf16[4,1,64,128]{3,2,1,0:T(8,128)(2,1)S(1)} %get-tuple-element.39), channel_id=1, source_target_pairs={{8,0},{16,8},{24,16},{32,24},{40,32},{48,40},{56,48},{9,1},{17,9},... | collective-permute-start | bytes 196616 | tf_op jit(solution)/shard_map/ppermute | solution.py:18
  33.3 21.3 %collective-permute-start = (bf16[4,1,64,128]{3,2,1,0:T(8,128)(2,1)S(1)}, bf16[4,1,64,128]{3,2,1,0:T(8,128)(2,1)S(1)}, u32[]{:S(2)}, u32[]{:S(2)}) collective-permute-start(bf16[4,1,64,128]{3,2,1,0:T(8,128)(2,1)S(1)} %get-tuple-element.40), channel_id=1, source_target_pairs={{0,8},{8,16},{16,24},{24,32},{32,40},{40,48},{48,56},{1,9},{9,17},... | collective-permute-start | bytes 196616 | tf_op jit(solution)/shard_map/ppermute | solution.py:15
  56.7 16.1 %collective-permute-start.7 = (bf16[12,16,256]{2,1,0:T(8,128)(2,1)S(1)}, bf16[12,16,256]{2,1,0:T(8,128)(2,1)S(1)}, u32[]{:S(2)}, u32[]{:S(2)}) collective-permute-start(bf16[12,16,256]{2,1,0:T(8,128)(2,1)S(1)} %maximum_select_fusion.8), channel_id=1, source_target_pairs={{0,32},{8,40},{16,48},{24,56},{32,0},{40,8},{48,16},{56,24},{1,33}... | collective-permute-start | bytes 294920 | tf_op jit(solution)/shard_map/ppermute | solution.py:44
  66.3 37.0 %collective-permute-start.6 = (bf16[4,6,64,256]{3,2,1,0:T(8,128)(2,1)S(1)}, bf16[4,6,64,256]{3,2,1,0:T(8,128)(2,1)S(1)}, u32[]{:S(2)}, u32[]{:S(2)}) collective-permute-start(bf16[4,6,64,256]{3,2,1,0:T(8,128)(2,1)S(1)} %get-tuple-element.28), channel_id=1, source_target_pairs={{0,6},{2,0},{4,2},{6,4},{1,7},{3,1},{5,3},{7,5},{8,14},{10,8},{12,... | collective-permute-start | bytes 2359304 | tf_op jit(solution)/shard_map/ppermute | solution.py:23
  68.8 34.6 %collective-permute-start.5 = (bf16[4,6,64,256]{3,2,1,0:T(8,128)(2,1)S(1)}, bf16[4,6,64,256]{3,2,1,0:T(8,128)(2,1)S(1)}, u32[]{:S(2)}, u32[]{:S(2)}) collective-permute-start(bf16[4,6,64,256]{3,2,1,0:T(8,128)(2,1)S(1)} %get-tuple-element.28), channel_id=1, source_target_pairs={{0,2},{2,4},{4,6},{6,0},{1,3},{3,5},{5,7},{7,1},{8,10},{10,12},{12... | collective-permute-start | bytes 2359304 | tf_op jit(solution)/shard_map/ppermute | solution.py:23
  80.5 22.7 %collective-permute-start.9 = (bf16[12,2,2,16,256]{4,3,1,0,2:T(8,128)(2,1)S(1)}, bf16[12,2,2,16,256]{4,3,1,0,2:T(8,128)(2,1)S(1)}, u32[]{:S(2)}, u32[]{:S(2)}) collective-permute-start(bf16[12,2,2,16,256]{4,3,1,0,2:T(8,128)(2,1)S(1)} %maximum_select_fusion.5), channel_id=1, source_target_pairs={{0,8},{8,0},{16,24},{24,16},{32,40},{40,32},{48,56},{56,48},{1,9},... | collective-permute-start | bytes 1179656 | tf_op jit(solution)/shard_map/ppermute | solution.py:44
  103.3 21.3 %collective-permute-start.13 = (bf16[12,128,256]{2,1,0:T(8,128)(2,1)S(1)}, bf16[12,128,256]{2,1,0:T(8,128)(2,1)}, u32[]{:S(2)}, u32[]{:S(2)}) collective-permute-start(bf16[12,128,256]{2,1,0:T(8,128)(2,1)S(1)} %bitcast.86), channel_id=1, source_target_pairs={{0,384},{128,0},{256,128},{384,256},{1,385},{129,1},{257,129},{385... | collective-permute-start | bytes 2359304 | tf_op jit(solution)/shard_map/ppermute | solution.py:23
  105.4 19.8 %collective-permute-start.12 = (bf16[12,128,256]{2,1,0:T(8,128)(2,1)S(1)}, bf16[12,128,256]{2,1,0:T(8,128)(2,1)S(1)}, u32[]{:S(2)}, u32[]{:S(2)}) collective-permute-start(bf16[12,128,256]{2,1,0:T(8,128)(2,1)S(1)} %bitcast.87), channel_id=1, source_target_pairs={{0,128},{128,256},{256,384},{384,0},{1,129},{129,257},{257,385},{3... | collective-permute-start | bytes 2359304 | tf_op jit(solution)/shard_map/ppermute | solution.py:23
  110.3 11.3 %collective-permute-start.11 = (bf16[4,6,64,128]{3,2,1,0:T(8,128)(2,1)}, bf16[4,6,64,128]{3,2,1,0:T(8,128)(2,1)S(1)}, u32[]{:S(2)}, u32[]{:S(2)}) collective-permute-start(bf16[4,6,64,128]{3,2,1,0:T(8,128)(2,1)} %slice.78), channel_id=1, source_target_pairs={{0,2},{2,4},{4,6},{6,0},{1,3},{3,5},{5,7},{7,1},{8,10},{10,12},{12... | collective-permute-start | bytes 1179656 | tf_op jit(solution)/shard_map/ppermute | solution.py:23
  112.4 12.2 %collective-permute-start.10 = (bf16[4,6,64,128]{3,2,1,0:T(8,128)(2,1)}, bf16[4,6,64,128]{3,2,1,0:T(8,128)(2,1)}, u32[]{:S(2)}, u32[]{:S(2)}) collective-permute-start(bf16[4,6,64,128]{3,2,1,0:T(8,128)(2,1)} %slice.77), channel_id=1, source_target_pairs={{0,6},{2,0},{4,2},{6,4},{1,7},{3,1},{5,3},{7,5},{8,14},{10,8},{12,... | collective-permute-start | bytes 1179656 | tf_op jit(solution)/shard_map/ppermute | solution.py:23
  126.5 10.9 %collective-permute-start.15 = (bf16[12,64,256]{2,1,0:T(8,128)(2,1)S(1)}, bf16[12,64,256]{2,1,0:T(8,128)(2,1)S(1)}, u32[]{:S(2)}, u32[]{:S(2)}) collective-permute-start(bf16[12,64,256]{2,1,0:T(8,128)(2,1)S(1)} %slice.80), channel_id=1, source_target_pairs={{0,128},{128,256},{256,384},{384,0},{1,129},{129,257},{257,385},{3... | collective-permute-start | bytes 1179656 | tf_op jit(solution)/shard_map/ppermute | solution.py:23
  130.2 11.8 %collective-permute-start.14 = (bf16[12,64,256]{2,1,0:T(8,128)(2,1)S(1)}, bf16[12,64,256]{2,1,0:T(8,128)(2,1)S(1)}, u32[]{:S(2)}, u32[]{:S(2)}) collective-permute-start(bf16[12,64,256]{2,1,0:T(8,128)(2,1)S(1)} %slice.79), channel_id=1, source_target_pairs={{0,384},{128,0},{256,128},{384,256},{1,385},{129,1},{257,129},{385... | collective-permute-start | bytes 1179656 | tf_op jit(solution)/shard_map/ppermute | solution.py:23
  142.1 32.2 %collective-permute-start.16 = (bf16[12,4,128,256]{3,2,1,0:T(8,128)(2,1)S(1)}, bf16[12,4,128,256]{3,2,1,0:T(8,128)(2,1)}, u32[]{:S(2)}, u32[]{:S(2)}) collective-permute-start(bf16[12,4,128,256]{3,2,1,0:T(8,128)(2,1)S(1)} %bitcast_dynamic-update-slice_fusion), channel_id=1, source_target_pairs={{0,64},{64,0},{1,65},{65,1},{2,66},{66,2},{3,67},{67,3},{4,68},{68... | collective-permute-start | bytes 9437192 | tf_op jit(solution)/shard_map/ppermute | solution.py:44
  147.2 13.0 %collective-permute-start.17 = (f32[2,128]{1,0:T(2,128)S(1)}, f32[2,128]{1,0:T(2,128)S(1)}, u32[]{:S(2)}, u32[]{:S(2)}) collective-permute-start(f32[2,128]{1,0:T(2,128)S(1)} %pad_maximum_fusion.3), channel_id=1, source_target_pairs={{0,1},{1,0},{2,3},{3,2},{4,5},{5,4},{6,7},{7,6},{8,9},{9,8},{10,11... | collective-permute-start | bytes 3080 | tf_op jit(solution)/shard_map/ppermute | solution.py:59
  188.3 14.1 %collective-permute-start.20 = (bf16[4,4,64,256]{3,2,1,0:T(8,128)(2,1)S(1)}, bf16[4,4,64,256]{3,2,1,0:T(8,128)(2,1)S(1)}, u32[]{:S(2)}, u32[]{:S(2)}) collective-permute-start(bf16[4,4,64,256]{3,2,1,0:T(8,128)(2,1)S(1)} %bitcast.97), channel_id=1, source_target_pairs={{0,2},{2,4},{4,6},{6,0},{1,3},{3,5},{5,7},{7,1},{8,10},{10,12},{12... | collective-permute-start | bytes 1572872 | tf_op jit(solution)/shard_map/ppermute | solution.py:23
  190.5 15.4 %collective-permute-start.18 = (bf16[4,4,64,256]{3,2,1,0:T(8,128)(2,1)S(1)}, bf16[4,4,64,256]{3,2,1,0:T(8,128)(2,1)S(1)}, u32[]{:S(2)}, u32[]{:S(2)}) collective-permute-start(bf16[4,4,64,256]{3,2,1,0:T(8,128)(2,1)S(1)} %bitcast.98), channel_id=1, source_target_pairs={{0,6},{2,0},{4,2},{6,4},{1,7},{3,1},{5,3},{7,5},{8,14},{10,8},{12,... | collective-permute-start | bytes 1572872 | tf_op jit(solution)/shard_map/ppermute | solution.py:23
  202.5 11.8 %collective-permute-start.21 = (bf16[4,4,64,128]{3,2,1,0:T(8,128)(2,1)S(1)}, bf16[4,4,64,128]{3,2,1,0:T(8,128)(2,1)S(1)}, u32[]{:S(2)}, u32[]{:S(2)}) collective-permute-start(bf16[4,4,64,128]{3,2,1,0:T(8,128)(2,1)S(1)} %slice.106), channel_id=1, source_target_pairs={{0,2},{2,4},{4,6},{6,0},{1,3},{3,5},{5,7},{7,1},{8,10},{10,12},{12... | collective-permute-start | bytes 786440 | tf_op jit(solution)/shard_map/ppermute | solution.py:23
  205.9 8.3 %collective-permute-start.19 = (bf16[4,4,64,128]{3,2,1,0:T(8,128)(2,1)S(1)}, bf16[4,4,64,128]{3,2,1,0:T(8,128)(2,1)S(1)}, u32[]{:S(2)}, u32[]{:S(2)}) collective-permute-start(bf16[4,4,64,128]{3,2,1,0:T(8,128)(2,1)S(1)} %slice.105), channel_id=1, source_target_pairs={{0,6},{2,0},{4,2},{6,4},{1,7},{3,1},{5,3},{7,5},{8,14},{10,8},{12,... | collective-permute-start | bytes 786440 | tf_op jit(solution)/shard_map/ppermute | solution.py:23
  214.6 15.1 %collective-permute-start.23 = (bf16[1,4,64,1024]{3,2,1,0:T(8,128)(2,1)S(1)}, bf16[1,4,64,1024]{3,2,1,0:T(8,128)(2,1)S(1)}, u32[]{:S(2)}, u32[]{:S(2)}) collective-permute-start(bf16[1,4,64,1024]{3,2,1,0:T(8,128)(2,1)S(1)} %get-tuple-element.33), channel_id=1, source_target_pairs={{64,0},{128,64},{192,128},{256,192},{320,256},{384,320},{448,384},... | collective-permute-start | bytes 1572872 | tf_op jit(solution)/shard_map/ppermute | solution.py:18
  221.5 10.6 %collective-permute-start.22 = (bf16[1,4,64,1024]{3,2,1,0:T(8,128)(2,1)S(1)}, bf16[1,4,64,1024]{3,2,1,0:T(8,128)(2,1)S(1)}, u32[]{:S(2)}, u32[]{:S(2)}) collective-permute-start(bf16[1,4,64,1024]{3,2,1,0:T(8,128)(2,1)S(1)} %get-tuple-element.32), channel_id=1, source_target_pairs={{0,64},{64,128},{128,192},{192,256},{256,320},{320,384},{384,448},... | collective-permute-start | bytes 1572872 | tf_op jit(solution)/shard_map/ppermute | solution.py:15
  233.0 33.5 %collective-permute-start.24 = (bf16[4,4,64,128]{3,2,1,0:T(8,128)(2,1)S(1)}, bf16[4,4,64,128]{3,2,1,0:T(8,128)(2,1)S(1)}, u32[]{:S(2)}, u32[]{:S(2)}) collective-permute-start(bf16[4,4,64,128]{3,2,1,0:T(8,128)(2,1)S(1)} %get-tuple-element.36), channel_id=1, source_target_pairs={{0,1},{1,0},{2,3},{3,2},{4,5},{5,4},{6,7},{7,6},{8,9},{9,8},{10,11... | collective-permute-start | bytes 786440 | tf_op jit(solution)/shard_map/ppermute | solution.py:133
  (13 other events, 155.5 us)

commit v11 on v10

--- a/solution.py
+++ b/solution.py
@@ -59,19 +59,26 @@
     biases = ordered_pair(biases, lax.ppermute(biases, "cz", SWAP), high, 1)
     rimmed = shift_halo(frames_in, "row", row_n, 1, 1)
     sent = lax.dynamic_slice_in_dim(frames_in, (1 - side) * (half - 1), half + 1, axis=1)
-    partner = lax.ppermute(sent, "cz", SWAP)
     edge = lax.dynamic_slice_in_dim(frames_in, side * (row_count - 1), 1, axis=1)
     diagonal = [(q * 2 + 1, q * 2 + 2) for q in range(row_n - 1)]
     diagonal += [(q * 2, q * 2 - 1) for q in range(1, row_n)]
     rim = lax.ppermute(edge, ("row", "cz"), diagonal)
+    bounds = (0, fr_count // 2, fr_count // 2 + fr_count // 4, fr_count)
+    chunks = []
+    chunks.append(lax.ppermute(sent[bounds[0] : bounds[1]], "cz", SWAP))
     w_block = ordered_pair(weight, lax.ppermute(weight, "cz", SWAP), high, 2)
-    rimmed, partner, rim, w_block = lax.optimization_barrier((rimmed, partner, rim, w_block))
+    rimmed, rim, w_block, chunks[0] = lax.optimization_barrier((rimmed, rim, w_block, chunks[0]))
+    for pos, bit in enumerate((4, 2)):
+        chunk = lax.ppermute(sent[bounds[pos + 1] : bounds[pos + 2]], "cz", SWAP)
+        w_block = xor_stack(w_block, "row", bit, 1 + pos)
+        chunk, w_block = lax.optimization_barrier((chunk, w_block))
+        chunks.append(chunk)
+    partner = jnp.concatenate(chunks, axis=0)
     mine = lax.dynamic_slice_in_dim(rimmed, side * half, half + 2, axis=1)
     pair = ordered_pair(mine, ordered_pair(rim, partner, high, 1), high, 3)
     from_left = ring_shift(pair, "cx", ring, 1)
     from_right = ring_shift(pair, "cx", ring, -1)
-    for pos, bit in enumerate((4, 2, 1)):
-        w_block = xor_stack(w_block, "row", bit, 1 + pos)
+    w_block = xor_stack(w_block, "row", 1, 3)
     w_block = w_block.reshape(taps, row_n * depth, -1)
     from_left, from_right, w_block = lax.optimization_barrier((from_left, from_right, w_block))
     fy_n = lax.axis_size("fy")

time: 269 us -> 285 us (1.059)
  the two profiles are of different devices: /device:TPU:87 before, /device:TPU:471 now
where the time goes in v11:
time: 285 us; the launch traced here: 284 us
  waiting for transfers between devices  131 us (46%)
  starting transfers between devices  103 us (36%)
  local copies, waits for them, and re-layouts  29.4 us (10%)
  other arithmetic  11 us (4%)
  matrix products  8.51 us (3%)
    ppermute x12, starting transfers between devices, ring_shift(): lax.ppermute(block, axis, [(i, (i + step) % count) for i in range(count)])  37.4 us
    ppermute x1, waiting for transfers between devices, body(): returned = lax.ppermute(given, 'cz', SWAP)  32.5 us
    ppermute x12, waiting for transfers between devices, ring_shift(): lax.ppermute(block, axis, [(i, (i + step) % count) for i in range(count)])  30.1 us
    ppermute x4, waiting for transfers between devices, xor_stack(): other = lax.ppermute(block, axis, [(i, i ^ bit) for i in range(count)])  28.7 us
    ppermute x2, starting transfers between devices, body(): chunk = lax.ppermute(sent[bounds[pos + 1]:bounds[pos + 2]], 'cz', SWAP)  14 us
    unnamed x38, local copies, waits for them, and re-layouts  14 us
    ppermute x1, waiting for transfers between devices, body(): rim = lax.ppermute(edge, ('row', 'cz'), diagonal)  14 us
    ppermute x2, waiting for transfers between devices, shift_halo(): lax.ppermute(lax.slice_in_dim(block, 0, width, axis=dim), axis, backward)  13.4 us
  transfers between devices with their start and end apart: 27, of which 17 were waited for; matrix products, arithmetic and copies ran while one was open for 10% of the time, Pallas kernels for 0%

profile of v11, /device:TPU:471, one launch (start us, length us, event | category | flops | bytes accessed | tf_op | source)
XLA Modules:
  0.0 283.9 jit_solution(13340830784332490402)
XLA Ops:
  1.5 5.1 %collective-permute-start.3 = (bf16[12,16,128]{2,1,0:T(8,128)(2,1)S(1)}, bf16[12,16,128]{2,1,0:T(8,128)(2,1)S(1)}, u32[]{:S(2)}, u32[]{:S(2)}) collective-permute-start(bf16[12,16,128]{2,1,0:T(8,128)(2,1)S(1)} %constant_dynamic-update-slice_fusion), channel_id=1, source_target_pairs={{0,1},{1,0},{2,3},{3,2},{4,5},{5,4},{6,7},{7,6},{8,9},{9,8},{10,11... | collective-permute-start | bytes 147464 | tf_op jit(solution)/shard_map/ppermute | solution.py:69
  7.6 8.8 %collective-permute-start.7 = (bf16[1,5,64,128]{3,2,1,0:T(8,128)(2,1)S(1)}, bf16[1,5,64,128]{3,2,1,0:T(8,128)(2,1)S(1)}, u32[]{:S(2)}, u32[]{:S(2)}) collective-permute-start(bf16[1,5,64,128]{3,2,1,0:T(8,128)(2,1)S(1)} %get-tuple-element.46), channel_id=1, source_target_pairs={{0,1},{1,0},{2,3},{3,2},{4,5},{5,4},{6,7},{7,6},{8,9},{9,8},{10,11... | collective-permute-start | bytes 245768 | tf_op jit(solution)/shard_map/ppermute | solution.py:72
  16.4 5.2 %collective-permute-start.5 = (bf16[1,5,64,128]{3,2,1,0:T(8,128)(2,1)S(1)}, bf16[1,5,64,128]{3,2,1,0:T(8,128)(2,1)S(1)}, u32[]{:S(2)}, u32[]{:S(2)}) collective-permute-start(bf16[1,5,64,128]{3,2,1,0:T(8,128)(2,1)S(1)} %get-tuple-element.47), channel_id=1, source_target_pairs={{0,1},{1,0},{2,3},{3,2},{4,5},{5,4},{6,7},{7,6},{8,9},{9,8},{10,11... | collective-permute-start | bytes 245768 | tf_op jit(solution)/shard_map/ppermute | solution.py:72
  22.6 8.8 %collective-permute-start.4 = (bf16[2,5,64,128]{3,2,1,0:T(8,128)(2,1)S(1)}, bf16[2,5,64,128]{3,2,1,0:T(8,128)(2,1)S(1)}, u32[]{:S(2)}, u32[]{:S(2)}) collective-permute-start(bf16[2,5,64,128]{3,2,1,0:T(8,128)(2,1)S(1)} %constant_dynamic-slice_fusion.1), channel_id=1, source_target_pairs={{0,1},{1,0},{2,3},{3,2},{4,5},{5,4},{6,7},{7,6},{8,9},{9,8},{10,11... | collective-permute-start | bytes 491528 | tf_op jit(solution)/shard_map/ppermute | solution.py:68
  37.7 10.4 %collective-permute-done.1 = bf16[4,1,64,128]{3,2,1,0:T(8,128)(2,1)S(1)} collective-permute-done((bf16[4,1,64,128]{3,2,1,0:T(8,128)(2,1)S(1)}, bf16[4,1,64,128]{3,2,1,0:T(8,128)(2,1)S(1)}, u32[]{:S(2)}, u32[]{:S(2)}) %collective-permute-start.1) | collective-permute-done | bytes 65568 | tf_op jit(solution)/shard_map/ppermute | solution.py:18
  48.1 5.7 %collective-permute-start.2 = (bf16[4,1,64,128]{3,2,1,0:T(8,128)(2,1)S(1)}, bf16[4,1,64,128]{3,2,1,0:T(8,128)(2,1)S(1)}, u32[]{:S(2)}, u32[]{:S(2)}) collective-permute-start(bf16[4,1,64,128]{3,2,1,0:T(8,128)(2,1)S(1)} %get-tuple-element.48), channel_id=1, source_target_pairs={{1,8},{9,16},{17,24},{25,32},{33,40},{41,48},{49,56},{8,1},{16,9},... | collective-permute-start | bytes 196616 | tf_op jit(solution)/shard_map/ppermute | solution.py:65
  55.0 14.0 %collective-permute-done.2 = bf16[4,1,64,128]{3,2,1,0:T(8,128)(2,1)S(1)} collective-permute-done((bf16[4,1,64,128]{3,2,1,0:T(8,128)(2,1)S(1)}, bf16[4,1,64,128]{3,2,1,0:T(8,128)(2,1)S(1)}, u32[]{:S(2)}, u32[]{:S(2)}) %collective-permute-start.2) | collective-permute-done | bytes 65568 | tf_op jit(solution)/shard_map/ppermute | solution.py:65
  70.9 11.3 %collective-permute-done.6 = bf16[12,16,256]{2,1,0:T(8,128)(2,1)S(1)} collective-permute-done((bf16[12,16,256]{2,1,0:T(8,128)(2,1)S(1)}, bf16[12,16,256]{2,1,0:T(8,128)(2,1)S(1)}, u32[]{:S(2)}, u32[]{:S(2)}) %collective-permute-start.6) | collective-permute-done | bytes 98336 | tf_op jit(solution)/shard_map/ppermute | solution.py:44
  84.3 7.8 %collective-permute-done.8 = bf16[12,2,16,256]{3,2,1,0:T(8,128)(2,1)S(1)} collective-permute-done((bf16[12,2,16,256]{3,2,1,0:T(8,128)(2,1)S(1)}, bf16[12,2,16,256]{3,2,1,0:T(8,128)(2,1)S(1)}, u32[]{:S(2)}, u32[]{:S(2)}) %collective-permute-start.8) | collective-permute-done | bytes 196640 | tf_op jit(solution)/shard_map/ppermute | solution.py:44
  102.0 9.5 %collective-permute-done.11 = bf16[12,2,2,16,256]{4,3,2,1,0:T(8,128)(2,1)S(1)} collective-permute-done((bf16[12,2,2,16,256]{4,3,2,1,0:T(8,128)(2,1)S(1)}, bf16[12,2,2,16,256]{4,3,2,1,0:T(8,128)(2,1)S(1)}, u32[]{:S(2)}, u32[]{:S(2)}) %collective-permute-start.11) | collective-permute-done | bytes 393248 | tf_op jit(solution)/shard_map/ppermute | solution.py:44
  123.2 5.2 %collective-permute-start.13 = (bf16[4,6,64,128]{3,2,1,0:T(8,128)(2,1)}, bf16[4,6,64,128]{3,2,1,0:T(8,128)(2,1)S(1)}, u32[]{:S(2)}, u32[]{:S(2)}) collective-permute-start(bf16[4,6,64,128]{3,2,1,0:T(8,128)(2,1)} %slice.90), channel_id=1, source_target_pairs={{0,2},{2,4},{4,6},{6,0},{1,3},{3,5},{5,7},{7,1},{8,10},{10,12},{12... | collective-permute-start | bytes 1179656 | tf_op jit(solution)/shard_map/ppermute | solution.py:23
  130.4 4.5 %collective-permute-done.13 = bf16[4,6,64,128]{3,2,1,0:T(8,128)(2,1)S(1)} collective-permute-done((bf16[4,6,64,128]{3,2,1,0:T(8,128)(2,1)}, bf16[4,6,64,128]{3,2,1,0:T(8,128)(2,1)S(1)}, u32[]{:S(2)}, u32[]{:S(2)}) %collective-permute-start.13) | collective-permute-done | bytes 393248 | tf_op jit(solution)/shard_map/ppermute | solution.py:23
  134.9 5.0 %collective-permute-done.12 = bf16[4,6,64,128]{3,2,1,0:T(8,128)(2,1)} collective-permute-done((bf16[4,6,64,128]{3,2,1,0:T(8,128)(2,1)}, bf16[4,6,64,128]{3,2,1,0:T(8,128)(2,1)}, u32[]{:S(2)}, u32[]{:S(2)}) %collective-permute-start.12) | collective-permute-done | bytes 393248 | tf_op jit(solution)/shard_map/ppermute | solution.py:23
  154.5 6.5 %collective-permute-start.18 = (bf16[12,4,128,256]{3,2,1,0:T(8,128)(2,1)S(1)}, bf16[12,4,128,256]{3,2,1,0:T(8,128)(2,1)}, u32[]{:S(2)}, u32[]{:S(2)}) collective-permute-start(bf16[12,4,128,256]{3,2,1,0:T(8,128)(2,1)S(1)} %bitcast_dynamic-update-slice_fusion), channel_id=1, source_target_pairs={{0,64},{64,0},{1,65},{65,1},{2,66},{66,2},{3,67},{67,3},{4,68},{68... | collective-permute-start | bytes 9437192 | tf_op jit(solution)/shard_map/ppermute | solution.py:44
  163.2 10.9 %collective-permute-done.19 = f32[2,128]{1,0:T(2,128)S(1)} collective-permute-done((f32[2,128]{1,0:T(2,128)S(1)}, f32[2,128]{1,0:T(2,128)S(1)}, u32[]{:S(2)}, u32[]{:S(2)}) %collective-permute-start.19) | collective-permute-done | bytes 1056 | tf_op jit(solution)/shard_map/ppermute | solution.py:59
  180.0 4.3 %copy.27 = bf16[6,4,64,1024]{3,1,2,0:T(4,128)(2,1)S(1)} copy(bf16[6,4,64,1024]{3,2,0,1:T(8,128)(2,1)} %bitcast.79) | data formatting | bytes 6291456
  188.2 4.2 %maximum_select_fusion = bf16[12,4,2,128,256]{4,3,2,1,0:T(8,128)(2,1)S(1)} fusion(bf16[12,4,1,128,256]{4,3,2,1,0:T(8,128)(2,1)S(1)} %bitcast.78, bf16[12,4,1,128,256]{4,3,2,1,0:T(8,128)(2,1)} %bitcast.18, pred[]{:T(512)S(6)} %eq.34), kind=kLoop, calls=%fused_computation.2 | loop fusion | flops 9437184 | bytes 12582913 | tf_op jit(solution)/shard_map/jit(_where)/select_n | solution.py:46
  195.1 6.3 %convert_add_fusion = (f32[4,32,9,256]{3,1,2,0:T(8,128)S(1)}, bf16[4,32,9,256]{3,1,2,0:T(8,128)(2,1)S(1)}) fusion(f32[256]{0:T(256)S(1)} %bitcast.101, f32[256]{0:T(256)S(1)} %bitcast.102, bf16[3,3,1024,256]{3,2,1,0:T(8,128)(2,1)S(1)} %bitcast.80, bf16[6,4,8,11,1024]{4,1,3,2,0:T(4,128)(2,1)S(1)} %fusion.1, pred[32,9]{0,1:T(8,128)(4,1)S(1)} %copy-done.12), kind=kOutput, calls=%fused_computation.17 | convolution fusion | flops 5438767104 | bytes 10815776 | tf_op jit(solution)/shard_map/conv_general_dilated | solution.py:105
  207.9 8.4 %collective-permute-done.22 = bf16[4,4,64,256]{3,2,1,0:T(8,128)(2,1)S(1)} collective-permute-done((bf16[4,4,64,256]{3,2,1,0:T(8,128)(2,1)S(1)}, bf16[4,4,64,256]{3,2,1,0:T(8,128)(2,1)S(1)}, u32[]{:S(2)}, u32[]{:S(2)}) %collective-permute-start.22) | collective-permute-done | bytes 524320 | tf_op jit(solution)/shard_map/ppermute | solution.py:23
  216.3 4.8 %collective-permute-start.23 = (bf16[4,4,64,128]{3,2,1,0:T(8,128)(2,1)S(1)}, bf16[4,4,64,128]{3,2,1,0:T(8,128)(2,1)S(1)}, u32[]{:S(2)}, u32[]{:S(2)}) collective-permute-start(bf16[4,4,64,128]{3,2,1,0:T(8,128)(2,1)S(1)} %slice.118), channel_id=1, source_target_pairs={{0,2},{2,4},{4,6},{6,0},{1,3},{3,5},{5,7},{7,1},{8,10},{10,12},{12... | collective-permute-start | bytes 786440 | tf_op jit(solution)/shard_map/ppermute | solution.py:23
  224.5 5.1 %collective-permute-done.21 = bf16[4,4,64,128]{3,2,1,0:T(8,128)(2,1)S(1)} collective-permute-done((bf16[4,4,64,128]{3,2,1,0:T(8,128)(2,1)S(1)}, bf16[4,4,64,128]{3,2,1,0:T(8,128)(2,1)S(1)}, u32[]{:S(2)}, u32[]{:S(2)}) %collective-permute-start.21) | collective-permute-done | bytes 262176 | tf_op jit(solution)/shard_map/ppermute | solution.py:23
  229.9 5.4 %collective-permute-start.25 = (bf16[1,4,64,1024]{3,2,1,0:T(8,128)(2,1)S(1)}, bf16[1,4,64,1024]{3,2,1,0:T(8,128)(2,1)S(1)}, u32[]{:S(2)}, u32[]{:S(2)}) collective-permute-start(bf16[1,4,64,1024]{3,2,1,0:T(8,128)(2,1)S(1)} %get-tuple-element.41), channel_id=1, source_target_pairs={{64,0},{128,64},{192,128},{256,192},{320,256},{384,320},{448,384},... | collective-permute-start | bytes 1572872 | tf_op jit(solution)/shard_map/ppermute | solution.py:18
  236.8 4.5 %collective-permute-start.24 = (bf16[1,4,64,1024]{3,2,1,0:T(8,128)(2,1)S(1)}, bf16[1,4,64,1024]{3,2,1,0:T(8,128)(2,1)S(1)}, u32[]{:S(2)}, u32[]{:S(2)}) collective-permute-start(bf16[1,4,64,1024]{3,2,1,0:T(8,128)(2,1)S(1)} %get-tuple-element.40), channel_id=1, source_target_pairs={{0,64},{64,128},{128,192},{192,256},{256,320},{320,384},{384,448},... | collective-permute-start | bytes 1572872 | tf_op jit(solution)/shard_map/ppermute | solution.py:15
  250.5 32.5 %collective-permute-done.26 = bf16[4,4,64,128]{3,2,1,0:T(8,128)(2,1)S(1)} collective-permute-done((bf16[4,4,64,128]{3,2,1,0:T(8,128)(2,1)S(1)}, bf16[4,4,64,128]{3,2,1,0:T(8,128)(2,1)S(1)}, u32[]{:S(2)}, u32[]{:S(2)}) %collective-permute-start.26) | collective-permute-done | bytes 262176 | tf_op jit(solution)/shard_map/ppermute | solution.py:140
  (117 shorter events, 88.6 us)
Async XLA Ops:
  1.5 33.6 %collective-permute-start.3 = (bf16[12,16,128]{2,1,0:T(8,128)(2,1)S(1)}, bf16[12,16,128]{2,1,0:T(8,128)(2,1)S(1)}, u32[]{:S(2)}, u32[]{:S(2)}) collective-permute-start(bf16[12,16,128]{2,1,0:T(8,128)(2,1)S(1)} %constant_dynamic-update-slice_fusion), channel_id=1, source_target_pairs={{0,1},{1,0},{2,3},{3,2},{4,5},{5,4},{6,7},{7,6},{8,9},{9,8},{10,11... | collective-permute-start | bytes 147464 | tf_op jit(solution)/shard_map/ppermute | solution.py:69
  7.6 84.6 %collective-permute-start.7 = (bf16[1,5,64,128]{3,2,1,0:T(8,128)(2,1)S(1)}, bf16[1,5,64,128]{3,2,1,0:T(8,128)(2,1)S(1)}, u32[]{:S(2)}, u32[]{:S(2)}) collective-permute-start(bf16[1,5,64,128]{3,2,1,0:T(8,128)(2,1)S(1)} %get-tuple-element.46), channel_id=1, source_target_pairs={{0,1},{1,0},{2,3},{3,2},{4,5},{5,4},{6,7},{7,6},{8,9},{9,8},{10,11... | collective-permute-start | bytes 245768 | tf_op jit(solution)/shard_map/ppermute | solution.py:72
  16.4 65.9 %collective-permute-start.5 = (bf16[1,5,64,128]{3,2,1,0:T(8,128)(2,1)S(1)}, bf16[1,5,64,128]{3,2,1,0:T(8,128)(2,1)S(1)}, u32[]{:S(2)}, u32[]{:S(2)}) collective-permute-start(bf16[1,5,64,128]{3,2,1,0:T(8,128)(2,1)S(1)} %get-tuple-element.47), channel_id=1, source_target_pairs={{0,1},{1,0},{2,3},{3,2},{4,5},{5,4},{6,7},{7,6},{8,9},{9,8},{10,11... | collective-permute-start | bytes 245768 | tf_op jit(solution)/shard_map/ppermute | solution.py:72
  22.6 46.4 %collective-permute-start.4 = (bf16[2,5,64,128]{3,2,1,0:T(8,128)(2,1)S(1)}, bf16[2,5,64,128]{3,2,1,0:T(8,128)(2,1)S(1)}, u32[]{:S(2)}, u32[]{:S(2)}) collective-permute-start(bf16[2,5,64,128]{3,2,1,0:T(8,128)(2,1)S(1)} %constant_dynamic-slice_fusion.1), channel_id=1, source_target_pairs={{0,1},{1,0},{2,3},{3,2},{4,5},{5,4},{6,7},{7,6},{8,9},{9,8},{10,11... | collective-permute-start | bytes 491528 | tf_op jit(solution)/shard_map/ppermute | solution.py:68
  32.3 15.8 %collective-permute-start.1 = (bf16[4,1,64,128]{3,2,1,0:T(8,128)(2,1)S(1)}, bf16[4,1,64,128]{3,2,1,0:T(8,128)(2,1)S(1)}, u32[]{:S(2)}, u32[]{:S(2)}) collective-permute-start(bf16[4,1,64,128]{3,2,1,0:T(8,128)(2,1)S(1)} %get-tuple-element.49), channel_id=1, source_target_pairs={{8,0},{16,8},{24,16},{32,24},{40,32},{48,40},{56,48},{9,1},{17,9},... | collective-permute-start | bytes 196616 | tf_op jit(solution)/shard_map/ppermute | solution.py:18
  35.1 18.8 %collective-permute-start = (bf16[4,1,64,128]{3,2,1,0:T(8,128)(2,1)S(1)}, bf16[4,1,64,128]{3,2,1,0:T(8,128)(2,1)S(1)}, u32[]{:S(2)}, u32[]{:S(2)}) collective-permute-start(bf16[4,1,64,128]{3,2,1,0:T(8,128)(2,1)S(1)} %get-tuple-element.50), channel_id=1, source_target_pairs={{0,8},{8,16},{16,24},{24,32},{32,40},{40,48},{48,56},{1,9},{9,17},... | collective-permute-start | bytes 196616 | tf_op jit(solution)/shard_map/ppermute | solution.py:15
  48.1 20.8 %collective-permute-start.2 = (bf16[4,1,64,128]{3,2,1,0:T(8,128)(2,1)S(1)}, bf16[4,1,64,128]{3,2,1,0:T(8,128)(2,1)S(1)}, u32[]{:S(2)}, u32[]{:S(2)}) collective-permute-start(bf16[4,1,64,128]{3,2,1,0:T(8,128)(2,1)S(1)} %get-tuple-element.48), channel_id=1, source_target_pairs={{1,8},{9,16},{17,24},{25,32},{33,40},{41,48},{49,56},{8,1},{16,9},... | collective-permute-start | bytes 196616 | tf_op jit(solution)/shard_map/ppermute | solution.py:65
  69.0 13.3 %collective-permute-start.6 = (bf16[12,16,256]{2,1,0:T(8,128)(2,1)S(1)}, bf16[12,16,256]{2,1,0:T(8,128)(2,1)S(1)}, u32[]{:S(2)}, u32[]{:S(2)}) collective-permute-start(bf16[12,16,256]{2,1,0:T(8,128)(2,1)S(1)} %maximum_select_fusion.7), channel_id=1, source_target_pairs={{0,32},{8,40},{16,48},{24,56},{32,0},{40,8},{48,16},{56,24},{1,33}... | collective-permute-start | bytes 294920 | tf_op jit(solution)/shard_map/ppermute | solution.py:44
  82.3 9.8 %collective-permute-start.8 = (bf16[12,2,16,256]{3,2,1,0:T(8,128)(2,1)S(1)}, bf16[12,2,16,256]{3,2,1,0:T(8,128)(2,1)S(1)}, u32[]{:S(2)}, u32[]{:S(2)}) collective-permute-start(bf16[12,2,16,256]{3,2,1,0:T(8,128)(2,1)S(1)} %maximum_select_fusion.6), channel_id=1, source_target_pairs={{0,16},{8,24},{16,0},{24,8},{32,48},{40,56},{48,32},{56,40},{1,17}... | collective-permute-start | bytes 589832 | tf_op jit(solution)/shard_map/ppermute | solution.py:44
  93.5 21.7 %collective-permute-start.10 = (bf16[4,6,64,256]{3,2,1,0:T(8,128)(2,1)S(1)}, bf16[4,6,64,256]{3,2,1,0:T(8,128)(2,1)S(1)}, u32[]{:S(2)}, u32[]{:S(2)}) collective-permute-start(bf16[4,6,64,256]{3,2,1,0:T(8,128)(2,1)S(1)} %get-tuple-element.36), channel_id=1, source_target_pairs={{0,6},{2,0},{4,2},{6,4},{1,7},{3,1},{5,3},{7,5},{8,14},{10,8},{12,... | collective-permute-start | bytes 2359304 | tf_op jit(solution)/shard_map/ppermute | solution.py:23
  96.0 20.2 %collective-permute-start.9 = (bf16[4,6,64,256]{3,2,1,0:T(8,128)(2,1)S(1)}, bf16[4,6,64,256]{3,2,1,0:T(8,128)(2,1)S(1)}, u32[]{:S(2)}, u32[]{:S(2)}) collective-permute-start(bf16[4,6,64,256]{3,2,1,0:T(8,128)(2,1)S(1)} %get-tuple-element.36), channel_id=1, source_target_pairs={{0,2},{2,4},{4,6},{6,0},{1,3},{3,5},{5,7},{7,1},{8,10},{10,12},{12... | collective-permute-start | bytes 2359304 | tf_op jit(solution)/shard_map/ppermute | solution.py:23
  100.0 11.5 %collective-permute-start.11 = (bf16[12,2,2,16,256]{4,3,2,1,0:T(8,128)(2,1)S(1)}, bf16[12,2,2,16,256]{4,3,2,1,0:T(8,128)(2,1)S(1)}, u32[]{:S(2)}, u32[]{:S(2)}) collective-permute-start(bf16[12,2,2,16,256]{4,3,2,1,0:T(8,128)(2,1)S(1)} %maximum_select_fusion.4), channel_id=1, source_target_pairs={{0,8},{8,0},{16,24},{24,16},{32,40},{40,32},{48,56},{56,48},{1,9},... | collective-permute-start | bytes 1179656 | tf_op jit(solution)/shard_map/ppermute | solution.py:44
  116.2 23.8 %collective-permute-start.15 = (bf16[12,128,256]{2,1,0:T(8,128)(2,1)S(1)}, bf16[12,128,256]{2,1,0:T(8,128)(2,1)}, u32[]{:S(2)}, u32[]{:S(2)}) collective-permute-start(bf16[12,128,256]{2,1,0:T(8,128)(2,1)S(1)} %bitcast.82), channel_id=1, source_target_pairs={{0,384},{128,0},{256,128},{384,256},{1,385},{129,1},{257,129},{385... | collective-permute-start | bytes 2359304 | tf_op jit(solution)/shard_map/ppermute | solution.py:23
  118.3 21.7 %collective-permute-start.14 = (bf16[12,128,256]{2,1,0:T(8,128)(2,1)S(1)}, bf16[12,128,256]{2,1,0:T(8,128)(2,1)S(1)}, u32[]{:S(2)}, u32[]{:S(2)}) collective-permute-start(bf16[12,128,256]{2,1,0:T(8,128)(2,1)S(1)} %bitcast.83), channel_id=1, source_target_pairs={{0,128},{128,256},{256,384},{384,0},{1,129},{129,257},{257,385},{3... | collective-permute-start | bytes 2359304 | tf_op jit(solution)/shard_map/ppermute | solution.py:23
  123.2 11.7 %collective-permute-start.13 = (bf16[4,6,64,128]{3,2,1,0:T(8,128)(2,1)}, bf16[4,6,64,128]{3,2,1,0:T(8,128)(2,1)S(1)}, u32[]{:S(2)}, u32[]{:S(2)}) collective-permute-start(bf16[4,6,64,128]{3,2,1,0:T(8,128)(2,1)} %slice.90), channel_id=1, source_target_pairs={{0,2},{2,4},{4,6},{6,0},{1,3},{3,5},{5,7},{7,1},{8,10},{10,12},{12... | collective-permute-start | bytes 1179656 | tf_op jit(solution)/shard_map/ppermute | solution.py:23
  128.4 11.6 %collective-permute-start.12 = (bf16[4,6,64,128]{3,2,1,0:T(8,128)(2,1)}, bf16[4,6,64,128]{3,2,1,0:T(8,128)(2,1)}, u32[]{:S(2)}, u32[]{:S(2)}) collective-permute-start(bf16[4,6,64,128]{3,2,1,0:T(8,128)(2,1)} %slice.89), channel_id=1, source_target_pairs={{0,6},{2,0},{4,2},{6,4},{1,7},{3,1},{5,3},{7,5},{8,14},{10,8},{12,... | collective-permute-start | bytes 1179656 | tf_op jit(solution)/shard_map/ppermute | solution.py:23
  154.5 33.7 %collective-permute-start.18 = (bf16[12,4,128,256]{3,2,1,0:T(8,128)(2,1)S(1)}, bf16[12,4,128,256]{3,2,1,0:T(8,128)(2,1)}, u32[]{:S(2)}, u32[]{:S(2)}) collective-permute-start(bf16[12,4,128,256]{3,2,1,0:T(8,128)(2,1)S(1)} %bitcast_dynamic-update-slice_fusion), channel_id=1, source_target_pairs={{0,64},{64,0},{1,65},{65,1},{2,66},{66,2},{3,67},{67,3},{4,68},{68... | collective-permute-start | bytes 9437192 | tf_op jit(solution)/shard_map/ppermute | solution.py:44
  161.1 13.0 %collective-permute-start.19 = (f32[2,128]{1,0:T(2,128)S(1)}, f32[2,128]{1,0:T(2,128)S(1)}, u32[]{:S(2)}, u32[]{:S(2)}) collective-permute-start(f32[2,128]{1,0:T(2,128)S(1)} %pad_maximum_fusion.1), channel_id=1, source_target_pairs={{0,1},{1,0},{2,3},{3,2},{4,5},{5,4},{6,7},{7,6},{8,9},{9,8},{10,11... | collective-permute-start | bytes 3080 | tf_op jit(solution)/shard_map/ppermute | solution.py:59
  202.1 14.1 %collective-permute-start.22 = (bf16[4,4,64,256]{3,2,1,0:T(8,128)(2,1)S(1)}, bf16[4,4,64,256]{3,2,1,0:T(8,128)(2,1)S(1)}, u32[]{:S(2)}, u32[]{:S(2)}) collective-permute-start(bf16[4,4,64,256]{3,2,1,0:T(8,128)(2,1)S(1)} %bitcast.89), channel_id=1, source_target_pairs={{0,2},{2,4},{4,6},{6,0},{1,3},{3,5},{5,7},{7,1},{8,10},{10,12},{12... | collective-permute-start | bytes 1572872 | tf_op jit(solution)/shard_map/ppermute | solution.py:23
  205.7 15.4 %collective-permute-start.20 = (bf16[4,4,64,256]{3,2,1,0:T(8,128)(2,1)S(1)}, bf16[4,4,64,256]{3,2,1,0:T(8,128)(2,1)S(1)}, u32[]{:S(2)}, u32[]{:S(2)}) collective-permute-start(bf16[4,4,64,256]{3,2,1,0:T(8,128)(2,1)S(1)} %bitcast.90), channel_id=1, source_target_pairs={{0,6},{2,0},{4,2},{6,4},{1,7},{3,1},{5,3},{7,5},{8,14},{10,8},{12,... | collective-permute-start | bytes 1572872 | tf_op jit(solution)/shard_map/ppermute | solution.py:23
  216.3 13.3 %collective-permute-start.23 = (bf16[4,4,64,128]{3,2,1,0:T(8,128)(2,1)S(1)}, bf16[4,4,64,128]{3,2,1,0:T(8,128)(2,1)S(1)}, u32[]{:S(2)}, u32[]{:S(2)}) collective-permute-start(bf16[4,4,64,128]{3,2,1,0:T(8,128)(2,1)S(1)} %slice.118), channel_id=1, source_target_pairs={{0,2},{2,4},{4,6},{6,0},{1,3},{3,5},{5,7},{7,1},{8,10},{10,12},{12... | collective-permute-start | bytes 786440 | tf_op jit(solution)/shard_map/ppermute | solution.py:23
  229.9 15.1 %collective-permute-start.25 = (bf16[1,4,64,1024]{3,2,1,0:T(8,128)(2,1)S(1)}, bf16[1,4,64,1024]{3,2,1,0:T(8,128)(2,1)S(1)}, u32[]{:S(2)}, u32[]{:S(2)}) collective-permute-start(bf16[1,4,64,1024]{3,2,1,0:T(8,128)(2,1)S(1)} %get-tuple-element.41), channel_id=1, source_target_pairs={{64,0},{128,64},{192,128},{256,192},{320,256},{384,320},{448,384},... | collective-permute-start | bytes 1572872 | tf_op jit(solution)/shard_map/ppermute | solution.py:18
  236.8 10.6 %collective-permute-start.24 = (bf16[1,4,64,1024]{3,2,1,0:T(8,128)(2,1)S(1)}, bf16[1,4,64,1024]{3,2,1,0:T(8,128)(2,1)S(1)}, u32[]{:S(2)}, u32[]{:S(2)}) collective-permute-start(bf16[1,4,64,1024]{3,2,1,0:T(8,128)(2,1)S(1)} %get-tuple-element.40), channel_id=1, source_target_pairs={{0,64},{64,128},{128,192},{192,256},{256,320},{320,384},{384,448},... | collective-permute-start | bytes 1572872 | tf_op jit(solution)/shard_map/ppermute | solution.py:15
  248.3 34.7 %collective-permute-start.26 = (bf16[4,4,64,128]{3,2,1,0:T(8,128)(2,1)S(1)}, bf16[4,4,64,128]{3,2,1,0:T(8,128)(2,1)S(1)}, u32[]{:S(2)}, u32[]{:S(2)}) collective-permute-start(bf16[4,4,64,128]{3,2,1,0:T(8,128)(2,1)S(1)} %get-tuple-element.44), channel_id=1, source_target_pairs={{0,1},{1,0},{2,3},{3,2},{4,5},{5,4},{6,7},{7,6},{8,9},{9,8},{10,11... | collective-permute-start | bytes 786440 | tf_op jit(solution)/shard_map/ppermute | solution.py:140
  (16 other events, 183.3 us)

commit v12 on v10

--- a/solution.py
+++ b/solution.py
@@ -80,7 +80,6 @@
     cut = pair.shape[3] // 2
     far_low = ring_shift(from_right[..., :cut], "cx", ring, -1)
     far_high = ring_shift(from_left[..., cut:], "cx", ring, 1)
-    far_low, far_high, w_left, w_right = lax.optimization_barrier((far_low, far_high, w_left, w_right))
     w_cut = w_block.shape[1] // 2
     w_far_low = ring_shift(w_right[:, :w_cut], "fy", fy_n, -1)
     w_far_high = ring_shift(w_left[:, w_cut:], "fy", fy_n, 1)

time: 269 us -> 275 us (1.022)
  starting transfers between devices: 113 us -> 117 us
  waiting for transfers between devices: 107 us -> 111 us
    ppermute x12, waiting for transfers between devices: 30.5 us -> 39 us  [ring_shift(): lax.ppermute(block, axis, [(i, (i + step) % count) for i in range(count)])]
    ppermute x1, waiting for transfers between devices: 8.51 us -> 5.14 us  [body(): biases = ordered_pair(biases, lax.ppermute(biases, 'cz', SWAP), high, 1)]
    ppermute x1, starting transfers between devices: 4.28 us -> 7.05 us  [body(): returned = lax.ppermute(given, 'cz', SWAP)]
where the time goes in v12:
time: 275 us; the launch traced here: 274 us
  starting transfers between devices  117 us (43%)
  waiting for transfers between devices  111 us (40%)
  local copies, waits for them, and re-layouts  26.9 us (10%)
  other arithmetic  10 us (4%)
  matrix products  8.51 us (3%)
    ppermute x12, waiting for transfers between devices, ring_shift(): lax.ppermute(block, axis, [(i, (i + step) % count) for i in range(count)])  39 us
    ppermute x12, starting transfers between devices, ring_shift(): lax.ppermute(block, axis, [(i, (i + step) % count) for i in range(count)])  33.8 us
    ppermute x4, starting transfers between devices, xor_stack(): other = lax.ppermute(block, axis, [(i, i ^ bit) for i in range(count)])  28.6 us
    ppermute x1, waiting for transfers between devices, body(): returned = lax.ppermute(given, 'cz', SWAP)  27.8 us
    ppermute x4, waiting for transfers between devices, xor_stack(): other = lax.ppermute(block, axis, [(i, i ^ bit) for i in range(count)])  14.6 us
    ppermute x1, starting transfers between devices, body(): w_block = ordered_pair(weight, lax.ppermute(weight, 'cz', SWAP), high, 2)  13.6 us
    ppermute x2, waiting for transfers between devices, shift_halo(): lax.ppermute(lax.slice_in_dim(block, block.shape[dim] - width, None, axis...  12.9 us
    unnamed x34, local copies, waits for them, and re-layouts  12.2 us
  transfers between devices with their start and end apart: 25, of which 16 were waited for; matrix products, arithmetic and copies ran while one was open for 10% of the time, Pallas kernels for 0%

profile of v12, /device:TPU:87, one launch (start us, length us, event | category | flops | bytes accessed | tf_op | source)
XLA Modules:
  0.0 274.0 jit_solution(16341725912331215671)
XLA Ops:
  1.5 13.6 %collective-permute-start.4 = (bf16[12,16,128]{2,1,0:T(8,128)(2,1)S(1)}, bf16[12,16,128]{2,1,0:T(8,128)(2,1)S(1)}, u32[]{:S(2)}, u32[]{:S(2)}) collective-permute-start(bf16[12,16,128]{2,1,0:T(8,128)(2,1)S(1)} %constant_dynamic-update-slice_fusion), channel_id=1, source_target_pairs={{0,1},{1,0},{2,3},{3,2},{4,5},{5,4},{6,7},{7,6},{8,9},{9,8},{10,11... | collective-permute-start | bytes 147464 | tf_op jit(solution)/shard_map/ppermute | solution.py:67
  19.0 11.6 %collective-permute-start.3 = (bf16[4,1,64,128]{3,2,1,0:T(8,128)(2,1)S(1)}, bf16[4,1,64,128]{3,2,1,0:T(8,128)(2,1)S(1)}, u32[]{:S(2)}, u32[]{:S(2)}) collective-permute-start(bf16[4,1,64,128]{3,2,1,0:T(8,128)(2,1)S(1)} %get-tuple-element.30), channel_id=1, source_target_pairs={{1,8},{9,16},{17,24},{25,32},{33,40},{41,48},{49,56},{8,1},{16,9},... | collective-permute-start | bytes 196616 | tf_op jit(solution)/shard_map/ppermute | solution.py:66
  36.0 7.4 %collective-permute-done.1 = bf16[4,1,64,128]{3,2,1,0:T(8,128)(2,1)S(1)} collective-permute-done((bf16[4,1,64,128]{3,2,1,0:T(8,128)(2,1)S(1)}, bf16[4,1,64,128]{3,2,1,0:T(8,128)(2,1)S(1)}, u32[]{:S(2)}, u32[]{:S(2)}) %collective-permute-start.1) | collective-permute-done | bytes 65568 | tf_op jit(solution)/shard_map/ppermute | solution.py:18
  43.4 11.2 %collective-permute-done = bf16[4,1,64,128]{3,2,1,0:T(8,128)(2,1)S(1)} collective-permute-done((bf16[4,1,64,128]{3,2,1,0:T(8,128)(2,1)S(1)}, bf16[4,1,64,128]{3,2,1,0:T(8,128)(2,1)S(1)}, u32[]{:S(2)}, u32[]{:S(2)}) %collective-permute-start) | collective-permute-done | bytes 65568 | tf_op jit(solution)/shard_map/ppermute | solution.py:15
  56.7 8.2 %collective-permute-start.7 = (bf16[12,16,256]{2,1,0:T(8,128)(2,1)S(1)}, bf16[12,16,256]{2,1,0:T(8,128)(2,1)S(1)}, u32[]{:S(2)}, u32[]{:S(2)}) collective-permute-start(bf16[12,16,256]{2,1,0:T(8,128)(2,1)S(1)} %maximum_select_fusion.8), channel_id=1, source_target_pairs={{0,32},{8,40},{16,48},{24,56},{32,0},{40,8},{48,16},{56,24},{1,33}... | collective-permute-start | bytes 294920 | tf_op jit(solution)/shard_map/ppermute | solution.py:44
  68.8 4.0 %collective-permute-start.5 = (bf16[4,6,64,256]{3,2,1,0:T(8,128)(2,1)S(1)}, bf16[4,6,64,256]{3,2,1,0:T(8,128)(2,1)S(1)}, u32[]{:S(2)}, u32[]{:S(2)}) collective-permute-start(bf16[4,6,64,256]{3,2,1,0:T(8,128)(2,1)S(1)} %get-tuple-element.20), channel_id=1, source_target_pairs={{0,2},{2,4},{4,6},{6,0},{1,3},{3,5},{5,7},{7,1},{8,10},{10,12},{12... | collective-permute-start | bytes 2359304 | tf_op jit(solution)/shard_map/ppermute | solution.py:23
  74.8 5.6 %collective-permute-done.8 = bf16[12,2,16,256]{3,2,1,0:T(8,128)(2,1)S(1)} collective-permute-done((bf16[12,2,16,256]{3,2,1,0:T(8,128)(2,1)S(1)}, bf16[12,2,16,256]{3,2,1,0:T(8,128)(2,1)S(1)}, u32[]{:S(2)}, u32[]{:S(2)}) %collective-permute-start.8) | collective-permute-done | bytes 196640 | tf_op jit(solution)/shard_map/ppermute | solution.py:44
  80.5 13.6 %collective-permute-start.9 = (bf16[12,2,2,16,256]{4,3,1,0,2:T(8,128)(2,1)S(1)}, bf16[12,2,2,16,256]{4,3,1,0,2:T(8,128)(2,1)S(1)}, u32[]{:S(2)}, u32[]{:S(2)}) collective-permute-start(bf16[12,2,2,16,256]{4,3,1,0,2:T(8,128)(2,1)S(1)} %maximum_select_fusion.5), channel_id=1, source_target_pairs={{0,8},{8,0},{16,24},{24,16},{32,40},{40,32},{48,56},{56,48},{1,9},... | collective-permute-start | bytes 1179656 | tf_op jit(solution)/shard_map/ppermute | solution.py:44
  94.2 9.0 %collective-permute-done.9 = bf16[12,2,2,16,256]{4,3,1,0,2:T(8,128)(2,1)S(1)} collective-permute-done((bf16[12,2,2,16,256]{4,3,1,0,2:T(8,128)(2,1)S(1)}, bf16[12,2,2,16,256]{4,3,1,0,2:T(8,128)(2,1)S(1)}, u32[]{:S(2)}, u32[]{:S(2)}) %collective-permute-start.9) | collective-permute-done | bytes 393248 | tf_op jit(solution)/shard_map/ppermute | solution.py:44
  108.7 14.7 %collective-permute-done.14 = bf16[12,128,256]{2,1,0:T(8,128)(2,1)S(1)} collective-permute-done((bf16[12,128,256]{2,1,0:T(8,128)(2,1)S(1)}, bf16[12,128,256]{2,1,0:T(8,128)(2,1)S(1)}, u32[]{:S(2)}, u32[]{:S(2)}) %collective-permute-start.14) | collective-permute-done | bytes 786464 | tf_op jit(solution)/shard_map/ppermute | solution.py:23
  138.1 4.9 %collective-permute-start.16 = (bf16[12,4,128,256]{3,2,1,0:T(8,128)(2,1)S(1)}, bf16[12,4,128,256]{3,2,1,0:T(8,128)(2,1)}, u32[]{:S(2)}, u32[]{:S(2)}) collective-permute-start(bf16[12,4,128,256]{3,2,1,0:T(8,128)(2,1)S(1)} %bitcast_dynamic-update-slice_fusion), channel_id=1, source_target_pairs={{0,64},{64,0},{1,65},{65,1},{2,66},{66,2},{3,67},{67,3},{4,68},{68... | collective-permute-start | bytes 9437192 | tf_op jit(solution)/shard_map/ppermute | solution.py:44
  143.0 4.3 %collective-permute-start.17 = (f32[2,128]{1,0:T(2,128)S(1)}, f32[2,128]{1,0:T(2,128)S(1)}, u32[]{:S(2)}, u32[]{:S(2)}) collective-permute-start(f32[2,128]{1,0:T(2,128)S(1)} %pad_maximum_fusion.3), channel_id=1, source_target_pairs={{0,1},{1,0},{2,3},{3,2},{4,5},{5,4},{6,7},{7,6},{8,9},{9,8},{10,11... | collective-permute-start | bytes 3080 | tf_op jit(solution)/shard_map/ppermute | solution.py:59
  150.9 5.1 %collective-permute-done.17 = f32[2,128]{1,0:T(2,128)S(1)} collective-permute-done((f32[2,128]{1,0:T(2,128)S(1)}, f32[2,128]{1,0:T(2,128)S(1)}, u32[]{:S(2)}, u32[]{:S(2)}) %collective-permute-start.17) | collective-permute-done | bytes 1056 | tf_op jit(solution)/shard_map/ppermute | solution.py:59
  162.8 5.6 %collective-permute-done.11 = bf16[4,6,64,128]{3,2,1,0:T(8,128)(2,1)S(1)} collective-permute-done((bf16[4,6,64,128]{3,2,1,0:T(8,128)(2,1)S(1)}, bf16[4,6,64,128]{3,2,1,0:T(8,128)(2,1)S(1)}, u32[]{:S(2)}, u32[]{:S(2)}) %collective-permute-start.11) | collective-permute-done | bytes 393248 | tf_op jit(solution)/shard_map/ppermute | solution.py:23
  170.3 4.3 %copy.32 = bf16[6,4,64,1024]{3,1,2,0:T(4,128)(2,1)S(1)} copy(bf16[6,4,64,1024]{3,2,0,1:T(8,128)(2,1)} %bitcast.83) | data formatting | bytes 6291456
  178.5 4.2 %maximum_select_fusion = bf16[12,4,2,128,256]{4,3,2,1,0:T(8,128)(2,1)S(1)} fusion(bf16[12,4,1,128,256]{4,3,2,1,0:T(8,128)(2,1)S(1)} %bitcast.82, bf16[12,4,1,128,256]{4,3,2,1,0:T(8,128)(2,1)} %bitcast.20, pred[]{:T(512)S(6)} %eq.34), kind=kLoop, calls=%fused_computation.2 | loop fusion | flops 9437184 | bytes 12582913 | tf_op jit(solution)/shard_map/jit(_where)/select_n | solution.py:46
  185.5 6.3 %convert_add_fusion = (f32[4,32,9,256]{3,1,2,0:T(8,128)S(1)}, bf16[4,32,9,256]{3,1,2,0:T(8,128)(2,1)S(1)}) fusion(f32[256]{0:T(256)S(1)} %bitcast.107, f32[256]{0:T(256)S(1)} %bitcast.108, bf16[3,3,1024,256]{3,2,1,0:T(8,128)(2,1)S(1)} %bitcast.84, bf16[6,4,8,11,1024]{4,1,3,2,0:T(4,128)(2,1)S(1)} %fusion.1, pred[32,9]{0,1:T(8,128)(4,1)S(1)} %copy-done.11), kind=kOutput, calls=%fused_computation.17 | convolution fusion | flops 5438767104 | bytes 10815776 | tf_op jit(solution)/shard_map/conv_general_dilated | solution.py:97
  198.0 7.7 %collective-permute-done.20 = bf16[4,4,64,256]{3,2,1,0:T(8,128)(2,1)S(1)} collective-permute-done((bf16[4,4,64,256]{3,2,1,0:T(8,128)(2,1)S(1)}, bf16[4,4,64,256]{3,2,1,0:T(8,128)(2,1)S(1)}, u32[]{:S(2)}, u32[]{:S(2)}) %collective-permute-start.20) | collective-permute-done | bytes 524320 | tf_op jit(solution)/shard_map/ppermute | solution.py:23
  205.8 4.5 %collective-permute-start.21 = (bf16[4,4,64,128]{3,2,1,0:T(8,128)(2,1)S(1)}, bf16[4,4,64,128]{3,2,1,0:T(8,128)(2,1)S(1)}, u32[]{:S(2)}, u32[]{:S(2)}) collective-permute-start(bf16[4,4,64,128]{3,2,1,0:T(8,128)(2,1)S(1)} %slice.108), channel_id=1, source_target_pairs={{0,2},{2,4},{4,6},{6,0},{1,3},{3,5},{5,7},{7,1},{8,10},{10,12},{12... | collective-permute-start | bytes 786440 | tf_op jit(solution)/shard_map/ppermute | solution.py:23
  213.7 5.1 %collective-permute-done.19 = bf16[4,4,64,128]{3,2,1,0:T(8,128)(2,1)S(1)} collective-permute-done((bf16[4,4,64,128]{3,2,1,0:T(8,128)(2,1)S(1)}, bf16[4,4,64,128]{3,2,1,0:T(8,128)(2,1)S(1)}, u32[]{:S(2)}, u32[]{:S(2)}) %collective-permute-start.19) | collective-permute-done | bytes 262176 | tf_op jit(solution)/shard_map/ppermute | solution.py:23
  219.1 6.3 %collective-permute-start.23 = (bf16[1,4,64,1024]{3,2,1,0:T(8,128)(2,1)S(1)}, bf16[1,4,64,1024]{3,2,1,0:T(8,128)(2,1)S(1)}, u32[]{:S(2)}, u32[]{:S(2)}) collective-permute-start(bf16[1,4,64,1024]{3,2,1,0:T(8,128)(2,1)S(1)} %get-tuple-element.25), channel_id=1, source_target_pairs={{64,0},{128,64},{192,128},{256,192},{320,256},{384,320},{448,384},... | collective-permute-start | bytes 1572872 | tf_op jit(solution)/shard_map/ppermute | solution.py:18
  226.9 4.3 %collective-permute-start.22 = (bf16[1,4,64,1024]{3,2,1,0:T(8,128)(2,1)S(1)}, bf16[1,4,64,1024]{3,2,1,0:T(8,128)(2,1)S(1)}, u32[]{:S(2)}, u32[]{:S(2)}) collective-permute-start(bf16[1,4,64,1024]{3,2,1,0:T(8,128)(2,1)S(1)} %get-tuple-element.24), channel_id=1, source_target_pairs={{0,64},{64,128},{128,192},{192,256},{256,320},{320,384},{384,448},... | collective-permute-start | bytes 1572872 | tf_op jit(solution)/shard_map/ppermute | solution.py:15
  238.3 7.0 %collective-permute-start.24 = (bf16[4,4,64,128]{3,2,1,0:T(8,128)(2,1)S(1)}, bf16[4,4,64,128]{3,2,1,0:T(8,128)(2,1)S(1)}, u32[]{:S(2)}, u32[]{:S(2)}) collective-permute-start(bf16[4,4,64,128]{3,2,1,0:T(8,128)(2,1)S(1)} %get-tuple-element.28), channel_id=1, source_target_pairs={{0,1},{1,0},{2,3},{3,2},{4,5},{5,4},{6,7},{7,6},{8,9},{9,8},{10,11... | collective-permute-start | bytes 786440 | tf_op jit(solution)/shard_map/ppermute | solution.py:132
  245.3 27.8 %collective-permute-done.24 = bf16[4,4,64,128]{3,2,1,0:T(8,128)(2,1)S(1)} collective-permute-done((bf16[4,4,64,128]{3,2,1,0:T(8,128)(2,1)S(1)}, bf16[4,4,64,128]{3,2,1,0:T(8,128)(2,1)S(1)}, u32[]{:S(2)}, u32[]{:S(2)}) %collective-permute-start.24) | collective-permute-done | bytes 262176 | tf_op jit(solution)/shard_map/ppermute | solution.py:132
  (111 shorter events, 76.5 us)
Async XLA Ops:
  1.5 34.5 %collective-permute-start.4 = (bf16[12,16,128]{2,1,0:T(8,128)(2,1)S(1)}, bf16[12,16,128]{2,1,0:T(8,128)(2,1)S(1)}, u32[]{:S(2)}, u32[]{:S(2)}) collective-permute-start(bf16[12,16,128]{2,1,0:T(8,128)(2,1)S(1)} %constant_dynamic-update-slice_fusion), channel_id=1, source_target_pairs={{0,1},{1,0},{2,3},{3,2},{4,5},{5,4},{6,7},{7,6},{8,9},{9,8},{10,11... | collective-permute-start | bytes 147464 | tf_op jit(solution)/shard_map/ppermute | solution.py:67
  16.1 40.6 %collective-permute-start.2 = (bf16[4,5,64,128]{3,2,1,0:T(8,128)(2,1)S(1)}, bf16[4,5,64,128]{3,2,1,0:T(8,128)(2,1)S(1)}, u32[]{:S(2)}, u32[]{:S(2)}) collective-permute-start(bf16[4,5,64,128]{3,2,1,0:T(8,128)(2,1)S(1)} %constant_dynamic-slice_fusion.4), channel_id=1, source_target_pairs={{0,1},{1,0},{2,3},{3,2},{4,5},{5,4},{6,7},{7,6},{8,9},{9,8},{10,11... | collective-permute-start | bytes 983048 | tf_op jit(solution)/shard_map/ppermute | solution.py:62
  19.0 37.7 %collective-permute-start.3 = (bf16[4,1,64,128]{3,2,1,0:T(8,128)(2,1)S(1)}, bf16[4,1,64,128]{3,2,1,0:T(8,128)(2,1)S(1)}, u32[]{:S(2)}, u32[]{:S(2)}) collective-permute-start(bf16[4,1,64,128]{3,2,1,0:T(8,128)(2,1)S(1)} %get-tuple-element.30), channel_id=1, source_target_pairs={{1,8},{9,16},{17,24},{25,32},{33,40},{41,48},{49,56},{8,1},{16,9},... | collective-permute-start | bytes 196616 | tf_op jit(solution)/shard_map/ppermute | solution.py:66
  30.6 12.8 %collective-permute-start.1 = (bf16[4,1,64,128]{3,2,1,0:T(8,128)(2,1)S(1)}, bf16[4,1,64,128]{3,2,1,0:T(8,128)(2,1)S(1)}, u32[]{:S(2)}, u32[]{:S(2)}) collective-permute-start(bf16[4,1,64,128]{3,2,1,0:T(8,128)(2,1)S(1)} %get-tuple-element.31), channel_id=1, source_target_pairs={{8,0},{16,8},{24,16},{32,24},{40,32},{48,40},{56,48},{9,1},{17,9},... | collective-permute-start | bytes 196616 | tf_op jit(solution)/shard_map/ppermute | solution.py:18
  33.3 21.3 %collective-permute-start = (bf16[4,1,64,128]{3,2,1,0:T(8,128)(2,1)S(1)}, bf16[4,1,64,128]{3,2,1,0:T(8,128)(2,1)S(1)}, u32[]{:S(2)}, u32[]{:S(2)}) collective-permute-start(bf16[4,1,64,128]{3,2,1,0:T(8,128)(2,1)S(1)} %get-tuple-element.32), channel_id=1, source_target_pairs={{0,8},{8,16},{16,24},{24,32},{32,40},{40,48},{48,56},{1,9},{9,17},... | collective-permute-start | bytes 196616 | tf_op jit(solution)/shard_map/ppermute | solution.py:15
  56.7 16.1 %collective-permute-start.7 = (bf16[12,16,256]{2,1,0:T(8,128)(2,1)S(1)}, bf16[12,16,256]{2,1,0:T(8,128)(2,1)S(1)}, u32[]{:S(2)}, u32[]{:S(2)}) collective-permute-start(bf16[12,16,256]{2,1,0:T(8,128)(2,1)S(1)} %maximum_select_fusion.8), channel_id=1, source_target_pairs={{0,32},{8,40},{16,48},{24,56},{32,0},{40,8},{48,16},{56,24},{1,33}... | collective-permute-start | bytes 294920 | tf_op jit(solution)/shard_map/ppermute | solution.py:44
  66.3 37.0 %collective-permute-start.6 = (bf16[4,6,64,256]{3,2,1,0:T(8,128)(2,1)S(1)}, bf16[4,6,64,256]{3,2,1,0:T(8,128)(2,1)S(1)}, u32[]{:S(2)}, u32[]{:S(2)}) collective-permute-start(bf16[4,6,64,256]{3,2,1,0:T(8,128)(2,1)S(1)} %get-tuple-element.20), channel_id=1, source_target_pairs={{0,6},{2,0},{4,2},{6,4},{1,7},{3,1},{5,3},{7,5},{8,14},{10,8},{12,... | collective-permute-start | bytes 2359304 | tf_op jit(solution)/shard_map/ppermute | solution.py:23
  68.8 34.6 %collective-permute-start.5 = (bf16[4,6,64,256]{3,2,1,0:T(8,128)(2,1)S(1)}, bf16[4,6,64,256]{3,2,1,0:T(8,128)(2,1)S(1)}, u32[]{:S(2)}, u32[]{:S(2)}) collective-permute-start(bf16[4,6,64,256]{3,2,1,0:T(8,128)(2,1)S(1)} %get-tuple-element.20), channel_id=1, source_target_pairs={{0,2},{2,4},{4,6},{6,0},{1,3},{3,5},{5,7},{7,1},{8,10},{10,12},{12... | collective-permute-start | bytes 2359304 | tf_op jit(solution)/shard_map/ppermute | solution.py:23
  80.5 22.7 %collective-permute-start.9 = (bf16[12,2,2,16,256]{4,3,1,0,2:T(8,128)(2,1)S(1)}, bf16[12,2,2,16,256]{4,3,1,0,2:T(8,128)(2,1)S(1)}, u32[]{:S(2)}, u32[]{:S(2)}) collective-permute-start(bf16[12,2,2,16,256]{4,3,1,0,2:T(8,128)(2,1)S(1)} %maximum_select_fusion.5), channel_id=1, source_target_pairs={{0,8},{8,0},{16,24},{24,16},{32,40},{40,32},{48,56},{56,48},{1,9},... | collective-permute-start | bytes 1179656 | tf_op jit(solution)/shard_map/ppermute | solution.py:44
  103.4 20.1 %collective-permute-start.14 = (bf16[12,128,256]{2,1,0:T(8,128)(2,1)S(1)}, bf16[12,128,256]{2,1,0:T(8,128)(2,1)S(1)}, u32[]{:S(2)}, u32[]{:S(2)}) collective-permute-start(bf16[12,128,256]{2,1,0:T(8,128)(2,1)S(1)} %bitcast.86), channel_id=1, source_target_pairs={{0,128},{128,256},{256,384},{384,0},{1,129},{129,257},{257,385},{3... | collective-permute-start | bytes 2359304 | tf_op jit(solution)/shard_map/ppermute | solution.py:23
  106.3 20.1 %collective-permute-start.12 = (bf16[12,128,256]{2,1,0:T(8,128)(2,1)S(1)}, bf16[12,128,256]{2,1,0:T(8,128)(2,1)}, u32[]{:S(2)}, u32[]{:S(2)}) collective-permute-start(bf16[12,128,256]{2,1,0:T(8,128)(2,1)S(1)} %bitcast.87), channel_id=1, source_target_pairs={{0,384},{128,0},{256,128},{384,256},{1,385},{129,1},{257,129},{385... | collective-permute-start | bytes 2359304 | tf_op jit(solution)/shard_map/ppermute | solution.py:23
  123.4 10.7 %collective-permute-start.15 = (bf16[12,64,256]{2,1,0:T(8,128)(2,1)S(1)}, bf16[12,64,256]{2,1,0:T(8,128)(2,1)S(1)}, u32[]{:S(2)}, u32[]{:S(2)}) collective-permute-start(bf16[12,64,256]{2,1,0:T(8,128)(2,1)S(1)} %slice.101), channel_id=1, source_target_pairs={{0,128},{128,256},{256,384},{384,0},{1,129},{129,257},{257,385},{3... | collective-permute-start | bytes 1179656 | tf_op jit(solution)/shard_map/ppermute | solution.py:23
  127.4 10.4 %collective-permute-start.13 = (bf16[12,64,256]{2,1,0:T(8,128)(2,1)S(1)}, bf16[12,64,256]{2,1,0:T(8,128)(2,1)S(1)}, u32[]{:S(2)}, u32[]{:S(2)}) collective-permute-start(bf16[12,64,256]{2,1,0:T(8,128)(2,1)S(1)} %slice.100), channel_id=1, source_target_pairs={{0,384},{128,0},{256,128},{384,256},{1,385},{129,1},{257,129},{385... | collective-permute-start | bytes 1179656 | tf_op jit(solution)/shard_map/ppermute | solution.py:23
  138.1 40.5 %collective-permute-start.16 = (bf16[12,4,128,256]{3,2,1,0:T(8,128)(2,1)S(1)}, bf16[12,4,128,256]{3,2,1,0:T(8,128)(2,1)}, u32[]{:S(2)}, u32[]{:S(2)}) collective-permute-start(bf16[12,4,128,256]{3,2,1,0:T(8,128)(2,1)S(1)} %bitcast_dynamic-update-slice_fusion), channel_id=1, source_target_pairs={{0,64},{64,0},{1,65},{65,1},{2,66},{66,2},{3,67},{67,3},{4,68},{68... | collective-permute-start | bytes 9437192 | tf_op jit(solution)/shard_map/ppermute | solution.py:44
  143.0 13.0 %collective-permute-start.17 = (f32[2,128]{1,0:T(2,128)S(1)}, f32[2,128]{1,0:T(2,128)S(1)}, u32[]{:S(2)}, u32[]{:S(2)}) collective-permute-start(f32[2,128]{1,0:T(2,128)S(1)} %pad_maximum_fusion.3), channel_id=1, source_target_pairs={{0,1},{1,0},{2,3},{3,2},{4,5},{5,4},{6,7},{7,6},{8,9},{9,8},{10,11... | collective-permute-start | bytes 3080 | tf_op jit(solution)/shard_map/ppermute | solution.py:59
  148.4 13.5 %collective-permute-start.10 = (bf16[4,6,64,128]{3,2,1,0:T(8,128)(2,1)S(1)}, bf16[4,6,64,128]{3,2,1,0:T(8,128)(2,1)S(1)}, u32[]{:S(2)}, u32[]{:S(2)}) collective-permute-start(bf16[4,6,64,128]{3,2,1,0:T(8,128)(2,1)S(1)} %slice.77), channel_id=1, source_target_pairs={{0,6},{2,0},{4,2},{6,4},{1,7},{3,1},{5,3},{7,5},{8,14},{10,8},{12,... | collective-permute-start | bytes 1179656 | tf_op jit(solution)/shard_map/ppermute | solution.py:23
  157.1 11.3 %collective-permute-start.11 = (bf16[4,6,64,128]{3,2,1,0:T(8,128)(2,1)S(1)}, bf16[4,6,64,128]{3,2,1,0:T(8,128)(2,1)S(1)}, u32[]{:S(2)}, u32[]{:S(2)}) collective-permute-start(bf16[4,6,64,128]{3,2,1,0:T(8,128)(2,1)S(1)} %slice.78), channel_id=1, source_target_pairs={{0,2},{2,4},{4,6},{6,0},{1,3},{3,5},{5,7},{7,1},{8,10},{10,12},{12... | collective-permute-start | bytes 1179656 | tf_op jit(solution)/shard_map/ppermute | solution.py:23
  192.5 13.2 %collective-permute-start.20 = (bf16[4,4,64,256]{3,2,1,0:T(8,128)(2,1)S(1)}, bf16[4,4,64,256]{3,2,1,0:T(8,128)(2,1)S(1)}, u32[]{:S(2)}, u32[]{:S(2)}) collective-permute-start(bf16[4,4,64,256]{3,2,1,0:T(8,128)(2,1)S(1)} %bitcast.97), channel_id=1, source_target_pairs={{0,2},{2,4},{4,6},{6,0},{1,3},{3,5},{5,7},{7,1},{8,10},{10,12},{12... | collective-permute-start | bytes 1572872 | tf_op jit(solution)/shard_map/ppermute | solution.py:23
  195.8 14.5 %collective-permute-start.18 = (bf16[4,4,64,256]{3,2,1,0:T(8,128)(2,1)S(1)}, bf16[4,4,64,256]{3,2,1,0:T(8,128)(2,1)S(1)}, u32[]{:S(2)}, u32[]{:S(2)}) collective-permute-start(bf16[4,4,64,256]{3,2,1,0:T(8,128)(2,1)S(1)} %bitcast.98), channel_id=1, source_target_pairs={{0,6},{2,0},{4,2},{6,4},{1,7},{3,1},{5,3},{7,5},{8,14},{10,8},{12,... | collective-permute-start | bytes 1572872 | tf_op jit(solution)/shard_map/ppermute | solution.py:23
  205.8 13.0 %collective-permute-start.21 = (bf16[4,4,64,128]{3,2,1,0:T(8,128)(2,1)S(1)}, bf16[4,4,64,128]{3,2,1,0:T(8,128)(2,1)S(1)}, u32[]{:S(2)}, u32[]{:S(2)}) collective-permute-start(bf16[4,4,64,128]{3,2,1,0:T(8,128)(2,1)S(1)} %slice.108), channel_id=1, source_target_pairs={{0,2},{2,4},{4,6},{6,0},{1,3},{3,5},{5,7},{7,1},{8,10},{10,12},{12... | collective-permute-start | bytes 786440 | tf_op jit(solution)/shard_map/ppermute | solution.py:23
  210.4 8.3 %collective-permute-start.19 = (bf16[4,4,64,128]{3,2,1,0:T(8,128)(2,1)S(1)}, bf16[4,4,64,128]{3,2,1,0:T(8,128)(2,1)S(1)}, u32[]{:S(2)}, u32[]{:S(2)}) collective-permute-start(bf16[4,4,64,128]{3,2,1,0:T(8,128)(2,1)S(1)} %slice.107), channel_id=1, source_target_pairs={{0,6},{2,0},{4,2},{6,4},{1,7},{3,1},{5,3},{7,5},{8,14},{10,8},{12,... | collective-permute-start | bytes 786440 | tf_op jit(solution)/shard_map/ppermute | solution.py:23
  219.1 15.9 %collective-permute-start.23 = (bf16[1,4,64,1024]{3,2,1,0:T(8,128)(2,1)S(1)}, bf16[1,4,64,1024]{3,2,1,0:T(8,128)(2,1)S(1)}, u32[]{:S(2)}, u32[]{:S(2)}) collective-permute-start(bf16[1,4,64,1024]{3,2,1,0:T(8,128)(2,1)S(1)} %get-tuple-element.25), channel_id=1, source_target_pairs={{64,0},{128,64},{192,128},{256,192},{320,256},{384,320},{448,384},... | collective-permute-start | bytes 1572872 | tf_op jit(solution)/shard_map/ppermute | solution.py:18
  226.9 10.4 %collective-permute-start.22 = (bf16[1,4,64,1024]{3,2,1,0:T(8,128)(2,1)S(1)}, bf16[1,4,64,1024]{3,2,1,0:T(8,128)(2,1)S(1)}, u32[]{:S(2)}, u32[]{:S(2)}) collective-permute-start(bf16[1,4,64,1024]{3,2,1,0:T(8,128)(2,1)S(1)} %get-tuple-element.24), channel_id=1, source_target_pairs={{0,64},{64,128},{128,192},{192,256},{256,320},{320,384},{384,448},... | collective-permute-start | bytes 1572872 | tf_op jit(solution)/shard_map/ppermute | solution.py:15
  238.3 34.9 %collective-permute-start.24 = (bf16[4,4,64,128]{3,2,1,0:T(8,128)(2,1)S(1)}, bf16[4,4,64,128]{3,2,1,0:T(8,128)(2,1)S(1)}, u32[]{:S(2)}, u32[]{:S(2)}) collective-permute-start(bf16[4,4,64,128]{3,2,1,0:T(8,128)(2,1)S(1)} %get-tuple-element.28), channel_id=1, source_target_pairs={{0,1},{1,0},{2,3},{3,2},{4,5},{5,4},{6,7},{7,6},{8,9},{9,8},{10,11... | collective-permute-start | bytes 786440 | tf_op jit(solution)/shard_map/ppermute | solution.py:132
  (13 other events, 149.4 us)

commit v13 on v10

--- a/solution.py
+++ b/solution.py
@@ -82,8 +82,8 @@
     far_high = ring_shift(from_left[..., cut:], "cx", ring, 1)
     far_low, far_high, w_left, w_right = lax.optimization_barrier((far_low, far_high, w_left, w_right))
     w_cut = w_block.shape[1] // 2
-    w_far_low = ring_shift(w_right[:, :w_cut], "fy", fy_n, -1)
-    w_far_high = ring_shift(w_left[:, w_cut:], "fy", fy_n, 1)
+    w_far_low = ring_shift(w_block[:, :w_cut], "fy", fy_n, -2)
+    w_far_high = ring_shift(w_block[:, w_cut:], "fy", fy_n, 2)
     gathered = jnp.concatenate([pair, from_right, far_low, far_high, from_left], axis=3)
     me_fy = lax.axis_index("fy")
     rotate = lax.axis_index("cx")

time: 269 us -> 271 us (level)
    unnamed x34 -> x28, local copies, waits for them, and re-layouts: 13.2 us -> 12.4 us
  transfers between devices with their start and end apart: 25 -> 25, of which waited for: 16 -> 15; matrix products, arithmetic and copies ran while one was open for 10% -> 10% of each run, Pallas kernels for 0% -> 0%
where the time goes in v13:
time: 271 us; the launch traced here: 269 us
  starting transfers between devices  113 us (42%)
  waiting for transfers between devices  109 us (40%)
  local copies, waits for them, and re-layouts  27.4 us (10%)
  other arithmetic  10.9 us (4%)
  matrix products  8.5 us (3%)
    ppermute x12, starting transfers between devices, ring_shift(): lax.ppermute(block, axis, [(i, (i + step) % count) for i in range(count)])  34.6 us
    ppermute x12, waiting for transfers between devices, ring_shift(): lax.ppermute(block, axis, [(i, (i + step) % count) for i in range(count)])  32.3 us
    ppermute x1, waiting for transfers between devices, body(): returned = lax.ppermute(given, 'cz', SWAP)  29.6 us
    ppermute x4, starting transfers between devices, xor_stack(): other = lax.ppermute(block, axis, [(i, i ^ bit) for i in range(count)])  27.5 us
    ppermute x4, waiting for transfers between devices, xor_stack(): other = lax.ppermute(block, axis, [(i, i ^ bit) for i in range(count)])  14.6 us
    ppermute x1, starting transfers between devices, body(): w_block = ordered_pair(weight, lax.ppermute(weight, 'cz', SWAP), high, 2)  13.6 us
    ppermute x2, waiting for transfers between devices, shift_halo(): lax.ppermute(lax.slice_in_dim(block, block.shape[dim] - width, None, axis...  12.9 us
    unnamed x28, local copies, waits for them, and re-layouts  12.4 us
  transfers between devices with their start and end apart: 25, of which 15 were waited for; matrix products, arithmetic and copies ran while one was open for 10% of the time, Pallas kernels for 0%

profile of v13, /device:TPU:87, one launch (start us, length us, event | category | flops | bytes accessed | tf_op | source)
XLA Modules:
  0.0 269.4 jit_solution(7799034547389650928)
XLA Ops:
  1.5 13.6 %collective-permute-start.4 = (bf16[12,16,128]{2,1,0:T(8,128)(2,1)S(1)}, bf16[12,16,128]{2,1,0:T(8,128)(2,1)S(1)}, u32[]{:S(2)}, u32[]{:S(2)}) collective-permute-start(bf16[12,16,128]{2,1,0:T(8,128)(2,1)S(1)} %constant_dynamic-update-slice_fusion), channel_id=1, source_target_pairs={{0,1},{1,0},{2,3},{3,2},{4,5},{5,4},{6,7},{7,6},{8,9},{9,8},{10,11... | collective-permute-start | bytes 147464 | tf_op jit(solution)/shard_map/ppermute | solution.py:67
  19.0 11.6 %collective-permute-start.3 = (bf16[4,1,64,128]{3,2,1,0:T(8,128)(2,1)S(1)}, bf16[4,1,64,128]{3,2,1,0:T(8,128)(2,1)S(1)}, u32[]{:S(2)}, u32[]{:S(2)}) collective-permute-start(bf16[4,1,64,128]{3,2,1,0:T(8,128)(2,1)S(1)} %get-tuple-element.40), channel_id=1, source_target_pairs={{1,8},{9,16},{17,24},{25,32},{33,40},{41,48},{49,56},{8,1},{16,9},... | collective-permute-start | bytes 196616 | tf_op jit(solution)/shard_map/ppermute | solution.py:66
  36.0 7.4 %collective-permute-done.1 = bf16[4,1,64,128]{3,2,1,0:T(8,128)(2,1)S(1)} collective-permute-done((bf16[4,1,64,128]{3,2,1,0:T(8,128)(2,1)S(1)}, bf16[4,1,64,128]{3,2,1,0:T(8,128)(2,1)S(1)}, u32[]{:S(2)}, u32[]{:S(2)}) %collective-permute-start.1) | collective-permute-done | bytes 65568 | tf_op jit(solution)/shard_map/ppermute | solution.py:18
  43.4 11.2 %collective-permute-done = bf16[4,1,64,128]{3,2,1,0:T(8,128)(2,1)S(1)} collective-permute-done((bf16[4,1,64,128]{3,2,1,0:T(8,128)(2,1)S(1)}, bf16[4,1,64,128]{3,2,1,0:T(8,128)(2,1)S(1)}, u32[]{:S(2)}, u32[]{:S(2)}) %collective-permute-start) | collective-permute-done | bytes 65568 | tf_op jit(solution)/shard_map/ppermute | solution.py:15
  56.7 8.2 %collective-permute-start.7 = (bf16[12,16,256]{2,1,0:T(8,128)(2,1)S(1)}, bf16[12,16,256]{2,1,0:T(8,128)(2,1)S(1)}, u32[]{:S(2)}, u32[]{:S(2)}) collective-permute-start(bf16[12,16,256]{2,1,0:T(8,128)(2,1)S(1)} %maximum_select_fusion.8), channel_id=1, source_target_pairs={{0,32},{8,40},{16,48},{24,56},{32,0},{40,8},{48,16},{56,24},{1,33}... | collective-permute-start | bytes 294920 | tf_op jit(solution)/shard_map/ppermute | solution.py:44
  68.8 4.0 %collective-permute-start.5 = (bf16[4,6,64,256]{3,2,1,0:T(8,128)(2,1)S(1)}, bf16[4,6,64,256]{3,2,1,0:T(8,128)(2,1)S(1)}, u32[]{:S(2)}, u32[]{:S(2)}) collective-permute-start(bf16[4,6,64,256]{3,2,1,0:T(8,128)(2,1)S(1)} %get-tuple-element.28), channel_id=1, source_target_pairs={{0,2},{2,4},{4,6},{6,0},{1,3},{3,5},{5,7},{7,1},{8,10},{10,12},{12... | collective-permute-start | bytes 2359304 | tf_op jit(solution)/shard_map/ppermute | solution.py:23
  74.8 5.6 %collective-permute-done.8 = bf16[12,2,16,256]{3,2,1,0:T(8,128)(2,1)S(1)} collective-permute-done((bf16[12,2,16,256]{3,2,1,0:T(8,128)(2,1)S(1)}, bf16[12,2,16,256]{3,2,1,0:T(8,128)(2,1)S(1)}, u32[]{:S(2)}, u32[]{:S(2)}) %collective-permute-start.8) | collective-permute-done | bytes 196640 | tf_op jit(solution)/shard_map/ppermute | solution.py:44
  80.5 13.6 %collective-permute-start.9 = (bf16[12,2,2,16,256]{4,3,1,0,2:T(8,128)(2,1)S(1)}, bf16[12,2,2,16,256]{4,3,1,0,2:T(8,128)(2,1)S(1)}, u32[]{:S(2)}, u32[]{:S(2)}) collective-permute-start(bf16[12,2,2,16,256]{4,3,1,0,2:T(8,128)(2,1)S(1)} %maximum_select_fusion.5), channel_id=1, source_target_pairs={{0,8},{8,0},{16,24},{24,16},{32,40},{40,32},{48,56},{56,48},{1,9},... | collective-permute-start | bytes 1179656 | tf_op jit(solution)/shard_map/ppermute | solution.py:44
  94.2 9.0 %collective-permute-done.9 = bf16[12,2,2,16,256]{4,3,1,0,2:T(8,128)(2,1)S(1)} collective-permute-done((bf16[12,2,2,16,256]{4,3,1,0,2:T(8,128)(2,1)S(1)}, bf16[12,2,2,16,256]{4,3,1,0,2:T(8,128)(2,1)S(1)}, u32[]{:S(2)}, u32[]{:S(2)}) %collective-permute-start.9) | collective-permute-done | bytes 393248 | tf_op jit(solution)/shard_map/ppermute | solution.py:44
  120.7 3.5 %collective-permute-start.15 = (bf16[12,64,256]{2,1,0:T(8,128)(2,1)S(1)}, bf16[12,64,256]{2,1,0:T(8,128)(2,1)S(1)}, u32[]{:S(2)}, u32[]{:S(2)}) collective-permute-start(bf16[12,64,256]{2,1,0:T(8,128)(2,1)S(1)} %get-tuple-element.35), channel_id=1, source_target_pairs={{0,256},{128,384},{256,0},{384,128},{1,257},{129,385},{257,1},{385... | collective-permute-start | bytes 1179656 | tf_op jit(solution)/shard_map/ppermute | solution.py:23
  127.5 8.6 %collective-permute-done.14 = bf16[12,64,256]{2,1,0:T(8,128)(2,1)S(1)} collective-permute-done((bf16[12,64,256]{2,1,0:T(8,128)(2,1)S(1)}, bf16[12,64,256]{2,1,0:T(8,128)(2,1)S(1)}, u32[]{:S(2)}, u32[]{:S(2)}) %collective-permute-start.14) | collective-permute-done | bytes 393248 | tf_op jit(solution)/shard_map/ppermute | solution.py:23
  136.1 8.4 %collective-permute-done.15 = bf16[12,64,256]{2,1,0:T(8,128)(2,1)S(1)} collective-permute-done((bf16[12,64,256]{2,1,0:T(8,128)(2,1)S(1)}, bf16[12,64,256]{2,1,0:T(8,128)(2,1)S(1)}, u32[]{:S(2)}, u32[]{:S(2)}) %collective-permute-start.15) | collective-permute-done | bytes 393248 | tf_op jit(solution)/shard_map/ppermute | solution.py:23
  145.8 3.8 %collective-permute-start.16 = (bf16[12,4,128,256]{3,2,1,0:T(8,128)(2,1)S(1)}, bf16[12,4,128,256]{3,2,1,0:T(8,128)(2,1)}, u32[]{:S(2)}, u32[]{:S(2)}) collective-permute-start(bf16[12,4,128,256]{3,2,1,0:T(8,128)(2,1)S(1)} %bitcast_dynamic-update-slice_fusion), channel_id=1, source_target_pairs={{0,64},{64,0},{1,65},{65,1},{2,66},{66,2},{3,67},{67,3},{4,68},{68... | collective-permute-start | bytes 9437192 | tf_op jit(solution)/shard_map/ppermute | solution.py:44
  149.6 4.8 %collective-permute-start.17 = (f32[2,128]{1,0:T(2,128)S(1)}, f32[2,128]{1,0:T(2,128)S(1)}, u32[]{:S(2)}, u32[]{:S(2)}) collective-permute-start(f32[2,128]{1,0:T(2,128)S(1)} %pad_maximum_fusion.3), channel_id=1, source_target_pairs={{0,1},{1,0},{2,3},{3,2},{4,5},{5,4},{6,7},{7,6},{8,9},{9,8},{10,11... | collective-permute-start | bytes 3080 | tf_op jit(solution)/shard_map/ppermute | solution.py:59
  154.5 8.2 %collective-permute-done.17 = f32[2,128]{1,0:T(2,128)S(1)} collective-permute-done((f32[2,128]{1,0:T(2,128)S(1)}, f32[2,128]{1,0:T(2,128)S(1)}, u32[]{:S(2)}, u32[]{:S(2)}) %collective-permute-start.17) | collective-permute-done | bytes 1056 | tf_op jit(solution)/shard_map/ppermute | solution.py:59
  168.6 4.3 %copy.32 = bf16[6,4,64,1024]{3,1,2,0:T(4,128)(2,1)S(1)} copy(bf16[6,4,64,1024]{3,2,0,1:T(8,128)(2,1)} %bitcast.83) | data formatting | bytes 6291456
  176.8 4.3 %maximum_select_fusion = bf16[12,4,2,128,256]{4,3,2,1,0:T(8,128)(2,1)S(1)} fusion(bf16[12,4,1,128,256]{4,3,2,1,0:T(8,128)(2,1)S(1)} %bitcast.82, bf16[12,4,1,128,256]{4,3,2,1,0:T(8,128)(2,1)} %bitcast.20, pred[]{:T(512)S(6)} %eq.34), kind=kLoop, calls=%fused_computation.2 | loop fusion | flops 9437184 | bytes 12582913 | tf_op jit(solution)/shard_map/jit(_where)/select_n | solution.py:46
  183.8 6.3 %convert_add_fusion = (f32[4,32,9,256]{3,1,2,0:T(8,128)S(1)}, bf16[4,32,9,256]{3,1,2,0:T(8,128)(2,1)S(1)}) fusion(f32[256]{0:T(256)S(1)} %bitcast.104, f32[256]{0:T(256)S(1)} %bitcast.105, bf16[3,3,1024,256]{3,2,1,0:T(8,128)(2,1)S(1)} %bitcast.84, bf16[6,4,8,11,1024]{4,1,3,2,0:T(4,128)(2,1)S(1)} %fusion.1, pred[32,9]{0,1:T(8,128)(4,1)S(1)} %copy-done.8), kind=kOutput, calls=%fused_computation.17 | convolution fusion | flops 5438767104 | bytes 10815776 | tf_op jit(solution)/shard_map/conv_general_dilated | solution.py:98
  196.4 8.6 %collective-permute-done.20 = bf16[4,4,64,256]{3,2,1,0:T(8,128)(2,1)S(1)} collective-permute-done((bf16[4,4,64,256]{3,2,1,0:T(8,128)(2,1)S(1)}, bf16[4,4,64,256]{3,2,1,0:T(8,128)(2,1)S(1)}, u32[]{:S(2)}, u32[]{:S(2)}) %collective-permute-start.20) | collective-permute-done | bytes 524320 | tf_op jit(solution)/shard_map/ppermute | solution.py:23
  205.0 3.3 %collective-permute-start.21 = (bf16[4,4,64,128]{3,2,1,0:T(8,128)(2,1)S(1)}, bf16[4,4,64,128]{3,2,1,0:T(8,128)(2,1)S(1)}, u32[]{:S(2)}, u32[]{:S(2)}) collective-permute-start(bf16[4,4,64,128]{3,2,1,0:T(8,128)(2,1)S(1)} %slice.106), channel_id=1, source_target_pairs={{0,2},{2,4},{4,6},{6,0},{1,3},{3,5},{5,7},{7,1},{8,10},{10,12},{12... | collective-permute-start | bytes 786440 | tf_op jit(solution)/shard_map/ppermute | solution.py:23
  211.7 5.0 %collective-permute-done.19 = bf16[4,4,64,128]{3,2,1,0:T(8,128)(2,1)S(1)} collective-permute-done((bf16[4,4,64,128]{3,2,1,0:T(8,128)(2,1)S(1)}, bf16[4,4,64,128]{3,2,1,0:T(8,128)(2,1)S(1)}, u32[]{:S(2)}, u32[]{:S(2)}) %collective-permute-start.19) | collective-permute-done | bytes 262176 | tf_op jit(solution)/shard_map/ppermute | solution.py:23
  217.1 5.4 %collective-permute-start.23 = (bf16[1,4,64,1024]{3,2,1,0:T(8,128)(2,1)S(1)}, bf16[1,4,64,1024]{3,2,1,0:T(8,128)(2,1)S(1)}, u32[]{:S(2)}, u32[]{:S(2)}) collective-permute-start(bf16[1,4,64,1024]{3,2,1,0:T(8,128)(2,1)S(1)} %get-tuple-element.33), channel_id=1, source_target_pairs={{64,0},{128,64},{192,128},{256,192},{320,256},{384,320},{448,384},... | collective-permute-start | bytes 1572872 | tf_op jit(solution)/shard_map/ppermute | solution.py:18
  234.4 4.6 %collective-permute-start.24 = (bf16[4,4,64,128]{3,2,1,0:T(8,128)(2,1)S(1)}, bf16[4,4,64,128]{3,2,1,0:T(8,128)(2,1)S(1)}, u32[]{:S(2)}, u32[]{:S(2)}) collective-permute-start(bf16[4,4,64,128]{3,2,1,0:T(8,128)(2,1)S(1)} %get-tuple-element.38), channel_id=1, source_target_pairs={{0,1},{1,0},{2,3},{3,2},{4,5},{5,4},{6,7},{7,6},{8,9},{9,8},{10,11... | collective-permute-start | bytes 786440 | tf_op jit(solution)/shard_map/ppermute | solution.py:133
  239.0 29.6 %collective-permute-done.24 = bf16[4,4,64,128]{3,2,1,0:T(8,128)(2,1)S(1)} collective-permute-done((bf16[4,4,64,128]{3,2,1,0:T(8,128)(2,1)S(1)}, bf16[4,4,64,128]{3,2,1,0:T(8,128)(2,1)S(1)}, u32[]{:S(2)}, u32[]{:S(2)}) %collective-permute-start.24) | collective-permute-done | bytes 262176 | tf_op jit(solution)/shard_map/ppermute | solution.py:133
  (104 shorter events, 75.5 us)
Async XLA Ops:
  1.5 34.5 %collective-permute-start.4 = (bf16[12,16,128]{2,1,0:T(8,128)(2,1)S(1)}, bf16[12,16,128]{2,1,0:T(8,128)(2,1)S(1)}, u32[]{:S(2)}, u32[]{:S(2)}) collective-permute-start(bf16[12,16,128]{2,1,0:T(8,128)(2,1)S(1)} %constant_dynamic-update-slice_fusion), channel_id=1, source_target_pairs={{0,1},{1,0},{2,3},{3,2},{4,5},{5,4},{6,7},{7,6},{8,9},{9,8},{10,11... | collective-permute-start | bytes 147464 | tf_op jit(solution)/shard_map/ppermute | solution.py:67
  16.1 40.6 %collective-permute-start.2 = (bf16[4,5,64,128]{3,2,1,0:T(8,128)(2,1)S(1)}, bf16[4,5,64,128]{3,2,1,0:T(8,128)(2,1)S(1)}, u32[]{:S(2)}, u32[]{:S(2)}) collective-permute-start(bf16[4,5,64,128]{3,2,1,0:T(8,128)(2,1)S(1)} %constant_dynamic-slice_fusion.4), channel_id=1, source_target_pairs={{0,1},{1,0},{2,3},{3,2},{4,5},{5,4},{6,7},{7,6},{8,9},{9,8},{10,11... | collective-permute-start | bytes 983048 | tf_op jit(solution)/shard_map/ppermute | solution.py:62
  19.0 37.7 %collective-permute-start.3 = (bf16[4,1,64,128]{3,2,1,0:T(8,128)(2,1)S(1)}, bf16[4,1,64,128]{3,2,1,0:T(8,128)(2,1)S(1)}, u32[]{:S(2)}, u32[]{:S(2)}) collective-permute-start(bf16[4,1,64,128]{3,2,1,0:T(8,128)(2,1)S(1)} %get-tuple-element.40), channel_id=1, source_target_pairs={{1,8},{9,16},{17,24},{25,32},{33,40},{41,48},{49,56},{8,1},{16,9},... | collective-permute-start | bytes 196616 | tf_op jit(solution)/shard_map/ppermute | solution.py:66
  30.6 12.8 %collective-permute-start.1 = (bf16[4,1,64,128]{3,2,1,0:T(8,128)(2,1)S(1)}, bf16[4,1,64,128]{3,2,1,0:T(8,128)(2,1)S(1)}, u32[]{:S(2)}, u32[]{:S(2)}) collective-permute-start(bf16[4,1,64,128]{3,2,1,0:T(8,128)(2,1)S(1)} %get-tuple-element.41), channel_id=1, source_target_pairs={{8,0},{16,8},{24,16},{32,24},{40,32},{48,40},{56,48},{9,1},{17,9},... | collective-permute-start | bytes 196616 | tf_op jit(solution)/shard_map/ppermute | solution.py:18
  33.3 21.3 %collective-permute-start = (bf16[4,1,64,128]{3,2,1,0:T(8,128)(2,1)S(1)}, bf16[4,1,64,128]{3,2,1,0:T(8,128)(2,1)S(1)}, u32[]{:S(2)}, u32[]{:S(2)}) collective-permute-start(bf16[4,1,64,128]{3,2,1,0:T(8,128)(2,1)S(1)} %get-tuple-element.42), channel_id=1, source_target_pairs={{0,8},{8,16},{16,24},{24,32},{32,40},{40,48},{48,56},{1,9},{9,17},... | collective-permute-start | bytes 196616 | tf_op jit(solution)/shard_map/ppermute | solution.py:15
  56.7 16.1 %collective-permute-start.7 = (bf16[12,16,256]{2,1,0:T(8,128)(2,1)S(1)}, bf16[12,16,256]{2,1,0:T(8,128)(2,1)S(1)}, u32[]{:S(2)}, u32[]{:S(2)}) collective-permute-start(bf16[12,16,256]{2,1,0:T(8,128)(2,1)S(1)} %maximum_select_fusion.8), channel_id=1, source_target_pairs={{0,32},{8,40},{16,48},{24,56},{32,0},{40,8},{48,16},{56,24},{1,33}... | collective-permute-start | bytes 294920 | tf_op jit(solution)/shard_map/ppermute | solution.py:44
  66.3 37.9 %collective-permute-start.6 = (bf16[4,6,64,256]{3,2,1,0:T(8,128)(2,1)S(1)}, bf16[4,6,64,256]{3,2,1,0:T(8,128)(2,1)S(1)}, u32[]{:S(2)}, u32[]{:S(2)}) collective-permute-start(bf16[4,6,64,256]{3,2,1,0:T(8,128)(2,1)S(1)} %get-tuple-element.28), channel_id=1, source_target_pairs={{0,6},{2,0},{4,2},{6,4},{1,7},{3,1},{5,3},{7,5},{8,14},{10,8},{12,... | collective-permute-start | bytes 2359304 | tf_op jit(solution)/shard_map/ppermute | solution.py:23
  68.8 35.5 %collective-permute-start.5 = (bf16[4,6,64,256]{3,2,1,0:T(8,128)(2,1)S(1)}, bf16[4,6,64,256]{3,2,1,0:T(8,128)(2,1)S(1)}, u32[]{:S(2)}, u32[]{:S(2)}) collective-permute-start(bf16[4,6,64,256]{3,2,1,0:T(8,128)(2,1)S(1)} %get-tuple-element.28), channel_id=1, source_target_pairs={{0,2},{2,4},{4,6},{6,0},{1,3},{3,5},{5,7},{7,1},{8,10},{10,12},{12... | collective-permute-start | bytes 2359304 | tf_op jit(solution)/shard_map/ppermute | solution.py:23
  80.5 22.7 %collective-permute-start.9 = (bf16[12,2,2,16,256]{4,3,1,0,2:T(8,128)(2,1)S(1)}, bf16[12,2,2,16,256]{4,3,1,0,2:T(8,128)(2,1)S(1)}, u32[]{:S(2)}, u32[]{:S(2)}) collective-permute-start(bf16[12,2,2,16,256]{4,3,1,0,2:T(8,128)(2,1)S(1)} %maximum_select_fusion.5), channel_id=1, source_target_pairs={{0,8},{8,0},{16,24},{24,16},{32,40},{40,32},{48,56},{56,48},{1,9},... | collective-permute-start | bytes 1179656 | tf_op jit(solution)/shard_map/ppermute | solution.py:44
  104.2 21.6 %collective-permute-start.13 = (bf16[12,128,256]{2,1,0:T(8,128)(2,1)}, bf16[12,128,256]{2,1,0:T(8,128)(2,1)}, u32[]{:S(2)}, u32[]{:S(2)}) collective-permute-start(bf16[12,128,256]{2,1,0:T(8,128)(2,1)} %bitcast.8), channel_id=1, source_target_pairs={{0,384},{128,0},{256,128},{384,256},{1,385},{129,1},{257,129},{385... | collective-permute-start | bytes 2359304 | tf_op jit(solution)/shard_map/ppermute | solution.py:23
  106.3 20.0 %collective-permute-start.12 = (bf16[12,128,256]{2,1,0:T(8,128)(2,1)}, bf16[12,128,256]{2,1,0:T(8,128)(2,1)}, u32[]{:S(2)}, u32[]{:S(2)}) collective-permute-start(bf16[12,128,256]{2,1,0:T(8,128)(2,1)} %bitcast.8), channel_id=1, source_target_pairs={{0,128},{128,256},{256,384},{384,0},{1,129},{129,257},{257,385},{3... | collective-permute-start | bytes 2359304 | tf_op jit(solution)/shard_map/ppermute | solution.py:23
  109.6 11.1 %collective-permute-start.11 = (bf16[4,6,64,128]{3,2,1,0:T(8,128)(2,1)S(1)}, bf16[4,6,64,128]{3,2,1,0:T(8,128)(2,1)S(1)}, u32[]{:S(2)}, u32[]{:S(2)}) collective-permute-start(bf16[4,6,64,128]{3,2,1,0:T(8,128)(2,1)S(1)} %slice.78), channel_id=1, source_target_pairs={{0,2},{2,4},{4,6},{6,0},{1,3},{3,5},{5,7},{7,1},{8,10},{10,12},{12... | collective-permute-start | bytes 1179656 | tf_op jit(solution)/shard_map/ppermute | solution.py:23
  111.9 13.9 %collective-permute-start.10 = (bf16[4,6,64,128]{3,2,1,0:T(8,128)(2,1)S(1)}, bf16[4,6,64,128]{3,2,1,0:T(8,128)(2,1)S(1)}, u32[]{:S(2)}, u32[]{:S(2)}) collective-permute-start(bf16[4,6,64,128]{3,2,1,0:T(8,128)(2,1)S(1)} %slice.77), channel_id=1, source_target_pairs={{0,6},{2,0},{4,2},{6,4},{1,7},{3,1},{5,3},{7,5},{8,14},{10,8},{12,... | collective-permute-start | bytes 1179656 | tf_op jit(solution)/shard_map/ppermute | solution.py:23
  116.2 19.8 %collective-permute-start.14 = (bf16[12,64,256]{2,1,0:T(8,128)(2,1)S(1)}, bf16[12,64,256]{2,1,0:T(8,128)(2,1)S(1)}, u32[]{:S(2)}, u32[]{:S(2)}) collective-permute-start(bf16[12,64,256]{2,1,0:T(8,128)(2,1)S(1)} %get-tuple-element.34), channel_id=1, source_target_pairs={{0,256},{128,384},{256,0},{384,128},{1,257},{129,385},{257,1},{385... | collective-permute-start | bytes 1179656 | tf_op jit(solution)/shard_map/ppermute | solution.py:23
  120.7 23.8 %collective-permute-start.15 = (bf16[12,64,256]{2,1,0:T(8,128)(2,1)S(1)}, bf16[12,64,256]{2,1,0:T(8,128)(2,1)S(1)}, u32[]{:S(2)}, u32[]{:S(2)}) collective-permute-start(bf16[12,64,256]{2,1,0:T(8,128)(2,1)S(1)} %get-tuple-element.35), channel_id=1, source_target_pairs={{0,256},{128,384},{256,0},{384,128},{1,257},{129,385},{257,1},{385... | collective-permute-start | bytes 1179656 | tf_op jit(solution)/shard_map/ppermute | solution.py:23
  145.8 31.0 %collective-permute-start.16 = (bf16[12,4,128,256]{3,2,1,0:T(8,128)(2,1)S(1)}, bf16[12,4,128,256]{3,2,1,0:T(8,128)(2,1)}, u32[]{:S(2)}, u32[]{:S(2)}) collective-permute-start(bf16[12,4,128,256]{3,2,1,0:T(8,128)(2,1)S(1)} %bitcast_dynamic-update-slice_fusion), channel_id=1, source_target_pairs={{0,64},{64,0},{1,65},{65,1},{2,66},{66,2},{3,67},{67,3},{4,68},{68... | collective-permute-start | bytes 9437192 | tf_op jit(solution)/shard_map/ppermute | solution.py:44
  149.6 13.0 %collective-permute-start.17 = (f32[2,128]{1,0:T(2,128)S(1)}, f32[2,128]{1,0:T(2,128)S(1)}, u32[]{:S(2)}, u32[]{:S(2)}) collective-permute-start(f32[2,128]{1,0:T(2,128)S(1)} %pad_maximum_fusion.3), channel_id=1, source_target_pairs={{0,1},{1,0},{2,3},{3,2},{4,5},{5,4},{6,7},{7,6},{8,9},{9,8},{10,11... | collective-permute-start | bytes 3080 | tf_op jit(solution)/shard_map/ppermute | solution.py:59
  190.8 14.1 %collective-permute-start.20 = (bf16[4,4,64,256]{3,2,1,0:T(8,128)(2,1)S(1)}, bf16[4,4,64,256]{3,2,1,0:T(8,128)(2,1)S(1)}, u32[]{:S(2)}, u32[]{:S(2)}) collective-permute-start(bf16[4,4,64,256]{3,2,1,0:T(8,128)(2,1)S(1)} %bitcast.94), channel_id=1, source_target_pairs={{0,2},{2,4},{4,6},{6,0},{1,3},{3,5},{5,7},{7,1},{8,10},{10,12},{12... | collective-permute-start | bytes 1572872 | tf_op jit(solution)/shard_map/ppermute | solution.py:23
  192.9 15.4 %collective-permute-start.18 = (bf16[4,4,64,256]{3,2,1,0:T(8,128)(2,1)S(1)}, bf16[4,4,64,256]{3,2,1,0:T(8,128)(2,1)S(1)}, u32[]{:S(2)}, u32[]{:S(2)}) collective-permute-start(bf16[4,4,64,256]{3,2,1,0:T(8,128)(2,1)S(1)} %bitcast.95), channel_id=1, source_target_pairs={{0,6},{2,0},{4,2},{6,4},{1,7},{3,1},{5,3},{7,5},{8,14},{10,8},{12,... | collective-permute-start | bytes 1572872 | tf_op jit(solution)/shard_map/ppermute | solution.py:23
  205.0 11.8 %collective-permute-start.21 = (bf16[4,4,64,128]{3,2,1,0:T(8,128)(2,1)S(1)}, bf16[4,4,64,128]{3,2,1,0:T(8,128)(2,1)S(1)}, u32[]{:S(2)}, u32[]{:S(2)}) collective-permute-start(bf16[4,4,64,128]{3,2,1,0:T(8,128)(2,1)S(1)} %slice.106), channel_id=1, source_target_pairs={{0,2},{2,4},{4,6},{6,0},{1,3},{3,5},{5,7},{7,1},{8,10},{10,12},{12... | collective-permute-start | bytes 786440 | tf_op jit(solution)/shard_map/ppermute | solution.py:23
  208.4 8.3 %collective-permute-start.19 = (bf16[4,4,64,128]{3,2,1,0:T(8,128)(2,1)S(1)}, bf16[4,4,64,128]{3,2,1,0:T(8,128)(2,1)S(1)}, u32[]{:S(2)}, u32[]{:S(2)}) collective-permute-start(bf16[4,4,64,128]{3,2,1,0:T(8,128)(2,1)S(1)} %slice.105), channel_id=1, source_target_pairs={{0,6},{2,0},{4,2},{6,4},{1,7},{3,1},{5,3},{7,5},{8,14},{10,8},{12,... | collective-permute-start | bytes 786440 | tf_op jit(solution)/shard_map/ppermute | solution.py:23
  217.1 14.0 %collective-permute-start.23 = (bf16[1,4,64,1024]{3,2,1,0:T(8,128)(2,1)S(1)}, bf16[1,4,64,1024]{3,2,1,0:T(8,128)(2,1)S(1)}, u32[]{:S(2)}, u32[]{:S(2)}) collective-permute-start(bf16[1,4,64,1024]{3,2,1,0:T(8,128)(2,1)S(1)} %get-tuple-element.33), channel_id=1, source_target_pairs={{64,0},{128,64},{192,128},{256,192},{320,256},{384,320},{448,384},... | collective-permute-start | bytes 1572872 | tf_op jit(solution)/shard_map/ppermute | solution.py:18
  224.0 9.4 %collective-permute-start.22 = (bf16[1,4,64,1024]{3,2,1,0:T(8,128)(2,1)S(1)}, bf16[1,4,64,1024]{3,2,1,0:T(8,128)(2,1)S(1)}, u32[]{:S(2)}, u32[]{:S(2)}) collective-permute-start(bf16[1,4,64,1024]{3,2,1,0:T(8,128)(2,1)S(1)} %get-tuple-element.32), channel_id=1, source_target_pairs={{0,64},{64,128},{128,192},{192,256},{256,320},{320,384},{384,448},... | collective-permute-start | bytes 1572872 | tf_op jit(solution)/shard_map/ppermute | solution.py:15
  234.4 34.2 %collective-permute-start.24 = (bf16[4,4,64,128]{3,2,1,0:T(8,128)(2,1)S(1)}, bf16[4,4,64,128]{3,2,1,0:T(8,128)(2,1)S(1)}, u32[]{:S(2)}, u32[]{:S(2)}) collective-permute-start(bf16[4,4,64,128]{3,2,1,0:T(8,128)(2,1)S(1)} %get-tuple-element.38), channel_id=1, source_target_pairs={{0,1},{1,0},{2,3},{3,2},{4,5},{5,4},{6,7},{7,6},{8,9},{9,8},{10,11... | collective-permute-start | bytes 786440 | tf_op jit(solution)/shard_map/ppermute | solution.py:133
  (10 other events, 135.0 us)

commit v14 on v10

--- a/solution.py
+++ b/solution.py
@@ -84,15 +84,34 @@
     w_cut = w_block.shape[1] // 2
     w_far_low = ring_shift(w_right[:, :w_cut], "fy", fy_n, -1)
     w_far_high = ring_shift(w_left[:, w_cut:], "fy", fy_n, 1)
+    frame_pos = [(f, c) for f in range(fy_n) for c in range(2)]
+    from_up = [((f + 1) % fy_n * 2 + 1 - c, f * 2 + c) for f, c in frame_pos]
+    from_down = [((f - 1) % fy_n * 2 + 1 - c, f * 2 + c) for f, c in frame_pos]
+    s_far_low = lax.ppermute(w_right[:, :w_cut], FRAME, from_up)
+    s_far_high = lax.ppermute(w_left[:, w_cut:], FRAME, from_down)
+    held = jnp.stack([w_block, w_right, w_left], axis=1)
+    s_held = lax.ppermute(held, "fc", SWAP)
     gathered = jnp.concatenate([pair, from_right, far_low, far_high, from_left], axis=3)
     me_fy = lax.axis_index("fy")
+    me_fc = lax.axis_index("fc")
     rotate = lax.axis_index("cx")
     w_far = jnp.concatenate([w_far_low, w_far_high], axis=1)
-    w_out = jnp.zeros((taps, fy_n) + w_block.shape[1:], w_block.dtype)
-    for offset, piece in ((0, w_block), (1, w_right), (2, w_far), (fy_n - 1, w_left)):
+    s_far = jnp.concatenate([s_far_low, s_far_high], axis=1)
+    w_out = jnp.zeros((taps, fy_n, 2) + w_block.shape[1:], w_block.dtype)
+    pieces = (
+        (0, me_fc, w_block),
+        (1, me_fc, w_right),
+        (2, me_fc, w_far),
+        (fy_n - 1, me_fc, w_left),
+        (0, 1 - me_fc, s_held[:, 0]),
+        (1, 1 - me_fc, s_held[:, 1]),
+        (2, 1 - me_fc, s_far),
+        (fy_n - 1, 1 - me_fc, s_held[:, 2]),
+    )
+    for offset, core, piece in pieces:
         place = (me_fy + offset - rotate + 2 * fy_n) % fy_n
-        w_out = lax.dynamic_update_slice(w_out, piece[:, None], (0, place, 0, 0))
-    both = xor_stack(w_out, "fc", 1, 2).reshape(taps, -1, w_block.shape[2])
+        w_out = lax.dynamic_update_slice(w_out, piece[:, None, None], (0, place, core, 0, 0))
+    both = w_out.reshape(taps, -1, w_block.shape[2])
     full_spatial, full_temporal = both[:9], both[9:]
     kernel = full_spatial.reshape((3, 3) + full_spatial.shape[1:])
     spatial = lax.conv_general_dilated(

time: 269 us -> 249 us (0.926)
  the two profiles are of different devices: /device:TPU:87 before, /device:TPU:1 now
where the time goes in v14:
time: 249 us; the launch traced here: 245 us
  starting transfers between devices  117 us (47%)
  waiting for transfers between devices  91.3 us (37%)
  local copies, waits for them, and re-layouts  20.6 us (8%)
  matrix products  8.51 us (3%)
  other arithmetic  6.35 us (3%)
    ppermute x12, starting transfers between devices, ring_shift(): lax.ppermute(block, axis, [(i, (i + step) % count) for i in range(count)])  41 us
    ppermute x1, waiting for transfers between devices, body(): returned = lax.ppermute(given, 'cz', SWAP)  20.6 us
    ppermute x2, waiting for transfers between devices, shift_halo(): lax.ppermute(lax.slice_in_dim(block, 0, width, axis=dim), axis, backward)  20.4 us
    ppermute x3, starting transfers between devices, xor_stack(): other = lax.ppermute(block, axis, [(i, i ^ bit) for i in range(count)])  20.2 us
    ppermute x1, starting transfers between devices, body(): partner = lax.ppermute(sent, 'cz', SWAP)  16.3 us
    ppermute x12, waiting for transfers between devices, ring_shift(): lax.ppermute(block, axis, [(i, (i + step) % count) for i in range(count)])  16.2 us
    ppermute x3, waiting for transfers between devices, xor_stack(): other = lax.ppermute(block, axis, [(i, i ^ bit) for i in range(count)])  10.5 us
    ppermute x1, starting transfers between devices, body(): returned = lax.ppermute(given, 'cz', SWAP)  9.35 us
  transfers between devices with their start and end apart: 27, of which 15 were waited for; matrix products, arithmetic and copies ran while one was open for 9% of the time, Pallas kernels for 0%

profile of v14, /device:TPU:1, one launch (start us, length us, event | category | flops | bytes accessed | tf_op | source)
XLA Modules:
  0.0 244.9 jit_solution(15640281581401886991)
XLA Ops:
  1.0 16.3 %collective-permute-start.2 = (bf16[4,5,64,128]{3,2,1,0:T(8,128)(2,1)S(1)}, bf16[4,5,64,128]{3,2,1,0:T(8,128)(2,1)S(1)}, u32[]{:S(2)}, u32[]{:S(2)}) collective-permute-start(bf16[4,5,64,128]{3,2,1,0:T(8,128)(2,1)S(1)} %constant_dynamic-slice_fusion.4), channel_id=1, source_target_pairs={{0,1},{1,0},{2,3},{3,2},{4,5},{5,4},{6,7},{7,6},{8,9},{9,8},{10,11... | collective-permute-start | bytes 983048 | tf_op jit(solution)/shard_map/ppermute | solution.py:62
  26.3 6.4 %collective-permute-done.4 = bf16[12,16,128]{2,1,0:T(8,128)(2,1)S(1)} collective-permute-done((bf16[12,16,128]{2,1,0:T(8,128)(2,1)S(1)}, bf16[12,16,128]{2,1,0:T(8,128)(2,1)S(1)}, u32[]{:S(2)}, u32[]{:S(2)}) %collective-permute-start.4) | collective-permute-done | bytes 49184 | tf_op jit(solution)/shard_map/ppermute | solution.py:67
  33.7 18.0 %collective-permute-done.1 = bf16[4,1,64,128]{3,2,1,0:T(8,128)(2,1)S(1)} collective-permute-done((bf16[4,1,64,128]{3,2,1,0:T(8,128)(2,1)S(1)}, bf16[4,1,64,128]{3,2,1,0:T(8,128)(2,1)S(1)}, u32[]{:S(2)}, u32[]{:S(2)}) %collective-permute-start.1) | collective-permute-done | bytes 65568 | tf_op jit(solution)/shard_map/ppermute | solution.py:18
  52.8 8.2 %collective-permute-start.7 = (bf16[12,16,256]{2,1,0:T(8,128)(2,1)S(1)}, bf16[12,16,256]{2,1,0:T(8,128)(2,1)S(1)}, u32[]{:S(2)}, u32[]{:S(2)}) collective-permute-start(bf16[12,16,256]{2,1,0:T(8,128)(2,1)S(1)} %maximum_select_fusion.7), channel_id=1, source_target_pairs={{0,32},{8,40},{16,48},{24,56},{32,0},{40,8},{48,16},{56,24},{1,33}... | collective-permute-start | bytes 294920 | tf_op jit(solution)/shard_map/ppermute | solution.py:44
  65.8 3.4 %collective-permute-start.6 = (bf16[4,6,64,256]{3,2,1,0:T(8,128)(2,1)}, bf16[4,6,64,256]{3,2,1,0:T(8,128)(2,1)S(1)}, u32[]{:S(2)}, u32[]{:S(2)}) collective-permute-start(bf16[4,6,64,256]{3,2,1,0:T(8,128)(2,1)} %get-tuple-element.28), channel_id=1, source_target_pairs={{0,6},{2,0},{4,2},{6,4},{1,7},{3,1},{5,3},{7,5},{8,14},{10,8},{12,... | collective-permute-start | bytes 2359304 | tf_op jit(solution)/shard_map/ppermute | solution.py:23
  69.2 3.9 %collective-permute-start.8 = (bf16[12,2,16,256]{3,2,1,0:T(8,128)(2,1)S(1)}, bf16[12,2,16,256]{3,2,1,0:T(8,128)(2,1)S(1)}, u32[]{:S(2)}, u32[]{:S(2)}) collective-permute-start(bf16[12,2,16,256]{3,2,1,0:T(8,128)(2,1)S(1)} %maximum_select_fusion.6), channel_id=1, source_target_pairs={{0,16},{8,24},{16,0},{24,8},{32,48},{40,56},{48,32},{56,40},{1,17}... | collective-permute-start | bytes 589832 | tf_op jit(solution)/shard_map/ppermute | solution.py:44
  73.2 3.7 %collective-permute-done.8 = bf16[12,2,16,256]{3,2,1,0:T(8,128)(2,1)S(1)} collective-permute-done((bf16[12,2,16,256]{3,2,1,0:T(8,128)(2,1)S(1)}, bf16[12,2,16,256]{3,2,1,0:T(8,128)(2,1)S(1)}, u32[]{:S(2)}, u32[]{:S(2)}) %collective-permute-start.8) | collective-permute-done | bytes 196640 | tf_op jit(solution)/shard_map/ppermute | solution.py:44
  76.9 8.1 %collective-permute-start.9 = (bf16[12,2,2,16,256]{4,3,1,0,2:T(8,128)(2,1)S(1)}, bf16[12,2,2,16,256]{4,3,1,0,2:T(8,128)(2,1)S(1)}, u32[]{:S(2)}, u32[]{:S(2)}) collective-permute-start(bf16[12,2,2,16,256]{4,3,1,0,2:T(8,128)(2,1)S(1)} %maximum_select_fusion.4), channel_id=1, source_target_pairs={{0,8},{8,0},{16,24},{24,16},{32,40},{40,32},{48,56},{56,48},{1,9},... | collective-permute-start | bytes 1179656 | tf_op jit(solution)/shard_map/ppermute | solution.py:44
  85.0 6.8 %collective-permute-done.9 = bf16[12,2,2,16,256]{4,3,1,0,2:T(8,128)(2,1)S(1)} collective-permute-done((bf16[12,2,2,16,256]{4,3,1,0,2:T(8,128)(2,1)S(1)}, bf16[12,2,2,16,256]{4,3,1,0,2:T(8,128)(2,1)S(1)}, u32[]{:S(2)}, u32[]{:S(2)}) %collective-permute-start.9) | collective-permute-done | bytes 393248 | tf_op jit(solution)/shard_map/ppermute | solution.py:44
  96.0 3.4 %collective-permute-start.13 = (bf16[12,128,256]{2,1,0:T(8,128)(2,1)S(1)}, bf16[12,128,256]{2,1,0:T(8,128)(2,1)S(1)}, u32[]{:S(2)}, u32[]{:S(2)}) collective-permute-start(bf16[12,128,256]{2,1,0:T(8,128)(2,1)S(1)} %bitcast.108), channel_id=1, source_target_pairs={{0,384},{128,0},{256,128},{384,256},{1,385},{129,1},{257,129},{385... | collective-permute-start | bytes 2359304 | tf_op jit(solution)/shard_map/ppermute | solution.py:23
  101.1 5.4 %collective-permute-start.10 = (bf16[4,6,64,128]{3,2,1,0:T(8,128)(2,1)}, bf16[4,6,64,128]{3,2,1,0:T(8,128)(2,1)S(1)}, u32[]{:S(2)}, u32[]{:S(2)}) collective-permute-start(bf16[4,6,64,128]{3,2,1,0:T(8,128)(2,1)} %slice.88), channel_id=1, source_target_pairs={{0,6},{2,0},{4,2},{6,4},{1,7},{3,1},{5,3},{7,5},{8,14},{10,8},{12,... | collective-permute-start | bytes 1179656 | tf_op jit(solution)/shard_map/ppermute | solution.py:23
  109.4 7.3 %collective-permute-start.19 = (f32[2,128]{1,0:T(2,128)S(1)}, f32[2,128]{1,0:T(2,128)S(1)}, u32[]{:S(2)}, u32[]{:S(2)}) collective-permute-start(f32[2,128]{1,0:T(2,128)S(1)} %pad_maximum_fusion.4), channel_id=1, source_target_pairs={{0,1},{1,0},{2,3},{3,2},{4,5},{5,4},{6,7},{7,6},{8,9},{9,8},{10,11... | collective-permute-start | bytes 3080 | tf_op jit(solution)/shard_map/ppermute | solution.py:59
  116.8 5.6 %collective-permute-done.19 = f32[2,128]{1,0:T(2,128)S(1)} collective-permute-done((f32[2,128]{1,0:T(2,128)S(1)}, f32[2,128]{1,0:T(2,128)S(1)}, u32[]{:S(2)}, u32[]{:S(2)}) %collective-permute-start.19) | collective-permute-done | bytes 1056 | tf_op jit(solution)/shard_map/ppermute | solution.py:59
  122.7 5.9 %collective-permute-start.16 = (bf16[12,3,128,256]{3,2,0,1:T(8,128)(2,1)S(1)}, bf16[12,3,128,256]{3,2,0,1:T(8,128)(2,1)S(1)}, u32[]{:S(2)}, u32[]{:S(2)}) collective-permute-start(bf16[12,3,128,256]{3,2,0,1:T(8,128)(2,1)S(1)} %pad_maximum_fusion), channel_id=1, source_target_pairs={{0,64},{64,0},{1,65},{65,1},{2,66},{66,2},{3,67},{67,3},{4,68},{68... | collective-permute-start | bytes 7077896 | tf_op jit(solution)/shard_map/ppermute | solution.py:93
  129.6 3.4 %collective-permute-start.14 = (bf16[12,64,256]{2,1,0:T(8,128)(2,1)S(1)}, bf16[12,64,256]{2,1,0:T(8,128)(2,1)S(1)}, u32[]{:S(2)}, u32[]{:S(2)}) collective-permute-start(bf16[12,64,256]{2,1,0:T(8,128)(2,1)S(1)} %slice.90), channel_id=1, source_target_pairs={{0,384},{128,0},{256,128},{384,256},{1,385},{129,1},{257,129},{385... | collective-permute-start | bytes 1179656 | tf_op jit(solution)/shard_map/ppermute | solution.py:23
  151.1 6.9 %collective-permute-done.18 = bf16[12,64,256]{2,1,0:T(8,128)(2,1)S(1)} collective-permute-done((bf16[12,64,256]{2,1,0:T(8,128)(2,1)S(1)}, bf16[12,64,256]{2,1,0:T(8,128)(2,1)S(1)}, u32[]{:S(2)}, u32[]{:S(2)}) %collective-permute-start.18) | collective-permute-done | bytes 393248 | tf_op jit(solution)/shard_map/ppermute | solution.py:91
  160.8 6.3 %convert_add_fusion = (f32[4,32,9,256]{3,1,2,0:T(8,128)S(1)}, bf16[4,32,9,256]{3,1,2,0:T(8,128)(2,1)S(1)}) fusion(f32[256]{0:T(256)S(1)} %bitcast.134, f32[256]{0:T(256)S(1)} %bitcast.135, bf16[3,3,1024,256]{3,2,1,0:T(8,128)(2,1)S(1)} %bitcast.114, bf16[6,4,8,11,1024]{4,1,3,2,0:T(4,128)(2,1)S(1)} %fusion.1, pred[32,9]{0,1:T(8,128)(4,1)S(1)} %copy-done.7), kind=kOutput, calls=%fused_computation.17 | convolution fusion | flops 5438767104 | bytes 10815776 | tf_op jit(solution)/shard_map/conv_general_dilated | solution.py:117
  167.9 4.9 %collective-permute-start.20 = (bf16[4,4,64,256]{3,2,1,0:T(8,128)(2,1)S(1)}, bf16[4,4,64,256]{3,2,1,0:T(8,128)(2,1)S(1)}, u32[]{:S(2)}, u32[]{:S(2)}) collective-permute-start(bf16[4,4,64,256]{3,2,1,0:T(8,128)(2,1)S(1)} %bitcast.124), channel_id=1, source_target_pairs={{0,6},{2,0},{4,2},{6,4},{1,7},{3,1},{5,3},{7,5},{8,14},{10,8},{12,... | collective-permute-start | bytes 1572872 | tf_op jit(solution)/shard_map/ppermute | solution.py:23
  174.9 9.1 %collective-permute-done.20 = bf16[4,4,64,256]{3,2,1,0:T(8,128)(2,1)S(1)} collective-permute-done((bf16[4,4,64,256]{3,2,1,0:T(8,128)(2,1)S(1)}, bf16[4,4,64,256]{3,2,1,0:T(8,128)(2,1)S(1)}, u32[]{:S(2)}, u32[]{:S(2)}) %collective-permute-start.20) | collective-permute-done | bytes 524320 | tf_op jit(solution)/shard_map/ppermute | solution.py:23
  184.0 5.3 %collective-permute-start.21 = (bf16[4,4,64,128]{3,2,1,0:T(8,128)(2,1)S(1)}, bf16[4,4,64,128]{3,2,1,0:T(8,128)(2,1)S(1)}, u32[]{:S(2)}, u32[]{:S(2)}) collective-permute-start(bf16[4,4,64,128]{3,2,1,0:T(8,128)(2,1)S(1)} %slice.122), channel_id=1, source_target_pairs={{0,6},{2,0},{4,2},{6,4},{1,7},{3,1},{5,3},{7,5},{8,14},{10,8},{12,... | collective-permute-start | bytes 786440 | tf_op jit(solution)/shard_map/ppermute | solution.py:23
  194.2 5.2 %collective-permute-done.23 = bf16[4,4,64,128]{3,2,1,0:T(8,128)(2,1)S(1)} collective-permute-done((bf16[4,4,64,128]{3,2,1,0:T(8,128)(2,1)S(1)}, bf16[4,4,64,128]{3,2,1,0:T(8,128)(2,1)S(1)}, u32[]{:S(2)}, u32[]{:S(2)}) %collective-permute-start.23) | collective-permute-done | bytes 262176 | tf_op jit(solution)/shard_map/ppermute | solution.py:23
  199.7 4.0 %collective-permute-start.25 = (bf16[1,4,64,1024]{3,2,1,0:T(8,128)(2,1)S(1)}, bf16[1,4,64,1024]{3,2,1,0:T(8,128)(2,1)S(1)}, u32[]{:S(2)}, u32[]{:S(2)}) collective-permute-start(bf16[1,4,64,1024]{3,2,1,0:T(8,128)(2,1)S(1)} %get-tuple-element.33), channel_id=1, source_target_pairs={{64,0},{128,64},{192,128},{256,192},{320,256},{384,320},{448,384},... | collective-permute-start | bytes 1572872 | tf_op jit(solution)/shard_map/ppermute | solution.py:18
  214.1 9.3 %collective-permute-start.26 = (bf16[4,4,64,128]{3,2,1,0:T(8,128)(2,1)S(1)}, bf16[4,4,64,128]{3,2,1,0:T(8,128)(2,1)S(1)}, u32[]{:S(2)}, u32[]{:S(2)}) collective-permute-start(bf16[4,4,64,128]{3,2,1,0:T(8,128)(2,1)S(1)} %get-tuple-element.36), channel_id=1, source_target_pairs={{0,1},{1,0},{2,3},{3,2},{4,5},{5,4},{6,7},{7,6},{8,9},{9,8},{10,11... | collective-permute-start | bytes 786440 | tf_op jit(solution)/shard_map/ppermute | solution.py:152
  223.4 20.6 %collective-permute-done.26 = bf16[4,4,64,128]{3,2,1,0:T(8,128)(2,1)S(1)} collective-permute-done((bf16[4,4,64,128]{3,2,1,0:T(8,128)(2,1)S(1)}, bf16[4,4,64,128]{3,2,1,0:T(8,128)(2,1)S(1)}, u32[]{:S(2)}, u32[]{:S(2)}) %collective-permute-start.26) | collective-permute-done | bytes 262176 | tf_op jit(solution)/shard_map/ppermute | solution.py:152
  (111 shorter events, 66.7 us)
Async XLA Ops:
  1.0 51.8 %collective-permute-start.2 = (bf16[4,5,64,128]{3,2,1,0:T(8,128)(2,1)S(1)}, bf16[4,5,64,128]{3,2,1,0:T(8,128)(2,1)S(1)}, u32[]{:S(2)}, u32[]{:S(2)}) collective-permute-start(bf16[4,5,64,128]{3,2,1,0:T(8,128)(2,1)S(1)} %constant_dynamic-slice_fusion.4), channel_id=1, source_target_pairs={{0,1},{1,0},{2,3},{3,2},{4,5},{5,4},{6,7},{7,6},{8,9},{9,8},{10,11... | collective-permute-start | bytes 983048 | tf_op jit(solution)/shard_map/ppermute | solution.py:62
  18.8 14.0 %collective-permute-start.4 = (bf16[12,16,128]{2,1,0:T(8,128)(2,1)S(1)}, bf16[12,16,128]{2,1,0:T(8,128)(2,1)S(1)}, u32[]{:S(2)}, u32[]{:S(2)}) collective-permute-start(bf16[12,16,128]{2,1,0:T(8,128)(2,1)S(1)} %constant_dynamic-update-slice_fusion), channel_id=1, source_target_pairs={{0,1},{1,0},{2,3},{3,2},{4,5},{5,4},{6,7},{7,6},{8,9},{9,8},{10,11... | collective-permute-start | bytes 147464 | tf_op jit(solution)/shard_map/ppermute | solution.py:67
  21.6 12.0 %collective-permute-start = (bf16[4,1,64,128]{3,2,1,0:T(8,128)(2,1)S(1)}, bf16[4,1,64,128]{3,2,1,0:T(8,128)(2,1)S(1)}, u32[]{:S(2)}, u32[]{:S(2)}) collective-permute-start(bf16[4,1,64,128]{3,2,1,0:T(8,128)(2,1)S(1)} %get-tuple-element.40), channel_id=1, source_target_pairs={{0,8},{8,16},{16,24},{24,32},{32,40},{40,48},{48,56},{1,9},{9,17},... | collective-permute-start | bytes 196616 | tf_op jit(solution)/shard_map/ppermute | solution.py:15
  24.3 27.4 %collective-permute-start.1 = (bf16[4,1,64,128]{3,2,1,0:T(8,128)(2,1)S(1)}, bf16[4,1,64,128]{3,2,1,0:T(8,128)(2,1)S(1)}, u32[]{:S(2)}, u32[]{:S(2)}) collective-permute-start(bf16[4,1,64,128]{3,2,1,0:T(8,128)(2,1)S(1)} %get-tuple-element.39), channel_id=1, source_target_pairs={{8,0},{16,8},{24,16},{32,24},{40,32},{48,40},{56,48},{9,1},{17,9},... | collective-permute-start | bytes 196616 | tf_op jit(solution)/shard_map/ppermute | solution.py:18
  25.6 27.2 %collective-permute-start.3 = (bf16[4,1,64,128]{3,2,1,0:T(8,128)(2,1)S(1)}, bf16[4,1,64,128]{3,2,1,0:T(8,128)(2,1)S(1)}, u32[]{:S(2)}, u32[]{:S(2)}) collective-permute-start(bf16[4,1,64,128]{3,2,1,0:T(8,128)(2,1)S(1)} %get-tuple-element.38), channel_id=1, source_target_pairs={{1,8},{9,16},{17,24},{25,32},{33,40},{41,48},{49,56},{8,1},{16,9},... | collective-permute-start | bytes 196616 | tf_op jit(solution)/shard_map/ppermute | solution.py:66
  52.8 16.4 %collective-permute-start.7 = (bf16[12,16,256]{2,1,0:T(8,128)(2,1)S(1)}, bf16[12,16,256]{2,1,0:T(8,128)(2,1)S(1)}, u32[]{:S(2)}, u32[]{:S(2)}) collective-permute-start(bf16[12,16,256]{2,1,0:T(8,128)(2,1)S(1)} %maximum_select_fusion.7), channel_id=1, source_target_pairs={{0,32},{8,40},{16,48},{24,56},{32,0},{40,8},{48,16},{56,24},{1,33}... | collective-permute-start | bytes 294920 | tf_op jit(solution)/shard_map/ppermute | solution.py:44
  62.7 29.2 %collective-permute-start.5 = (bf16[4,6,64,256]{3,2,1,0:T(8,128)(2,1)}, bf16[4,6,64,256]{3,2,1,0:T(8,128)(2,1)S(1)}, u32[]{:S(2)}, u32[]{:S(2)}) collective-permute-start(bf16[4,6,64,256]{3,2,1,0:T(8,128)(2,1)} %get-tuple-element.28), channel_id=1, source_target_pairs={{0,2},{2,4},{4,6},{6,0},{1,3},{3,5},{5,7},{7,1},{8,10},{10,12},{12... | collective-permute-start | bytes 2359304 | tf_op jit(solution)/shard_map/ppermute | solution.py:23
  65.8 26.1 %collective-permute-start.6 = (bf16[4,6,64,256]{3,2,1,0:T(8,128)(2,1)}, bf16[4,6,64,256]{3,2,1,0:T(8,128)(2,1)S(1)}, u32[]{:S(2)}, u32[]{:S(2)}) collective-permute-start(bf16[4,6,64,256]{3,2,1,0:T(8,128)(2,1)} %get-tuple-element.28), channel_id=1, source_target_pairs={{0,6},{2,0},{4,2},{6,4},{1,7},{3,1},{5,3},{7,5},{8,14},{10,8},{12,... | collective-permute-start | bytes 2359304 | tf_op jit(solution)/shard_map/ppermute | solution.py:23
  76.9 14.9 %collective-permute-start.9 = (bf16[12,2,2,16,256]{4,3,1,0,2:T(8,128)(2,1)S(1)}, bf16[12,2,2,16,256]{4,3,1,0,2:T(8,128)(2,1)S(1)}, u32[]{:S(2)}, u32[]{:S(2)}) collective-permute-start(bf16[12,2,2,16,256]{4,3,1,0,2:T(8,128)(2,1)S(1)} %maximum_select_fusion.4), channel_id=1, source_target_pairs={{0,8},{8,0},{16,24},{24,16},{32,40},{40,32},{48,56},{56,48},{1,9},... | collective-permute-start | bytes 1179656 | tf_op jit(solution)/shard_map/ppermute | solution.py:44
  92.8 29.6 %collective-permute-start.12 = (bf16[12,128,256]{2,1,0:T(8,128)(2,1)S(1)}, bf16[12,128,256]{2,1,0:T(8,128)(2,1)S(1)}, u32[]{:S(2)}, u32[]{:S(2)}) collective-permute-start(bf16[12,128,256]{2,1,0:T(8,128)(2,1)S(1)} %bitcast.107), channel_id=1, source_target_pairs={{0,128},{128,256},{256,384},{384,0},{1,129},{129,257},{257,385},{3... | collective-permute-start | bytes 2359304 | tf_op jit(solution)/shard_map/ppermute | solution.py:23
  96.0 26.4 %collective-permute-start.13 = (bf16[12,128,256]{2,1,0:T(8,128)(2,1)S(1)}, bf16[12,128,256]{2,1,0:T(8,128)(2,1)S(1)}, u32[]{:S(2)}, u32[]{:S(2)}) collective-permute-start(bf16[12,128,256]{2,1,0:T(8,128)(2,1)S(1)} %bitcast.108), channel_id=1, source_target_pairs={{0,384},{128,0},{256,128},{384,256},{1,385},{129,1},{257,129},{385... | collective-permute-start | bytes 2359304 | tf_op jit(solution)/shard_map/ppermute | solution.py:23
  101.1 21.3 %collective-permute-start.10 = (bf16[4,6,64,128]{3,2,1,0:T(8,128)(2,1)}, bf16[4,6,64,128]{3,2,1,0:T(8,128)(2,1)S(1)}, u32[]{:S(2)}, u32[]{:S(2)}) collective-permute-start(bf16[4,6,64,128]{3,2,1,0:T(8,128)(2,1)} %slice.88), channel_id=1, source_target_pairs={{0,6},{2,0},{4,2},{6,4},{1,7},{3,1},{5,3},{7,5},{8,14},{10,8},{12,... | collective-permute-start | bytes 1179656 | tf_op jit(solution)/shard_map/ppermute | solution.py:23
  107.4 15.0 %collective-permute-start.11 = (bf16[4,6,64,128]{3,2,1,0:T(8,128)(2,1)}, bf16[4,6,64,128]{3,2,1,0:T(8,128)(2,1)}, u32[]{:S(2)}, u32[]{:S(2)}) collective-permute-start(bf16[4,6,64,128]{3,2,1,0:T(8,128)(2,1)} %slice.89), channel_id=1, source_target_pairs={{0,2},{2,4},{4,6},{6,0},{1,3},{3,5},{5,7},{7,1},{8,10},{10,12},{12... | collective-permute-start | bytes 1179656 | tf_op jit(solution)/shard_map/ppermute | solution.py:23
  109.4 13.0 %collective-permute-start.19 = (f32[2,128]{1,0:T(2,128)S(1)}, f32[2,128]{1,0:T(2,128)S(1)}, u32[]{:S(2)}, u32[]{:S(2)}) collective-permute-start(f32[2,128]{1,0:T(2,128)S(1)} %pad_maximum_fusion.4), channel_id=1, source_target_pairs={{0,1},{1,0},{2,3},{3,2},{4,5},{5,4},{6,7},{7,6},{8,9},{9,8},{10,11... | collective-permute-start | bytes 3080 | tf_op jit(solution)/shard_map/ppermute | solution.py:59
  122.7 26.7 %collective-permute-start.16 = (bf16[12,3,128,256]{3,2,0,1:T(8,128)(2,1)S(1)}, bf16[12,3,128,256]{3,2,0,1:T(8,128)(2,1)S(1)}, u32[]{:S(2)}, u32[]{:S(2)}) collective-permute-start(bf16[12,3,128,256]{3,2,0,1:T(8,128)(2,1)S(1)} %pad_maximum_fusion), channel_id=1, source_target_pairs={{0,64},{64,0},{1,65},{65,1},{2,66},{66,2},{3,67},{67,3},{4,68},{68... | collective-permute-start | bytes 7077896 | tf_op jit(solution)/shard_map/ppermute | solution.py:93
  129.6 19.2 %collective-permute-start.14 = (bf16[12,64,256]{2,1,0:T(8,128)(2,1)S(1)}, bf16[12,64,256]{2,1,0:T(8,128)(2,1)S(1)}, u32[]{:S(2)}, u32[]{:S(2)}) collective-permute-start(bf16[12,64,256]{2,1,0:T(8,128)(2,1)S(1)} %slice.90), channel_id=1, source_target_pairs={{0,384},{128,0},{256,128},{384,256},{1,385},{129,1},{257,129},{385... | collective-permute-start | bytes 1179656 | tf_op jit(solution)/shard_map/ppermute | solution.py:23
  133.1 18.0 %collective-permute-start.17 = (bf16[12,64,256]{2,1,0:T(8,128)(2,1)S(1)}, bf16[12,64,256]{2,1,0:T(8,128)(2,1)S(1)}, u32[]{:S(2)}, u32[]{:S(2)}) collective-permute-start(bf16[12,64,256]{2,1,0:T(8,128)(2,1)S(1)} %slice.90), channel_id=1, source_target_pairs={{192,0},{128,64},{320,128},{256,192},{448,256},{384,320},{64,384},... | collective-permute-start | bytes 1179656 | tf_op jit(solution)/shard_map/ppermute | solution.py:90
  135.6 13.6 %collective-permute-start.15 = (bf16[12,64,256]{2,1,0:T(8,128)(2,1)S(1)}, bf16[12,64,256]{2,1,0:T(8,128)(2,1)S(1)}, u32[]{:S(2)}, u32[]{:S(2)}) collective-permute-start(bf16[12,64,256]{2,1,0:T(8,128)(2,1)S(1)} %slice.91), channel_id=1, source_target_pairs={{0,128},{128,256},{256,384},{384,0},{1,129},{129,257},{257,385},{3... | collective-permute-start | bytes 1179656 | tf_op jit(solution)/shard_map/ppermute | solution.py:23
  138.6 19.5 %collective-permute-start.18 = (bf16[12,64,256]{2,1,0:T(8,128)(2,1)S(1)}, bf16[12,64,256]{2,1,0:T(8,128)(2,1)S(1)}, u32[]{:S(2)}, u32[]{:S(2)}) collective-permute-start(bf16[12,64,256]{2,1,0:T(8,128)(2,1)S(1)} %slice.91), channel_id=1, source_target_pairs={{448,0},{384,64},{64,128},{0,192},{192,256},{128,320},{320,384},{2... | collective-permute-start | bytes 1179656 | tf_op jit(solution)/shard_map/ppermute | solution.py:91
  167.9 16.1 %collective-permute-start.20 = (bf16[4,4,64,256]{3,2,1,0:T(8,128)(2,1)S(1)}, bf16[4,4,64,256]{3,2,1,0:T(8,128)(2,1)S(1)}, u32[]{:S(2)}, u32[]{:S(2)}) collective-permute-start(bf16[4,4,64,256]{3,2,1,0:T(8,128)(2,1)S(1)} %bitcast.124), channel_id=1, source_target_pairs={{0,6},{2,0},{4,2},{6,4},{1,7},{3,1},{5,3},{7,5},{8,14},{10,8},{12,... | collective-permute-start | bytes 1572872 | tf_op jit(solution)/shard_map/ppermute | solution.py:23
  172.7 16.7 %collective-permute-start.22 = (bf16[4,4,64,256]{3,2,1,0:T(8,128)(2,1)S(1)}, bf16[4,4,64,256]{3,2,1,0:T(8,128)(2,1)S(1)}, u32[]{:S(2)}, u32[]{:S(2)}) collective-permute-start(bf16[4,4,64,256]{3,2,1,0:T(8,128)(2,1)S(1)} %bitcast.125), channel_id=1, source_target_pairs={{0,2},{2,4},{4,6},{6,0},{1,3},{3,5},{5,7},{7,1},{8,10},{10,12},{12... | collective-permute-start | bytes 1572872 | tf_op jit(solution)/shard_map/ppermute | solution.py:23
  184.0 10.1 %collective-permute-start.21 = (bf16[4,4,64,128]{3,2,1,0:T(8,128)(2,1)S(1)}, bf16[4,4,64,128]{3,2,1,0:T(8,128)(2,1)S(1)}, u32[]{:S(2)}, u32[]{:S(2)}) collective-permute-start(bf16[4,4,64,128]{3,2,1,0:T(8,128)(2,1)S(1)} %slice.122), channel_id=1, source_target_pairs={{0,6},{2,0},{4,2},{6,4},{1,7},{3,1},{5,3},{7,5},{8,14},{10,8},{12,... | collective-permute-start | bytes 786440 | tf_op jit(solution)/shard_map/ppermute | solution.py:23
  199.7 10.5 %collective-permute-start.25 = (bf16[1,4,64,1024]{3,2,1,0:T(8,128)(2,1)S(1)}, bf16[1,4,64,1024]{3,2,1,0:T(8,128)(2,1)S(1)}, u32[]{:S(2)}, u32[]{:S(2)}) collective-permute-start(bf16[1,4,64,1024]{3,2,1,0:T(8,128)(2,1)S(1)} %get-tuple-element.33), channel_id=1, source_target_pairs={{64,0},{128,64},{192,128},{256,192},{320,256},{384,320},{448,384},... | collective-permute-start | bytes 1572872 | tf_op jit(solution)/shard_map/ppermute | solution.py:18
  214.1 30.0 %collective-permute-start.26 = (bf16[4,4,64,128]{3,2,1,0:T(8,128)(2,1)S(1)}, bf16[4,4,64,128]{3,2,1,0:T(8,128)(2,1)S(1)}, u32[]{:S(2)}, u32[]{:S(2)}) collective-permute-start(bf16[4,4,64,128]{3,2,1,0:T(8,128)(2,1)S(1)} %get-tuple-element.36), channel_id=1, source_target_pairs={{0,1},{1,0},{2,3},{3,2},{4,5},{5,4},{6,7},{7,6},{8,9},{9,8},{10,11... | collective-permute-start | bytes 786440 | tf_op jit(solution)/shard_map/ppermute | solution.py:152
  (11 other events, 128.1 us)

commit v15 on v14

--- a/solution.py
+++ b/solution.py
@@ -64,14 +64,22 @@
     diagonal = [(q * 2 + 1, q * 2 + 2) for q in range(row_n - 1)]
     diagonal += [(q * 2, q * 2 - 1) for q in range(1, row_n)]
     rim = lax.ppermute(edge, ("row", "cz"), diagonal)
-    w_block = ordered_pair(weight, lax.ppermute(weight, "cz", SWAP), high, 2)
+    far_row = row_n // 2
+    cross = [(q * 2 + c, (q ^ far_row) * 2 + 1 - c) for q in range(row_n) for c in range(2)]
+    w_cz = lax.ppermute(weight, "cz", SWAP)
+    w_row = lax.ppermute(weight, "row", [(q, q ^ far_row) for q in range(row_n)])
+    w_cross = lax.ppermute(weight, ("row", "cz"), cross)
+    near = ordered_pair(weight, w_cz, high, 2)
+    away = ordered_pair(w_row, w_cross, high, 2)
+    row_high = (lax.axis_index("row") // far_row) % 2 == 1
+    w_block = jnp.where(row_high, jnp.stack([away, near], axis=1), jnp.stack([near, away], axis=1))
     rimmed, partner, rim, w_block = lax.optimization_barrier((rimmed, partner, rim, w_block))
     mine = lax.dynamic_slice_in_dim(rimmed, side * half, half + 2, axis=1)
     pair = ordered_pair(mine, ordered_pair(rim, partner, high, 1), high, 3)
     from_left = ring_shift(pair, "cx", ring, 1)
     from_right = ring_shift(pair, "cx", ring, -1)
-    for pos, bit in enumerate((4, 2, 1)):
-        w_block = xor_stack(w_block, "row", bit, 1 + pos)
+    for pos, bit in enumerate((2, 1)):
+        w_block = xor_stack(w_block, "row", bit, 2 + pos)
     w_block = w_block.reshape(taps, row_n * depth, -1)
     from_left, from_right, w_block = lax.optimization_barrier((from_left, from_right, w_block))
     fy_n = lax.axis_size("fy")

time: 249 us -> 264 us (1.060)
  the two profiles are of different devices: /device:TPU:1 before, /device:TPU:40 now
where the time goes in v15:
time: 264 us; the launch traced here: 263 us
  waiting for transfers between devices  118 us (45%)
  starting transfers between devices  109 us (41%)
  local copies, waits for them, and re-layouts  20.6 us (8%)
  matrix products  8.5 us (3%)
  other arithmetic  6.34 us (2%)
    ppermute x12, starting transfers between devices, ring_shift(): lax.ppermute(block, axis, [(i, (i + step) % count) for i in range(count)])  40.1 us
    ppermute x1, waiting for transfers between devices, body(): rim = lax.ppermute(edge, ('row', 'cz'), diagonal)  36 us
    ppermute x1, waiting for transfers between devices, body(): returned = lax.ppermute(given, 'cz', SWAP)  26.7 us
    ppermute x12, waiting for transfers between devices, ring_shift(): lax.ppermute(block, axis, [(i, (i + step) % count) for i in range(count)])  23.9 us
    ppermute x1, starting transfers between devices, body(): w_cross = lax.ppermute(weight, ('row', 'cz'), cross)  11.8 us
    ppermute x1, starting transfers between devices, body(): partner = lax.ppermute(sent, 'cz', SWAP)  10.8 us
    ppermute x2, waiting for transfers between devices, xor_stack(): other = lax.ppermute(block, axis, [(i, i ^ bit) for i in range(count)])  10.3 us
    unnamed x26, local copies, waits for them, and re-layouts  7.94 us
  transfers between devices with their start and end apart: 28, of which 14 were waited for; matrix products, arithmetic and copies ran while one was open for 8% of the time, Pallas kernels for 0%

profile of v15, /device:TPU:40, one launch (start us, length us, event | category | flops | bytes accessed | tf_op | source)
XLA Modules:
  0.0 263.3 jit_solution(8833303075169802204)
XLA Ops:
  1.5 11.8 %collective-permute-start.4 = (bf16[12,16,128]{2,1,0:T(8,128)(2,1)S(1)}, bf16[12,16,128]{2,1,0:T(8,128)(2,1)S(1)}, u32[]{:S(2)}, u32[]{:S(2)}) collective-permute-start(bf16[12,16,128]{2,1,0:T(8,128)(2,1)S(1)} %constant_dynamic-update-slice_fusion), channel_id=1, source_target_pairs={{0,33},{1,32},{8,41},{9,40},{16,49},{17,48},{24,57},{25,56},{32,1}... | collective-permute-start | bytes 147464 | tf_op jit(solution)/shard_map/ppermute | solution.py:71
  13.3 5.5 %collective-permute-start.5 = (bf16[12,16,128]{2,1,0:T(8,128)(2,1)S(1)}, bf16[12,16,128]{2,1,0:T(8,128)(2,1)S(1)}, u32[]{:S(2)}, u32[]{:S(2)}) collective-permute-start(bf16[12,16,128]{2,1,0:T(8,128)(2,1)S(1)} %constant_dynamic-update-slice_fusion), channel_id=1, source_target_pairs={{0,32},{8,40},{16,48},{24,56},{32,0},{40,8},{48,16},{56,24},{1,33}... | collective-permute-start | bytes 147464 | tf_op jit(solution)/shard_map/ppermute | solution.py:70
  18.8 3.7 %collective-permute-start.6 = (bf16[12,16,128]{2,1,0:T(8,128)(2,1)S(1)}, bf16[12,16,128]{2,1,0:T(8,128)(2,1)S(1)}, u32[]{:S(2)}, u32[]{:S(2)}) collective-permute-start(bf16[12,16,128]{2,1,0:T(8,128)(2,1)S(1)} %constant_dynamic-update-slice_fusion), channel_id=1, source_target_pairs={{0,1},{1,0},{2,3},{3,2},{4,5},{5,4},{6,7},{7,6},{8,9},{9,8},{10,11... | collective-permute-start | bytes 147464 | tf_op jit(solution)/shard_map/ppermute | solution.py:69
  30.4 10.8 %collective-permute-start.2 = (bf16[4,5,64,128]{3,2,1,0:T(8,128)(2,1)S(1)}, bf16[4,5,64,128]{3,2,1,0:T(8,128)(2,1)S(1)}, u32[]{:S(2)}, u32[]{:S(2)}) collective-permute-start(bf16[4,5,64,128]{3,2,1,0:T(8,128)(2,1)S(1)} %constant_dynamic-slice_fusion.4), channel_id=1, source_target_pairs={{0,1},{1,0},{2,3},{3,2},{4,5},{5,4},{6,7},{7,6},{8,9},{9,8},{10,11... | collective-permute-start | bytes 983048 | tf_op jit(solution)/shard_map/ppermute | solution.py:62
  44.4 36.0 %collective-permute-done.3 = bf16[4,1,64,128]{3,2,1,0:T(8,128)(2,1)S(1)} collective-permute-done((bf16[4,1,64,128]{3,2,1,0:T(8,128)(2,1)S(1)}, bf16[4,1,64,128]{3,2,1,0:T(8,128)(2,1)S(1)}, u32[]{:S(2)}, u32[]{:S(2)}) %collective-permute-start.3) | collective-permute-done | bytes 65568 | tf_op jit(solution)/shard_map/ppermute | solution.py:66
  83.9 3.4 %collective-permute-start.7 = (bf16[4,6,64,256]{3,2,1,0:T(8,128)(2,1)}, bf16[4,6,64,256]{3,2,1,0:T(8,128)(2,1)S(1)}, u32[]{:S(2)}, u32[]{:S(2)}) collective-permute-start(bf16[4,6,64,256]{3,2,1,0:T(8,128)(2,1)} %get-tuple-element.28), channel_id=1, source_target_pairs={{0,2},{2,4},{4,6},{6,0},{1,3},{3,5},{5,7},{7,1},{8,10},{10,12},{12... | collective-permute-start | bytes 2359304 | tf_op jit(solution)/shard_map/ppermute | solution.py:23
  87.3 3.7 %collective-permute-start.8 = (bf16[4,6,64,256]{3,2,1,0:T(8,128)(2,1)}, bf16[4,6,64,256]{3,2,1,0:T(8,128)(2,1)S(1)}, u32[]{:S(2)}, u32[]{:S(2)}) collective-permute-start(bf16[4,6,64,256]{3,2,1,0:T(8,128)(2,1)} %get-tuple-element.28), channel_id=1, source_target_pairs={{0,6},{2,0},{4,2},{6,4},{1,7},{3,1},{5,3},{7,5},{8,14},{10,8},{12,... | collective-permute-start | bytes 2359304 | tf_op jit(solution)/shard_map/ppermute | solution.py:23
  93.1 10.3 %collective-permute-done.10 = bf16[12,2,2,16,256]{4,3,1,0,2:T(8,128)(2,1)S(1)} collective-permute-done((bf16[12,2,2,16,256]{4,3,1,0,2:T(8,128)(2,1)S(1)}, bf16[12,2,2,16,256]{4,3,1,0,2:T(8,128)(2,1)S(1)}, u32[]{:S(2)}, u32[]{:S(2)}) %collective-permute-start.10) | collective-permute-done | bytes 393248 | tf_op jit(solution)/shard_map/ppermute | solution.py:44
  103.5 3.1 %collective-permute-done.7 = bf16[4,6,64,256]{3,2,1,0:T(8,128)(2,1)S(1)} collective-permute-done((bf16[4,6,64,256]{3,2,1,0:T(8,128)(2,1)}, bf16[4,6,64,256]{3,2,1,0:T(8,128)(2,1)S(1)}, u32[]{:S(2)}, u32[]{:S(2)}) %collective-permute-start.7) | collective-permute-done | bytes 786464 | tf_op jit(solution)/shard_map/ppermute | solution.py:23
  109.4 3.5 %collective-permute-start.13 = (bf16[12,128,256]{2,1,0:T(8,128)(2,1)S(1)}, bf16[12,128,256]{2,1,0:T(8,128)(2,1)S(1)}, u32[]{:S(2)}, u32[]{:S(2)}) collective-permute-start(bf16[12,128,256]{2,1,0:T(8,128)(2,1)S(1)} %bitcast.116), channel_id=1, source_target_pairs={{0,128},{128,256},{256,384},{384,0},{1,129},{129,257},{257,385},{3... | collective-permute-start | bytes 2359304 | tf_op jit(solution)/shard_map/ppermute | solution.py:23
  117.0 4.9 %collective-permute-start.11 = (bf16[4,6,64,128]{3,2,1,0:T(8,128)(2,1)}, bf16[4,6,64,128]{3,2,1,0:T(8,128)(2,1)S(1)}, u32[]{:S(2)}, u32[]{:S(2)}) collective-permute-start(bf16[4,6,64,128]{3,2,1,0:T(8,128)(2,1)} %slice.88), channel_id=1, source_target_pairs={{0,6},{2,0},{4,2},{6,4},{1,7},{3,1},{5,3},{7,5},{8,14},{10,8},{12,... | collective-permute-start | bytes 1179656 | tf_op jit(solution)/shard_map/ppermute | solution.py:23
  124.6 6.7 %collective-permute-start.20 = (f32[2,128]{1,0:T(2,128)S(1)}, f32[2,128]{1,0:T(2,128)S(1)}, u32[]{:S(2)}, u32[]{:S(2)}) collective-permute-start(f32[2,128]{1,0:T(2,128)S(1)} %pad_maximum_fusion.2), channel_id=1, source_target_pairs={{0,1},{1,0},{2,3},{3,2},{4,5},{5,4},{6,7},{7,6},{8,9},{9,8},{10,11... | collective-permute-start | bytes 3080 | tf_op jit(solution)/shard_map/ppermute | solution.py:59
  131.4 7.4 %collective-permute-done.20 = f32[2,128]{1,0:T(2,128)S(1)} collective-permute-done((f32[2,128]{1,0:T(2,128)S(1)}, f32[2,128]{1,0:T(2,128)S(1)}, u32[]{:S(2)}, u32[]{:S(2)}) %collective-permute-start.20) | collective-permute-done | bytes 1056 | tf_op jit(solution)/shard_map/ppermute | solution.py:59
  142.1 3.6 %collective-permute-start.15 = (bf16[12,64,256]{2,1,0:T(8,128)(2,1)S(1)}, bf16[12,64,256]{2,1,0:T(8,128)(2,1)S(1)}, u32[]{:S(2)}, u32[]{:S(2)}) collective-permute-start(bf16[12,64,256]{2,1,0:T(8,128)(2,1)S(1)} %slice.90), channel_id=1, source_target_pairs={{0,384},{128,0},{256,128},{384,256},{1,385},{129,1},{257,129},{385... | collective-permute-start | bytes 1179656 | tf_op jit(solution)/shard_map/ppermute | solution.py:23
  145.7 3.5 %collective-permute-start.18 = (bf16[12,64,256]{2,1,0:T(8,128)(2,1)S(1)}, bf16[12,64,256]{2,1,0:T(8,128)(2,1)S(1)}, u32[]{:S(2)}, u32[]{:S(2)}) collective-permute-start(bf16[12,64,256]{2,1,0:T(8,128)(2,1)S(1)} %slice.90), channel_id=1, source_target_pairs={{192,0},{128,64},{320,128},{256,192},{448,256},{384,320},{64,384},... | collective-permute-start | bytes 1179656 | tf_op jit(solution)/shard_map/ppermute | solution.py:98
  163.5 6.7 %collective-permute-done.19 = bf16[12,64,256]{2,1,0:T(8,128)(2,1)S(1)} collective-permute-done((bf16[12,64,256]{2,1,0:T(8,128)(2,1)S(1)}, bf16[12,64,256]{2,1,0:T(8,128)(2,1)S(1)}, u32[]{:S(2)}, u32[]{:S(2)}) %collective-permute-start.19) | collective-permute-done | bytes 393248 | tf_op jit(solution)/shard_map/ppermute | solution.py:99
  173.0 6.3 %convert_add_fusion = (f32[4,32,9,256]{3,1,2,0:T(8,128)S(1)}, bf16[4,32,9,256]{3,1,2,0:T(8,128)(2,1)S(1)}) fusion(f32[256]{0:T(256)S(1)} %bitcast.144, f32[256]{0:T(256)S(1)} %bitcast.145, bf16[3,3,1024,256]{3,2,1,0:T(8,128)(2,1)S(1)} %bitcast.123, bf16[6,4,8,11,1024]{4,1,3,2,0:T(4,128)(2,1)S(1)} %fusion.1, pred[32,9]{0,1:T(8,128)(4,1)S(1)} %copy-done.7), kind=kOutput, calls=%fused_computation.17 | convolution fusion | flops 5438767104 | bytes 10815776 | tf_op jit(solution)/shard_map/conv_general_dilated | solution.py:125
  180.1 5.1 %collective-permute-start.21 = (bf16[4,4,64,256]{3,2,1,0:T(8,128)(2,1)S(1)}, bf16[4,4,64,256]{3,2,1,0:T(8,128)(2,1)S(1)}, u32[]{:S(2)}, u32[]{:S(2)}) collective-permute-start(bf16[4,4,64,256]{3,2,1,0:T(8,128)(2,1)S(1)} %bitcast.132), channel_id=1, source_target_pairs={{0,6},{2,0},{4,2},{6,4},{1,7},{3,1},{5,3},{7,5},{8,14},{10,8},{12,... | collective-permute-start | bytes 1572872 | tf_op jit(solution)/shard_map/ppermute | solution.py:23
  187.4 9.6 %collective-permute-done.21 = bf16[4,4,64,256]{3,2,1,0:T(8,128)(2,1)S(1)} collective-permute-done((bf16[4,4,64,256]{3,2,1,0:T(8,128)(2,1)S(1)}, bf16[4,4,64,256]{3,2,1,0:T(8,128)(2,1)S(1)}, u32[]{:S(2)}, u32[]{:S(2)}) %collective-permute-start.21) | collective-permute-done | bytes 524320 | tf_op jit(solution)/shard_map/ppermute | solution.py:23
  197.0 5.6 %collective-permute-start.22 = (bf16[4,4,64,128]{3,2,1,0:T(8,128)(2,1)S(1)}, bf16[4,4,64,128]{3,2,1,0:T(8,128)(2,1)S(1)}, u32[]{:S(2)}, u32[]{:S(2)}) collective-permute-start(bf16[4,4,64,128]{3,2,1,0:T(8,128)(2,1)S(1)} %slice.122), channel_id=1, source_target_pairs={{0,6},{2,0},{4,2},{6,4},{1,7},{3,1},{5,3},{7,5},{8,14},{10,8},{12,... | collective-permute-start | bytes 786440 | tf_op jit(solution)/shard_map/ppermute | solution.py:23
  208.1 5.5 %collective-permute-done.24 = bf16[4,4,64,128]{3,2,1,0:T(8,128)(2,1)S(1)} collective-permute-done((bf16[4,4,64,128]{3,2,1,0:T(8,128)(2,1)S(1)}, bf16[4,4,64,128]{3,2,1,0:T(8,128)(2,1)S(1)}, u32[]{:S(2)}, u32[]{:S(2)}) %collective-permute-start.24) | collective-permute-done | bytes 262176 | tf_op jit(solution)/shard_map/ppermute | solution.py:23
  223.2 4.9 %collective-permute-done.25 = bf16[1,4,64,1024]{3,2,1,0:T(8,128)(2,1)S(1)} collective-permute-done((bf16[1,4,64,1024]{3,2,1,0:T(8,128)(2,1)S(1)}, bf16[1,4,64,1024]{3,2,1,0:T(8,128)(2,1)S(1)}, u32[]{:S(2)}, u32[]{:S(2)}) %collective-permute-start.25) | collective-permute-done | bytes 524320 | tf_op jit(solution)/shard_map/ppermute | solution.py:15
  229.0 6.7 %collective-permute-start.27 = (bf16[4,4,64,128]{3,2,1,0:T(8,128)(2,1)S(1)}, bf16[4,4,64,128]{3,2,1,0:T(8,128)(2,1)S(1)}, u32[]{:S(2)}, u32[]{:S(2)}) collective-permute-start(bf16[4,4,64,128]{3,2,1,0:T(8,128)(2,1)S(1)} %get-tuple-element.36), channel_id=1, source_target_pairs={{0,1},{1,0},{2,3},{3,2},{4,5},{5,4},{6,7},{7,6},{8,9},{9,8},{10,11... | collective-permute-start | bytes 786440 | tf_op jit(solution)/shard_map/ppermute | solution.py:160
  235.7 26.7 %collective-permute-done.27 = bf16[4,4,64,128]{3,2,1,0:T(8,128)(2,1)S(1)} collective-permute-done((bf16[4,4,64,128]{3,2,1,0:T(8,128)(2,1)S(1)}, bf16[4,4,64,128]{3,2,1,0:T(8,128)(2,1)S(1)}, u32[]{:S(2)}, u32[]{:S(2)}) %collective-permute-start.27) | collective-permute-done | bytes 262176 | tf_op jit(solution)/shard_map/ppermute | solution.py:160
  (111 shorter events, 67.5 us)
Async XLA Ops:
  1.5 28.9 %collective-permute-start.4 = (bf16[12,16,128]{2,1,0:T(8,128)(2,1)S(1)}, bf16[12,16,128]{2,1,0:T(8,128)(2,1)S(1)}, u32[]{:S(2)}, u32[]{:S(2)}) collective-permute-start(bf16[12,16,128]{2,1,0:T(8,128)(2,1)S(1)} %constant_dynamic-update-slice_fusion), channel_id=1, source_target_pairs={{0,33},{1,32},{8,41},{9,40},{16,49},{17,48},{24,57},{25,56},{32,1}... | collective-permute-start | bytes 147464 | tf_op jit(solution)/shard_map/ppermute | solution.py:71
  13.3 27.9 %collective-permute-start.5 = (bf16[12,16,128]{2,1,0:T(8,128)(2,1)S(1)}, bf16[12,16,128]{2,1,0:T(8,128)(2,1)S(1)}, u32[]{:S(2)}, u32[]{:S(2)}) collective-permute-start(bf16[12,16,128]{2,1,0:T(8,128)(2,1)S(1)} %constant_dynamic-update-slice_fusion), channel_id=1, source_target_pairs={{0,32},{8,40},{16,48},{24,56},{32,0},{40,8},{48,16},{56,24},{1,33}... | collective-permute-start | bytes 147464 | tf_op jit(solution)/shard_map/ppermute | solution.py:70
  18.8 24.4 %collective-permute-start.6 = (bf16[12,16,128]{2,1,0:T(8,128)(2,1)S(1)}, bf16[12,16,128]{2,1,0:T(8,128)(2,1)S(1)}, u32[]{:S(2)}, u32[]{:S(2)}) collective-permute-start(bf16[12,16,128]{2,1,0:T(8,128)(2,1)S(1)} %constant_dynamic-update-slice_fusion), channel_id=1, source_target_pairs={{0,1},{1,0},{2,3},{3,2},{4,5},{5,4},{6,7},{7,6},{8,9},{9,8},{10,11... | collective-permute-start | bytes 147464 | tf_op jit(solution)/shard_map/ppermute | solution.py:69
  23.5 19.8 %collective-permute-start = (bf16[4,1,64,128]{3,2,1,0:T(8,128)(2,1)S(1)}, bf16[4,1,64,128]{3,2,1,0:T(8,128)(2,1)S(1)}, u32[]{:S(2)}, u32[]{:S(2)}) collective-permute-start(bf16[4,1,64,128]{3,2,1,0:T(8,128)(2,1)S(1)} %get-tuple-element.40), channel_id=1, source_target_pairs={{0,8},{8,16},{16,24},{24,32},{32,40},{40,48},{48,56},{1,9},{9,17},... | collective-permute-start | bytes 196616 | tf_op jit(solution)/shard_map/ppermute | solution.py:15
  26.4 16.9 %collective-permute-start.1 = (bf16[4,1,64,128]{3,2,1,0:T(8,128)(2,1)S(1)}, bf16[4,1,64,128]{3,2,1,0:T(8,128)(2,1)S(1)}, u32[]{:S(2)}, u32[]{:S(2)}) collective-permute-start(bf16[4,1,64,128]{3,2,1,0:T(8,128)(2,1)S(1)} %get-tuple-element.39), channel_id=1, source_target_pairs={{8,0},{16,8},{24,16},{32,24},{40,32},{48,40},{56,48},{9,1},{17,9},... | collective-permute-start | bytes 196616 | tf_op jit(solution)/shard_map/ppermute | solution.py:18
  30.4 50.0 %collective-permute-start.2 = (bf16[4,5,64,128]{3,2,1,0:T(8,128)(2,1)S(1)}, bf16[4,5,64,128]{3,2,1,0:T(8,128)(2,1)S(1)}, u32[]{:S(2)}, u32[]{:S(2)}) collective-permute-start(bf16[4,5,64,128]{3,2,1,0:T(8,128)(2,1)S(1)} %constant_dynamic-slice_fusion.4), channel_id=1, source_target_pairs={{0,1},{1,0},{2,3},{3,2},{4,5},{5,4},{6,7},{7,6},{8,9},{9,8},{10,11... | collective-permute-start | bytes 983048 | tf_op jit(solution)/shard_map/ppermute | solution.py:62
  41.2 39.1 %collective-permute-start.3 = (bf16[4,1,64,128]{3,2,1,0:T(8,128)(2,1)S(1)}, bf16[4,1,64,128]{3,2,1,0:T(8,128)(2,1)S(1)}, u32[]{:S(2)}, u32[]{:S(2)}) collective-permute-start(bf16[4,1,64,128]{3,2,1,0:T(8,128)(2,1)S(1)} %get-tuple-element.38), channel_id=1, source_target_pairs={{1,8},{9,16},{17,24},{25,32},{33,40},{41,48},{49,56},{8,1},{16,9},... | collective-permute-start | bytes 196616 | tf_op jit(solution)/shard_map/ppermute | solution.py:66
  83.9 22.7 %collective-permute-start.7 = (bf16[4,6,64,256]{3,2,1,0:T(8,128)(2,1)}, bf16[4,6,64,256]{3,2,1,0:T(8,128)(2,1)S(1)}, u32[]{:S(2)}, u32[]{:S(2)}) collective-permute-start(bf16[4,6,64,256]{3,2,1,0:T(8,128)(2,1)} %get-tuple-element.28), channel_id=1, source_target_pairs={{0,2},{2,4},{4,6},{6,0},{1,3},{3,5},{5,7},{7,1},{8,10},{10,12},{12... | collective-permute-start | bytes 2359304 | tf_op jit(solution)/shard_map/ppermute | solution.py:23
  87.3 21.2 %collective-permute-start.8 = (bf16[4,6,64,256]{3,2,1,0:T(8,128)(2,1)}, bf16[4,6,64,256]{3,2,1,0:T(8,128)(2,1)S(1)}, u32[]{:S(2)}, u32[]{:S(2)}) collective-permute-start(bf16[4,6,64,256]{3,2,1,0:T(8,128)(2,1)} %get-tuple-element.28), channel_id=1, source_target_pairs={{0,6},{2,0},{4,2},{6,4},{1,7},{3,1},{5,3},{7,5},{8,14},{10,8},{12,... | collective-permute-start | bytes 2359304 | tf_op jit(solution)/shard_map/ppermute | solution.py:23
  91.1 12.3 %collective-permute-start.10 = (bf16[12,2,2,16,256]{4,3,1,0,2:T(8,128)(2,1)S(1)}, bf16[12,2,2,16,256]{4,3,1,0,2:T(8,128)(2,1)S(1)}, u32[]{:S(2)}, u32[]{:S(2)}) collective-permute-start(bf16[12,2,2,16,256]{4,3,1,0,2:T(8,128)(2,1)S(1)} %maximum_select_fusion.4), channel_id=1, source_target_pairs={{0,8},{8,0},{16,24},{24,16},{32,40},{40,32},{48,56},{56,48},{1,9},... | collective-permute-start | bytes 1179656 | tf_op jit(solution)/shard_map/ppermute | solution.py:44
  109.4 29.5 %collective-permute-start.13 = (bf16[12,128,256]{2,1,0:T(8,128)(2,1)S(1)}, bf16[12,128,256]{2,1,0:T(8,128)(2,1)S(1)}, u32[]{:S(2)}, u32[]{:S(2)}) collective-permute-start(bf16[12,128,256]{2,1,0:T(8,128)(2,1)S(1)} %bitcast.116), channel_id=1, source_target_pairs={{0,128},{128,256},{256,384},{384,0},{1,129},{129,257},{257,385},{3... | collective-permute-start | bytes 2359304 | tf_op jit(solution)/shard_map/ppermute | solution.py:23
  112.8 26.0 %collective-permute-start.14 = (bf16[12,128,256]{2,1,0:T(8,128)(2,1)S(1)}, bf16[12,128,256]{2,1,0:T(8,128)(2,1)S(1)}, u32[]{:S(2)}, u32[]{:S(2)}) collective-permute-start(bf16[12,128,256]{2,1,0:T(8,128)(2,1)S(1)} %bitcast.117), channel_id=1, source_target_pairs={{0,384},{128,0},{256,128},{384,256},{1,385},{129,1},{257,129},{385... | collective-permute-start | bytes 2359304 | tf_op jit(solution)/shard_map/ppermute | solution.py:23
  117.0 21.8 %collective-permute-start.11 = (bf16[4,6,64,128]{3,2,1,0:T(8,128)(2,1)}, bf16[4,6,64,128]{3,2,1,0:T(8,128)(2,1)S(1)}, u32[]{:S(2)}, u32[]{:S(2)}) collective-permute-start(bf16[4,6,64,128]{3,2,1,0:T(8,128)(2,1)} %slice.88), channel_id=1, source_target_pairs={{0,6},{2,0},{4,2},{6,4},{1,7},{3,1},{5,3},{7,5},{8,14},{10,8},{12,... | collective-permute-start | bytes 1179656 | tf_op jit(solution)/shard_map/ppermute | solution.py:23
  122.7 16.2 %collective-permute-start.12 = (bf16[4,6,64,128]{3,2,1,0:T(8,128)(2,1)}, bf16[4,6,64,128]{3,2,1,0:T(8,128)(2,1)}, u32[]{:S(2)}, u32[]{:S(2)}) collective-permute-start(bf16[4,6,64,128]{3,2,1,0:T(8,128)(2,1)} %slice.89), channel_id=1, source_target_pairs={{0,2},{2,4},{4,6},{6,0},{1,3},{3,5},{5,7},{7,1},{8,10},{10,12},{12... | collective-permute-start | bytes 1179656 | tf_op jit(solution)/shard_map/ppermute | solution.py:23
  124.6 14.2 %collective-permute-start.20 = (f32[2,128]{1,0:T(2,128)S(1)}, f32[2,128]{1,0:T(2,128)S(1)}, u32[]{:S(2)}, u32[]{:S(2)}) collective-permute-start(f32[2,128]{1,0:T(2,128)S(1)} %pad_maximum_fusion.2), channel_id=1, source_target_pairs={{0,1},{1,0},{2,3},{3,2},{4,5},{5,4},{6,7},{7,6},{8,9},{9,8},{10,11... | collective-permute-start | bytes 3080 | tf_op jit(solution)/shard_map/ppermute | solution.py:59
  139.1 24.1 %collective-permute-start.17 = (bf16[12,3,128,256]{3,2,0,1:T(8,128)(2,1)S(1)}, bf16[12,3,128,256]{3,2,0,1:T(8,128)(2,1)S(1)}, u32[]{:S(2)}, u32[]{:S(2)}) collective-permute-start(bf16[12,3,128,256]{3,2,0,1:T(8,128)(2,1)S(1)} %pad_maximum_fusion), channel_id=1, source_target_pairs={{0,64},{64,0},{1,65},{65,1},{2,66},{66,2},{3,67},{67,3},{4,68},{68... | collective-permute-start | bytes 7077896 | tf_op jit(solution)/shard_map/ppermute | solution.py:101
  142.1 19.2 %collective-permute-start.15 = (bf16[12,64,256]{2,1,0:T(8,128)(2,1)S(1)}, bf16[12,64,256]{2,1,0:T(8,128)(2,1)S(1)}, u32[]{:S(2)}, u32[]{:S(2)}) collective-permute-start(bf16[12,64,256]{2,1,0:T(8,128)(2,1)S(1)} %slice.90), channel_id=1, source_target_pairs={{0,384},{128,0},{256,128},{384,256},{1,385},{129,1},{257,129},{385... | collective-permute-start | bytes 1179656 | tf_op jit(solution)/shard_map/ppermute | solution.py:23
  145.7 17.9 %collective-permute-start.18 = (bf16[12,64,256]{2,1,0:T(8,128)(2,1)S(1)}, bf16[12,64,256]{2,1,0:T(8,128)(2,1)S(1)}, u32[]{:S(2)}, u32[]{:S(2)}) collective-permute-start(bf16[12,64,256]{2,1,0:T(8,128)(2,1)S(1)} %slice.90), channel_id=1, source_target_pairs={{192,0},{128,64},{320,128},{256,192},{448,256},{384,320},{64,384},... | collective-permute-start | bytes 1179656 | tf_op jit(solution)/shard_map/ppermute | solution.py:98
  149.2 13.8 %collective-permute-start.16 = (bf16[12,64,256]{2,1,0:T(8,128)(2,1)S(1)}, bf16[12,64,256]{2,1,0:T(8,128)(2,1)S(1)}, u32[]{:S(2)}, u32[]{:S(2)}) collective-permute-start(bf16[12,64,256]{2,1,0:T(8,128)(2,1)S(1)} %slice.91), channel_id=1, source_target_pairs={{0,128},{128,256},{256,384},{384,0},{1,129},{129,257},{257,385},{3... | collective-permute-start | bytes 1179656 | tf_op jit(solution)/shard_map/ppermute | solution.py:23
  151.3 18.9 %collective-permute-start.19 = (bf16[12,64,256]{2,1,0:T(8,128)(2,1)S(1)}, bf16[12,64,256]{2,1,0:T(8,128)(2,1)S(1)}, u32[]{:S(2)}, u32[]{:S(2)}) collective-permute-start(bf16[12,64,256]{2,1,0:T(8,128)(2,1)S(1)} %slice.91), channel_id=1, source_target_pairs={{448,0},{384,64},{64,128},{0,192},{192,256},{128,320},{320,384},{2... | collective-permute-start | bytes 1179656 | tf_op jit(solution)/shard_map/ppermute | solution.py:99
  180.1 16.9 %collective-permute-start.21 = (bf16[4,4,64,256]{3,2,1,0:T(8,128)(2,1)S(1)}, bf16[4,4,64,256]{3,2,1,0:T(8,128)(2,1)S(1)}, u32[]{:S(2)}, u32[]{:S(2)}) collective-permute-start(bf16[4,4,64,256]{3,2,1,0:T(8,128)(2,1)S(1)} %bitcast.132), channel_id=1, source_target_pairs={{0,6},{2,0},{4,2},{6,4},{1,7},{3,1},{5,3},{7,5},{8,14},{10,8},{12,... | collective-permute-start | bytes 1572872 | tf_op jit(solution)/shard_map/ppermute | solution.py:23
  185.2 17.4 %collective-permute-start.23 = (bf16[4,4,64,256]{3,2,1,0:T(8,128)(2,1)S(1)}, bf16[4,4,64,256]{3,2,1,0:T(8,128)(2,1)S(1)}, u32[]{:S(2)}, u32[]{:S(2)}) collective-permute-start(bf16[4,4,64,256]{3,2,1,0:T(8,128)(2,1)S(1)} %bitcast.133), channel_id=1, source_target_pairs={{0,2},{2,4},{4,6},{6,0},{1,3},{3,5},{5,7},{7,1},{8,10},{10,12},{12... | collective-permute-start | bytes 1572872 | tf_op jit(solution)/shard_map/ppermute | solution.py:23
  197.0 11.0 %collective-permute-start.22 = (bf16[4,4,64,128]{3,2,1,0:T(8,128)(2,1)S(1)}, bf16[4,4,64,128]{3,2,1,0:T(8,128)(2,1)S(1)}, u32[]{:S(2)}, u32[]{:S(2)}) collective-permute-start(bf16[4,4,64,128]{3,2,1,0:T(8,128)(2,1)S(1)} %slice.122), channel_id=1, source_target_pairs={{0,6},{2,0},{4,2},{6,4},{1,7},{3,1},{5,3},{7,5},{8,14},{10,8},{12,... | collective-permute-start | bytes 786440 | tf_op jit(solution)/shard_map/ppermute | solution.py:23
  229.0 33.4 %collective-permute-start.27 = (bf16[4,4,64,128]{3,2,1,0:T(8,128)(2,1)S(1)}, bf16[4,4,64,128]{3,2,1,0:T(8,128)(2,1)S(1)}, u32[]{:S(2)}, u32[]{:S(2)}) collective-permute-start(bf16[4,4,64,128]{3,2,1,0:T(8,128)(2,1)S(1)} %get-tuple-element.36), channel_id=1, source_target_pairs={{0,1},{1,0},{2,3},{3,2},{4,5},{5,4},{6,7},{7,6},{8,9},{9,8},{10,11... | collective-permute-start | bytes 786440 | tf_op jit(solution)/shard_map/ppermute | solution.py:160
  (12 other events, 141.5 us)

commit v16 on v14

--- a/solution.py
+++ b/solution.py
@@ -130,7 +130,38 @@
     local_ids = lax.dynamic_slice_in_dim(padded_ids, index * fr_count, fr_count + 2)
     prev_ok = (local_ids[1:-1] == local_ids[:-2]).astype(jnp.float32).reshape(fr_count, 1, 1, 1)
     next_ok = (local_ids[1:-1] == local_ids[2:]).astype(jnp.float32).reshape(fr_count, 1, 1, 1)
-    whole = shift_halo(x_gather(active), FRAME, lax.axis_size(FRAME), 0, 1)
+    fr_n = lax.axis_size(FRAME)
+    half_c = active.shape[3] // 2
+    from_left = ring_shift(active, "cx", ring, 1)
+    from_right = ring_shift(active, "cx", ring, -1)
+    far_low = ring_shift(from_right[..., :half_c], "cx", ring, -1)
+    far_high = ring_shift(from_left[..., half_c:], "cx", ring, 1)
+    forward = [(g, g + 1) for g in range(fr_n - 1)]
+    backward = [(g + 1, g) for g in range(fr_n - 1)]
+    near_last = jnp.concatenate([active[-1:], from_right[-1:], from_left[-1:]], axis=3)
+    near_first = jnp.concatenate([active[:1], from_right[:1], from_left[:1]], axis=3)
+    low_near = lax.ppermute(near_last, FRAME, forward)
+    high_near = lax.ppermute(near_first, FRAME, backward)
+    axes = FRAME + ("row", "cx")
+
+    def diagonal(step_f, step_x):
+        first = 1 if step_f < 0 else 0
+        return [
+            ((g * row_n + r) * ring + x, ((g + step_f) * row_n + r) * ring + (x + step_x) % ring)
+            for g in range(first, fr_n - 1 + first)
+            for r in range(row_n)
+            for x in range(ring)
+        ]
+
+    low_a = lax.ppermute(from_right[-1:, ..., :half_c], axes, diagonal(1, -1))
+    low_b = lax.ppermute(from_left[-1:, ..., half_c:], axes, diagonal(1, 1))
+    high_a = lax.ppermute(from_right[:1, ..., :half_c], axes, diagonal(-1, -1))
+    high_b = lax.ppermute(from_left[:1, ..., half_c:], axes, diagonal(-1, 1))
+    split = 2 * active.shape[3]
+    rim_low = jnp.concatenate([low_near[..., :split], low_a, low_b, low_near[..., split:]], axis=3)
+    rim_high = jnp.concatenate([high_near[..., :split], high_a, high_b, high_near[..., split:]], axis=3)
+    own = jnp.concatenate([active, from_right, far_low, far_high, from_left], axis=3)
+    whole = jnp.concatenate([rim_low, own, rim_high], axis=0)
     taps_out = [
         jnp.einsum(
             "fhwc,cd->fhwd",

time: 249 us -> 253 us (1.016)
  the two profiles are of different devices: /device:TPU:1 before, /device:TPU:104 now
where the time goes in v16:
time: 253 us; the launch traced here: 252 us
  starting transfers between devices  120 us (47%)
  waiting for transfers between devices  95.3 us (38%)
  local copies, waits for them, and re-layouts  18 us (7%)
  matrix products  8.68 us (3%)
  other arithmetic  8.24 us (3%)
    ppermute x12, starting transfers between devices, ring_shift(): lax.ppermute(block, axis, [(i, (i + step) % count) for i in range(count)])  36.5 us
    ppermute x1, waiting for transfers between devices, body(): returned = lax.ppermute(given, 'cz', SWAP)  27.8 us
    ppermute x12, waiting for transfers between devices, ring_shift(): lax.ppermute(block, axis, [(i, (i + step) % count) for i in range(count)])  19.8 us
    ppermute x3, waiting for transfers between devices, xor_stack(): other = lax.ppermute(block, axis, [(i, i ^ bit) for i in range(count)])  18.3 us
    ppermute x1, starting transfers between devices, body(): partner = lax.ppermute(sent, 'cz', SWAP)  13 us
    ppermute x1, starting transfers between devices, body(): rim = lax.ppermute(edge, ('row', 'cz'), diagonal)  11.5 us
    ppermute x3, starting transfers between devices, xor_stack(): other = lax.ppermute(block, axis, [(i, i ^ bit) for i in range(count)])  10.9 us
    ppermute x1, waiting for transfers between devices, shift_halo(): lax.ppermute(lax.slice_in_dim(block, block.shape[dim] - width, None, axis...  9.6 us
  transfers between devices with their start and end apart: 31, of which 14 were waited for; matrix products, arithmetic and copies ran while one was open for 9% of the time, Pallas kernels for 0%

profile of v16, /device:TPU:104, one launch (start us, length us, event | category | flops | bytes accessed | tf_op | source)
XLA Modules:
  0.0 251.6 jit_solution(4798321724943093954)
XLA Ops:
  1.0 13.0 %collective-permute-start.2 = (bf16[4,5,64,128]{3,2,1,0:T(8,128)(2,1)S(1)}, bf16[4,5,64,128]{3,2,1,0:T(8,128)(2,1)S(1)}, u32[]{:S(2)}, u32[]{:S(2)}) collective-permute-start(bf16[4,5,64,128]{3,2,1,0:T(8,128)(2,1)S(1)} %constant_dynamic-slice_fusion.4), channel_id=1, source_target_pairs={{0,1},{1,0},{2,3},{3,2},{4,5},{5,4},{6,7},{7,6},{8,9},{9,8},{10,11... | collective-permute-start | bytes 983048 | tf_op jit(solution)/shard_map/ppermute | solution.py:62
  18.4 4.6 %collective-permute-start = (bf16[4,1,64,128]{3,2,1,0:T(8,128)(2,1)S(1)}, bf16[4,1,64,128]{3,2,1,0:T(8,128)(2,1)S(1)}, u32[]{:S(2)}, u32[]{:S(2)}) collective-permute-start(bf16[4,1,64,128]{3,2,1,0:T(8,128)(2,1)S(1)} %get-tuple-element.48), channel_id=1, source_target_pairs={{0,8},{8,16},{16,24},{24,32},{32,40},{40,48},{48,56},{1,9},{9,17},... | collective-permute-start | bytes 196616 | tf_op jit(solution)/shard_map/ppermute | solution.py:15
  25.0 11.5 %collective-permute-start.3 = (bf16[4,1,64,128]{3,2,1,0:T(8,128)(2,1)S(1)}, bf16[4,1,64,128]{3,2,1,0:T(8,128)(2,1)S(1)}, u32[]{:S(2)}, u32[]{:S(2)}) collective-permute-start(bf16[4,1,64,128]{3,2,1,0:T(8,128)(2,1)S(1)} %get-tuple-element.46), channel_id=1, source_target_pairs={{1,8},{9,16},{17,24},{25,32},{33,40},{41,48},{49,56},{8,1},{16,9},... | collective-permute-start | bytes 196616 | tf_op jit(solution)/shard_map/ppermute | solution.py:66
  36.5 4.6 %collective-permute-done.4 = bf16[12,16,128]{2,1,0:T(8,128)(2,1)S(1)} collective-permute-done((bf16[12,16,128]{2,1,0:T(8,128)(2,1)S(1)}, bf16[12,16,128]{2,1,0:T(8,128)(2,1)S(1)}, u32[]{:S(2)}, u32[]{:S(2)}) %collective-permute-start.4) | collective-permute-done | bytes 49184 | tf_op jit(solution)/shard_map/ppermute | solution.py:67
  41.1 9.6 %collective-permute-done = bf16[4,1,64,128]{3,2,1,0:T(8,128)(2,1)S(1)} collective-permute-done((bf16[4,1,64,128]{3,2,1,0:T(8,128)(2,1)S(1)}, bf16[4,1,64,128]{3,2,1,0:T(8,128)(2,1)S(1)}, u32[]{:S(2)}, u32[]{:S(2)}) %collective-permute-start) | collective-permute-done | bytes 65568 | tf_op jit(solution)/shard_map/ppermute | solution.py:15
  58.8 3.5 %collective-permute-start.5 = (bf16[4,6,64,256]{3,2,1,0:T(8,128)(2,1)}, bf16[4,6,64,256]{3,2,1,0:T(8,128)(2,1)S(1)}, u32[]{:S(2)}, u32[]{:S(2)}) collective-permute-start(bf16[4,6,64,256]{3,2,1,0:T(8,128)(2,1)} %get-tuple-element.28), channel_id=1, source_target_pairs={{0,2},{2,4},{4,6},{6,0},{1,3},{3,5},{5,7},{7,1},{8,10},{10,12},{12... | collective-permute-start | bytes 2359304 | tf_op jit(solution)/shard_map/ppermute | solution.py:23
  62.3 3.7 %collective-permute-start.6 = (bf16[4,6,64,256]{3,2,1,0:T(8,128)(2,1)}, bf16[4,6,64,256]{3,2,1,0:T(8,128)(2,1)S(1)}, u32[]{:S(2)}, u32[]{:S(2)}) collective-permute-start(bf16[4,6,64,256]{3,2,1,0:T(8,128)(2,1)} %get-tuple-element.28), channel_id=1, source_target_pairs={{0,6},{2,0},{4,2},{6,4},{1,7},{3,1},{5,3},{7,5},{8,14},{10,8},{12,... | collective-permute-start | bytes 2359304 | tf_op jit(solution)/shard_map/ppermute | solution.py:23
  66.0 7.1 %collective-permute-start.8 = (bf16[12,2,16,256]{3,2,1,0:T(8,128)(2,1)S(1)}, bf16[12,2,16,256]{3,2,1,0:T(8,128)(2,1)S(1)}, u32[]{:S(2)}, u32[]{:S(2)}) collective-permute-start(bf16[12,2,16,256]{3,2,1,0:T(8,128)(2,1)S(1)} %maximum_select_fusion.6), channel_id=1, source_target_pairs={{0,16},{8,24},{16,0},{24,8},{32,48},{40,56},{48,32},{56,40},{1,17}... | collective-permute-start | bytes 589832 | tf_op jit(solution)/shard_map/ppermute | solution.py:44
  73.1 7.5 %collective-permute-done.8 = bf16[12,2,16,256]{3,2,1,0:T(8,128)(2,1)S(1)} collective-permute-done((bf16[12,2,16,256]{3,2,1,0:T(8,128)(2,1)S(1)}, bf16[12,2,16,256]{3,2,1,0:T(8,128)(2,1)S(1)}, u32[]{:S(2)}, u32[]{:S(2)}) %collective-permute-start.8) | collective-permute-done | bytes 196640 | tf_op jit(solution)/shard_map/ppermute | solution.py:44
  82.7 10.8 %collective-permute-done.9 = bf16[12,2,2,16,256]{4,3,1,0,2:T(8,128)(2,1)S(1)} collective-permute-done((bf16[12,2,2,16,256]{4,3,1,0,2:T(8,128)(2,1)S(1)}, bf16[12,2,2,16,256]{4,3,1,0,2:T(8,128)(2,1)S(1)}, u32[]{:S(2)}, u32[]{:S(2)}) %collective-permute-start.9) | collective-permute-done | bytes 393248 | tf_op jit(solution)/shard_map/ppermute | solution.py:44
  94.6 3.5 %collective-permute-start.12 = (bf16[12,128,256]{2,1,0:T(8,128)(2,1)S(1)}, bf16[12,128,256]{2,1,0:T(8,128)(2,1)S(1)}, u32[]{:S(2)}, u32[]{:S(2)}) collective-permute-start(bf16[12,128,256]{2,1,0:T(8,128)(2,1)S(1)} %bitcast.107), channel_id=1, source_target_pairs={{0,128},{128,256},{256,384},{384,0},{1,129},{129,257},{257,385},{3... | collective-permute-start | bytes 2359304 | tf_op jit(solution)/shard_map/ppermute | solution.py:23
  100.4 7.4 %collective-permute-start.19 = (f32[2,128]{1,0:T(2,128)S(1)}, f32[2,128]{1,0:T(2,128)S(1)}, u32[]{:S(2)}, u32[]{:S(2)}) collective-permute-start(f32[2,128]{1,0:T(2,128)S(1)} %pad_maximum_fusion.6), channel_id=1, source_target_pairs={{0,1},{1,0},{2,3},{3,2},{4,5},{5,4},{6,7},{7,6},{8,9},{9,8},{10,11... | collective-permute-start | bytes 3080 | tf_op jit(solution)/shard_map/ppermute | solution.py:59
  119.5 5.6 %collective-permute-done.11 = bf16[4,6,64,128]{3,2,1,0:T(8,128)(2,1)} collective-permute-done((bf16[4,6,64,128]{3,2,1,0:T(8,128)(2,1)}, bf16[4,6,64,128]{3,2,1,0:T(8,128)(2,1)}, u32[]{:S(2)}, u32[]{:S(2)}) %collective-permute-start.11) | collective-permute-done | bytes 393248 | tf_op jit(solution)/shard_map/ppermute | solution.py:23
  128.4 3.6 %collective-permute-start.14 = (bf16[12,64,256]{2,1,0:T(8,128)(2,1)S(1)}, bf16[12,64,256]{2,1,0:T(8,128)(2,1)S(1)}, u32[]{:S(2)}, u32[]{:S(2)}) collective-permute-start(bf16[12,64,256]{2,1,0:T(8,128)(2,1)S(1)} %slice.126), channel_id=1, source_target_pairs={{0,384},{128,0},{256,128},{384,256},{1,385},{129,1},{257,129},{385... | collective-permute-start | bytes 1179656 | tf_op jit(solution)/shard_map/ppermute | solution.py:23
  131.9 3.5 %collective-permute-start.17 = (bf16[12,64,256]{2,1,0:T(8,128)(2,1)S(1)}, bf16[12,64,256]{2,1,0:T(8,128)(2,1)S(1)}, u32[]{:S(2)}, u32[]{:S(2)}) collective-permute-start(bf16[12,64,256]{2,1,0:T(8,128)(2,1)S(1)} %slice.126), channel_id=1, source_target_pairs={{192,0},{128,64},{320,128},{256,192},{448,256},{384,320},{64,384},... | collective-permute-start | bytes 1179656 | tf_op jit(solution)/shard_map/ppermute | solution.py:90
  149.8 6.7 %collective-permute-done.18 = bf16[12,64,256]{2,1,0:T(8,128)(2,1)S(1)} collective-permute-done((bf16[12,64,256]{2,1,0:T(8,128)(2,1)S(1)}, bf16[12,64,256]{2,1,0:T(8,128)(2,1)S(1)}, u32[]{:S(2)}, u32[]{:S(2)}) %collective-permute-start.18) | collective-permute-done | bytes 393248 | tf_op jit(solution)/shard_map/ppermute | solution.py:91
  157.3 6.3 %convert_add_fusion = (f32[4,32,9,256]{3,1,2,0:T(8,128)S(1)}, bf16[4,32,9,256]{3,1,2,0:T(8,128)(2,1)S(1)}) fusion(f32[256]{0:T(256)S(1)} %bitcast.135, f32[256]{0:T(256)S(1)} %bitcast.136, bf16[3,3,1024,256]{3,2,1,0:T(8,128)(2,1)S(1)} %bitcast.114, bf16[6,4,8,11,1024]{4,1,3,2,0:T(4,128)(2,1)S(1)} %fusion.1, pred[32,9]{0,1:T(8,128)(4,1)S(1)} %copy-done.7), kind=kOutput, calls=%fused_computation.29 | convolution fusion | flops 5438767104 | bytes 10815776 | tf_op jit(solution)/shard_map/conv_general_dilated | solution.py:117
  166.3 4.1 %collective-permute-start.21 = (bf16[4,4,64,256]{3,2,1,0:T(8,128)(2,1)S(1)}, bf16[4,4,64,256]{3,2,1,0:T(8,128)(2,1)S(1)}, u32[]{:S(2)}, u32[]{:S(2)}) collective-permute-start(bf16[4,4,64,256]{3,2,1,0:T(8,128)(2,1)S(1)} %bitcast.121), channel_id=1, source_target_pairs={{0,2},{2,4},{4,6},{6,0},{1,3},{3,5},{5,7},{7,1},{8,10},{10,12},{12... | collective-permute-start | bytes 1572872 | tf_op jit(solution)/shard_map/ppermute | solution.py:23
  171.6 8.9 %collective-permute-done.20 = bf16[4,4,64,256]{3,2,1,0:T(8,128)(2,1)S(1)} collective-permute-done((bf16[4,4,64,256]{3,2,1,0:T(8,128)(2,1)S(1)}, bf16[4,4,64,256]{3,2,1,0:T(8,128)(2,1)S(1)}, u32[]{:S(2)}, u32[]{:S(2)}) %collective-permute-start.20) | collective-permute-done | bytes 524320 | tf_op jit(solution)/shard_map/ppermute | solution.py:23
  187.7 4.0 %collective-permute-start.26 = (bf16[4,4,64,128]{3,2,1,0:T(8,128)(2,1)S(1)}, bf16[4,4,64,128]{3,2,1,0:T(8,128)(2,1)S(1)}, u32[]{:S(2)}, u32[]{:S(2)}) collective-permute-start(bf16[4,4,64,128]{3,2,1,0:T(8,128)(2,1)S(1)} %slice.178), channel_id=1, source_target_pairs={{0,2},{2,4},{4,6},{6,0},{1,3},{3,5},{5,7},{7,1},{8,10},{10,12},{12... | collective-permute-start | bytes 786440 | tf_op jit(solution)/shard_map/ppermute | solution.py:23
  200.1 4.9 %collective-permute-start.23 = (bf16[1,4,64,128]{3,2,1,0:T(8,128)(2,1)S(1)}, bf16[1,4,64,128]{3,2,1,0:T(8,128)(2,1)S(1)}, u32[]{:S(2)}, u32[]{:S(2)}) collective-permute-start(bf16[1,4,64,128]{3,2,1,0:T(8,128)(2,1)S(1)} %get-tuple-element.36), channel_id=1, source_target_pairs={{0,70},{2,64},{4,66},{6,68},{8,78},{10,72},{12,74},{14,76},{16,86}... | collective-permute-start | bytes 196616 | tf_op jit(solution)/shard_map/ppermute | solution.py:156
  208.8 5.0 %collective-permute-done.24 = bf16[1,4,64,128]{3,2,1,0:T(8,128)(2,1)S(1)} collective-permute-done((bf16[1,4,64,128]{3,2,1,0:T(8,128)(2,1)S(1)}, bf16[1,4,64,128]{3,2,1,0:T(8,128)(2,1)S(1)}, u32[]{:S(2)}, u32[]{:S(2)}) %collective-permute-start.24) | collective-permute-done | bytes 65568 | tf_op jit(solution)/shard_map/ppermute | solution.py:157
  214.9 8.2 %collective-permute-start.30 = (bf16[4,4,64,128]{3,2,1,0:T(8,128)(2,1)S(1)}, bf16[4,4,64,128]{3,2,1,0:T(8,128)(2,1)S(1)}, u32[]{:S(2)}, u32[]{:S(2)}) collective-permute-start(bf16[4,4,64,128]{3,2,1,0:T(8,128)(2,1)S(1)} %get-tuple-element.34), channel_id=1, source_target_pairs={{0,1},{1,0},{2,3},{3,2},{4,5},{5,4},{6,7},{7,6},{8,9},{9,8},{10,11... | collective-permute-start | bytes 786440 | tf_op jit(solution)/shard_map/ppermute | solution.py:183
  223.0 27.8 %collective-permute-done.30 = bf16[4,4,64,128]{3,2,1,0:T(8,128)(2,1)S(1)} collective-permute-done((bf16[4,4,64,128]{3,2,1,0:T(8,128)(2,1)S(1)}, bf16[4,4,64,128]{3,2,1,0:T(8,128)(2,1)S(1)}, u32[]{:S(2)}, u32[]{:S(2)}) %collective-permute-start.30) | collective-permute-done | bytes 262176 | tf_op jit(solution)/shard_map/ppermute | solution.py:183
  (129 shorter events, 75.5 us)
Async XLA Ops:
  1.0 54.2 %collective-permute-start.2 = (bf16[4,5,64,128]{3,2,1,0:T(8,128)(2,1)S(1)}, bf16[4,5,64,128]{3,2,1,0:T(8,128)(2,1)S(1)}, u32[]{:S(2)}, u32[]{:S(2)}) collective-permute-start(bf16[4,5,64,128]{3,2,1,0:T(8,128)(2,1)S(1)} %constant_dynamic-slice_fusion.4), channel_id=1, source_target_pairs={{0,1},{1,0},{2,3},{3,2},{4,5},{5,4},{6,7},{7,6},{8,9},{9,8},{10,11... | collective-permute-start | bytes 983048 | tf_op jit(solution)/shard_map/ppermute | solution.py:62
  15.5 25.5 %collective-permute-start.4 = (bf16[12,16,128]{2,1,0:T(8,128)(2,1)S(1)}, bf16[12,16,128]{2,1,0:T(8,128)(2,1)S(1)}, u32[]{:S(2)}, u32[]{:S(2)}) collective-permute-start(bf16[12,16,128]{2,1,0:T(8,128)(2,1)S(1)} %constant_dynamic-update-slice_fusion), channel_id=1, source_target_pairs={{0,1},{1,0},{2,3},{3,2},{4,5},{5,4},{6,7},{7,6},{8,9},{9,8},{10,11... | collective-permute-start | bytes 147464 | tf_op jit(solution)/shard_map/ppermute | solution.py:67
  18.4 32.3 %collective-permute-start = (bf16[4,1,64,128]{3,2,1,0:T(8,128)(2,1)S(1)}, bf16[4,1,64,128]{3,2,1,0:T(8,128)(2,1)S(1)}, u32[]{:S(2)}, u32[]{:S(2)}) collective-permute-start(bf16[4,1,64,128]{3,2,1,0:T(8,128)(2,1)S(1)} %get-tuple-element.48), channel_id=1, source_target_pairs={{0,8},{8,16},{16,24},{24,32},{32,40},{40,48},{48,56},{1,9},{9,17},... | collective-permute-start | bytes 196616 | tf_op jit(solution)/shard_map/ppermute | solution.py:15
  23.0 27.6 %collective-permute-start.1 = (bf16[4,1,64,128]{3,2,1,0:T(8,128)(2,1)S(1)}, bf16[4,1,64,128]{3,2,1,0:T(8,128)(2,1)S(1)}, u32[]{:S(2)}, u32[]{:S(2)}) collective-permute-start(bf16[4,1,64,128]{3,2,1,0:T(8,128)(2,1)S(1)} %get-tuple-element.47), channel_id=1, source_target_pairs={{8,0},{16,8},{24,16},{32,24},{40,32},{48,40},{56,48},{9,1},{17,9},... | collective-permute-start | bytes 196616 | tf_op jit(solution)/shard_map/ppermute | solution.py:18
  25.0 30.2 %collective-permute-start.3 = (bf16[4,1,64,128]{3,2,1,0:T(8,128)(2,1)S(1)}, bf16[4,1,64,128]{3,2,1,0:T(8,128)(2,1)S(1)}, u32[]{:S(2)}, u32[]{:S(2)}) collective-permute-start(bf16[4,1,64,128]{3,2,1,0:T(8,128)(2,1)S(1)} %get-tuple-element.46), channel_id=1, source_target_pairs={{1,8},{9,16},{17,24},{25,32},{33,40},{41,48},{49,56},{8,1},{16,9},... | collective-permute-start | bytes 196616 | tf_op jit(solution)/shard_map/ppermute | solution.py:66
  58.8 34.9 %collective-permute-start.5 = (bf16[4,6,64,256]{3,2,1,0:T(8,128)(2,1)}, bf16[4,6,64,256]{3,2,1,0:T(8,128)(2,1)S(1)}, u32[]{:S(2)}, u32[]{:S(2)}) collective-permute-start(bf16[4,6,64,256]{3,2,1,0:T(8,128)(2,1)} %get-tuple-element.28), channel_id=1, source_target_pairs={{0,2},{2,4},{4,6},{6,0},{1,3},{3,5},{5,7},{7,1},{8,10},{10,12},{12... | collective-permute-start | bytes 2359304 | tf_op jit(solution)/shard_map/ppermute | solution.py:23
  62.3 31.4 %collective-permute-start.6 = (bf16[4,6,64,256]{3,2,1,0:T(8,128)(2,1)}, bf16[4,6,64,256]{3,2,1,0:T(8,128)(2,1)S(1)}, u32[]{:S(2)}, u32[]{:S(2)}) collective-permute-start(bf16[4,6,64,256]{3,2,1,0:T(8,128)(2,1)} %get-tuple-element.28), channel_id=1, source_target_pairs={{0,6},{2,0},{4,2},{6,4},{1,7},{3,1},{5,3},{7,5},{8,14},{10,8},{12,... | collective-permute-start | bytes 2359304 | tf_op jit(solution)/shard_map/ppermute | solution.py:23
  66.0 14.7 %collective-permute-start.8 = (bf16[12,2,16,256]{3,2,1,0:T(8,128)(2,1)S(1)}, bf16[12,2,16,256]{3,2,1,0:T(8,128)(2,1)S(1)}, u32[]{:S(2)}, u32[]{:S(2)}) collective-permute-start(bf16[12,2,16,256]{3,2,1,0:T(8,128)(2,1)S(1)} %maximum_select_fusion.6), channel_id=1, source_target_pairs={{0,16},{8,24},{16,0},{24,8},{32,48},{40,56},{48,32},{56,40},{1,17}... | collective-permute-start | bytes 589832 | tf_op jit(solution)/shard_map/ppermute | solution.py:44
  80.7 12.8 %collective-permute-start.9 = (bf16[12,2,2,16,256]{4,3,1,0,2:T(8,128)(2,1)S(1)}, bf16[12,2,2,16,256]{4,3,1,0,2:T(8,128)(2,1)S(1)}, u32[]{:S(2)}, u32[]{:S(2)}) collective-permute-start(bf16[12,2,2,16,256]{4,3,1,0,2:T(8,128)(2,1)S(1)} %maximum_select_fusion.4), channel_id=1, source_target_pairs={{0,8},{8,0},{16,24},{24,16},{32,40},{40,32},{48,56},{56,48},{1,9},... | collective-permute-start | bytes 1179656 | tf_op jit(solution)/shard_map/ppermute | solution.py:44
  94.6 30.6 %collective-permute-start.12 = (bf16[12,128,256]{2,1,0:T(8,128)(2,1)S(1)}, bf16[12,128,256]{2,1,0:T(8,128)(2,1)S(1)}, u32[]{:S(2)}, u32[]{:S(2)}) collective-permute-start(bf16[12,128,256]{2,1,0:T(8,128)(2,1)S(1)} %bitcast.107), channel_id=1, source_target_pairs={{0,128},{128,256},{256,384},{384,0},{1,129},{129,257},{257,385},{3... | collective-permute-start | bytes 2359304 | tf_op jit(solution)/shard_map/ppermute | solution.py:23
  98.0 27.1 %collective-permute-start.13 = (bf16[12,128,256]{2,1,0:T(8,128)(2,1)S(1)}, bf16[12,128,256]{2,1,0:T(8,128)(2,1)S(1)}, u32[]{:S(2)}, u32[]{:S(2)}) collective-permute-start(bf16[12,128,256]{2,1,0:T(8,128)(2,1)S(1)} %bitcast.108), channel_id=1, source_target_pairs={{0,384},{128,0},{256,128},{384,256},{1,385},{129,1},{257,129},{385... | collective-permute-start | bytes 2359304 | tf_op jit(solution)/shard_map/ppermute | solution.py:23
  100.4 18.6 %collective-permute-start.19 = (f32[2,128]{1,0:T(2,128)S(1)}, f32[2,128]{1,0:T(2,128)S(1)}, u32[]{:S(2)}, u32[]{:S(2)}) collective-permute-start(f32[2,128]{1,0:T(2,128)S(1)} %pad_maximum_fusion.6), channel_id=1, source_target_pairs={{0,1},{1,0},{2,3},{3,2},{4,5},{5,4},{6,7},{7,6},{8,9},{9,8},{10,11... | collective-permute-start | bytes 3080 | tf_op jit(solution)/shard_map/ppermute | solution.py:59
  125.4 24.1 %collective-permute-start.16 = (bf16[12,3,128,256]{3,2,0,1:T(8,128)(2,1)S(1)}, bf16[12,3,128,256]{3,2,0,1:T(8,128)(2,1)S(1)}, u32[]{:S(2)}, u32[]{:S(2)}) collective-permute-start(bf16[12,3,128,256]{3,2,0,1:T(8,128)(2,1)S(1)} %pad_maximum_fusion), channel_id=1, source_target_pairs={{0,64},{64,0},{1,65},{65,1},{2,66},{66,2},{3,67},{67,3},{4,68},{68... | collective-permute-start | bytes 7077896 | tf_op jit(solution)/shard_map/ppermute | solution.py:93
  128.4 19.2 %collective-permute-start.14 = (bf16[12,64,256]{2,1,0:T(8,128)(2,1)S(1)}, bf16[12,64,256]{2,1,0:T(8,128)(2,1)S(1)}, u32[]{:S(2)}, u32[]{:S(2)}) collective-permute-start(bf16[12,64,256]{2,1,0:T(8,128)(2,1)S(1)} %slice.126), channel_id=1, source_target_pairs={{0,384},{128,0},{256,128},{384,256},{1,385},{129,1},{257,129},{385... | collective-permute-start | bytes 1179656 | tf_op jit(solution)/shard_map/ppermute | solution.py:23
  131.9 17.9 %collective-permute-start.17 = (bf16[12,64,256]{2,1,0:T(8,128)(2,1)S(1)}, bf16[12,64,256]{2,1,0:T(8,128)(2,1)S(1)}, u32[]{:S(2)}, u32[]{:S(2)}) collective-permute-start(bf16[12,64,256]{2,1,0:T(8,128)(2,1)S(1)} %slice.126), channel_id=1, source_target_pairs={{192,0},{128,64},{320,128},{256,192},{448,256},{384,320},{64,384},... | collective-permute-start | bytes 1179656 | tf_op jit(solution)/shard_map/ppermute | solution.py:90
  135.5 13.8 %collective-permute-start.15 = (bf16[12,64,256]{2,1,0:T(8,128)(2,1)S(1)}, bf16[12,64,256]{2,1,0:T(8,128)(2,1)S(1)}, u32[]{:S(2)}, u32[]{:S(2)}) collective-permute-start(bf16[12,64,256]{2,1,0:T(8,128)(2,1)S(1)} %slice.127), channel_id=1, source_target_pairs={{0,128},{128,256},{256,384},{384,0},{1,129},{129,257},{257,385},{3... | collective-permute-start | bytes 1179656 | tf_op jit(solution)/shard_map/ppermute | solution.py:23
  137.6 18.9 %collective-permute-start.18 = (bf16[12,64,256]{2,1,0:T(8,128)(2,1)S(1)}, bf16[12,64,256]{2,1,0:T(8,128)(2,1)S(1)}, u32[]{:S(2)}, u32[]{:S(2)}) collective-permute-start(bf16[12,64,256]{2,1,0:T(8,128)(2,1)S(1)} %slice.127), channel_id=1, source_target_pairs={{448,0},{384,64},{64,128},{0,192},{192,256},{128,320},{320,384},{2... | collective-permute-start | bytes 1179656 | tf_op jit(solution)/shard_map/ppermute | solution.py:91
  164.4 16.2 %collective-permute-start.20 = (bf16[4,4,64,256]{3,2,1,0:T(8,128)(2,1)S(1)}, bf16[4,4,64,256]{3,2,1,0:T(8,128)(2,1)S(1)}, u32[]{:S(2)}, u32[]{:S(2)}) collective-permute-start(bf16[4,4,64,256]{3,2,1,0:T(8,128)(2,1)S(1)} %bitcast.120), channel_id=1, source_target_pairs={{0,6},{2,0},{4,2},{6,4},{1,7},{3,1},{5,3},{7,5},{8,14},{10,8},{12,... | collective-permute-start | bytes 1572872 | tf_op jit(solution)/shard_map/ppermute | solution.py:23
  166.3 17.4 %collective-permute-start.21 = (bf16[4,4,64,256]{3,2,1,0:T(8,128)(2,1)S(1)}, bf16[4,4,64,256]{3,2,1,0:T(8,128)(2,1)S(1)}, u32[]{:S(2)}, u32[]{:S(2)}) collective-permute-start(bf16[4,4,64,256]{3,2,1,0:T(8,128)(2,1)S(1)} %bitcast.121), channel_id=1, source_target_pairs={{0,2},{2,4},{4,6},{6,0},{1,3},{3,5},{5,7},{7,1},{8,10},{10,12},{12... | collective-permute-start | bytes 1572872 | tf_op jit(solution)/shard_map/ppermute | solution.py:23
  183.7 25.0 %collective-permute-start.22 = (bf16[1,4,64,768]{3,2,1,0:T(8,128)(2,1)S(1)}, bf16[1,4,64,768]{3,2,1,0:T(8,128)(2,1)S(1)}, u32[]{:S(2)}, u32[]{:S(2)}) collective-permute-start(bf16[1,4,64,768]{3,2,1,0:T(8,128)(2,1)S(1)} %pad_maximum_fusion.2), channel_id=1, source_target_pairs={{0,64},{64,128},{128,192},{192,256},{256,320},{320,384},{384,448},... | collective-permute-start | bytes 1179656 | tf_op jit(solution)/shard_map/ppermute | solution.py:143
  187.7 12.4 %collective-permute-start.26 = (bf16[4,4,64,128]{3,2,1,0:T(8,128)(2,1)S(1)}, bf16[4,4,64,128]{3,2,1,0:T(8,128)(2,1)S(1)}, u32[]{:S(2)}, u32[]{:S(2)}) collective-permute-start(bf16[4,4,64,128]{3,2,1,0:T(8,128)(2,1)S(1)} %slice.178), channel_id=1, source_target_pairs={{0,2},{2,4},{4,6},{6,0},{1,3},{3,5},{5,7},{7,1},{8,10},{10,12},{12... | collective-permute-start | bytes 786440 | tf_op jit(solution)/shard_map/ppermute | solution.py:23
  191.7 14.1 %collective-permute-start.27 = (bf16[1,4,64,768]{3,2,1,0:T(8,128)(2,1)S(1)}, bf16[1,4,64,768]{3,2,1,0:T(8,128)(2,1)S(1)}, u32[]{:S(2)}, u32[]{:S(2)}) collective-permute-start(bf16[1,4,64,768]{3,2,1,0:T(8,128)(2,1)S(1)} %pad_maximum_fusion.3), channel_id=1, source_target_pairs={{64,0},{128,64},{192,128},{256,192},{320,256},{384,320},{448,384},... | collective-permute-start | bytes 1179656 | tf_op jit(solution)/shard_map/ppermute | solution.py:144
  194.8 13.2 %collective-permute-start.28 = (bf16[1,4,64,128]{3,2,1,0:T(8,128)(2,1)S(1)}, bf16[1,4,64,128]{3,2,1,0:T(8,128)(2,1)S(1)}, u32[]{:S(2)}, u32[]{:S(2)}) collective-permute-start(bf16[1,4,64,128]{3,2,1,0:T(8,128)(2,1)S(1)} %get-tuple-element.37), channel_id=1, source_target_pairs={{64,6},{66,0},{68,2},{70,4},{72,14},{74,8},{76,10},{78,12},{80,22}... | collective-permute-start | bytes 196616 | tf_op jit(solution)/shard_map/ppermute | solution.py:158
  214.9 35.9 %collective-permute-start.30 = (bf16[4,4,64,128]{3,2,1,0:T(8,128)(2,1)S(1)}, bf16[4,4,64,128]{3,2,1,0:T(8,128)(2,1)S(1)}, u32[]{:S(2)}, u32[]{:S(2)}) collective-permute-start(bf16[4,4,64,128]{3,2,1,0:T(8,128)(2,1)S(1)} %get-tuple-element.34), channel_id=1, source_target_pairs={{0,1},{1,0},{2,3},{3,2},{4,5},{5,4},{6,7},{7,6},{8,9},{9,8},{10,11... | collective-permute-start | bytes 786440 | tf_op jit(solution)/shard_map/ppermute | solution.py:183
  (15 other events, 186.0 us)

commit v17 on v14

--- a/solution.py
+++ b/solution.py
@@ -73,14 +73,16 @@
     for pos, bit in enumerate((4, 2, 1)):
         w_block = xor_stack(w_block, "row", bit, 1 + pos)
     w_block = w_block.reshape(taps, row_n * depth, -1)
-    from_left, from_right, w_block = lax.optimization_barrier((from_left, from_right, w_block))
+    cut = pair.shape[3] // 2
+    far_low = ring_shift(pair[..., :cut], "cx", ring, -2)
+    far_high = ring_shift(pair[..., cut:], "cx", ring, 2)
+    from_left, from_right, far_low, far_high, w_block = lax.optimization_barrier(
+        (from_left, from_right, far_low, far_high, w_block)
+    )
     fy_n = lax.axis_size("fy")
     w_left = ring_shift(w_block, "fy", fy_n, 1)
     w_right = ring_shift(w_block, "fy", fy_n, -1)
-    cut = pair.shape[3] // 2
-    far_low = ring_shift(from_right[..., :cut], "cx", ring, -1)
-    far_high = ring_shift(from_left[..., cut:], "cx", ring, 1)
-    far_low, far_high, w_left, w_right = lax.optimization_barrier((far_low, far_high, w_left, w_right))
+    w_left, w_right = lax.optimization_barrier((w_left, w_right))
     w_cut = w_block.shape[1] // 2
     w_far_low = ring_shift(w_right[:, :w_cut], "fy", fy_n, -1)
     w_far_high = ring_shift(w_left[:, w_cut:], "fy", fy_n, 1)

time: 249 us -> 259 us (1.040)
  waiting for transfers between devices: 91.3 us -> 108 us
  starting transfers between devices: 117 us -> 113 us
    ppermute x12, waiting for transfers between devices: 16.2 us -> 35.1 us  [ring_shift(): lax.ppermute(block, axis, [(i, (i + step) % count) for i in range(count)])]
    ppermute x3, waiting for transfers between devices: 10.5 us -> 3.68 us  [xor_stack(): other = lax.ppermute(block, axis, [(i, i ^ bit) for i in range(count)])]
    ppermute x1, starting transfers between devices: 9.35 us -> 6.61 us  [body(): returned = lax.ppermute(given, 'cz', SWAP)]
  transfers between devices with their start and end apart: 27 -> 27, of which waited for: 15 -> 17; matrix products, arithmetic and copies ran while one was open for 9% -> 8% of each run, Pallas kernels for 0% -> 0%
where the time goes in v17:
time: 259 us; the launch traced here: 257 us
  starting transfers between devices  113 us (44%)
  waiting for transfers between devices  108 us (42%)
  local copies, waits for them, and re-layouts  19.1 us (7%)
  matrix products  8.5 us (3%)
  other arithmetic  6.82 us (3%)
    ppermute x12, starting transfers between devices, ring_shift(): lax.ppermute(block, axis, [(i, (i + step) % count) for i in range(count)])  39.7 us
    ppermute x12, waiting for transfers between devices, ring_shift(): lax.ppermute(block, axis, [(i, (i + step) % count) for i in range(count)])  35.1 us
    ppermute x1, waiting for transfers between devices, body(): returned = lax.ppermute(given, 'cz', SWAP)  23.1 us
    ppermute x2, waiting for transfers between devices, shift_halo(): lax.ppermute(lax.slice_in_dim(block, 0, width, axis=dim), axis, backward)  20.5 us
    ppermute x3, starting transfers between devices, xor_stack(): other = lax.ppermute(block, axis, [(i, i ^ bit) for i in range(count)])  20.4 us
    ppermute x1, starting transfers between devices, body(): partner = lax.ppermute(sent, 'cz', SWAP)  16.3 us
    unnamed x26, local copies, waits for them, and re-layouts  7.94 us
    ppermute x1, waiting for transfers between devices, body(): biases = ordered_pair(biases, lax.ppermute(biases, 'cz', SWAP), high, 1)  7.71 us
  transfers between devices with their start and end apart: 27, of which 17 were waited for; matrix products, arithmetic and copies ran while one was open for 8% of the time, Pallas kernels for 0%

profile of v17, /device:TPU:1, one launch (start us, length us, event | category | flops | bytes accessed | tf_op | source)
XLA Modules:
  0.0 256.7 jit_solution(9447550290495670704)
XLA Ops:
  1.0 16.3 %collective-permute-start.2 = (bf16[4,5,64,128]{3,2,1,0:T(8,128)(2,1)S(1)}, bf16[4,5,64,128]{3,2,1,0:T(8,128)(2,1)S(1)}, u32[]{:S(2)}, u32[]{:S(2)}) collective-permute-start(bf16[4,5,64,128]{3,2,1,0:T(8,128)(2,1)S(1)} %constant_dynamic-slice_fusion.4), channel_id=1, source_target_pairs={{0,1},{1,0},{2,3},{3,2},{4,5},{5,4},{6,7},{7,6},{8,9},{9,8},{10,11... | collective-permute-start | bytes 983048 | tf_op jit(solution)/shard_map/ppermute | solution.py:62
  26.3 6.4 %collective-permute-done.4 = bf16[12,16,128]{2,1,0:T(8,128)(2,1)S(1)} collective-permute-done((bf16[12,16,128]{2,1,0:T(8,128)(2,1)S(1)}, bf16[12,16,128]{2,1,0:T(8,128)(2,1)S(1)}, u32[]{:S(2)}, u32[]{:S(2)}) %collective-permute-start.4) | collective-permute-done | bytes 49184 | tf_op jit(solution)/shard_map/ppermute | solution.py:67
  33.7 18.0 %collective-permute-done.1 = bf16[4,1,64,128]{3,2,1,0:T(8,128)(2,1)S(1)} collective-permute-done((bf16[4,1,64,128]{3,2,1,0:T(8,128)(2,1)S(1)}, bf16[4,1,64,128]{3,2,1,0:T(8,128)(2,1)S(1)}, u32[]{:S(2)}, u32[]{:S(2)}) %collective-permute-start.1) | collective-permute-done | bytes 65568 | tf_op jit(solution)/shard_map/ppermute | solution.py:18
  52.8 8.2 %collective-permute-start.9 = (bf16[12,16,256]{2,1,0:T(8,128)(2,1)S(1)}, bf16[12,16,256]{2,1,0:T(8,128)(2,1)S(1)}, u32[]{:S(2)}, u32[]{:S(2)}) collective-permute-start(bf16[12,16,256]{2,1,0:T(8,128)(2,1)S(1)} %maximum_select_fusion.7), channel_id=1, source_target_pairs={{0,32},{8,40},{16,48},{24,56},{32,0},{40,8},{48,16},{56,24},{1,33}... | collective-permute-start | bytes 294920 | tf_op jit(solution)/shard_map/ppermute | solution.py:44
  68.9 3.9 %collective-permute-start.10 = (bf16[12,2,16,256]{3,2,1,0:T(8,128)(2,1)S(1)}, bf16[12,2,16,256]{3,2,1,0:T(8,128)(2,1)S(1)}, u32[]{:S(2)}, u32[]{:S(2)}) collective-permute-start(bf16[12,2,16,256]{3,2,1,0:T(8,128)(2,1)S(1)} %maximum_select_fusion.6), channel_id=1, source_target_pairs={{0,16},{8,24},{16,0},{24,8},{32,48},{40,56},{48,32},{56,40},{1,17}... | collective-permute-start | bytes 589832 | tf_op jit(solution)/shard_map/ppermute | solution.py:44
  72.9 3.7 %collective-permute-done.10 = bf16[12,2,16,256]{3,2,1,0:T(8,128)(2,1)S(1)} collective-permute-done((bf16[12,2,16,256]{3,2,1,0:T(8,128)(2,1)S(1)}, bf16[12,2,16,256]{3,2,1,0:T(8,128)(2,1)S(1)}, u32[]{:S(2)}, u32[]{:S(2)}) %collective-permute-start.10) | collective-permute-done | bytes 196640 | tf_op jit(solution)/shard_map/ppermute | solution.py:44
  77.4 8.3 %collective-permute-start.11 = (bf16[12,2,2,16,256]{4,3,1,0,2:T(8,128)(2,1)}, bf16[12,2,2,16,256]{4,3,1,0,2:T(8,128)(2,1)S(1)}, u32[]{:S(2)}, u32[]{:S(2)}) collective-permute-start(bf16[12,2,2,16,256]{4,3,1,0,2:T(8,128)(2,1)} %maximum_select_fusion.4), channel_id=1, source_target_pairs={{0,8},{8,0},{16,24},{24,16},{32,40},{40,32},{48,56},{56,48},{1,9},... | collective-permute-start | bytes 1179656 | tf_op jit(solution)/shard_map/ppermute | solution.py:44
  86.8 4.5 %collective-permute-start.7 = (bf16[4,6,64,128]{3,2,1,0:T(8,128)(2,1)}, bf16[4,6,64,128]{3,2,1,0:T(8,128)(2,1)S(1)}, u32[]{:S(2)}, u32[]{:S(2)}) collective-permute-start(bf16[4,6,64,128]{3,2,1,0:T(8,128)(2,1)} %get-tuple-element.35), channel_id=1, source_target_pairs={{0,4},{2,6},{4,0},{6,2},{1,5},{3,7},{5,1},{7,3},{8,12},{10,14},{12... | collective-permute-start | bytes 1179656 | tf_op jit(solution)/shard_map/ppermute | solution.py:23
  93.8 5.5 %collective-permute-done.7 = bf16[4,6,64,128]{3,2,1,0:T(8,128)(2,1)S(1)} collective-permute-done((bf16[4,6,64,128]{3,2,1,0:T(8,128)(2,1)}, bf16[4,6,64,128]{3,2,1,0:T(8,128)(2,1)S(1)}, u32[]{:S(2)}, u32[]{:S(2)}) %collective-permute-start.7) | collective-permute-done | bytes 393248 | tf_op jit(solution)/shard_map/ppermute | solution.py:23
  99.3 8.5 %collective-permute-done.8 = bf16[4,6,64,128]{3,2,1,0:T(8,128)(2,1)} collective-permute-done((bf16[4,6,64,128]{3,2,1,0:T(8,128)(2,1)}, bf16[4,6,64,128]{3,2,1,0:T(8,128)(2,1)}, u32[]{:S(2)}, u32[]{:S(2)}) %collective-permute-start.8) | collective-permute-done | bytes 393248 | tf_op jit(solution)/shard_map/ppermute | solution.py:23
  115.3 5.2 %collective-permute-start.19 = (f32[2,128]{1,0:T(2,128)S(1)}, f32[2,128]{1,0:T(2,128)S(1)}, u32[]{:S(2)}, u32[]{:S(2)}) collective-permute-start(f32[2,128]{1,0:T(2,128)S(1)} %pad_maximum_fusion.4), channel_id=1, source_target_pairs={{0,1},{1,0},{2,3},{3,2},{4,5},{5,4},{6,7},{7,6},{8,9},{9,8},{10,11... | collective-permute-start | bytes 3080 | tf_op jit(solution)/shard_map/ppermute | solution.py:59
  120.6 7.7 %collective-permute-done.19 = f32[2,128]{1,0:T(2,128)S(1)} collective-permute-done((f32[2,128]{1,0:T(2,128)S(1)}, f32[2,128]{1,0:T(2,128)S(1)}, u32[]{:S(2)}, u32[]{:S(2)}) %collective-permute-start.19) | collective-permute-done | bytes 1056 | tf_op jit(solution)/shard_map/ppermute | solution.py:59
  130.2 5.7 %collective-permute-start.16 = (bf16[12,3,128,256]{3,2,0,1:T(8,128)(2,1)S(1)}, bf16[12,3,128,256]{3,2,0,1:T(8,128)(2,1)S(1)}, u32[]{:S(2)}, u32[]{:S(2)}) collective-permute-start(bf16[12,3,128,256]{3,2,0,1:T(8,128)(2,1)S(1)} %pad_maximum_fusion), channel_id=1, source_target_pairs={{0,64},{64,0},{1,65},{65,1},{2,66},{66,2},{3,67},{67,3},{4,68},{68... | collective-permute-start | bytes 7077896 | tf_op jit(solution)/shard_map/ppermute | solution.py:95
  143.9 4.6 %collective-permute-start.14 = (bf16[12,64,256]{2,1,0:T(8,128)(2,1)S(1)}, bf16[12,64,256]{2,1,0:T(8,128)(2,1)S(1)}, u32[]{:S(2)}, u32[]{:S(2)}) collective-permute-start(bf16[12,64,256]{2,1,0:T(8,128)(2,1)S(1)} %slice.90), channel_id=1, source_target_pairs={{0,384},{128,0},{256,128},{384,256},{1,385},{129,1},{257,129},{385... | collective-permute-start | bytes 1179656 | tf_op jit(solution)/shard_map/ppermute | solution.py:23
  151.3 5.0 %collective-permute-start.17 = (bf16[12,64,256]{2,1,0:T(8,128)(2,1)S(1)}, bf16[12,64,256]{2,1,0:T(8,128)(2,1)S(1)}, u32[]{:S(2)}, u32[]{:S(2)}) collective-permute-start(bf16[12,64,256]{2,1,0:T(8,128)(2,1)S(1)} %slice.90), channel_id=1, source_target_pairs={{192,0},{128,64},{320,128},{256,192},{448,256},{384,320},{64,384},... | collective-permute-start | bytes 1179656 | tf_op jit(solution)/shard_map/ppermute | solution.py:92
  165.4 5.4 %collective-permute-done.18 = bf16[12,64,256]{2,1,0:T(8,128)(2,1)S(1)} collective-permute-done((bf16[12,64,256]{2,1,0:T(8,128)(2,1)S(1)}, bf16[12,64,256]{2,1,0:T(8,128)(2,1)S(1)}, u32[]{:S(2)}, u32[]{:S(2)}) %collective-permute-start.18) | collective-permute-done | bytes 393248 | tf_op jit(solution)/shard_map/ppermute | solution.py:93
  173.7 6.3 %convert_add_fusion = (f32[4,32,9,256]{3,1,2,0:T(8,128)S(1)}, bf16[4,32,9,256]{3,1,2,0:T(8,128)(2,1)S(1)}) fusion(f32[256]{0:T(256)S(1)} %bitcast.134, f32[256]{0:T(256)S(1)} %bitcast.135, bf16[3,3,1024,256]{3,2,1,0:T(8,128)(2,1)S(1)} %bitcast.114, bf16[6,4,8,11,1024]{4,1,3,2,0:T(4,128)(2,1)S(1)} %fusion.1, pred[32,9]{0,1:T(8,128)(4,1)S(1)} %copy-done.7), kind=kOutput, calls=%fused_computation.17 | convolution fusion | flops 5438767104 | bytes 10815776 | tf_op jit(solution)/shard_map/conv_general_dilated | solution.py:119
  180.7 4.2 %collective-permute-start.20 = (bf16[4,4,64,256]{3,2,1,0:T(8,128)(2,1)S(1)}, bf16[4,4,64,256]{3,2,1,0:T(8,128)(2,1)S(1)}, u32[]{:S(2)}, u32[]{:S(2)}) collective-permute-start(bf16[4,4,64,256]{3,2,1,0:T(8,128)(2,1)S(1)} %bitcast.124), channel_id=1, source_target_pairs={{0,6},{2,0},{4,2},{6,4},{1,7},{3,1},{5,3},{7,5},{8,14},{10,8},{12,... | collective-permute-start | bytes 1572872 | tf_op jit(solution)/shard_map/ppermute | solution.py:23
  187.1 9.2 %collective-permute-done.20 = bf16[4,4,64,256]{3,2,1,0:T(8,128)(2,1)S(1)} collective-permute-done((bf16[4,4,64,256]{3,2,1,0:T(8,128)(2,1)S(1)}, bf16[4,4,64,256]{3,2,1,0:T(8,128)(2,1)S(1)}, u32[]{:S(2)}, u32[]{:S(2)}) %collective-permute-start.20) | collective-permute-done | bytes 524320 | tf_op jit(solution)/shard_map/ppermute | solution.py:23
  196.4 5.3 %collective-permute-start.21 = (bf16[4,4,64,128]{3,2,1,0:T(8,128)(2,1)S(1)}, bf16[4,4,64,128]{3,2,1,0:T(8,128)(2,1)S(1)}, u32[]{:S(2)}, u32[]{:S(2)}) collective-permute-start(bf16[4,4,64,128]{3,2,1,0:T(8,128)(2,1)S(1)} %slice.124), channel_id=1, source_target_pairs={{0,6},{2,0},{4,2},{6,4},{1,7},{3,1},{5,3},{7,5},{8,14},{10,8},{12,... | collective-permute-start | bytes 786440 | tf_op jit(solution)/shard_map/ppermute | solution.py:23
  206.7 5.0 %collective-permute-done.23 = bf16[4,4,64,128]{3,2,1,0:T(8,128)(2,1)S(1)} collective-permute-done((bf16[4,4,64,128]{3,2,1,0:T(8,128)(2,1)S(1)}, bf16[4,4,64,128]{3,2,1,0:T(8,128)(2,1)S(1)}, u32[]{:S(2)}, u32[]{:S(2)}) %collective-permute-start.23) | collective-permute-done | bytes 262176 | tf_op jit(solution)/shard_map/ppermute | solution.py:23
  211.9 3.9 %collective-permute-start.25 = (bf16[1,4,64,1024]{3,2,1,0:T(8,128)(2,1)S(1)}, bf16[1,4,64,1024]{3,2,1,0:T(8,128)(2,1)S(1)}, u32[]{:S(2)}, u32[]{:S(2)}) collective-permute-start(bf16[1,4,64,1024]{3,2,1,0:T(8,128)(2,1)S(1)} %get-tuple-element.33), channel_id=1, source_target_pairs={{64,0},{128,64},{192,128},{256,192},{320,256},{384,320},{448,384},... | collective-permute-start | bytes 1572872 | tf_op jit(solution)/shard_map/ppermute | solution.py:18
  226.2 6.6 %collective-permute-start.26 = (bf16[4,4,64,128]{3,2,1,0:T(8,128)(2,1)S(1)}, bf16[4,4,64,128]{3,2,1,0:T(8,128)(2,1)S(1)}, u32[]{:S(2)}, u32[]{:S(2)}) collective-permute-start(bf16[4,4,64,128]{3,2,1,0:T(8,128)(2,1)S(1)} %get-tuple-element.38), channel_id=1, source_target_pairs={{0,1},{1,0},{2,3},{3,2},{4,5},{5,4},{6,7},{7,6},{8,9},{9,8},{10,11... | collective-permute-start | bytes 786440 | tf_op jit(solution)/shard_map/ppermute | solution.py:154
  232.8 23.1 %collective-permute-done.26 = bf16[4,4,64,128]{3,2,1,0:T(8,128)(2,1)S(1)} collective-permute-done((bf16[4,4,64,128]{3,2,1,0:T(8,128)(2,1)S(1)}, bf16[4,4,64,128]{3,2,1,0:T(8,128)(2,1)S(1)}, u32[]{:S(2)}, u32[]{:S(2)}) %collective-permute-start.26) | collective-permute-done | bytes 262176 | tf_op jit(solution)/shard_map/ppermute | solution.py:154
  (110 shorter events, 75.3 us)
Async XLA Ops:
  1.0 51.8 %collective-permute-start.2 = (bf16[4,5,64,128]{3,2,1,0:T(8,128)(2,1)S(1)}, bf16[4,5,64,128]{3,2,1,0:T(8,128)(2,1)S(1)}, u32[]{:S(2)}, u32[]{:S(2)}) collective-permute-start(bf16[4,5,64,128]{3,2,1,0:T(8,128)(2,1)S(1)} %constant_dynamic-slice_fusion.4), channel_id=1, source_target_pairs={{0,1},{1,0},{2,3},{3,2},{4,5},{5,4},{6,7},{7,6},{8,9},{9,8},{10,11... | collective-permute-start | bytes 983048 | tf_op jit(solution)/shard_map/ppermute | solution.py:62
  18.8 14.0 %collective-permute-start.4 = (bf16[12,16,128]{2,1,0:T(8,128)(2,1)S(1)}, bf16[12,16,128]{2,1,0:T(8,128)(2,1)S(1)}, u32[]{:S(2)}, u32[]{:S(2)}) collective-permute-start(bf16[12,16,128]{2,1,0:T(8,128)(2,1)S(1)} %constant_dynamic-update-slice_fusion), channel_id=1, source_target_pairs={{0,1},{1,0},{2,3},{3,2},{4,5},{5,4},{6,7},{7,6},{8,9},{9,8},{10,11... | collective-permute-start | bytes 147464 | tf_op jit(solution)/shard_map/ppermute | solution.py:67
  21.6 12.0 %collective-permute-start = (bf16[4,1,64,128]{3,2,1,0:T(8,128)(2,1)S(1)}, bf16[4,1,64,128]{3,2,1,0:T(8,128)(2,1)S(1)}, u32[]{:S(2)}, u32[]{:S(2)}) collective-permute-start(bf16[4,1,64,128]{3,2,1,0:T(8,128)(2,1)S(1)} %get-tuple-element.42), channel_id=1, source_target_pairs={{0,8},{8,16},{16,24},{24,32},{32,40},{40,48},{48,56},{1,9},{9,17},... | collective-permute-start | bytes 196616 | tf_op jit(solution)/shard_map/ppermute | solution.py:15
  24.3 27.4 %collective-permute-start.1 = (bf16[4,1,64,128]{3,2,1,0:T(8,128)(2,1)S(1)}, bf16[4,1,64,128]{3,2,1,0:T(8,128)(2,1)S(1)}, u32[]{:S(2)}, u32[]{:S(2)}) collective-permute-start(bf16[4,1,64,128]{3,2,1,0:T(8,128)(2,1)S(1)} %get-tuple-element.41), channel_id=1, source_target_pairs={{8,0},{16,8},{24,16},{32,24},{40,32},{48,40},{56,48},{9,1},{17,9},... | collective-permute-start | bytes 196616 | tf_op jit(solution)/shard_map/ppermute | solution.py:18
  25.6 27.2 %collective-permute-start.3 = (bf16[4,1,64,128]{3,2,1,0:T(8,128)(2,1)S(1)}, bf16[4,1,64,128]{3,2,1,0:T(8,128)(2,1)S(1)}, u32[]{:S(2)}, u32[]{:S(2)}) collective-permute-start(bf16[4,1,64,128]{3,2,1,0:T(8,128)(2,1)S(1)} %get-tuple-element.40), channel_id=1, source_target_pairs={{1,8},{9,16},{17,24},{25,32},{33,40},{41,48},{49,56},{8,1},{16,9},... | collective-permute-start | bytes 196616 | tf_op jit(solution)/shard_map/ppermute | solution.py:66
  52.8 16.1 %collective-permute-start.9 = (bf16[12,16,256]{2,1,0:T(8,128)(2,1)S(1)}, bf16[12,16,256]{2,1,0:T(8,128)(2,1)S(1)}, u32[]{:S(2)}, u32[]{:S(2)}) collective-permute-start(bf16[12,16,256]{2,1,0:T(8,128)(2,1)S(1)} %maximum_select_fusion.7), channel_id=1, source_target_pairs={{0,32},{8,40},{16,48},{24,56},{32,0},{40,8},{48,16},{56,24},{1,33}... | collective-permute-start | bytes 294920 | tf_op jit(solution)/shard_map/ppermute | solution.py:44
  62.4 45.4 %collective-permute-start.5 = (bf16[4,6,64,256]{3,2,1,0:T(8,128)(2,1)S(1)}, bf16[4,6,64,256]{3,2,1,0:T(8,128)(2,1)S(1)}, u32[]{:S(2)}, u32[]{:S(2)}) collective-permute-start(bf16[4,6,64,256]{3,2,1,0:T(8,128)(2,1)S(1)} %get-tuple-element.28), channel_id=1, source_target_pairs={{0,2},{2,4},{4,6},{6,0},{1,3},{3,5},{5,7},{7,1},{8,10},{10,12},{12... | collective-permute-start | bytes 2359304 | tf_op jit(solution)/shard_map/ppermute | solution.py:23
  65.5 42.3 %collective-permute-start.6 = (bf16[4,6,64,256]{3,2,1,0:T(8,128)(2,1)S(1)}, bf16[4,6,64,256]{3,2,1,0:T(8,128)(2,1)S(1)}, u32[]{:S(2)}, u32[]{:S(2)}) collective-permute-start(bf16[4,6,64,256]{3,2,1,0:T(8,128)(2,1)S(1)} %get-tuple-element.28), channel_id=1, source_target_pairs={{0,6},{2,0},{4,2},{6,4},{1,7},{3,1},{5,3},{7,5},{8,14},{10,8},{12,... | collective-permute-start | bytes 2359304 | tf_op jit(solution)/shard_map/ppermute | solution.py:23
  77.4 16.3 %collective-permute-start.11 = (bf16[12,2,2,16,256]{4,3,1,0,2:T(8,128)(2,1)}, bf16[12,2,2,16,256]{4,3,1,0,2:T(8,128)(2,1)S(1)}, u32[]{:S(2)}, u32[]{:S(2)}) collective-permute-start(bf16[12,2,2,16,256]{4,3,1,0,2:T(8,128)(2,1)} %maximum_select_fusion.4), channel_id=1, source_target_pairs={{0,8},{8,0},{16,24},{24,16},{32,40},{40,32},{48,56},{56,48},{1,9},... | collective-permute-start | bytes 1179656 | tf_op jit(solution)/shard_map/ppermute | solution.py:44
  86.8 12.5 %collective-permute-start.7 = (bf16[4,6,64,128]{3,2,1,0:T(8,128)(2,1)}, bf16[4,6,64,128]{3,2,1,0:T(8,128)(2,1)S(1)}, u32[]{:S(2)}, u32[]{:S(2)}) collective-permute-start(bf16[4,6,64,128]{3,2,1,0:T(8,128)(2,1)} %get-tuple-element.35), channel_id=1, source_target_pairs={{0,4},{2,6},{4,0},{6,2},{1,5},{3,7},{5,1},{7,3},{8,12},{10,14},{12... | collective-permute-start | bytes 1179656 | tf_op jit(solution)/shard_map/ppermute | solution.py:23
  91.3 16.5 %collective-permute-start.8 = (bf16[4,6,64,128]{3,2,1,0:T(8,128)(2,1)}, bf16[4,6,64,128]{3,2,1,0:T(8,128)(2,1)}, u32[]{:S(2)}, u32[]{:S(2)}) collective-permute-start(bf16[4,6,64,128]{3,2,1,0:T(8,128)(2,1)} %get-tuple-element.34), channel_id=1, source_target_pairs={{0,4},{2,6},{4,0},{6,2},{1,5},{3,7},{5,1},{7,3},{8,12},{10,14},{12... | collective-permute-start | bytes 1179656 | tf_op jit(solution)/shard_map/ppermute | solution.py:23
  108.7 19.7 %collective-permute-start.12 = (bf16[12,128,256]{2,1,0:T(8,128)(2,1)S(1)}, bf16[12,128,256]{2,1,0:T(8,128)(2,1)S(1)}, u32[]{:S(2)}, u32[]{:S(2)}) collective-permute-start(bf16[12,128,256]{2,1,0:T(8,128)(2,1)S(1)} %bitcast.107), channel_id=1, source_target_pairs={{0,128},{128,256},{256,384},{384,0},{1,129},{129,257},{257,385},{3... | collective-permute-start | bytes 2359304 | tf_op jit(solution)/shard_map/ppermute | solution.py:23
  111.9 18.1 %collective-permute-start.13 = (bf16[12,128,256]{2,1,0:T(8,128)(2,1)S(1)}, bf16[12,128,256]{2,1,0:T(8,128)(2,1)S(1)}, u32[]{:S(2)}, u32[]{:S(2)}) collective-permute-start(bf16[12,128,256]{2,1,0:T(8,128)(2,1)S(1)} %bitcast.108), channel_id=1, source_target_pairs={{0,384},{128,0},{256,128},{384,256},{1,385},{129,1},{257,129},{385... | collective-permute-start | bytes 2359304 | tf_op jit(solution)/shard_map/ppermute | solution.py:23
  115.3 13.0 %collective-permute-start.19 = (f32[2,128]{1,0:T(2,128)S(1)}, f32[2,128]{1,0:T(2,128)S(1)}, u32[]{:S(2)}, u32[]{:S(2)}) collective-permute-start(f32[2,128]{1,0:T(2,128)S(1)} %pad_maximum_fusion.4), channel_id=1, source_target_pairs={{0,1},{1,0},{2,3},{3,2},{4,5},{5,4},{6,7},{7,6},{8,9},{9,8},{10,11... | collective-permute-start | bytes 3080 | tf_op jit(solution)/shard_map/ppermute | solution.py:59
  130.2 31.9 %collective-permute-start.16 = (bf16[12,3,128,256]{3,2,0,1:T(8,128)(2,1)S(1)}, bf16[12,3,128,256]{3,2,0,1:T(8,128)(2,1)S(1)}, u32[]{:S(2)}, u32[]{:S(2)}) collective-permute-start(bf16[12,3,128,256]{3,2,0,1:T(8,128)(2,1)S(1)} %pad_maximum_fusion), channel_id=1, source_target_pairs={{0,64},{64,0},{1,65},{65,1},{2,66},{66,2},{3,67},{67,3},{4,68},{68... | collective-permute-start | bytes 7077896 | tf_op jit(solution)/shard_map/ppermute | solution.py:95
  143.9 14.6 %collective-permute-start.14 = (bf16[12,64,256]{2,1,0:T(8,128)(2,1)S(1)}, bf16[12,64,256]{2,1,0:T(8,128)(2,1)S(1)}, u32[]{:S(2)}, u32[]{:S(2)}) collective-permute-start(bf16[12,64,256]{2,1,0:T(8,128)(2,1)S(1)} %slice.90), channel_id=1, source_target_pairs={{0,384},{128,0},{256,128},{384,256},{1,385},{129,1},{257,129},{385... | collective-permute-start | bytes 1179656 | tf_op jit(solution)/shard_map/ppermute | solution.py:23
  148.5 13.5 %collective-permute-start.15 = (bf16[12,64,256]{2,1,0:T(8,128)(2,1)S(1)}, bf16[12,64,256]{2,1,0:T(8,128)(2,1)S(1)}, u32[]{:S(2)}, u32[]{:S(2)}) collective-permute-start(bf16[12,64,256]{2,1,0:T(8,128)(2,1)S(1)} %slice.91), channel_id=1, source_target_pairs={{0,128},{128,256},{256,384},{384,0},{1,129},{129,257},{257,385},{3... | collective-permute-start | bytes 1179656 | tf_op jit(solution)/shard_map/ppermute | solution.py:23
  151.3 14.2 %collective-permute-start.17 = (bf16[12,64,256]{2,1,0:T(8,128)(2,1)S(1)}, bf16[12,64,256]{2,1,0:T(8,128)(2,1)S(1)}, u32[]{:S(2)}, u32[]{:S(2)}) collective-permute-start(bf16[12,64,256]{2,1,0:T(8,128)(2,1)S(1)} %slice.90), channel_id=1, source_target_pairs={{192,0},{128,64},{320,128},{256,192},{448,256},{384,320},{64,384},... | collective-permute-start | bytes 1179656 | tf_op jit(solution)/shard_map/ppermute | solution.py:92
  156.3 14.6 %collective-permute-start.18 = (bf16[12,64,256]{2,1,0:T(8,128)(2,1)S(1)}, bf16[12,64,256]{2,1,0:T(8,128)(2,1)S(1)}, u32[]{:S(2)}, u32[]{:S(2)}) collective-permute-start(bf16[12,64,256]{2,1,0:T(8,128)(2,1)S(1)} %slice.91), channel_id=1, source_target_pairs={{448,0},{384,64},{64,128},{0,192},{192,256},{128,320},{320,384},{2... | collective-permute-start | bytes 1179656 | tf_op jit(solution)/shard_map/ppermute | solution.py:93
  180.7 15.6 %collective-permute-start.20 = (bf16[4,4,64,256]{3,2,1,0:T(8,128)(2,1)S(1)}, bf16[4,4,64,256]{3,2,1,0:T(8,128)(2,1)S(1)}, u32[]{:S(2)}, u32[]{:S(2)}) collective-permute-start(bf16[4,4,64,256]{3,2,1,0:T(8,128)(2,1)S(1)} %bitcast.124), channel_id=1, source_target_pairs={{0,6},{2,0},{4,2},{6,4},{1,7},{3,1},{5,3},{7,5},{8,14},{10,8},{12,... | collective-permute-start | bytes 1572872 | tf_op jit(solution)/shard_map/ppermute | solution.py:23
  185.0 16.8 %collective-permute-start.22 = (bf16[4,4,64,256]{3,2,1,0:T(8,128)(2,1)S(1)}, bf16[4,4,64,256]{3,2,1,0:T(8,128)(2,1)S(1)}, u32[]{:S(2)}, u32[]{:S(2)}) collective-permute-start(bf16[4,4,64,256]{3,2,1,0:T(8,128)(2,1)S(1)} %bitcast.125), channel_id=1, source_target_pairs={{0,2},{2,4},{4,6},{6,0},{1,3},{3,5},{5,7},{7,1},{8,10},{10,12},{12... | collective-permute-start | bytes 1572872 | tf_op jit(solution)/shard_map/ppermute | solution.py:23
  196.4 10.2 %collective-permute-start.21 = (bf16[4,4,64,128]{3,2,1,0:T(8,128)(2,1)S(1)}, bf16[4,4,64,128]{3,2,1,0:T(8,128)(2,1)S(1)}, u32[]{:S(2)}, u32[]{:S(2)}) collective-permute-start(bf16[4,4,64,128]{3,2,1,0:T(8,128)(2,1)S(1)} %slice.124), channel_id=1, source_target_pairs={{0,6},{2,0},{4,2},{6,4},{1,7},{3,1},{5,3},{7,5},{8,14},{10,8},{12,... | collective-permute-start | bytes 786440 | tf_op jit(solution)/shard_map/ppermute | solution.py:23
  211.9 10.5 %collective-permute-start.25 = (bf16[1,4,64,1024]{3,2,1,0:T(8,128)(2,1)S(1)}, bf16[1,4,64,1024]{3,2,1,0:T(8,128)(2,1)S(1)}, u32[]{:S(2)}, u32[]{:S(2)}) collective-permute-start(bf16[1,4,64,1024]{3,2,1,0:T(8,128)(2,1)S(1)} %get-tuple-element.33), channel_id=1, source_target_pairs={{64,0},{128,64},{192,128},{256,192},{320,256},{384,320},{448,384},... | collective-permute-start | bytes 1572872 | tf_op jit(solution)/shard_map/ppermute | solution.py:18
  226.2 29.7 %collective-permute-start.26 = (bf16[4,4,64,128]{3,2,1,0:T(8,128)(2,1)S(1)}, bf16[4,4,64,128]{3,2,1,0:T(8,128)(2,1)S(1)}, u32[]{:S(2)}, u32[]{:S(2)}) collective-permute-start(bf16[4,4,64,128]{3,2,1,0:T(8,128)(2,1)S(1)} %get-tuple-element.38), channel_id=1, source_target_pairs={{0,1},{1,0},{2,3},{3,2},{4,5},{5,4},{6,7},{7,6},{8,9},{9,8},{10,11... | collective-permute-start | bytes 786440 | tf_op jit(solution)/shard_map/ppermute | solution.py:154
  (11 other events, 146.8 us)

commit v18 on v14

--- a/solution.py
+++ b/solution.py
@@ -97,7 +97,7 @@
     rotate = lax.axis_index("cx")
     w_far = jnp.concatenate([w_far_low, w_far_high], axis=1)
     s_far = jnp.concatenate([s_far_low, s_far_high], axis=1)
-    w_out = jnp.zeros((taps, fy_n, 2) + w_block.shape[1:], w_block.dtype)
+    w_outs = [jnp.zeros((count, fy_n, 2) + w_block.shape[1:], w_block.dtype) for count in (9, taps - 9)]
     pieces = (
         (0, me_fc, w_block),
         (1, me_fc, w_right),
@@ -110,9 +110,12 @@
     )
     for offset, core, piece in pieces:
         place = (me_fy + offset - rotate + 2 * fy_n) % fy_n
-        w_out = lax.dynamic_update_slice(w_out, piece[:, None, None], (0, place, core, 0, 0))
-    both = w_out.reshape(taps, -1, w_block.shape[2])
-    full_spatial, full_temporal = both[:9], both[9:]
+        for k, (lo, hi) in enumerate(((0, 9), (9, taps))):
+            w_outs[k] = lax.dynamic_update_slice(
+                w_outs[k], piece[lo:hi, None, None], (0, place, core, 0, 0)
+            )
+    full_spatial = w_outs[0].reshape(9, -1, w_block.shape[2])
+    full_temporal = w_outs[1].reshape(taps - 9, -1, w_block.shape[2])
     kernel = full_spatial.reshape((3, 3) + full_spatial.shape[1:])
     spatial = lax.conv_general_dilated(
         gathered,

time: 249 us -> 245 us (0.984)
  waiting for transfers between devices: 91.3 us -> 63.9 us
  starting transfers between devices: 117 us -> 141 us
    ppermute x2, waiting for transfers between devices: 20.4 us -> 3.58 us  [shift_halo(): lax.ppermute(lax.slice_in_dim(block, 0, width, axis=dim), axis, backward)]
    ppermute x1, starting transfers between devices: 7.3 us -> 22.5 us  [body(): biases = ordered_pair(biases, lax.ppermute(biases, 'cz', SWAP), high, 1)]
    ppermute x1, starting transfers between devices: 1.91 us -> 14.2 us  [body(): w_block = ordered_pair(weight, lax.ppermute(weight, 'cz', SWAP), high, 2)]
    ppermute x1, waiting for transfers between devices: 6.43 us -> 0.25 us  [body(): w_block = ordered_pair(weight, lax.ppermute(weight, 'cz', SWAP), high, 2)]
    ppermute x12, starting transfers between devices: 41 us -> 35.2 us  [ring_shift(): lax.ppermute(block, axis, [(i, (i + step) % count) for i in range(count)])]
    ppermute x1, starting transfers between devices: 2.55 us -> 8.31 us  [body(): s_far_low = lax.ppermute(w_right[:, :w_cut], FRAME, from_up)]
    ppermute x12, waiting for transfers between devices: 16.2 us -> 21.9 us  [ring_shift(): lax.ppermute(block, axis, [(i, (i + step) % count) for i in range(count)])]
    ppermute x1, waiting for transfers between devices: 5.63 us -> 0.01 us  [body(): biases = ordered_pair(biases, lax.ppermute(biases, 'cz', SWAP), high, 1)]
  transfers between devices with their start and end apart: 27 -> 27, of which waited for: 15 -> 12; matrix products, arithmetic and copies ran while one was open for 9% -> 10% of each run, Pallas kernels for 0% -> 0%
where the time goes in v18:
time: 245 us; the launch traced here: 241 us
  starting transfers between devices  141 us (58%)
  waiting for transfers between devices  63.9 us (26%)
  local copies, waits for them, and re-layouts  18.3 us (7%)
  other arithmetic  8.52 us (3%)
  matrix products  8.5 us (3%)
    ppermute x12, starting transfers between devices, ring_shift(): lax.ppermute(block, axis, [(i, (i + step) % count) for i in range(count)])  35.2 us
    ppermute x1, starting transfers between devices, body(): biases = ordered_pair(biases, lax.ppermute(biases, 'cz', SWAP), high, 1)  22.5 us
    ppermute x12, waiting for transfers between devices, ring_shift(): lax.ppermute(block, axis, [(i, (i + step) % count) for i in range(count)])  21.9 us
    ppermute x3, starting transfers between devices, xor_stack(): other = lax.ppermute(block, axis, [(i, i ^ bit) for i in range(count)])  20.4 us
    ppermute x1, waiting for transfers between devices, body(): returned = lax.ppermute(given, 'cz', SWAP)  17.6 us
    ppermute x1, starting transfers between devices, body(): partner = lax.ppermute(sent, 'cz', SWAP)  14.5 us
    ppermute x1, starting transfers between devices, body(): w_block = ordered_pair(weight, lax.ppermute(weight, 'cz', SWAP), high, 2)  14.2 us
    ppermute x3, waiting for transfers between devices, xor_stack(): other = lax.ppermute(block, axis, [(i, i ^ bit) for i in range(count)])  12.7 us
  transfers between devices with their start and end apart: 27, of which 12 were waited for; matrix products, arithmetic and copies ran while one was open for 10% of the time, Pallas kernels for 0%

profile of v18, /device:TPU:1, one launch (start us, length us, event | category | flops | bytes accessed | tf_op | source)
XLA Modules:
  0.0 240.9 jit_solution(7983494931880570151)
XLA Ops:
  0.9 4.4 %collective-permute-start = (bf16[4,1,64,128]{3,2,1,0:T(8,128)(2,1)S(1)}, bf16[4,1,64,128]{3,2,1,0:T(8,128)(2,1)S(1)}, u32[]{:S(2)}, u32[]{:S(2)}) collective-permute-start(bf16[4,1,64,128]{3,2,1,0:T(8,128)(2,1)S(1)} %get-tuple-element.40), channel_id=1, source_target_pairs={{0,8},{8,16},{16,24},{24,32},{32,40},{40,48},{48,56},{1,9},{9,17},... | collective-permute-start | bytes 196616 | tf_op jit(solution)/shard_map/ppermute | solution.py:15
  7.6 14.5 %collective-permute-start.2 = (bf16[4,5,64,128]{3,2,1,0:T(8,128)(2,1)S(1)}, bf16[4,5,64,128]{3,2,1,0:T(8,128)(2,1)S(1)}, u32[]{:S(2)}, u32[]{:S(2)}) collective-permute-start(bf16[4,5,64,128]{3,2,1,0:T(8,128)(2,1)S(1)} %constant_dynamic-slice_fusion.4), channel_id=1, source_target_pairs={{0,1},{1,0},{2,3},{3,2},{4,5},{5,4},{6,7},{7,6},{8,9},{9,8},{10,11... | collective-permute-start | bytes 983048 | tf_op jit(solution)/shard_map/ppermute | solution.py:62
  24.3 14.2 %collective-permute-start.4 = (bf16[12,16,128]{2,1,0:T(8,128)(2,1)S(1)}, bf16[12,16,128]{2,1,0:T(8,128)(2,1)S(1)}, u32[]{:S(2)}, u32[]{:S(2)}) collective-permute-start(bf16[12,16,128]{2,1,0:T(8,128)(2,1)S(1)} %constant_dynamic-update-slice_fusion), channel_id=1, source_target_pairs={{0,1},{1,0},{2,3},{3,2},{4,5},{5,4},{6,7},{7,6},{8,9},{9,8},{10,11... | collective-permute-start | bytes 147464 | tf_op jit(solution)/shard_map/ppermute | solution.py:67
  40.3 22.5 %collective-permute-start.19 = (f32[2,128]{1,0:T(2,128)S(1)}, f32[2,128]{1,0:T(2,128)S(1)}, u32[]{:S(2)}, u32[]{:S(2)}) collective-permute-start(f32[2,128]{1,0:T(2,128)S(1)} %pad_maximum_fusion.4), channel_id=1, source_target_pairs={{0,1},{1,0},{2,3},{3,2},{4,5},{5,4},{6,7},{7,6},{8,9},{9,8},{10,11... | collective-permute-start | bytes 3080 | tf_op jit(solution)/shard_map/ppermute | solution.py:59
  64.0 16.5 %collective-permute-start.7 = (bf16[12,16,256]{2,1,0:T(8,128)(2,1)S(1)}, bf16[12,16,256]{2,1,0:T(8,128)(2,1)S(1)}, u32[]{:S(2)}, u32[]{:S(2)}) collective-permute-start(bf16[12,16,256]{2,1,0:T(8,128)(2,1)S(1)} %maximum_select_fusion.7), channel_id=1, source_target_pairs={{0,32},{8,40},{16,48},{24,56},{32,0},{40,8},{48,16},{56,24},{1,33}... | collective-permute-start | bytes 294920 | tf_op jit(solution)/shard_map/ppermute | solution.py:44
  85.0 3.4 %collective-permute-start.6 = (bf16[4,6,64,256]{3,2,1,0:T(8,128)(2,1)}, bf16[4,6,64,256]{3,2,1,0:T(8,128)(2,1)}, u32[]{:S(2)}, u32[]{:S(2)}) collective-permute-start(bf16[4,6,64,256]{3,2,1,0:T(8,128)(2,1)} %get-tuple-element.28), channel_id=1, source_target_pairs={{0,6},{2,0},{4,2},{6,4},{1,7},{3,1},{5,3},{7,5},{8,14},{10,8},{12,... | collective-permute-start | bytes 2359304 | tf_op jit(solution)/shard_map/ppermute | solution.py:23
  90.4 5.7 %collective-permute-done.8 = bf16[12,2,16,256]{3,2,1,0:T(8,128)(2,1)S(1)} collective-permute-done((bf16[12,2,16,256]{3,2,1,0:T(8,128)(2,1)S(1)}, bf16[12,2,16,256]{3,2,1,0:T(8,128)(2,1)S(1)}, u32[]{:S(2)}, u32[]{:S(2)}) %collective-permute-start.8) | collective-permute-done | bytes 196640 | tf_op jit(solution)/shard_map/ppermute | solution.py:44
  99.6 7.0 %collective-permute-done.9 = bf16[12,2,2,16,256]{4,3,1,0,2:T(8,128)(2,1)} collective-permute-done((bf16[12,2,2,16,256]{4,3,1,0,2:T(8,128)(2,1)}, bf16[12,2,2,16,256]{4,3,1,0,2:T(8,128)(2,1)}, u32[]{:S(2)}, u32[]{:S(2)}) %collective-permute-start.9) | collective-permute-done | bytes 393248 | tf_op jit(solution)/shard_map/ppermute | solution.py:44
  107.7 3.2 %collective-permute-start.12 = (bf16[12,128,256]{2,1,0:T(8,128)(2,1)S(1)}, bf16[12,128,256]{2,1,0:T(8,128)(2,1)S(1)}, u32[]{:S(2)}, u32[]{:S(2)}) collective-permute-start(bf16[12,128,256]{2,1,0:T(8,128)(2,1)S(1)} %bitcast.135), channel_id=1, source_target_pairs={{0,128},{128,256},{256,384},{384,0},{1,129},{129,257},{257,385},{3... | collective-permute-start | bytes 2359304 | tf_op jit(solution)/shard_map/ppermute | solution.py:23
  110.9 3.4 %collective-permute-start.13 = (bf16[12,128,256]{2,1,0:T(8,128)(2,1)S(1)}, bf16[12,128,256]{2,1,0:T(8,128)(2,1)S(1)}, u32[]{:S(2)}, u32[]{:S(2)}) collective-permute-start(bf16[12,128,256]{2,1,0:T(8,128)(2,1)S(1)} %bitcast.136), channel_id=1, source_target_pairs={{0,384},{128,0},{256,128},{384,256},{1,385},{129,1},{257,129},{385... | collective-permute-start | bytes 2359304 | tf_op jit(solution)/shard_map/ppermute | solution.py:23
  115.3 3.2 %collective-permute-start.10 = (bf16[4,6,64,128]{3,2,1,0:T(8,128)(2,1)S(1)}, bf16[4,6,64,128]{3,2,1,0:T(8,128)(2,1)S(1)}, u32[]{:S(2)}, u32[]{:S(2)}) collective-permute-start(bf16[4,6,64,128]{3,2,1,0:T(8,128)(2,1)S(1)} %slice.133), channel_id=1, source_target_pairs={{0,6},{2,0},{4,2},{6,4},{1,7},{3,1},{5,3},{7,5},{8,14},{10,8},{12,... | collective-permute-start | bytes 1179656 | tf_op jit(solution)/shard_map/ppermute | solution.py:23
  124.1 5.4 %collective-permute-done.11 = bf16[4,6,64,128]{3,2,1,0:T(8,128)(2,1)S(1)} collective-permute-done((bf16[4,6,64,128]{3,2,1,0:T(8,128)(2,1)S(1)}, bf16[4,6,64,128]{3,2,1,0:T(8,128)(2,1)S(1)}, u32[]{:S(2)}, u32[]{:S(2)}) %collective-permute-start.11) | collective-permute-done | bytes 393248 | tf_op jit(solution)/shard_map/ppermute | solution.py:23
  129.6 3.4 %collective-permute-start.14 = (bf16[12,64,256]{2,1,0:T(8,128)(2,1)S(1)}, bf16[12,64,256]{2,1,0:T(8,128)(2,1)S(1)}, u32[]{:S(2)}, u32[]{:S(2)}) collective-permute-start(bf16[12,64,256]{2,1,0:T(8,128)(2,1)S(1)} %slice.137), channel_id=1, source_target_pairs={{0,384},{128,0},{256,128},{384,256},{1,385},{129,1},{257,129},{385... | collective-permute-start | bytes 1179656 | tf_op jit(solution)/shard_map/ppermute | solution.py:23
  132.9 8.3 %collective-permute-start.17 = (bf16[12,64,256]{2,1,0:T(8,128)(2,1)S(1)}, bf16[12,64,256]{2,1,0:T(8,128)(2,1)S(1)}, u32[]{:S(2)}, u32[]{:S(2)}) collective-permute-start(bf16[12,64,256]{2,1,0:T(8,128)(2,1)S(1)} %slice.137), channel_id=1, source_target_pairs={{192,0},{128,64},{320,128},{256,192},{448,256},{384,320},{64,384},... | collective-permute-start | bytes 1179656 | tf_op jit(solution)/shard_map/ppermute | solution.py:90
  157.0 6.8 %collective-permute-done.18 = bf16[12,64,256]{2,1,0:T(8,128)(2,1)S(1)} collective-permute-done((bf16[12,64,256]{2,1,0:T(8,128)(2,1)S(1)}, bf16[12,64,256]{2,1,0:T(8,128)(2,1)S(1)}, u32[]{:S(2)}, u32[]{:S(2)}) %collective-permute-start.18) | collective-permute-done | bytes 393248 | tf_op jit(solution)/shard_map/ppermute | solution.py:91
  164.9 6.3 %convert_add_fusion = (f32[4,32,9,256]{3,1,2,0:T(8,128)S(1)}, bf16[4,32,9,256]{3,1,2,0:T(8,128)(2,1)S(1)}) fusion(f32[256]{0:T(256)S(1)} %bitcast.163, f32[256]{0:T(256)S(1)} %bitcast.164, bf16[3,3,1024,256]{3,2,1,0:T(8,128)(2,1)S(1)} %bitcast.143, bf16[6,4,8,11,1024]{4,1,3,2,0:T(4,128)(2,1)S(1)} %fusion.1, pred[32,9]{0,1:T(8,128)(4,1)S(1)} %copy-done.4), kind=kOutput, calls=%fused_computation.17 | convolution fusion | flops 5438767104 | bytes 10815776 | tf_op jit(solution)/shard_map/conv_general_dilated | solution.py:120
  173.9 3.4 %collective-permute-start.22 = (bf16[4,4,64,256]{3,2,1,0:T(8,128)(2,1)S(1)}, bf16[4,4,64,256]{3,2,1,0:T(8,128)(2,1)S(1)}, u32[]{:S(2)}, u32[]{:S(2)}) collective-permute-start(bf16[4,4,64,256]{3,2,1,0:T(8,128)(2,1)S(1)} %bitcast.154), channel_id=1, source_target_pairs={{0,2},{2,4},{4,6},{6,0},{1,3},{3,5},{5,7},{7,1},{8,10},{10,12},{12... | collective-permute-start | bytes 1572872 | tf_op jit(solution)/shard_map/ppermute | solution.py:23
  177.4 9.5 %collective-permute-done.20 = bf16[4,4,64,256]{3,2,1,0:T(8,128)(2,1)S(1)} collective-permute-done((bf16[4,4,64,256]{3,2,1,0:T(8,128)(2,1)S(1)}, bf16[4,4,64,256]{3,2,1,0:T(8,128)(2,1)S(1)}, u32[]{:S(2)}, u32[]{:S(2)}) %collective-permute-start.20) | collective-permute-done | bytes 524320 | tf_op jit(solution)/shard_map/ppermute | solution.py:23
  187.0 3.3 %collective-permute-start.21 = (bf16[4,4,64,128]{3,2,1,0:T(8,128)(2,1)S(1)}, bf16[4,4,64,128]{3,2,1,0:T(8,128)(2,1)S(1)}, u32[]{:S(2)}, u32[]{:S(2)}) collective-permute-start(bf16[4,4,64,128]{3,2,1,0:T(8,128)(2,1)S(1)} %slice.180), channel_id=1, source_target_pairs={{0,6},{2,0},{4,2},{6,4},{1,7},{3,1},{5,3},{7,5},{8,14},{10,8},{12,... | collective-permute-start | bytes 786440 | tf_op jit(solution)/shard_map/ppermute | solution.py:23
  195.5 4.5 %collective-permute-done.23 = bf16[4,4,64,128]{3,2,1,0:T(8,128)(2,1)S(1)} collective-permute-done((bf16[4,4,64,128]{3,2,1,0:T(8,128)(2,1)S(1)}, bf16[4,4,64,128]{3,2,1,0:T(8,128)(2,1)S(1)}, u32[]{:S(2)}, u32[]{:S(2)}) %collective-permute-start.23) | collective-permute-done | bytes 262176 | tf_op jit(solution)/shard_map/ppermute | solution.py:23
  200.2 4.1 %collective-permute-start.25 = (bf16[1,4,64,1024]{3,2,1,0:T(8,128)(2,1)S(1)}, bf16[1,4,64,1024]{3,2,1,0:T(8,128)(2,1)S(1)}, u32[]{:S(2)}, u32[]{:S(2)}) collective-permute-start(bf16[1,4,64,1024]{3,2,1,0:T(8,128)(2,1)S(1)} %get-tuple-element.30), channel_id=1, source_target_pairs={{64,0},{128,64},{192,128},{256,192},{320,256},{384,320},{448,384},... | collective-permute-start | bytes 1572872 | tf_op jit(solution)/shard_map/ppermute | solution.py:18
  207.2 3.6 %collective-permute-done.25 = bf16[1,4,64,1024]{3,2,1,0:T(8,128)(2,1)S(1)} collective-permute-done((bf16[1,4,64,1024]{3,2,1,0:T(8,128)(2,1)S(1)}, bf16[1,4,64,1024]{3,2,1,0:T(8,128)(2,1)S(1)}, u32[]{:S(2)}, u32[]{:S(2)}) %collective-permute-start.25) | collective-permute-done | bytes 524320 | tf_op jit(solution)/shard_map/ppermute | solution.py:18
  213.5 9.0 %collective-permute-start.26 = (bf16[4,4,64,128]{3,2,1,0:T(8,128)(2,1)S(1)}, bf16[4,4,64,128]{3,2,1,0:T(8,128)(2,1)S(1)}, u32[]{:S(2)}, u32[]{:S(2)}) collective-permute-start(bf16[4,4,64,128]{3,2,1,0:T(8,128)(2,1)S(1)} %get-tuple-element.36), channel_id=1, source_target_pairs={{0,1},{1,0},{2,3},{3,2},{4,5},{5,4},{6,7},{7,6},{8,9},{9,8},{10,11... | collective-permute-start | bytes 786440 | tf_op jit(solution)/shard_map/ppermute | solution.py:155
  222.4 17.6 %collective-permute-done.26 = bf16[4,4,64,128]{3,2,1,0:T(8,128)(2,1)S(1)} collective-permute-done((bf16[4,4,64,128]{3,2,1,0:T(8,128)(2,1)S(1)}, bf16[4,4,64,128]{3,2,1,0:T(8,128)(2,1)S(1)}, u32[]{:S(2)}, u32[]{:S(2)}) %collective-permute-start.26) | collective-permute-done | bytes 262176 | tf_op jit(solution)/shard_map/ppermute | solution.py:155
  (118 shorter events, 57.0 us)
Async XLA Ops:
  0.9 61.9 %collective-permute-start = (bf16[4,1,64,128]{3,2,1,0:T(8,128)(2,1)S(1)}, bf16[4,1,64,128]{3,2,1,0:T(8,128)(2,1)S(1)}, u32[]{:S(2)}, u32[]{:S(2)}) collective-permute-start(bf16[4,1,64,128]{3,2,1,0:T(8,128)(2,1)S(1)} %get-tuple-element.40), channel_id=1, source_target_pairs={{0,8},{8,16},{16,24},{24,32},{32,40},{40,48},{48,56},{1,9},{9,17},... | collective-permute-start | bytes 196616 | tf_op jit(solution)/shard_map/ppermute | solution.py:15
  5.3 57.5 %collective-permute-start.1 = (bf16[4,1,64,128]{3,2,1,0:T(8,128)(2,1)S(1)}, bf16[4,1,64,128]{3,2,1,0:T(8,128)(2,1)S(1)}, u32[]{:S(2)}, u32[]{:S(2)}) collective-permute-start(bf16[4,1,64,128]{3,2,1,0:T(8,128)(2,1)S(1)} %get-tuple-element.39), channel_id=1, source_target_pairs={{8,0},{16,8},{24,16},{32,24},{40,32},{48,40},{56,48},{9,1},{17,9},... | collective-permute-start | bytes 196616 | tf_op jit(solution)/shard_map/ppermute | solution.py:18
  7.6 56.4 %collective-permute-start.2 = (bf16[4,5,64,128]{3,2,1,0:T(8,128)(2,1)S(1)}, bf16[4,5,64,128]{3,2,1,0:T(8,128)(2,1)S(1)}, u32[]{:S(2)}, u32[]{:S(2)}) collective-permute-start(bf16[4,5,64,128]{3,2,1,0:T(8,128)(2,1)S(1)} %constant_dynamic-slice_fusion.4), channel_id=1, source_target_pairs={{0,1},{1,0},{2,3},{3,2},{4,5},{5,4},{6,7},{7,6},{8,9},{9,8},{10,11... | collective-permute-start | bytes 983048 | tf_op jit(solution)/shard_map/ppermute | solution.py:62
  22.2 41.8 %collective-permute-start.3 = (bf16[4,1,64,128]{3,2,1,0:T(8,128)(2,1)S(1)}, bf16[4,1,64,128]{3,2,1,0:T(8,128)(2,1)S(1)}, u32[]{:S(2)}, u32[]{:S(2)}) collective-permute-start(bf16[4,1,64,128]{3,2,1,0:T(8,128)(2,1)S(1)} %get-tuple-element.38), channel_id=1, source_target_pairs={{1,8},{9,16},{17,24},{25,32},{33,40},{41,48},{49,56},{8,1},{16,9},... | collective-permute-start | bytes 196616 | tf_op jit(solution)/shard_map/ppermute | solution.py:66
  24.3 16.0 %collective-permute-start.4 = (bf16[12,16,128]{2,1,0:T(8,128)(2,1)S(1)}, bf16[12,16,128]{2,1,0:T(8,128)(2,1)S(1)}, u32[]{:S(2)}, u32[]{:S(2)}) collective-permute-start(bf16[12,16,128]{2,1,0:T(8,128)(2,1)S(1)} %constant_dynamic-update-slice_fusion), channel_id=1, source_target_pairs={{0,1},{1,0},{2,3},{3,2},{4,5},{5,4},{6,7},{7,6},{8,9},{9,8},{10,11... | collective-permute-start | bytes 147464 | tf_op jit(solution)/shard_map/ppermute | solution.py:67
  40.3 59.2 %collective-permute-start.19 = (f32[2,128]{1,0:T(2,128)S(1)}, f32[2,128]{1,0:T(2,128)S(1)}, u32[]{:S(2)}, u32[]{:S(2)}) collective-permute-start(f32[2,128]{1,0:T(2,128)S(1)} %pad_maximum_fusion.4), channel_id=1, source_target_pairs={{0,1},{1,0},{2,3},{3,2},{4,5},{5,4},{6,7},{7,6},{8,9},{9,8},{10,11... | collective-permute-start | bytes 3080 | tf_op jit(solution)/shard_map/ppermute | solution.py:59
  64.0 24.3 %collective-permute-start.7 = (bf16[12,16,256]{2,1,0:T(8,128)(2,1)S(1)}, bf16[12,16,256]{2,1,0:T(8,128)(2,1)S(1)}, u32[]{:S(2)}, u32[]{:S(2)}) collective-permute-start(bf16[12,16,256]{2,1,0:T(8,128)(2,1)S(1)} %maximum_select_fusion.7), channel_id=1, source_target_pairs={{0,32},{8,40},{16,48},{24,56},{32,0},{40,8},{48,16},{56,24},{1,33}... | collective-permute-start | bytes 294920 | tf_op jit(solution)/shard_map/ppermute | solution.py:44
  81.8 25.8 %collective-permute-start.5 = (bf16[4,6,64,256]{3,2,1,0:T(8,128)(2,1)}, bf16[4,6,64,256]{3,2,1,0:T(8,128)(2,1)}, u32[]{:S(2)}, u32[]{:S(2)}) collective-permute-start(bf16[4,6,64,256]{3,2,1,0:T(8,128)(2,1)} %get-tuple-element.28), channel_id=1, source_target_pairs={{0,2},{2,4},{4,6},{6,0},{1,3},{3,5},{5,7},{7,1},{8,10},{10,12},{12... | collective-permute-start | bytes 2359304 | tf_op jit(solution)/shard_map/ppermute | solution.py:23
  85.0 22.7 %collective-permute-start.6 = (bf16[4,6,64,256]{3,2,1,0:T(8,128)(2,1)}, bf16[4,6,64,256]{3,2,1,0:T(8,128)(2,1)}, u32[]{:S(2)}, u32[]{:S(2)}) collective-permute-start(bf16[4,6,64,256]{3,2,1,0:T(8,128)(2,1)} %get-tuple-element.28), channel_id=1, source_target_pairs={{0,6},{2,0},{4,2},{6,4},{1,7},{3,1},{5,3},{7,5},{8,14},{10,8},{12,... | collective-permute-start | bytes 2359304 | tf_op jit(solution)/shard_map/ppermute | solution.py:23
  96.9 9.6 %collective-permute-start.9 = (bf16[12,2,2,16,256]{4,3,1,0,2:T(8,128)(2,1)}, bf16[12,2,2,16,256]{4,3,1,0,2:T(8,128)(2,1)}, u32[]{:S(2)}, u32[]{:S(2)}) collective-permute-start(bf16[12,2,2,16,256]{4,3,1,0,2:T(8,128)(2,1)} %maximum_select_fusion.4), channel_id=1, source_target_pairs={{0,8},{8,0},{16,24},{24,16},{32,40},{40,32},{48,56},{56,48},{1,9},... | collective-permute-start | bytes 1179656 | tf_op jit(solution)/shard_map/ppermute | solution.py:44
  107.7 21.9 %collective-permute-start.12 = (bf16[12,128,256]{2,1,0:T(8,128)(2,1)S(1)}, bf16[12,128,256]{2,1,0:T(8,128)(2,1)S(1)}, u32[]{:S(2)}, u32[]{:S(2)}) collective-permute-start(bf16[12,128,256]{2,1,0:T(8,128)(2,1)S(1)} %bitcast.135), channel_id=1, source_target_pairs={{0,128},{128,256},{256,384},{384,0},{1,129},{129,257},{257,385},{3... | collective-permute-start | bytes 2359304 | tf_op jit(solution)/shard_map/ppermute | solution.py:23
  110.9 18.6 %collective-permute-start.13 = (bf16[12,128,256]{2,1,0:T(8,128)(2,1)S(1)}, bf16[12,128,256]{2,1,0:T(8,128)(2,1)S(1)}, u32[]{:S(2)}, u32[]{:S(2)}) collective-permute-start(bf16[12,128,256]{2,1,0:T(8,128)(2,1)S(1)} %bitcast.136), channel_id=1, source_target_pairs={{0,384},{128,0},{256,128},{384,256},{1,385},{129,1},{257,129},{385... | collective-permute-start | bytes 2359304 | tf_op jit(solution)/shard_map/ppermute | solution.py:23
  115.3 8.8 %collective-permute-start.10 = (bf16[4,6,64,128]{3,2,1,0:T(8,128)(2,1)S(1)}, bf16[4,6,64,128]{3,2,1,0:T(8,128)(2,1)S(1)}, u32[]{:S(2)}, u32[]{:S(2)}) collective-permute-start(bf16[4,6,64,128]{3,2,1,0:T(8,128)(2,1)S(1)} %slice.133), channel_id=1, source_target_pairs={{0,6},{2,0},{4,2},{6,4},{1,7},{3,1},{5,3},{7,5},{8,14},{10,8},{12,... | collective-permute-start | bytes 1179656 | tf_op jit(solution)/shard_map/ppermute | solution.py:23
  119.5 10.0 %collective-permute-start.11 = (bf16[4,6,64,128]{3,2,1,0:T(8,128)(2,1)S(1)}, bf16[4,6,64,128]{3,2,1,0:T(8,128)(2,1)S(1)}, u32[]{:S(2)}, u32[]{:S(2)}) collective-permute-start(bf16[4,6,64,128]{3,2,1,0:T(8,128)(2,1)S(1)} %slice.134), channel_id=1, source_target_pairs={{0,2},{2,4},{4,6},{6,0},{1,3},{3,5},{5,7},{7,1},{8,10},{10,12},{12... | collective-permute-start | bytes 1179656 | tf_op jit(solution)/shard_map/ppermute | solution.py:23
  129.6 27.3 %collective-permute-start.14 = (bf16[12,64,256]{2,1,0:T(8,128)(2,1)S(1)}, bf16[12,64,256]{2,1,0:T(8,128)(2,1)S(1)}, u32[]{:S(2)}, u32[]{:S(2)}) collective-permute-start(bf16[12,64,256]{2,1,0:T(8,128)(2,1)S(1)} %slice.137), channel_id=1, source_target_pairs={{0,384},{128,0},{256,128},{384,256},{1,385},{129,1},{257,129},{385... | collective-permute-start | bytes 1179656 | tf_op jit(solution)/shard_map/ppermute | solution.py:23
  132.9 24.0 %collective-permute-start.17 = (bf16[12,64,256]{2,1,0:T(8,128)(2,1)S(1)}, bf16[12,64,256]{2,1,0:T(8,128)(2,1)S(1)}, u32[]{:S(2)}, u32[]{:S(2)}) collective-permute-start(bf16[12,64,256]{2,1,0:T(8,128)(2,1)S(1)} %slice.137), channel_id=1, source_target_pairs={{192,0},{128,64},{320,128},{256,192},{448,256},{384,320},{64,384},... | collective-permute-start | bytes 1179656 | tf_op jit(solution)/shard_map/ppermute | solution.py:90
  141.3 15.7 %collective-permute-start.15 = (bf16[12,64,256]{2,1,0:T(8,128)(2,1)S(1)}, bf16[12,64,256]{2,1,0:T(8,128)(2,1)S(1)}, u32[]{:S(2)}, u32[]{:S(2)}) collective-permute-start(bf16[12,64,256]{2,1,0:T(8,128)(2,1)S(1)} %slice.138), channel_id=1, source_target_pairs={{0,128},{128,256},{256,384},{384,0},{1,129},{129,257},{257,385},{3... | collective-permute-start | bytes 1179656 | tf_op jit(solution)/shard_map/ppermute | solution.py:23
  144.2 19.6 %collective-permute-start.18 = (bf16[12,64,256]{2,1,0:T(8,128)(2,1)S(1)}, bf16[12,64,256]{2,1,0:T(8,128)(2,1)S(1)}, u32[]{:S(2)}, u32[]{:S(2)}) collective-permute-start(bf16[12,64,256]{2,1,0:T(8,128)(2,1)S(1)} %slice.138), channel_id=1, source_target_pairs={{448,0},{384,64},{64,128},{0,192},{192,256},{128,320},{320,384},{2... | collective-permute-start | bytes 1179656 | tf_op jit(solution)/shard_map/ppermute | solution.py:91
  152.4 11.7 %collective-permute-start.16 = (bf16[12,3,128,256]{3,2,0,1:T(8,128)(2,1)S(1)}, bf16[12,3,128,256]{3,2,0,1:T(8,128)(2,1)S(1)}, u32[]{:S(2)}, u32[]{:S(2)}) collective-permute-start(bf16[12,3,128,256]{3,2,0,1:T(8,128)(2,1)S(1)} %pad_maximum_fusion), channel_id=1, source_target_pairs={{0,64},{64,0},{1,65},{65,1},{2,66},{66,2},{3,67},{67,3},{4,68},{68... | collective-permute-start | bytes 7077896 | tf_op jit(solution)/shard_map/ppermute | solution.py:93
  171.9 15.0 %collective-permute-start.20 = (bf16[4,4,64,256]{3,2,1,0:T(8,128)(2,1)S(1)}, bf16[4,4,64,256]{3,2,1,0:T(8,128)(2,1)S(1)}, u32[]{:S(2)}, u32[]{:S(2)}) collective-permute-start(bf16[4,4,64,256]{3,2,1,0:T(8,128)(2,1)S(1)} %bitcast.153), channel_id=1, source_target_pairs={{0,6},{2,0},{4,2},{6,4},{1,7},{3,1},{5,3},{7,5},{8,14},{10,8},{12,... | collective-permute-start | bytes 1572872 | tf_op jit(solution)/shard_map/ppermute | solution.py:23
  173.9 16.5 %collective-permute-start.22 = (bf16[4,4,64,256]{3,2,1,0:T(8,128)(2,1)S(1)}, bf16[4,4,64,256]{3,2,1,0:T(8,128)(2,1)S(1)}, u32[]{:S(2)}, u32[]{:S(2)}) collective-permute-start(bf16[4,4,64,256]{3,2,1,0:T(8,128)(2,1)S(1)} %bitcast.154), channel_id=1, source_target_pairs={{0,2},{2,4},{4,6},{6,0},{1,3},{3,5},{5,7},{7,1},{8,10},{10,12},{12... | collective-permute-start | bytes 1572872 | tf_op jit(solution)/shard_map/ppermute | solution.py:23
  190.4 9.6 %collective-permute-start.23 = (bf16[4,4,64,128]{3,2,1,0:T(8,128)(2,1)S(1)}, bf16[4,4,64,128]{3,2,1,0:T(8,128)(2,1)S(1)}, u32[]{:S(2)}, u32[]{:S(2)}) collective-permute-start(bf16[4,4,64,128]{3,2,1,0:T(8,128)(2,1)S(1)} %slice.181), channel_id=1, source_target_pairs={{0,2},{2,4},{4,6},{6,0},{1,3},{3,5},{5,7},{7,1},{8,10},{10,12},{12... | collective-permute-start | bytes 786440 | tf_op jit(solution)/shard_map/ppermute | solution.py:23
  200.2 10.5 %collective-permute-start.25 = (bf16[1,4,64,1024]{3,2,1,0:T(8,128)(2,1)S(1)}, bf16[1,4,64,1024]{3,2,1,0:T(8,128)(2,1)S(1)}, u32[]{:S(2)}, u32[]{:S(2)}) collective-permute-start(bf16[1,4,64,1024]{3,2,1,0:T(8,128)(2,1)S(1)} %get-tuple-element.30), channel_id=1, source_target_pairs={{64,0},{128,64},{192,128},{256,192},{320,256},{384,320},{448,384},... | collective-permute-start | bytes 1572872 | tf_op jit(solution)/shard_map/ppermute | solution.py:18
  213.5 26.5 %collective-permute-start.26 = (bf16[4,4,64,128]{3,2,1,0:T(8,128)(2,1)S(1)}, bf16[4,4,64,128]{3,2,1,0:T(8,128)(2,1)S(1)}, u32[]{:S(2)}, u32[]{:S(2)}) collective-permute-start(bf16[4,4,64,128]{3,2,1,0:T(8,128)(2,1)S(1)} %get-tuple-element.36), channel_id=1, source_target_pairs={{0,1},{1,0},{2,3},{3,2},{4,5},{5,4},{6,7},{7,6},{8,9},{9,8},{10,11... | collective-permute-start | bytes 786440 | tf_op jit(solution)/shard_map/ppermute | solution.py:155
  (8 other events, 70.6 us)

commit v19 on v18

--- a/solution.py
+++ b/solution.py
@@ -134,25 +134,24 @@
     prev_ok = (local_ids[1:-1] == local_ids[:-2]).astype(jnp.float32).reshape(fr_count, 1, 1, 1)
     next_ok = (local_ids[1:-1] == local_ids[2:]).astype(jnp.float32).reshape(fr_count, 1, 1, 1)
     whole = shift_halo(x_gather(active), FRAME, lax.axis_size(FRAME), 0, 1)
-    taps_out = [
-        jnp.einsum(
-            "fhwc,cd->fhwd",
-            whole[tap : tap + fr_count],
-            full_temporal[tap],
-            preferred_element_type=jnp.float32,
-        )
-        for tap in range(3)
-    ]
-    total = (
-        hidden.astype(jnp.float32)
-        + biases[1]
-        + prev_ok * taps_out[0]
-        + taps_out[1]
-        + next_ok * taps_out[2]
-    ).astype(jnp.bfloat16)
-    kept = lax.dynamic_slice_in_dim(total, side * col_width, col_width, axis=3)
-    given = lax.dynamic_slice_in_dim(total, (1 - side) * col_width, col_width, axis=3)
+    def block_out(start):
+        cols = [lax.dynamic_slice_in_dim(full_temporal[tap], start, col_width, axis=1) for tap in range(3)]
+        terms = [
+            jnp.einsum(
+                "fhwc,cd->fhwd",
+                whole[tap : tap + fr_count],
+                cols[tap],
+                preferred_element_type=jnp.float32,
+            )
+            for tap in range(3)
+        ]
+        base = lax.dynamic_slice_in_dim(hidden, start, col_width, axis=3).astype(jnp.float32)
+        bias = lax.dynamic_slice_in_dim(biases[1], start, col_width, axis=0)
+        return (base + bias + prev_ok * terms[0] + terms[1] + next_ok * terms[2]).astype(jnp.bfloat16)
+
+    given = block_out((1 - side) * col_width)
     returned = lax.ppermute(given, "cz", SWAP)
+    kept = block_out(side * col_width)
     return ordered_pair(kept, returned, high, 1)
 
 

time: 245 us -> 256 us (1.045)
  the two profiles are of different devices: /device:TPU:1 before, /device:TPU:80 now
where the time goes in v19:
time: 256 us; the launch traced here: 255 us
  waiting for transfers between devices  109 us (43%)
  starting transfers between devices  105 us (41%)
  local copies, waits for them, and re-layouts  21.1 us (8%)
  matrix products  10.6 us (4%)
  other arithmetic  8.51 us (3%)
    ppermute x12, starting transfers between devices, ring_shift(): lax.ppermute(block, axis, [(i, (i + step) % count) for i in range(count)])  38.2 us
    ppermute x1, waiting for transfers between devices, body(): w_block = ordered_pair(weight, lax.ppermute(weight, 'cz', SWAP), high, 2)  27.2 us
    ppermute x1, waiting for transfers between devices, body(): returned = lax.ppermute(given, 'cz', SWAP)  24.6 us
    ppermute x12, waiting for transfers between devices, ring_shift(): lax.ppermute(block, axis, [(i, (i + step) % count) for i in range(count)])  23.4 us
    ppermute x3, waiting for transfers between devices, xor_stack(): other = lax.ppermute(block, axis, [(i, i ^ bit) for i in range(count)])  15.3 us
    ppermute x1, starting transfers between devices, body(): biases = ordered_pair(biases, lax.ppermute(biases, 'cz', SWAP), high, 1)  13.9 us
    ppermute x1, starting transfers between devices, body(): w_block = ordered_pair(weight, lax.ppermute(weight, 'cz', SWAP), high, 2)  12.6 us
    ppermute x1, waiting for transfers between devices, body(): rim = lax.ppermute(edge, ('row', 'cz'), diagonal)  12 us
  transfers between devices with their start and end apart: 27, of which 14 were waited for; matrix products, arithmetic and copies ran while one was open for 12% of the time, Pallas kernels for 0%

profile of v19, /device:TPU:80, one launch (start us, length us, event | category | flops | bytes accessed | tf_op | source)
XLA Modules:
  0.0 254.9 jit_solution(16875929587140975535)
XLA Ops:
  0.7 13.9 %collective-permute-start.19 = (f32[2,128]{1,0:T(2,128)S(1)}, f32[2,128]{1,0:T(2,128)S(1)}, u32[]{:S(2)}, u32[]{:S(2)}) collective-permute-start(f32[2,128]{1,0:T(2,128)S(1)} %pad_maximum_fusion.34), channel_id=1, source_target_pairs={{0,1},{1,0},{2,3},{3,2},{4,5},{5,4},{6,7},{7,6},{8,9},{9,8},{10,11... | collective-permute-start | bytes 3080 | tf_op jit(solution)/shard_map/ppermute | solution.py:59
  15.6 2.9 %collective-permute-start.1 = (bf16[4,1,64,128]{3,2,1,0:T(8,128)(2,1)S(1)}, bf16[4,1,64,128]{3,2,1,0:T(8,128)(2,1)S(1)}, u32[]{:S(2)}, u32[]{:S(2)}) collective-permute-start(bf16[4,1,64,128]{3,2,1,0:T(8,128)(2,1)S(1)} %get-tuple-element.37), channel_id=1, source_target_pairs={{8,0},{16,8},{24,16},{32,24},{40,32},{48,40},{56,48},{9,1},{17,9},... | collective-permute-start | bytes 196616 | tf_op jit(solution)/shard_map/ppermute | solution.py:18
  18.5 2.9 %collective-permute-start = (bf16[4,1,64,128]{3,2,1,0:T(8,128)(2,1)S(1)}, bf16[4,1,64,128]{3,2,1,0:T(8,128)(2,1)S(1)}, u32[]{:S(2)}, u32[]{:S(2)}) collective-permute-start(bf16[4,1,64,128]{3,2,1,0:T(8,128)(2,1)S(1)} %get-tuple-element.38), channel_id=1, source_target_pairs={{0,8},{8,16},{16,24},{24,32},{32,40},{40,48},{48,56},{1,9},{9,17},... | collective-permute-start | bytes 196616 | tf_op jit(solution)/shard_map/ppermute | solution.py:15
  25.8 12.6 %collective-permute-start.4 = (bf16[12,16,128]{2,1,0:T(8,128)(2,1)S(1)}, bf16[12,16,128]{2,1,0:T(8,128)(2,1)S(1)}, u32[]{:S(2)}, u32[]{:S(2)}) collective-permute-start(bf16[12,16,128]{2,1,0:T(8,128)(2,1)S(1)} %constant_dynamic-update-slice_fusion), channel_id=1, source_target_pairs={{0,1},{1,0},{2,3},{3,2},{4,5},{5,4},{6,7},{7,6},{8,9},{9,8},{10,11... | collective-permute-start | bytes 147464 | tf_op jit(solution)/shard_map/ppermute | solution.py:67
  39.3 27.2 %collective-permute-done.4 = bf16[12,16,128]{2,1,0:T(8,128)(2,1)S(1)} collective-permute-done((bf16[12,16,128]{2,1,0:T(8,128)(2,1)S(1)}, bf16[12,16,128]{2,1,0:T(8,128)(2,1)S(1)}, u32[]{:S(2)}, u32[]{:S(2)}) %collective-permute-start.4) | collective-permute-done | bytes 49184 | tf_op jit(solution)/shard_map/ppermute | solution.py:67
  69.9 12.0 %collective-permute-done.3 = bf16[4,1,64,128]{3,2,1,0:T(8,128)(2,1)S(1)} collective-permute-done((bf16[4,1,64,128]{3,2,1,0:T(8,128)(2,1)S(1)}, bf16[4,1,64,128]{3,2,1,0:T(8,128)(2,1)S(1)}, u32[]{:S(2)}, u32[]{:S(2)}) %collective-permute-start.3) | collective-permute-done | bytes 65568 | tf_op jit(solution)/shard_map/ppermute | solution.py:66
  81.9 3.8 %collective-permute-start.7 = (bf16[12,16,256]{2,1,0:T(8,128)(2,1)S(1)}, bf16[12,16,256]{2,1,0:T(8,128)(2,1)S(1)}, u32[]{:S(2)}, u32[]{:S(2)}) collective-permute-start(bf16[12,16,256]{2,1,0:T(8,128)(2,1)S(1)} %maximum_select_fusion.7), channel_id=1, source_target_pairs={{0,32},{8,40},{16,48},{24,56},{32,0},{40,8},{48,16},{56,24},{1,33}... | collective-permute-start | bytes 294920 | tf_op jit(solution)/shard_map/ppermute | solution.py:44
  87.1 3.4 %collective-permute-start.5 = (bf16[4,6,64,256]{3,2,1,0:T(8,128)(2,1)}, bf16[4,6,64,256]{3,2,1,0:T(8,128)(2,1)}, u32[]{:S(2)}, u32[]{:S(2)}) collective-permute-start(bf16[4,6,64,256]{3,2,1,0:T(8,128)(2,1)} %get-tuple-element.28), channel_id=1, source_target_pairs={{0,2},{2,4},{4,6},{6,0},{1,3},{3,5},{5,7},{7,1},{8,10},{10,12},{12... | collective-permute-start | bytes 2359304 | tf_op jit(solution)/shard_map/ppermute | solution.py:23
  90.5 3.7 %collective-permute-start.6 = (bf16[4,6,64,256]{3,2,1,0:T(8,128)(2,1)}, bf16[4,6,64,256]{3,2,1,0:T(8,128)(2,1)}, u32[]{:S(2)}, u32[]{:S(2)}) collective-permute-start(bf16[4,6,64,256]{3,2,1,0:T(8,128)(2,1)} %get-tuple-element.28), channel_id=1, source_target_pairs={{0,6},{2,0},{4,2},{6,4},{1,7},{3,1},{5,3},{7,5},{8,14},{10,8},{12,... | collective-permute-start | bytes 2359304 | tf_op jit(solution)/shard_map/ppermute | solution.py:23
  97.4 6.7 %collective-permute-done.8 = bf16[12,2,16,256]{3,2,1,0:T(8,128)(2,1)S(1)} collective-permute-done((bf16[12,2,16,256]{3,2,1,0:T(8,128)(2,1)S(1)}, bf16[12,2,16,256]{3,2,1,0:T(8,128)(2,1)S(1)}, u32[]{:S(2)}, u32[]{:S(2)}) %collective-permute-start.8) | collective-permute-done | bytes 196640 | tf_op jit(solution)/shard_map/ppermute | solution.py:44
  107.6 7.3 %collective-permute-done.9 = bf16[12,2,2,16,256]{4,3,1,0,2:T(8,128)(2,1)} collective-permute-done((bf16[12,2,2,16,256]{4,3,1,0,2:T(8,128)(2,1)}, bf16[12,2,2,16,256]{4,3,1,0,2:T(8,128)(2,1)}, u32[]{:S(2)}, u32[]{:S(2)}) %collective-permute-start.9) | collective-permute-done | bytes 393248 | tf_op jit(solution)/shard_map/ppermute | solution.py:44
  116.1 3.2 %collective-permute-start.12 = (bf16[12,128,256]{2,1,0:T(8,128)(2,1)S(1)}, bf16[12,128,256]{2,1,0:T(8,128)(2,1)S(1)}, u32[]{:S(2)}, u32[]{:S(2)}) collective-permute-start(bf16[12,128,256]{2,1,0:T(8,128)(2,1)S(1)} %bitcast.154), channel_id=1, source_target_pairs={{0,128},{128,256},{256,384},{384,0},{1,129},{129,257},{257,385},{3... | collective-permute-start | bytes 2359304 | tf_op jit(solution)/shard_map/ppermute | solution.py:23
  123.0 5.7 %collective-permute-start.10 = (bf16[4,6,64,128]{3,2,1,0:T(8,128)(2,1)S(1)}, bf16[4,6,64,128]{3,2,1,0:T(8,128)(2,1)S(1)}, u32[]{:S(2)}, u32[]{:S(2)}) collective-permute-start(bf16[4,6,64,128]{3,2,1,0:T(8,128)(2,1)S(1)} %slice.139), channel_id=1, source_target_pairs={{0,6},{2,0},{4,2},{6,4},{1,7},{3,1},{5,3},{7,5},{8,14},{10,8},{12,... | collective-permute-start | bytes 1179656 | tf_op jit(solution)/shard_map/ppermute | solution.py:23
  133.9 6.6 %collective-permute-done.11 = bf16[4,6,64,128]{3,2,1,0:T(8,128)(2,1)S(1)} collective-permute-done((bf16[4,6,64,128]{3,2,1,0:T(8,128)(2,1)S(1)}, bf16[4,6,64,128]{3,2,1,0:T(8,128)(2,1)S(1)}, u32[]{:S(2)}, u32[]{:S(2)}) %collective-permute-start.11) | collective-permute-done | bytes 393248 | tf_op jit(solution)/shard_map/ppermute | solution.py:23
  145.0 3.5 %collective-permute-start.15 = (bf16[12,64,256]{2,1,0:T(8,128)(2,1)S(1)}, bf16[12,64,256]{2,1,0:T(8,128)(2,1)}, u32[]{:S(2)}, u32[]{:S(2)}) collective-permute-start(bf16[12,64,256]{2,1,0:T(8,128)(2,1)S(1)} %slice.144), channel_id=1, source_target_pairs={{0,128},{128,256},{256,384},{384,0},{1,129},{129,257},{257,385},{3... | collective-permute-start | bytes 1179656 | tf_op jit(solution)/shard_map/ppermute | solution.py:23
  148.4 4.6 %collective-permute-start.18 = (bf16[12,64,256]{2,1,0:T(8,128)(2,1)S(1)}, bf16[12,64,256]{2,1,0:T(8,128)(2,1)S(1)}, u32[]{:S(2)}, u32[]{:S(2)}) collective-permute-start(bf16[12,64,256]{2,1,0:T(8,128)(2,1)S(1)} %slice.144), channel_id=1, source_target_pairs={{448,0},{384,64},{64,128},{0,192},{192,256},{128,320},{320,384},{2... | collective-permute-start | bytes 1179656 | tf_op jit(solution)/shard_map/ppermute | solution.py:91
  168.3 6.2 %fusion.33 = (bf16[4,32,9,256]{3,1,2,0:T(8,128)(2,1)S(1)}, bf16[4,32,9,256]{3,1,2,0:T(8,128)(2,1)S(1)}) fusion(f32[256]{0:T(256)S(1)} %bitcast.185, bf16[3,3,1024,256]{3,2,1,0:T(8,128)(2,1)S(1)} %bitcast.162, bf16[6,4,8,11,1024]{4,1,3,2,0:T(4,128)(2,1)S(1)} %fusion.1, pred[32,9]{0,1:T(8,128)(4,1)S(1)} %copy-done.4), kind=kOutput, calls=%fused_computation.33 | convolution fusion | flops 5438472192 | bytes 10224928 | tf_op jit(solution)/shard_map/conv_general_dilated | solution.py:120
  177.3 4.1 %collective-permute-start.22 = (bf16[4,4,64,256]{3,2,1,0:T(8,128)(2,1)S(1)}, bf16[4,4,64,256]{3,2,1,0:T(8,128)(2,1)S(1)}, u32[]{:S(2)}, u32[]{:S(2)}) collective-permute-start(bf16[4,4,64,256]{3,2,1,0:T(8,128)(2,1)S(1)} %bitcast.174), channel_id=1, source_target_pairs={{0,2},{2,4},{4,6},{6,0},{1,3},{3,5},{5,7},{7,1},{8,10},{10,12},{12... | collective-permute-start | bytes 1572872 | tf_op jit(solution)/shard_map/ppermute | solution.py:23
  181.7 9.2 %collective-permute-done.20 = bf16[4,4,64,256]{3,2,1,0:T(8,128)(2,1)S(1)} collective-permute-done((bf16[4,4,64,256]{3,2,1,0:T(8,128)(2,1)S(1)}, bf16[4,4,64,256]{3,2,1,0:T(8,128)(2,1)S(1)}, u32[]{:S(2)}, u32[]{:S(2)}) %collective-permute-start.20) | collective-permute-done | bytes 524320 | tf_op jit(solution)/shard_map/ppermute | solution.py:23
  190.9 3.4 %collective-permute-start.21 = (bf16[4,4,64,128]{3,2,1,0:T(8,128)(2,1)S(1)}, bf16[4,4,64,128]{3,2,1,0:T(8,128)(2,1)S(1)}, u32[]{:S(2)}, u32[]{:S(2)}) collective-permute-start(bf16[4,4,64,128]{3,2,1,0:T(8,128)(2,1)S(1)} %slice.186), channel_id=1, source_target_pairs={{0,6},{2,0},{4,2},{6,4},{1,7},{3,1},{5,3},{7,5},{8,14},{10,8},{12,... | collective-permute-start | bytes 786440 | tf_op jit(solution)/shard_map/ppermute | solution.py:23
  199.9 5.3 %collective-permute-done.23 = bf16[4,4,64,128]{3,2,1,0:T(8,128)(2,1)S(1)} collective-permute-done((bf16[4,4,64,128]{3,2,1,0:T(8,128)(2,1)S(1)}, bf16[4,4,64,128]{3,2,1,0:T(8,128)(2,1)S(1)}, u32[]{:S(2)}, u32[]{:S(2)}) %collective-permute-start.23) | collective-permute-done | bytes 262176 | tf_op jit(solution)/shard_map/ppermute | solution.py:23
  214.9 3.1 %collective-permute-done.24 = bf16[1,4,64,1024]{3,2,1,0:T(8,128)(2,1)S(1)} collective-permute-done((bf16[1,4,64,1024]{3,2,1,0:T(8,128)(2,1)S(1)}, bf16[1,4,64,1024]{3,2,1,0:T(8,128)(2,1)S(1)}, u32[]{:S(2)}, u32[]{:S(2)}) %collective-permute-start.24) | collective-permute-done | bytes 524320 | tf_op jit(solution)/shard_map/ppermute | solution.py:15
  218.7 9.2 %collective-permute-start.26 = (bf16[4,4,64,128]{3,2,1,0:T(8,128)(2,1)S(1)}, bf16[4,4,64,128]{3,2,1,0:T(8,128)(2,1)S(1)}, u32[]{:S(2)}, u32[]{:S(2)}) collective-permute-start(bf16[4,4,64,128]{3,2,1,0:T(8,128)(2,1)S(1)} %fusion.29), channel_id=1, source_target_pairs={{0,1},{1,0},{2,3},{3,2},{4,5},{5,4},{6,7},{7,6},{8,9},{9,8},{10,11... | collective-permute-start | bytes 786440 | tf_op jit(solution)/shard_map/ppermute | solution.py:153
  229.4 24.6 %collective-permute-done.26 = bf16[4,4,64,128]{3,2,1,0:T(8,128)(2,1)S(1)} collective-permute-done((bf16[4,4,64,128]{3,2,1,0:T(8,128)(2,1)S(1)}, bf16[4,4,64,128]{3,2,1,0:T(8,128)(2,1)S(1)}, u32[]{:S(2)}, u32[]{:S(2)}) %collective-permute-start.26) | collective-permute-done | bytes 262176 | tf_op jit(solution)/shard_map/ppermute | solution.py:153
  (122 shorter events, 68.8 us)
Async XLA Ops:
  0.7 106.8 %collective-permute-start.19 = (f32[2,128]{1,0:T(2,128)S(1)}, f32[2,128]{1,0:T(2,128)S(1)}, u32[]{:S(2)}, u32[]{:S(2)}) collective-permute-start(f32[2,128]{1,0:T(2,128)S(1)} %pad_maximum_fusion.34), channel_id=1, source_target_pairs={{0,1},{1,0},{2,3},{3,2},{4,5},{5,4},{6,7},{7,6},{8,9},{9,8},{10,11... | collective-permute-start | bytes 3080 | tf_op jit(solution)/shard_map/ppermute | solution.py:59
  15.6 53.2 %collective-permute-start.1 = (bf16[4,1,64,128]{3,2,1,0:T(8,128)(2,1)S(1)}, bf16[4,1,64,128]{3,2,1,0:T(8,128)(2,1)S(1)}, u32[]{:S(2)}, u32[]{:S(2)}) collective-permute-start(bf16[4,1,64,128]{3,2,1,0:T(8,128)(2,1)S(1)} %get-tuple-element.37), channel_id=1, source_target_pairs={{8,0},{16,8},{24,16},{32,24},{40,32},{48,40},{56,48},{9,1},{17,9},... | collective-permute-start | bytes 196616 | tf_op jit(solution)/shard_map/ppermute | solution.py:18
  18.5 50.3 %collective-permute-start = (bf16[4,1,64,128]{3,2,1,0:T(8,128)(2,1)S(1)}, bf16[4,1,64,128]{3,2,1,0:T(8,128)(2,1)S(1)}, u32[]{:S(2)}, u32[]{:S(2)}) collective-permute-start(bf16[4,1,64,128]{3,2,1,0:T(8,128)(2,1)S(1)} %get-tuple-element.38), channel_id=1, source_target_pairs={{0,8},{8,16},{16,24},{24,32},{32,40},{40,48},{48,56},{1,9},{9,17},... | collective-permute-start | bytes 196616 | tf_op jit(solution)/shard_map/ppermute | solution.py:15
  22.4 59.5 %collective-permute-start.2 = (bf16[4,5,64,128]{3,2,1,0:T(8,128)(2,1)S(1)}, bf16[4,5,64,128]{3,2,1,0:T(8,128)(2,1)S(1)}, u32[]{:S(2)}, u32[]{:S(2)}) collective-permute-start(bf16[4,5,64,128]{3,2,1,0:T(8,128)(2,1)S(1)} %constant_dynamic-slice_fusion.6), channel_id=1, source_target_pairs={{0,1},{1,0},{2,3},{3,2},{4,5},{5,4},{6,7},{7,6},{8,9},{9,8},{10,11... | collective-permute-start | bytes 983048 | tf_op jit(solution)/shard_map/ppermute | solution.py:62
  25.8 40.6 %collective-permute-start.4 = (bf16[12,16,128]{2,1,0:T(8,128)(2,1)S(1)}, bf16[12,16,128]{2,1,0:T(8,128)(2,1)S(1)}, u32[]{:S(2)}, u32[]{:S(2)}) collective-permute-start(bf16[12,16,128]{2,1,0:T(8,128)(2,1)S(1)} %constant_dynamic-update-slice_fusion), channel_id=1, source_target_pairs={{0,1},{1,0},{2,3},{3,2},{4,5},{5,4},{6,7},{7,6},{8,9},{9,8},{10,11... | collective-permute-start | bytes 147464 | tf_op jit(solution)/shard_map/ppermute | solution.py:67
  66.5 15.4 %collective-permute-start.3 = (bf16[4,1,64,128]{3,2,1,0:T(8,128)(2,1)S(1)}, bf16[4,1,64,128]{3,2,1,0:T(8,128)(2,1)S(1)}, u32[]{:S(2)}, u32[]{:S(2)}) collective-permute-start(bf16[4,1,64,128]{3,2,1,0:T(8,128)(2,1)S(1)} %get-tuple-element.36), channel_id=1, source_target_pairs={{1,8},{9,16},{17,24},{25,32},{33,40},{41,48},{49,56},{8,1},{16,9},... | collective-permute-start | bytes 196616 | tf_op jit(solution)/shard_map/ppermute | solution.py:66
  81.9 13.5 %collective-permute-start.7 = (bf16[12,16,256]{2,1,0:T(8,128)(2,1)S(1)}, bf16[12,16,256]{2,1,0:T(8,128)(2,1)S(1)}, u32[]{:S(2)}, u32[]{:S(2)}) collective-permute-start(bf16[12,16,256]{2,1,0:T(8,128)(2,1)S(1)} %maximum_select_fusion.7), channel_id=1, source_target_pairs={{0,32},{8,40},{16,48},{24,56},{32,0},{40,8},{48,16},{56,24},{1,33}... | collective-permute-start | bytes 294920 | tf_op jit(solution)/shard_map/ppermute | solution.py:44
  87.1 29.0 %collective-permute-start.5 = (bf16[4,6,64,256]{3,2,1,0:T(8,128)(2,1)}, bf16[4,6,64,256]{3,2,1,0:T(8,128)(2,1)}, u32[]{:S(2)}, u32[]{:S(2)}) collective-permute-start(bf16[4,6,64,256]{3,2,1,0:T(8,128)(2,1)} %get-tuple-element.28), channel_id=1, source_target_pairs={{0,2},{2,4},{4,6},{6,0},{1,3},{3,5},{5,7},{7,1},{8,10},{10,12},{12... | collective-permute-start | bytes 2359304 | tf_op jit(solution)/shard_map/ppermute | solution.py:23
  90.5 25.6 %collective-permute-start.6 = (bf16[4,6,64,256]{3,2,1,0:T(8,128)(2,1)}, bf16[4,6,64,256]{3,2,1,0:T(8,128)(2,1)}, u32[]{:S(2)}, u32[]{:S(2)}) collective-permute-start(bf16[4,6,64,256]{3,2,1,0:T(8,128)(2,1)} %get-tuple-element.28), channel_id=1, source_target_pairs={{0,6},{2,0},{4,2},{6,4},{1,7},{3,1},{5,3},{7,5},{8,14},{10,8},{12,... | collective-permute-start | bytes 2359304 | tf_op jit(solution)/shard_map/ppermute | solution.py:23
  104.9 10.0 %collective-permute-start.9 = (bf16[12,2,2,16,256]{4,3,1,0,2:T(8,128)(2,1)}, bf16[12,2,2,16,256]{4,3,1,0,2:T(8,128)(2,1)}, u32[]{:S(2)}, u32[]{:S(2)}) collective-permute-start(bf16[12,2,2,16,256]{4,3,1,0,2:T(8,128)(2,1)} %maximum_select_fusion.4), channel_id=1, source_target_pairs={{0,8},{8,0},{16,24},{24,16},{32,40},{40,32},{48,56},{56,48},{1,9},... | collective-permute-start | bytes 1179656 | tf_op jit(solution)/shard_map/ppermute | solution.py:44
  116.1 24.5 %collective-permute-start.12 = (bf16[12,128,256]{2,1,0:T(8,128)(2,1)S(1)}, bf16[12,128,256]{2,1,0:T(8,128)(2,1)S(1)}, u32[]{:S(2)}, u32[]{:S(2)}) collective-permute-start(bf16[12,128,256]{2,1,0:T(8,128)(2,1)S(1)} %bitcast.154), channel_id=1, source_target_pairs={{0,128},{128,256},{256,384},{384,0},{1,129},{129,257},{257,385},{3... | collective-permute-start | bytes 2359304 | tf_op jit(solution)/shard_map/ppermute | solution.py:23
  119.3 21.3 %collective-permute-start.13 = (bf16[12,128,256]{2,1,0:T(8,128)(2,1)S(1)}, bf16[12,128,256]{2,1,0:T(8,128)(2,1)S(1)}, u32[]{:S(2)}, u32[]{:S(2)}) collective-permute-start(bf16[12,128,256]{2,1,0:T(8,128)(2,1)S(1)} %bitcast.155), channel_id=1, source_target_pairs={{0,384},{128,0},{256,128},{384,256},{1,385},{129,1},{257,129},{385... | collective-permute-start | bytes 2359304 | tf_op jit(solution)/shard_map/ppermute | solution.py:23
  123.0 11.0 %collective-permute-start.10 = (bf16[4,6,64,128]{3,2,1,0:T(8,128)(2,1)S(1)}, bf16[4,6,64,128]{3,2,1,0:T(8,128)(2,1)S(1)}, u32[]{:S(2)}, u32[]{:S(2)}) collective-permute-start(bf16[4,6,64,128]{3,2,1,0:T(8,128)(2,1)S(1)} %slice.139), channel_id=1, source_target_pairs={{0,6},{2,0},{4,2},{6,4},{1,7},{3,1},{5,3},{7,5},{8,14},{10,8},{12,... | collective-permute-start | bytes 1179656 | tf_op jit(solution)/shard_map/ppermute | solution.py:23
  129.7 10.9 %collective-permute-start.11 = (bf16[4,6,64,128]{3,2,1,0:T(8,128)(2,1)S(1)}, bf16[4,6,64,128]{3,2,1,0:T(8,128)(2,1)S(1)}, u32[]{:S(2)}, u32[]{:S(2)}) collective-permute-start(bf16[4,6,64,128]{3,2,1,0:T(8,128)(2,1)S(1)} %slice.140), channel_id=1, source_target_pairs={{0,2},{2,4},{4,6},{6,0},{1,3},{3,5},{5,7},{7,1},{8,10},{10,12},{12... | collective-permute-start | bytes 1179656 | tf_op jit(solution)/shard_map/ppermute | solution.py:23
  140.6 22.8 %collective-permute-start.14 = (bf16[12,64,256]{2,1,0:T(8,128)(2,1)S(1)}, bf16[12,64,256]{2,1,0:T(8,128)(2,1)}, u32[]{:S(2)}, u32[]{:S(2)}) collective-permute-start(bf16[12,64,256]{2,1,0:T(8,128)(2,1)S(1)} %slice.143), channel_id=1, source_target_pairs={{0,384},{128,0},{256,128},{384,256},{1,385},{129,1},{257,129},{385... | collective-permute-start | bytes 1179656 | tf_op jit(solution)/shard_map/ppermute | solution.py:23
  143.0 21.5 %collective-permute-start.17 = (bf16[12,64,256]{2,1,0:T(8,128)(2,1)S(1)}, bf16[12,64,256]{2,1,0:T(8,128)(2,1)}, u32[]{:S(2)}, u32[]{:S(2)}) collective-permute-start(bf16[12,64,256]{2,1,0:T(8,128)(2,1)S(1)} %slice.143), channel_id=1, source_target_pairs={{192,0},{128,64},{320,128},{256,192},{448,256},{384,320},{64,384},... | collective-permute-start | bytes 1179656 | tf_op jit(solution)/shard_map/ppermute | solution.py:90
  145.0 20.5 %collective-permute-start.15 = (bf16[12,64,256]{2,1,0:T(8,128)(2,1)S(1)}, bf16[12,64,256]{2,1,0:T(8,128)(2,1)}, u32[]{:S(2)}, u32[]{:S(2)}) collective-permute-start(bf16[12,64,256]{2,1,0:T(8,128)(2,1)S(1)} %slice.144), channel_id=1, source_target_pairs={{0,128},{128,256},{256,384},{384,0},{1,129},{129,257},{257,385},{3... | collective-permute-start | bytes 1179656 | tf_op jit(solution)/shard_map/ppermute | solution.py:23
  148.4 18.8 %collective-permute-start.18 = (bf16[12,64,256]{2,1,0:T(8,128)(2,1)S(1)}, bf16[12,64,256]{2,1,0:T(8,128)(2,1)S(1)}, u32[]{:S(2)}, u32[]{:S(2)}) collective-permute-start(bf16[12,64,256]{2,1,0:T(8,128)(2,1)S(1)} %slice.144), channel_id=1, source_target_pairs={{448,0},{384,64},{64,128},{0,192},{192,256},{128,320},{320,384},{2... | collective-permute-start | bytes 1179656 | tf_op jit(solution)/shard_map/ppermute | solution.py:91
  153.3 14.2 %collective-permute-start.16 = (bf16[12,3,128,256]{3,2,0,1:T(8,128)(2,1)S(1)}, bf16[12,3,128,256]{3,2,0,1:T(8,128)(2,1)S(1)}, u32[]{:S(2)}, u32[]{:S(2)}) collective-permute-start(bf16[12,3,128,256]{3,2,0,1:T(8,128)(2,1)S(1)} %pad_maximum_fusion.2), channel_id=1, source_target_pairs={{0,64},{64,0},{1,65},{65,1},{2,66},{66,2},{3,67},{67,3},{4,68},{68... | collective-permute-start | bytes 7077896 | tf_op jit(solution)/shard_map/ppermute | solution.py:93
  175.3 15.5 %collective-permute-start.20 = (bf16[4,4,64,256]{3,2,1,0:T(8,128)(2,1)S(1)}, bf16[4,4,64,256]{3,2,1,0:T(8,128)(2,1)S(1)}, u32[]{:S(2)}, u32[]{:S(2)}) collective-permute-start(bf16[4,4,64,256]{3,2,1,0:T(8,128)(2,1)S(1)} %bitcast.173), channel_id=1, source_target_pairs={{0,6},{2,0},{4,2},{6,4},{1,7},{3,1},{5,3},{7,5},{8,14},{10,8},{12,... | collective-permute-start | bytes 1572872 | tf_op jit(solution)/shard_map/ppermute | solution.py:23
  177.3 17.7 %collective-permute-start.22 = (bf16[4,4,64,256]{3,2,1,0:T(8,128)(2,1)S(1)}, bf16[4,4,64,256]{3,2,1,0:T(8,128)(2,1)S(1)}, u32[]{:S(2)}, u32[]{:S(2)}) collective-permute-start(bf16[4,4,64,256]{3,2,1,0:T(8,128)(2,1)S(1)} %bitcast.174), channel_id=1, source_target_pairs={{0,2},{2,4},{4,6},{6,0},{1,3},{3,5},{5,7},{7,1},{8,10},{10,12},{12... | collective-permute-start | bytes 1572872 | tf_op jit(solution)/shard_map/ppermute | solution.py:23
  195.1 10.2 %collective-permute-start.23 = (bf16[4,4,64,128]{3,2,1,0:T(8,128)(2,1)S(1)}, bf16[4,4,64,128]{3,2,1,0:T(8,128)(2,1)S(1)}, u32[]{:S(2)}, u32[]{:S(2)}) collective-permute-start(bf16[4,4,64,128]{3,2,1,0:T(8,128)(2,1)S(1)} %slice.187), channel_id=1, source_target_pairs={{0,2},{2,4},{4,6},{6,0},{1,3},{3,5},{5,7},{7,1},{8,10},{10,12},{12... | collective-permute-start | bytes 786440 | tf_op jit(solution)/shard_map/ppermute | solution.py:23
  207.5 10.5 %collective-permute-start.24 = (bf16[1,4,64,1024]{3,2,1,0:T(8,128)(2,1)S(1)}, bf16[1,4,64,1024]{3,2,1,0:T(8,128)(2,1)S(1)}, u32[]{:S(2)}, u32[]{:S(2)}) collective-permute-start(bf16[1,4,64,1024]{3,2,1,0:T(8,128)(2,1)S(1)} %get-tuple-element.29), channel_id=1, source_target_pairs={{0,64},{64,128},{128,192},{192,256},{256,320},{320,384},{384,448},... | collective-permute-start | bytes 1572872 | tf_op jit(solution)/shard_map/ppermute | solution.py:15
  218.7 35.3 %collective-permute-start.26 = (bf16[4,4,64,128]{3,2,1,0:T(8,128)(2,1)S(1)}, bf16[4,4,64,128]{3,2,1,0:T(8,128)(2,1)S(1)}, u32[]{:S(2)}, u32[]{:S(2)}) collective-permute-start(bf16[4,4,64,128]{3,2,1,0:T(8,128)(2,1)S(1)} %fusion.29), channel_id=1, source_target_pairs={{0,1},{1,0},{2,3},{3,2},{4,5},{5,4},{6,7},{7,6},{8,9},{9,8},{10,11... | collective-permute-start | bytes 786440 | tf_op jit(solution)/shard_map/ppermute | solution.py:153
  (8 other events, 80.6 us)

commit v20 on v18

--- a/solution.py
+++ b/solution.py
@@ -133,15 +133,23 @@
     local_ids = lax.dynamic_slice_in_dim(padded_ids, index * fr_count, fr_count + 2)
     prev_ok = (local_ids[1:-1] == local_ids[:-2]).astype(jnp.float32).reshape(fr_count, 1, 1, 1)
     next_ok = (local_ids[1:-1] == local_ids[2:]).astype(jnp.float32).reshape(fr_count, 1, 1, 1)
-    whole = shift_halo(x_gather(active), FRAME, lax.axis_size(FRAME), 0, 1)
+    own = x_gather(active)
+    fr_n = lax.axis_size(FRAME)
+    rim_low = lax.ppermute(own[-1:], FRAME, [(g, g + 1) for g in range(fr_n - 1)])
+    rim_high = lax.ppermute(own[:1], FRAME, [(g + 1, g) for g in range(fr_n - 1)])
+
+    def apply(frames, tap):
+        return jnp.einsum(
+            "fhwc,cd->fhwd", frames, full_temporal[tap], preferred_element_type=jnp.float32
+        )
+
+    middle = apply(own, 1)
+    before = apply(own[:-1], 0)
+    after = apply(own[1:], 2)
     taps_out = [
-        jnp.einsum(
-            "fhwc,cd->fhwd",
-            whole[tap : tap + fr_count],
-            full_temporal[tap],
-            preferred_element_type=jnp.float32,
-        )
-        for tap in range(3)
+        jnp.concatenate([apply(rim_low, 0), before], axis=0),
+        middle,
+        jnp.concatenate([after, apply(rim_high, 2)], axis=0),
     ]
     total = (
         hidden.astype(jnp.float32)

time: 245 us -> 258 us (1.053)
  the two profiles are of different devices: /device:TPU:1 before, /device:TPU:73 now
where the time goes in v20:
time: 258 us; the launch traced here: 257 us
  starting transfers between devices  122 us (47%)
  waiting for transfers between devices  95.9 us (37%)
  local copies, waits for them, and re-layouts  21.3 us (8%)
  matrix products  8.85 us (3%)
  other arithmetic  8.52 us (3%)
    ppermute x12, starting transfers between devices, ring_shift(): lax.ppermute(block, axis, [(i, (i + step) % count) for i in range(count)])  33.4 us
    ppermute x1, waiting for transfers between devices, body(): returned = lax.ppermute(given, 'cz', SWAP)  26.8 us
    ppermute x1, waiting for transfers between devices, body(): w_block = ordered_pair(weight, lax.ppermute(weight, 'cz', SWAP), high, 2)  19.2 us
    ppermute x12, waiting for transfers between devices, ring_shift(): lax.ppermute(block, axis, [(i, (i + step) % count) for i in range(count)])  19 us
    ppermute x3, starting transfers between devices, xor_stack(): other = lax.ppermute(block, axis, [(i, i ^ bit) for i in range(count)])  16.6 us
    ppermute x1, starting transfers between devices, body(): s_far_low = lax.ppermute(w_right[:, :w_cut], FRAME, from_up)  14.8 us
    ppermute x1, starting transfers between devices, body(): biases = ordered_pair(biases, lax.ppermute(biases, 'cz', SWAP), high, 1)  13.6 us
    ppermute x3, waiting for transfers between devices, xor_stack(): other = lax.ppermute(block, axis, [(i, i ^ bit) for i in range(count)])  12.2 us
  transfers between devices with their start and end apart: 27, of which 13 were waited for; matrix products, arithmetic and copies ran while one was open for 11% of the time, Pallas kernels for 0%

profile of v20, /device:TPU:73, one launch (start us, length us, event | category | flops | bytes accessed | tf_op | source)
XLA Modules:
  0.0 256.9 jit_solution(2381853179770295841)
XLA Ops:
  0.7 13.6 %collective-permute-start.19 = (f32[2,128]{1,0:T(2,128)S(1)}, f32[2,128]{1,0:T(2,128)S(1)}, u32[]{:S(2)}, u32[]{:S(2)}) collective-permute-start(f32[2,128]{1,0:T(2,128)S(1)} %pad_maximum_fusion.4), channel_id=1, source_target_pairs={{0,1},{1,0},{2,3},{3,2},{4,5},{5,4},{6,7},{7,6},{8,9},{9,8},{10,11... | collective-permute-start | bytes 3080 | tf_op jit(solution)/shard_map/ppermute | solution.py:59
  25.0 12.1 %collective-permute-start.4 = (bf16[12,16,128]{2,1,0:T(8,128)(2,1)S(1)}, bf16[12,16,128]{2,1,0:T(8,128)(2,1)S(1)}, u32[]{:S(2)}, u32[]{:S(2)}) collective-permute-start(bf16[12,16,128]{2,1,0:T(8,128)(2,1)S(1)} %constant_dynamic-update-slice_fusion), channel_id=1, source_target_pairs={{0,1},{1,0},{2,3},{3,2},{4,5},{5,4},{6,7},{7,6},{8,9},{9,8},{10,11... | collective-permute-start | bytes 147464 | tf_op jit(solution)/shard_map/ppermute | solution.py:67
  37.9 19.2 %collective-permute-done.4 = bf16[12,16,128]{2,1,0:T(8,128)(2,1)S(1)} collective-permute-done((bf16[12,16,128]{2,1,0:T(8,128)(2,1)S(1)}, bf16[12,16,128]{2,1,0:T(8,128)(2,1)S(1)}, u32[]{:S(2)}, u32[]{:S(2)}) %collective-permute-start.4) | collective-permute-done | bytes 49184 | tf_op jit(solution)/shard_map/ppermute | solution.py:67
  60.2 9.8 %collective-permute-done.3 = bf16[4,1,64,128]{3,2,1,0:T(8,128)(2,1)S(1)} collective-permute-done((bf16[4,1,64,128]{3,2,1,0:T(8,128)(2,1)S(1)}, bf16[4,1,64,128]{3,2,1,0:T(8,128)(2,1)S(1)}, u32[]{:S(2)}, u32[]{:S(2)}) %collective-permute-start.3) | collective-permute-done | bytes 65568 | tf_op jit(solution)/shard_map/ppermute | solution.py:66
  70.0 12.8 %collective-permute-start.7 = (bf16[12,16,256]{2,1,0:T(8,128)(2,1)S(1)}, bf16[12,16,256]{2,1,0:T(8,128)(2,1)S(1)}, u32[]{:S(2)}, u32[]{:S(2)}) collective-permute-start(bf16[12,16,256]{2,1,0:T(8,128)(2,1)S(1)} %maximum_select_fusion.7), channel_id=1, source_target_pairs={{0,32},{8,40},{16,48},{24,56},{32,0},{40,8},{48,16},{56,24},{1,33}... | collective-permute-start | bytes 294920 | tf_op jit(solution)/shard_map/ppermute | solution.py:44
  84.1 3.1 %collective-permute-start.5 = (bf16[4,6,64,256]{3,2,1,0:T(8,128)(2,1)}, bf16[4,6,64,256]{3,2,1,0:T(8,128)(2,1)}, u32[]{:S(2)}, u32[]{:S(2)}) collective-permute-start(bf16[4,6,64,256]{3,2,1,0:T(8,128)(2,1)} %get-tuple-element.28), channel_id=1, source_target_pairs={{0,2},{2,4},{4,6},{6,0},{1,3},{3,5},{5,7},{7,1},{8,10},{10,12},{12... | collective-permute-start | bytes 2359304 | tf_op jit(solution)/shard_map/ppermute | solution.py:23
  87.2 3.4 %collective-permute-start.6 = (bf16[4,6,64,256]{3,2,1,0:T(8,128)(2,1)}, bf16[4,6,64,256]{3,2,1,0:T(8,128)(2,1)}, u32[]{:S(2)}, u32[]{:S(2)}) collective-permute-start(bf16[4,6,64,256]{3,2,1,0:T(8,128)(2,1)} %get-tuple-element.28), channel_id=1, source_target_pairs={{0,6},{2,0},{4,2},{6,4},{1,7},{3,1},{5,3},{7,5},{8,14},{10,8},{12,... | collective-permute-start | bytes 2359304 | tf_op jit(solution)/shard_map/ppermute | solution.py:23
  92.7 5.7 %collective-permute-done.8 = bf16[12,2,16,256]{3,2,1,0:T(8,128)(2,1)S(1)} collective-permute-done((bf16[12,2,16,256]{3,2,1,0:T(8,128)(2,1)S(1)}, bf16[12,2,16,256]{3,2,1,0:T(8,128)(2,1)S(1)}, u32[]{:S(2)}, u32[]{:S(2)}) %collective-permute-start.8) | collective-permute-done | bytes 196640 | tf_op jit(solution)/shard_map/ppermute | solution.py:44
  101.8 6.5 %collective-permute-done.9 = bf16[12,2,2,16,256]{4,3,1,0,2:T(8,128)(2,1)} collective-permute-done((bf16[12,2,2,16,256]{4,3,1,0,2:T(8,128)(2,1)}, bf16[12,2,2,16,256]{4,3,1,0,2:T(8,128)(2,1)}, u32[]{:S(2)}, u32[]{:S(2)}) %collective-permute-start.9) | collective-permute-done | bytes 393248 | tf_op jit(solution)/shard_map/ppermute | solution.py:44
  109.4 3.2 %collective-permute-start.12 = (bf16[12,128,256]{2,1,0:T(8,128)(2,1)S(1)}, bf16[12,128,256]{2,1,0:T(8,128)(2,1)S(1)}, u32[]{:S(2)}, u32[]{:S(2)}) collective-permute-start(bf16[12,128,256]{2,1,0:T(8,128)(2,1)S(1)} %bitcast.153), channel_id=1, source_target_pairs={{0,128},{128,256},{256,384},{384,0},{1,129},{129,257},{257,385},{3... | collective-permute-start | bytes 2359304 | tf_op jit(solution)/shard_map/ppermute | solution.py:23
  115.8 3.2 %collective-permute-start.10 = (bf16[4,6,64,128]{3,2,1,0:T(8,128)(2,1)S(1)}, bf16[4,6,64,128]{3,2,1,0:T(8,128)(2,1)S(1)}, u32[]{:S(2)}, u32[]{:S(2)}) collective-permute-start(bf16[4,6,64,128]{3,2,1,0:T(8,128)(2,1)S(1)} %slice.133), channel_id=1, source_target_pairs={{0,6},{2,0},{4,2},{6,4},{1,7},{3,1},{5,3},{7,5},{8,14},{10,8},{12,... | collective-permute-start | bytes 1179656 | tf_op jit(solution)/shard_map/ppermute | solution.py:23
  124.6 5.1 %collective-permute-done.11 = bf16[4,6,64,128]{3,2,1,0:T(8,128)(2,1)S(1)} collective-permute-done((bf16[4,6,64,128]{3,2,1,0:T(8,128)(2,1)S(1)}, bf16[4,6,64,128]{3,2,1,0:T(8,128)(2,1)S(1)}, u32[]{:S(2)}, u32[]{:S(2)}) %collective-permute-start.11) | collective-permute-done | bytes 393248 | tf_op jit(solution)/shard_map/ppermute | solution.py:23
  129.8 3.7 %collective-permute-start.14 = (bf16[12,64,256]{2,1,0:T(8,128)(2,1)S(1)}, bf16[12,64,256]{2,1,0:T(8,128)(2,1)}, u32[]{:S(2)}, u32[]{:S(2)}) collective-permute-start(bf16[12,64,256]{2,1,0:T(8,128)(2,1)S(1)} %slice.137), channel_id=1, source_target_pairs={{0,384},{128,0},{256,128},{384,256},{1,385},{129,1},{257,129},{385... | collective-permute-start | bytes 1179656 | tf_op jit(solution)/shard_map/ppermute | solution.py:23
  133.4 14.8 %collective-permute-start.17 = (bf16[12,64,256]{2,1,0:T(8,128)(2,1)S(1)}, bf16[12,64,256]{2,1,0:T(8,128)(2,1)}, u32[]{:S(2)}, u32[]{:S(2)}) collective-permute-start(bf16[12,64,256]{2,1,0:T(8,128)(2,1)S(1)} %slice.137), channel_id=1, source_target_pairs={{192,0},{128,64},{320,128},{256,192},{448,256},{384,320},{64,384},... | collective-permute-start | bytes 1179656 | tf_op jit(solution)/shard_map/ppermute | solution.py:90
  168.9 6.3 %convert_add_fusion = (f32[4,32,9,256]{3,1,2,0:T(8,128)S(1)}, bf16[4,32,9,256]{3,1,2,0:T(8,128)(2,1)S(1)}) fusion(f32[256]{0:T(256)S(1)} %bitcast.183, f32[256]{0:T(256)S(1)} %bitcast.184, bf16[3,3,1024,256]{3,2,1,0:T(8,128)(2,1)S(1)} %bitcast.161, bf16[6,4,8,11,1024]{4,1,3,2,0:T(4,128)(2,1)S(1)} %fusion.1, pred[32,9]{0,1:T(8,128)(4,1)S(1)} %copy-done.4), kind=kOutput, calls=%fused_computation.9 | convolution fusion | flops 5438767104 | bytes 10815776 | tf_op jit(solution)/shard_map/conv_general_dilated | solution.py:120
  177.9 3.6 %collective-permute-start.22 = (bf16[4,4,64,256]{3,2,1,0:T(8,128)(2,1)S(1)}, bf16[4,4,64,256]{3,2,1,0:T(8,128)(2,1)S(1)}, u32[]{:S(2)}, u32[]{:S(2)}) collective-permute-start(bf16[4,4,64,256]{3,2,1,0:T(8,128)(2,1)S(1)} %bitcast.175), channel_id=1, source_target_pairs={{0,2},{2,4},{4,6},{6,0},{1,3},{3,5},{5,7},{7,1},{8,10},{10,12},{12... | collective-permute-start | bytes 1572872 | tf_op jit(solution)/shard_map/ppermute | solution.py:23
  181.7 8.2 %collective-permute-done.20 = bf16[4,4,64,256]{3,2,1,0:T(8,128)(2,1)S(1)} collective-permute-done((bf16[4,4,64,256]{3,2,1,0:T(8,128)(2,1)S(1)}, bf16[4,4,64,256]{3,2,1,0:T(8,128)(2,1)S(1)}, u32[]{:S(2)}, u32[]{:S(2)}) %collective-permute-start.20) | collective-permute-done | bytes 524320 | tf_op jit(solution)/shard_map/ppermute | solution.py:23
  190.0 3.4 %collective-permute-start.21 = (bf16[4,4,64,128]{3,2,1,0:T(8,128)(2,1)S(1)}, bf16[4,4,64,128]{3,2,1,0:T(8,128)(2,1)S(1)}, u32[]{:S(2)}, u32[]{:S(2)}) collective-permute-start(bf16[4,4,64,128]{3,2,1,0:T(8,128)(2,1)S(1)} %slice.180), channel_id=1, source_target_pairs={{0,6},{2,0},{4,2},{6,4},{1,7},{3,1},{5,3},{7,5},{8,14},{10,8},{12,... | collective-permute-start | bytes 786440 | tf_op jit(solution)/shard_map/ppermute | solution.py:23
  197.5 4.2 %collective-permute-done.23 = bf16[4,4,64,128]{3,2,1,0:T(8,128)(2,1)S(1)} collective-permute-done((bf16[4,4,64,128]{3,2,1,0:T(8,128)(2,1)S(1)}, bf16[4,4,64,128]{3,2,1,0:T(8,128)(2,1)S(1)}, u32[]{:S(2)}, u32[]{:S(2)}) %collective-permute-start.23) | collective-permute-done | bytes 262176 | tf_op jit(solution)/shard_map/ppermute | solution.py:23
  202.0 6.6 %collective-permute-start.24 = (bf16[1,4,64,1024]{3,2,1,0:T(8,128)(2,1)S(1)}, bf16[1,4,64,1024]{3,2,1,0:T(8,128)(2,1)S(1)}, u32[]{:S(2)}, u32[]{:S(2)}) collective-permute-start(bf16[1,4,64,1024]{3,2,1,0:T(8,128)(2,1)S(1)} %get-tuple-element.30), channel_id=1, source_target_pairs={{0,64},{64,128},{128,192},{192,256},{256,320},{320,384},{384,448},... | collective-permute-start | bytes 1572872 | tf_op jit(solution)/shard_map/ppermute | solution.py:138
  211.7 3.0 %collective-permute-done.24 = bf16[1,4,64,1024]{3,2,1,0:T(8,128)(2,1)S(1)} collective-permute-done((bf16[1,4,64,1024]{3,2,1,0:T(8,128)(2,1)S(1)}, bf16[1,4,64,1024]{3,2,1,0:T(8,128)(2,1)S(1)}, u32[]{:S(2)}, u32[]{:S(2)}) %collective-permute-start.24) | collective-permute-done | bytes 524320 | tf_op jit(solution)/shard_map/ppermute | solution.py:138
  215.0 4.1 %collective-permute-done.25 = bf16[1,4,64,1024]{3,2,1,0:T(8,128)(2,1)S(1)} collective-permute-done((bf16[1,4,64,1024]{3,2,1,0:T(8,128)(2,1)S(1)}, bf16[1,4,64,1024]{3,2,1,0:T(8,128)(2,1)S(1)}, u32[]{:S(2)}, u32[]{:S(2)}) %collective-permute-start.25) | collective-permute-done | bytes 524320 | tf_op jit(solution)/shard_map/ppermute | solution.py:139
  220.3 9.0 %collective-permute-start.26 = (bf16[4,4,64,128]{3,2,1,0:T(8,128)(2,1)S(1)}, bf16[4,4,64,128]{3,2,1,0:T(8,128)(2,1)S(1)}, u32[]{:S(2)}, u32[]{:S(2)}) collective-permute-start(bf16[4,4,64,128]{3,2,1,0:T(8,128)(2,1)S(1)} %get-tuple-element.36), channel_id=1, source_target_pairs={{0,1},{1,0},{2,3},{3,2},{4,5},{5,4},{6,7},{7,6},{8,9},{9,8},{10,11... | collective-permute-start | bytes 786440 | tf_op jit(solution)/shard_map/ppermute | solution.py:163
  229.3 26.8 %collective-permute-done.26 = bf16[4,4,64,128]{3,2,1,0:T(8,128)(2,1)S(1)} collective-permute-done((bf16[4,4,64,128]{3,2,1,0:T(8,128)(2,1)S(1)}, bf16[4,4,64,128]{3,2,1,0:T(8,128)(2,1)S(1)}, u32[]{:S(2)}, u32[]{:S(2)}) %collective-permute-start.26) | collective-permute-done | bytes 262176 | tf_op jit(solution)/shard_map/ppermute | solution.py:163
  (120 shorter events, 64.9 us)
Async XLA Ops:
  0.7 101.1 %collective-permute-start.19 = (f32[2,128]{1,0:T(2,128)S(1)}, f32[2,128]{1,0:T(2,128)S(1)}, u32[]{:S(2)}, u32[]{:S(2)}) collective-permute-start(f32[2,128]{1,0:T(2,128)S(1)} %pad_maximum_fusion.4), channel_id=1, source_target_pairs={{0,1},{1,0},{2,3},{3,2},{4,5},{5,4},{6,7},{7,6},{8,9},{9,8},{10,11... | collective-permute-start | bytes 3080 | tf_op jit(solution)/shard_map/ppermute | solution.py:59
  15.3 43.8 %collective-permute-start.1 = (bf16[4,1,64,128]{3,2,1,0:T(8,128)(2,1)S(1)}, bf16[4,1,64,128]{3,2,1,0:T(8,128)(2,1)S(1)}, u32[]{:S(2)}, u32[]{:S(2)}) collective-permute-start(bf16[4,1,64,128]{3,2,1,0:T(8,128)(2,1)S(1)} %get-tuple-element.39), channel_id=1, source_target_pairs={{8,0},{16,8},{24,16},{32,24},{40,32},{48,40},{56,48},{9,1},{17,9},... | collective-permute-start | bytes 196616 | tf_op jit(solution)/shard_map/ppermute | solution.py:18
  17.9 41.1 %collective-permute-start = (bf16[4,1,64,128]{3,2,1,0:T(8,128)(2,1)S(1)}, bf16[4,1,64,128]{3,2,1,0:T(8,128)(2,1)S(1)}, u32[]{:S(2)}, u32[]{:S(2)}) collective-permute-start(bf16[4,1,64,128]{3,2,1,0:T(8,128)(2,1)S(1)} %get-tuple-element.40), channel_id=1, source_target_pairs={{0,8},{8,16},{16,24},{24,32},{32,40},{40,48},{48,56},{1,9},{9,17},... | collective-permute-start | bytes 196616 | tf_op jit(solution)/shard_map/ppermute | solution.py:15
  21.6 48.4 %collective-permute-start.2 = (bf16[4,5,64,128]{3,2,1,0:T(8,128)(2,1)S(1)}, bf16[4,5,64,128]{3,2,1,0:T(8,128)(2,1)S(1)}, u32[]{:S(2)}, u32[]{:S(2)}) collective-permute-start(bf16[4,5,64,128]{3,2,1,0:T(8,128)(2,1)S(1)} %constant_dynamic-slice_fusion.4), channel_id=1, source_target_pairs={{0,1},{1,0},{2,3},{3,2},{4,5},{5,4},{6,7},{7,6},{8,9},{9,8},{10,11... | collective-permute-start | bytes 983048 | tf_op jit(solution)/shard_map/ppermute | solution.py:62
  25.0 32.1 %collective-permute-start.4 = (bf16[12,16,128]{2,1,0:T(8,128)(2,1)S(1)}, bf16[12,16,128]{2,1,0:T(8,128)(2,1)S(1)}, u32[]{:S(2)}, u32[]{:S(2)}) collective-permute-start(bf16[12,16,128]{2,1,0:T(8,128)(2,1)S(1)} %constant_dynamic-update-slice_fusion), channel_id=1, source_target_pairs={{0,1},{1,0},{2,3},{3,2},{4,5},{5,4},{6,7},{7,6},{8,9},{9,8},{10,11... | collective-permute-start | bytes 147464 | tf_op jit(solution)/shard_map/ppermute | solution.py:67
  57.1 12.9 %collective-permute-start.3 = (bf16[4,1,64,128]{3,2,1,0:T(8,128)(2,1)S(1)}, bf16[4,1,64,128]{3,2,1,0:T(8,128)(2,1)S(1)}, u32[]{:S(2)}, u32[]{:S(2)}) collective-permute-start(bf16[4,1,64,128]{3,2,1,0:T(8,128)(2,1)S(1)} %get-tuple-element.38), channel_id=1, source_target_pairs={{1,8},{9,16},{17,24},{25,32},{33,40},{41,48},{49,56},{8,1},{16,9},... | collective-permute-start | bytes 196616 | tf_op jit(solution)/shard_map/ppermute | solution.py:66
  70.0 20.6 %collective-permute-start.7 = (bf16[12,16,256]{2,1,0:T(8,128)(2,1)S(1)}, bf16[12,16,256]{2,1,0:T(8,128)(2,1)S(1)}, u32[]{:S(2)}, u32[]{:S(2)}) collective-permute-start(bf16[12,16,256]{2,1,0:T(8,128)(2,1)S(1)} %maximum_select_fusion.7), channel_id=1, source_target_pairs={{0,32},{8,40},{16,48},{24,56},{32,0},{40,8},{48,16},{56,24},{1,33}... | collective-permute-start | bytes 294920 | tf_op jit(solution)/shard_map/ppermute | solution.py:44
  84.1 25.3 %collective-permute-start.5 = (bf16[4,6,64,256]{3,2,1,0:T(8,128)(2,1)}, bf16[4,6,64,256]{3,2,1,0:T(8,128)(2,1)}, u32[]{:S(2)}, u32[]{:S(2)}) collective-permute-start(bf16[4,6,64,256]{3,2,1,0:T(8,128)(2,1)} %get-tuple-element.28), channel_id=1, source_target_pairs={{0,2},{2,4},{4,6},{6,0},{1,3},{3,5},{5,7},{7,1},{8,10},{10,12},{12... | collective-permute-start | bytes 2359304 | tf_op jit(solution)/shard_map/ppermute | solution.py:23
  87.2 22.2 %collective-permute-start.6 = (bf16[4,6,64,256]{3,2,1,0:T(8,128)(2,1)}, bf16[4,6,64,256]{3,2,1,0:T(8,128)(2,1)}, u32[]{:S(2)}, u32[]{:S(2)}) collective-permute-start(bf16[4,6,64,256]{3,2,1,0:T(8,128)(2,1)} %get-tuple-element.28), channel_id=1, source_target_pairs={{0,6},{2,0},{4,2},{6,4},{1,7},{3,1},{5,3},{7,5},{8,14},{10,8},{12,... | collective-permute-start | bytes 2359304 | tf_op jit(solution)/shard_map/ppermute | solution.py:23
  99.2 9.1 %collective-permute-start.9 = (bf16[12,2,2,16,256]{4,3,1,0,2:T(8,128)(2,1)}, bf16[12,2,2,16,256]{4,3,1,0,2:T(8,128)(2,1)}, u32[]{:S(2)}, u32[]{:S(2)}) collective-permute-start(bf16[12,2,2,16,256]{4,3,1,0,2:T(8,128)(2,1)} %maximum_select_fusion.4), channel_id=1, source_target_pairs={{0,8},{8,0},{16,24},{24,16},{32,40},{40,32},{48,56},{56,48},{1,9},... | collective-permute-start | bytes 1179656 | tf_op jit(solution)/shard_map/ppermute | solution.py:44
  109.4 20.3 %collective-permute-start.12 = (bf16[12,128,256]{2,1,0:T(8,128)(2,1)S(1)}, bf16[12,128,256]{2,1,0:T(8,128)(2,1)S(1)}, u32[]{:S(2)}, u32[]{:S(2)}) collective-permute-start(bf16[12,128,256]{2,1,0:T(8,128)(2,1)S(1)} %bitcast.153), channel_id=1, source_target_pairs={{0,128},{128,256},{256,384},{384,0},{1,129},{129,257},{257,385},{3... | collective-permute-start | bytes 2359304 | tf_op jit(solution)/shard_map/ppermute | solution.py:23
  112.6 17.1 %collective-permute-start.13 = (bf16[12,128,256]{2,1,0:T(8,128)(2,1)S(1)}, bf16[12,128,256]{2,1,0:T(8,128)(2,1)S(1)}, u32[]{:S(2)}, u32[]{:S(2)}) collective-permute-start(bf16[12,128,256]{2,1,0:T(8,128)(2,1)S(1)} %bitcast.154), channel_id=1, source_target_pairs={{0,384},{128,0},{256,128},{384,256},{1,385},{129,1},{257,129},{385... | collective-permute-start | bytes 2359304 | tf_op jit(solution)/shard_map/ppermute | solution.py:23
  115.8 8.8 %collective-permute-start.10 = (bf16[4,6,64,128]{3,2,1,0:T(8,128)(2,1)S(1)}, bf16[4,6,64,128]{3,2,1,0:T(8,128)(2,1)S(1)}, u32[]{:S(2)}, u32[]{:S(2)}) collective-permute-start(bf16[4,6,64,128]{3,2,1,0:T(8,128)(2,1)S(1)} %slice.133), channel_id=1, source_target_pairs={{0,6},{2,0},{4,2},{6,4},{1,7},{3,1},{5,3},{7,5},{8,14},{10,8},{12,... | collective-permute-start | bytes 1179656 | tf_op jit(solution)/shard_map/ppermute | solution.py:23
  120.0 9.7 %collective-permute-start.11 = (bf16[4,6,64,128]{3,2,1,0:T(8,128)(2,1)S(1)}, bf16[4,6,64,128]{3,2,1,0:T(8,128)(2,1)S(1)}, u32[]{:S(2)}, u32[]{:S(2)}) collective-permute-start(bf16[4,6,64,128]{3,2,1,0:T(8,128)(2,1)S(1)} %slice.134), channel_id=1, source_target_pairs={{0,2},{2,4},{4,6},{6,0},{1,3},{3,5},{5,7},{7,1},{8,10},{10,12},{12... | collective-permute-start | bytes 1179656 | tf_op jit(solution)/shard_map/ppermute | solution.py:23
  129.8 33.1 %collective-permute-start.14 = (bf16[12,64,256]{2,1,0:T(8,128)(2,1)S(1)}, bf16[12,64,256]{2,1,0:T(8,128)(2,1)}, u32[]{:S(2)}, u32[]{:S(2)}) collective-permute-start(bf16[12,64,256]{2,1,0:T(8,128)(2,1)S(1)} %slice.137), channel_id=1, source_target_pairs={{0,384},{128,0},{256,128},{384,256},{1,385},{129,1},{257,129},{385... | collective-permute-start | bytes 1179656 | tf_op jit(solution)/shard_map/ppermute | solution.py:23
  133.4 30.5 %collective-permute-start.17 = (bf16[12,64,256]{2,1,0:T(8,128)(2,1)S(1)}, bf16[12,64,256]{2,1,0:T(8,128)(2,1)}, u32[]{:S(2)}, u32[]{:S(2)}) collective-permute-start(bf16[12,64,256]{2,1,0:T(8,128)(2,1)S(1)} %slice.137), channel_id=1, source_target_pairs={{192,0},{128,64},{320,128},{256,192},{448,256},{384,320},{64,384},... | collective-permute-start | bytes 1179656 | tf_op jit(solution)/shard_map/ppermute | solution.py:90
  148.2 16.7 %collective-permute-start.15 = (bf16[12,64,256]{2,1,0:T(8,128)(2,1)S(1)}, bf16[12,64,256]{2,1,0:T(8,128)(2,1)}, u32[]{:S(2)}, u32[]{:S(2)}) collective-permute-start(bf16[12,64,256]{2,1,0:T(8,128)(2,1)S(1)} %slice.138), channel_id=1, source_target_pairs={{0,128},{128,256},{256,384},{384,0},{1,129},{129,257},{257,385},{3... | collective-permute-start | bytes 1179656 | tf_op jit(solution)/shard_map/ppermute | solution.py:23
  150.1 17.7 %collective-permute-start.18 = (bf16[12,64,256]{2,1,0:T(8,128)(2,1)S(1)}, bf16[12,64,256]{2,1,0:T(8,128)(2,1)S(1)}, u32[]{:S(2)}, u32[]{:S(2)}) collective-permute-start(bf16[12,64,256]{2,1,0:T(8,128)(2,1)S(1)} %slice.138), channel_id=1, source_target_pairs={{448,0},{384,64},{64,128},{0,192},{192,256},{128,320},{320,384},{2... | collective-permute-start | bytes 1179656 | tf_op jit(solution)/shard_map/ppermute | solution.py:91
  152.5 15.6 %collective-permute-start.16 = (bf16[12,3,128,256]{3,2,0,1:T(8,128)(2,1)S(1)}, bf16[12,3,128,256]{3,2,0,1:T(8,128)(2,1)S(1)}, u32[]{:S(2)}, u32[]{:S(2)}) collective-permute-start(bf16[12,3,128,256]{3,2,0,1:T(8,128)(2,1)S(1)} %pad_maximum_fusion), channel_id=1, source_target_pairs={{0,64},{64,0},{1,65},{65,1},{2,66},{66,2},{3,67},{67,3},{4,68},{68... | collective-permute-start | bytes 7077896 | tf_op jit(solution)/shard_map/ppermute | solution.py:93
  175.9 14.0 %collective-permute-start.20 = (bf16[4,4,64,256]{3,2,1,0:T(8,128)(2,1)S(1)}, bf16[4,4,64,256]{3,2,1,0:T(8,128)(2,1)S(1)}, u32[]{:S(2)}, u32[]{:S(2)}) collective-permute-start(bf16[4,4,64,256]{3,2,1,0:T(8,128)(2,1)S(1)} %bitcast.174), channel_id=1, source_target_pairs={{0,6},{2,0},{4,2},{6,4},{1,7},{3,1},{5,3},{7,5},{8,14},{10,8},{12,... | collective-permute-start | bytes 1572872 | tf_op jit(solution)/shard_map/ppermute | solution.py:23
  177.9 15.5 %collective-permute-start.22 = (bf16[4,4,64,256]{3,2,1,0:T(8,128)(2,1)S(1)}, bf16[4,4,64,256]{3,2,1,0:T(8,128)(2,1)S(1)}, u32[]{:S(2)}, u32[]{:S(2)}) collective-permute-start(bf16[4,4,64,256]{3,2,1,0:T(8,128)(2,1)S(1)} %bitcast.175), channel_id=1, source_target_pairs={{0,2},{2,4},{4,6},{6,0},{1,3},{3,5},{5,7},{7,1},{8,10},{10,12},{12... | collective-permute-start | bytes 1572872 | tf_op jit(solution)/shard_map/ppermute | solution.py:23
  202.0 12.7 %collective-permute-start.24 = (bf16[1,4,64,1024]{3,2,1,0:T(8,128)(2,1)S(1)}, bf16[1,4,64,1024]{3,2,1,0:T(8,128)(2,1)S(1)}, u32[]{:S(2)}, u32[]{:S(2)}) collective-permute-start(bf16[1,4,64,1024]{3,2,1,0:T(8,128)(2,1)S(1)} %get-tuple-element.30), channel_id=1, source_target_pairs={{0,64},{64,128},{128,192},{192,256},{256,320},{320,384},{384,448},... | collective-permute-start | bytes 1572872 | tf_op jit(solution)/shard_map/ppermute | solution.py:138
  208.6 10.5 %collective-permute-start.25 = (bf16[1,4,64,1024]{3,2,1,0:T(8,128)(2,1)S(1)}, bf16[1,4,64,1024]{3,2,1,0:T(8,128)(2,1)S(1)}, u32[]{:S(2)}, u32[]{:S(2)}) collective-permute-start(bf16[1,4,64,1024]{3,2,1,0:T(8,128)(2,1)S(1)} %get-tuple-element.29), channel_id=1, source_target_pairs={{64,0},{128,64},{192,128},{256,192},{320,256},{384,320},{448,384},... | collective-permute-start | bytes 1572872 | tf_op jit(solution)/shard_map/ppermute | solution.py:139
  220.3 35.8 %collective-permute-start.26 = (bf16[4,4,64,128]{3,2,1,0:T(8,128)(2,1)S(1)}, bf16[4,4,64,128]{3,2,1,0:T(8,128)(2,1)S(1)}, u32[]{:S(2)}, u32[]{:S(2)}) collective-permute-start(bf16[4,4,64,128]{3,2,1,0:T(8,128)(2,1)S(1)} %get-tuple-element.36), channel_id=1, source_target_pairs={{0,1},{1,0},{2,3},{3,2},{4,5},{5,4},{6,7},{7,6},{8,9},{9,8},{10,11... | collective-permute-start | bytes 786440 | tf_op jit(solution)/shard_map/ppermute | solution.py:163
  (8 other events, 78.5 us)
